TPU v7x, 256 devices: a whole 4x4x8 slice. The times are simulated.
256 devices in a mesh: grid: 2 (over x_hi), prow: 4 (over x_lo, core), pcol: 32 (over z, y).
Axes of the slice: x: 4 (x_hi: 2, x_lo: 2; x = x_hi * 2 + x_lo), y: 4, z: 8, core: 2. Of those that a mesh axis runs over, the one named last changes fastest.
Arguments:
- sub_rhs: float32 [8, 3, 64, 3072], P('grid', None, None, 'prow'), may hold values from -6 to 6
- root_rhs: float32 [64, 3072], P(None, 'prow'), may hold values from -6 to 6
- diag_inverse: bfloat16 [3, 3072, 24576], P(None, 'prow', ('grid', 'pcol'))
- root_inverse: bfloat16 [3072, 3072], P('prow', 'grid')
- inner_factor: bfloat16 [3, 24576, 3072], P(None, ('grid', 'pcol'), 'prow'), may hold values from -0.078125 to 0.078125
- inner_mask: int32 [3, 192, 24], P(None, ('grid', 'pcol')), may hold values 0 or 1
- root_factor: bfloat16 [3, 24576, 3072], P(None, ('grid', 'pcol'), 'prow'), may hold values from -0.078125 to 0.078125
- root_mask: int32 [3, 192, 24], P(None, ('grid', 'pcol')), may hold values 0 or 1
Outputs:
- sub_solution: float32 [3, 64, 24576], P(None, None, ('grid', 'pcol'))
- root_solution: float32 [64, 3072], P(None, 'grid')
Inputs may be any that keep to these rules, and one draw needn't show every extreme that they name: `inner_mask`: 1 keeps a tile of 128 x 128 entries, 0 makes it zero. `root_mask`: 1 keeps a tile of 128 x 128 entries, 0 makes it zero.
All inputs are finite; a program needn't handle non-finite values. No bound on the sum of `inner_mask` or of `root_mask` on one device may be relied on, other than what follows from the above.
Results may differ from a plain program's by a relative error of at most 0.0065.
Values sent between devices are 32-bit elements; how exact they have to be, the bound alone decides.
No kernel may reach another device: no remote copies, remote signals or barrier semaphores. Data moves between devices by JAX's collectives and lax.ppermute only.
A program may use at most 64 MiB of HBM per device.

v0:
```python
import jax
import jax.numpy as jnp
from jax import lax
from jax.sharding import PartitionSpec as P

NS = 3072
LEVELS = 3
TILE = 128


def from_everyone(shard, axis):
    count = lax.axis_size(axis)
    return lax.all_to_all(
        jnp.broadcast_to(shard[None], (count, *shard.shape)), axis, 0, 0, tiled=True
    )


def taken_together(shard, axis):
    return from_everyone(shard, axis).sum(axis=0)


def from_partner(shard, axis, bit):
    return lax.ppermute(shard, axis, [(i, i ^ 1 << bit) for i in range(lax.axis_size(axis))])


def cut_along(shard, dim, count):
    lengths = shard.shape
    blocks = shard.reshape(*lengths[:dim], count, lengths[dim] // count, *lengths[dim + 1 :])
    return jnp.moveaxis(blocks, dim, 0)


def summed_on_arrival(shard, axis, dim):
    blocks = cut_along(shard, dim, lax.axis_size(axis))
    arrived = lax.all_to_all(blocks, axis, split_axis=0, concat_axis=0, tiled=True)
    return arrived.sum(axis=0)


def rows_for(lines, count):
    spare = -len(lines) % count
    return jnp.pad(lines, [(0, spare)] + [(0, 0)] * (lines.ndim - 1))


def joined_along(blocks, dim):
    blocks = jnp.moveaxis(blocks, 0, dim)
    lengths = blocks.shape
    return blocks.reshape(*lengths[:dim], lengths[dim] * lengths[dim + 1], *lengths[dim + 2 :])


def gather_directly(shard, axis, dim):
    return joined_along(from_everyone(shard, axis), dim)


def total_of(shard, axes):
    lines = shard.reshape(-1, shard.shape[-1])
    own = summed_on_arrival(rows_for(lines, lax.axis_size(axes)), axes, 0)
    whole = gather_directly(own, axes, 0)
    return whole[: len(lines)].reshape(shard.shape)


def selector(positions, count):
    return (positions[:, None] // TILE == jnp.arange(count)[None, :]).astype(jnp.float32)


def masked(factor, mask, row_select, col_select):
    expanded = jnp.dot(jnp.dot(row_select, mask.astype(jnp.float32)), col_select.T)
    return factor * expanded.astype(jnp.bfloat16)


def solve_block(residual, inverse):
    partial_sum = jnp.dot(
        residual.astype(jnp.bfloat16), inverse, preferred_element_type=jnp.float32
    )
    return taken_together(partial_sum, "prow")


def group_sum(partial_sum, owners):
    summed = partial_sum
    for bit_number in range(owners.bit_length() - 1):
        summed = summed + from_partner(summed, "pcol", bit_number)
    return summed


def shards(
    sub_rhs, root_rhs, diag_inverse, root_inverse, inner_factor, inner_mask, root_factor, root_mask
):
    rows_here = inner_factor.shape[1]
    out_cols = inner_factor.shape[2]
    owners = NS // rows_here
    own_tree = lax.axis_index("pcol") // owners
    col_positions = lax.axis_index("prow") * out_cols + jnp.arange(out_cols)
    row_select = selector(jnp.arange(rows_here), inner_mask.shape[1])
    col_select = selector(col_positions, inner_mask.shape[2])
    own_rhs = lax.dynamic_index_in_dim(sub_rhs, own_tree, 0, keepdims=False)
    kept = []
    solved_all = []
    pair = 0
    for level in range(LEVELS):
        residual = own_rhs[level]
        if level > 0:
            local_update = jnp.zeros(residual.shape, jnp.float32)
            for source in range(level):
                factor_tile = masked(inner_factor[pair], inner_mask[pair], row_select, col_select)
                local_update = local_update + jnp.dot(
                    kept[source], factor_tile, preferred_element_type=jnp.float32
                )
                pair += 1
            residual = residual - group_sum(local_update, owners)
        solved = solve_block(residual, diag_inverse[level])
        solved_all.append(solved)
        kept.append(solved.astype(jnp.bfloat16))
    root_local = jnp.zeros(root_rhs.shape, jnp.float32)
    for source in range(LEVELS):
        factor_tile = masked(root_factor[source], root_mask[source], row_select, col_select)
        root_local = root_local + jnp.dot(
            kept[source], factor_tile, preferred_element_type=jnp.float32
        )
    root_update = total_of(root_local, ("grid", "pcol"))
    root_solution = solve_block(root_rhs - root_update, root_inverse)
    return (jnp.stack(solved_all), root_solution)


def solution(mesh):
    return jax.shard_map(
        shards,
        mesh=mesh,
        in_specs=(
            P("grid", None, None, "prow"),
            P(None, "prow"),
            P(None, "prow", ("grid", "pcol")),
            P("prow", "grid"),
            P(None, ("grid", "pcol"), "prow"),
            P(None, ("grid", "pcol"), None),
            P(None, ("grid", "pcol"), "prow"),
            P(None, ("grid", "pcol"), None),
        ),
        out_specs=(P(None, None, ("grid", "pcol")), P(None, "grid")),
        check_vma=False,
    )
```

profile of v0, /device:TPU:1, one launch (start us, length us, event | category | flops | bytes accessed | tf_op | source)
XLA Modules:
  0.0 161.2 jit_solution(4230962559205158833)
XLA Ops:
  0.6 0.0 copy-start
  0.6 0.0 copy-start.2
  0.7 1.5 fusion.26
  2.2 0.8 broadcast_in_dim.10
  3.0 6.7 %all-to-all-start = ((f32[4,64,384]{2,1,0:T(8,128)}), f32[4,64,384]{2,1,0:T(8,128)S(1)}, u32[]{:S(2)}, u32[]{:S(2)}) async-start(f32[4,64,384]{2,1,0:T(8,128)} %broadcast_in_dim.10), calls=%async_computation | async-start | bytes 786432 | tf_op jit(solution)/shard_map/all_to_all | solution.py:13
  9.7 0.0 copy-done.2
  9.7 0.2 fusion.59
  9.9 6.3 %all-to-all-done = f32[4,64,384]{2,1,0:T(8,128)S(1)} async-done(((f32[4,64,384]{2,1,0:T(8,128)}), f32[4,64,384]{2,1,0:T(8,128)S(1)}, u32[]{:S(2)}, u32[]{:S(2)}) %all-to-all-start) | async-done | bytes 393248 | tf_op jit(solution)/shard_map/all_to_all | solution.py:13
  16.3 1.7 %fusion.11 = f32[64,768]{1,0:T(8,128)S(1)} fusion(bf16[384,24]{0,1:T(8,128)(2,1)S(1)} %fusion.59, bf16[3,384,768]{2,1,0:T(8,128)(2,1)} %param.12, s32[768]{0:T(1024)S(1)} %add_select_fusion, f32[64,384]{1,0:T(8,128)S(1)} %reduce_sum.45), kind=kOutput, calls=%fused_computation.17 | convolution fusion | flops 52242432 | bytes 906240 | tf_op jit(solution)/shard_map/dot_general | solution.py:103
  17.9 0.1 collective-permute-start
  18.0 5.5 %collective-permute-done = f32[64,768]{1,0:T(8,128)S(1)} collective-permute-done((f32[64,768]{1,0:T(8,128)S(1)}, f32[64,768]{1,0:T(8,128)S(1)}, u32[]{:S(2)}, u32[]{:S(2)}) %collective-permute-start) | collective-permute-done | bytes 196640 | tf_op jit(solution)/shard_map/ppermute | solution.py:23
  23.6 1.3 collective-permute-start.1
  24.9 4.9 %collective-permute-done.1 = f32[64,768]{1,0:T(8,128)S(1)} collective-permute-done((f32[64,768]{1,0:T(8,128)S(1)}, f32[64,768]{1,0:T(8,128)S(1)}, u32[]{:S(2)}, u32[]{:S(2)}) %collective-permute-start.1) | collective-permute-done | bytes 196640 | tf_op jit(solution)/shard_map/ppermute | solution.py:23
  29.7 0.1 collective-permute-start.2
  29.8 4.5 %collective-permute-done.2 = f32[64,768]{1,0:T(8,128)S(1)} collective-permute-done((f32[64,768]{1,0:T(8,128)S(1)}, f32[64,768]{1,0:T(8,128)S(1)}, u32[]{:S(2)}, u32[]{:S(2)}) %collective-permute-start.2) | collective-permute-done | bytes 196640 | tf_op jit(solution)/shard_map/ppermute | solution.py:23
  34.3 1.4 fusion.23
  35.7 0.8 broadcast_in_dim.11
  36.5 0.0 copy-start.3
  36.5 7.6 %all-to-all-start.1 = ((f32[4,64,384]{2,1,0:T(8,128)}), f32[4,64,384]{2,1,0:T(8,128)S(1)}, u32[]{:S(2)}, u32[]{:S(2)}) async-start(f32[4,64,384]{2,1,0:T(8,128)} %broadcast_in_dim.11), calls=%async_computation.1 | async-start | bytes 786432 | tf_op jit(solution)/shard_map/all_to_all | solution.py:13
  44.1 0.2 fusion.57
  44.4 0.3 fusion.58
  44.6 6.1 %all-to-all-done.1 = f32[4,64,384]{2,1,0:T(8,128)S(1)} async-done(((f32[4,64,384]{2,1,0:T(8,128)}), f32[4,64,384]{2,1,0:T(8,128)S(1)}, u32[]{:S(2)}, u32[]{:S(2)}) %all-to-all-start.1) | async-done | bytes 393248 | tf_op jit(solution)/shard_map/all_to_all | solution.py:13
  50.7 1.7 %fusion.9 = f32[64,768]{1,0:T(8,128)S(1)} fusion(bf16[384,24]{0,1:T(8,128)(2,1)S(1)} %fusion.57, bf16[3,384,768]{2,1,0:T(8,128)(2,1)} %param.12, s32[768]{0:T(1024)S(1)} %add_select_fusion, f32[64,384]{1,0:T(8,128)S(1)} %reduce_sum.46), kind=kOutput, calls=%fused_computation.15 | convolution fusion | flops 52242432 | bytes 906240 | tf_op jit(solution)/shard_map/dot_general | solution.py:103
  52.4 1.7 %fusion.12 = f32[64,768]{1,0:T(8,128)S(1)} fusion(f32[64,768]{1,0:T(8,128)S(1)} %fusion.9, bf16[384,24]{0,1:T(8,128)(2,1)S(1)} %fusion.58, bf16[3,384,768]{2,1,0:T(8,128)(2,1)} %param.12, s32[768]{0:T(1024)S(1)} %add_select_fusion, f32[64,384]{1,0:T(8,128)S(1)} %reduce_sum.45), kind=kOutput, calls=%fused_computation.18 | convolution fusion | flops 52291584 | bytes 1102848 | tf_op jit(solution)/shard_map/dot_general | solution.py:103
  54.1 0.3 collective-permute-start.3
  54.4 0.0 copy-done.3
  54.4 0.2 fusion.54
  54.6 5.1 %collective-permute-done.3 = f32[64,768]{1,0:T(8,128)S(1)} collective-permute-done((f32[64,768]{1,0:T(8,128)S(1)}, f32[64,768]{1,0:T(8,128)S(1)}, u32[]{:S(2)}, u32[]{:S(2)}) %collective-permute-start.3) | collective-permute-done | bytes 196640 | tf_op jit(solution)/shard_map/ppermute | solution.py:23
  59.8 1.3 collective-permute-start.4
  61.0 0.2 fusion.55
  61.3 4.6 %collective-permute-done.4 = f32[64,768]{1,0:T(8,128)S(1)} collective-permute-done((f32[64,768]{1,0:T(8,128)S(1)}, f32[64,768]{1,0:T(8,128)S(1)}, u32[]{:S(2)}, u32[]{:S(2)}) %collective-permute-start.4) | collective-permute-done | bytes 196640 | tf_op jit(solution)/shard_map/ppermute | solution.py:23
  65.9 0.1 collective-permute-start.5
  66.0 0.2 fusion.56
  66.3 4.3 %collective-permute-done.5 = f32[64,768]{1,0:T(8,128)S(1)} collective-permute-done((f32[64,768]{1,0:T(8,128)S(1)}, f32[64,768]{1,0:T(8,128)S(1)}, u32[]{:S(2)}, u32[]{:S(2)}) %collective-permute-start.5) | collective-permute-done | bytes 196640 | tf_op jit(solution)/shard_map/ppermute | solution.py:23
  70.5 1.4 fusion.19
  71.9 0.8 broadcast_in_dim.12
  72.7 7.5 %all-to-all-start.2 = ((f32[4,64,384]{2,1,0:T(8,128)}), f32[4,64,384]{2,1,0:T(8,128)S(1)}, u32[]{:S(2)}, u32[]{:S(2)}) async-start(f32[4,64,384]{2,1,0:T(8,128)} %broadcast_in_dim.12), calls=%async_computation.2 | async-start | bytes 786432 | tf_op jit(solution)/shard_map/all_to_all | solution.py:13
  80.2 1.7 %fusion.7 = f32[64,768]{1,0:T(8,128)S(1)} fusion(bf16[384,24]{0,1:T(8,128)(2,1)S(1)} %fusion.55, bf16[3,384,768]{2,1,0:T(8,128)(2,1)} %param.14, s32[768]{0:T(1024)S(1)} %add_select_fusion, f32[64,384]{1,0:T(8,128)S(1)} %reduce_sum.46), kind=kOutput, calls=%fused_computation.13 | convolution fusion | flops 52242432 | bytes 906240 | tf_op jit(solution)/shard_map/dot_general | solution.py:114
  81.8 1.7 %fusion.13 = f32[64,768]{1,0:T(8,128)S(1)} fusion(f32[64,768]{1,0:T(8,128)S(1)} %fusion.7, bf16[384,24]{0,1:T(8,128)(2,1)S(1)} %fusion.56, bf16[3,384,768]{2,1,0:T(8,128)(2,1)} %param.14, s32[768]{0:T(1024)S(1)} %add_select_fusion, f32[64,384]{1,0:T(8,128)S(1)} %reduce_sum.45), kind=kOutput, calls=%fused_computation.19 | convolution fusion | flops 52291584 | bytes 1102848 | tf_op jit(solution)/shard_map/dot_general | solution.py:114
  83.5 0.0 copy-start.1
  83.5 3.2 %all-to-all-done.2 = f32[4,64,384]{2,1,0:T(8,128)S(1)} async-done(((f32[4,64,384]{2,1,0:T(8,128)}), f32[4,64,384]{2,1,0:T(8,128)S(1)}, u32[]{:S(2)}, u32[]{:S(2)}) %all-to-all-start.2) | async-done | bytes 393248 | tf_op jit(solution)/shard_map/all_to_all | solution.py:13
  86.8 1.7 %fusion.15 = f32[64,1,768]{2,0,1:T(8,128)S(1)} fusion(f32[64,768]{1,0:T(8,128)S(1)} %fusion.13, bf16[384,24]{0,1:T(8,128)(2,1)S(1)} %fusion.54, bf16[3,384,768]{2,1,0:T(8,128)(2,1)} %param.14, s32[768]{0:T(1024)S(1)} %add_select_fusion, f32[64,384]{1,0:T(8,128)S(1)} %reduce_sum.47), kind=kOutput, calls=%fused_computation.21 | convolution fusion | flops 52291584 | bytes 1102848 | tf_op jit(solution)/shard_map/dot_general | solution.py:114
  88.5 0.2 copy.11
  88.7 24.2 %all_to_all.30 = f32[64,1,768]{2,1,0:T(1,128)S(1)} all-to-all(f32[64,1,768]{2,1,0:T(1,128)S(1)} %copy.11), channel_id=1, replica_groups=mesh['grid'=2,'prow'=4,'pcol'=32] {'grid','pcol'}, dimensions={0} | all-to-all | bytes 393216 | tf_op jit(solution)/shard_map/all_to_all | solution.py:34
  112.9 0.1 reduce_sum.48
  113.0 0.1 broadcast_in_dim.13
  113.1 17.4 %all_to_all.31 = f32[64,1,768]{2,1,0:T(1,128)S(1)} all-to-all(f32[64,1,768]{2,1,0:T(1,128)S(1)} %broadcast_in_dim.13), channel_id=1, replica_groups=mesh['grid'=2,'prow'=4,'pcol'=32] {'grid','pcol'}, dimensions={0} | all-to-all | bytes 393216 | tf_op jit(solution)/shard_map/all_to_all | solution.py:13
  130.5 0.0 copy-done
  130.5 0.0 copy-done.1
  130.5 0.5 fusion.60
  131.0 1.4 broadcast_in_dim.14
  132.4 7.2 %all-to-all-start.5 = ((f32[4,64,1536]{2,1,0:T(8,128)}), f32[4,64,1536]{2,1,0:T(8,128)}, u32[]{:S(2)}, u32[]{:S(2)}) async-start(f32[4,64,1536]{2,1,0:T(8,128)} %broadcast_in_dim.14), calls=%async_computation.5 | async-start | bytes 3145728 | tf_op jit(solution)/shard_map/all_to_all | solution.py:13
  139.6 0.7 pad_maximum_fusion
  140.3 18.6 %all-to-all-done.5 = f32[4,64,1536]{2,1,0:T(8,128)} async-done(((f32[4,64,1536]{2,1,0:T(8,128)}), f32[4,64,1536]{2,1,0:T(8,128)}, u32[]{:S(2)}, u32[]{:S(2)}) %all-to-all-start.5) | async-done | bytes 1572896 | tf_op jit(solution)/shard_map/all_to_all | solution.py:13
  158.9 2.3 %reduce_sum.49 = f32[64,1536]{1,0:T(8,128)} reduce(f32[4,64,1536]{2,1,0:T(8,128)} %all-to-all-done.5, f32[]{:T(128)} %constant.53.clone.1), dimensions={0}, to_apply=%region_4.5 | reduce | flops 294912 | bytes 1966084 | tf_op jit(solution)/shard_map/reduce_sum | solution.py:19
  (9 shorter events, 0.2 us)
Async XLA Ops:
  0.6 129.8 %copy-start = (bf16[768,1536]{1,0:T(8,128)(2,1)S(1)}, bf16[768,1536]{1,0:T(8,128)(2,1)}, u32[]{:S(2)}) copy-start(bf16[768,1536]{1,0:T(8,128)(2,1)} %param.11) | copy-start | bytes 7077892
  0.6 9.0 %copy-start.2 = (s32[3,3,24]{2,1,0:T(4,128)S(1)}, s32[3,3,24]{2,1,0:T(4,128)}, u32[]{:S(2)}) copy-start(s32[3,3,24]{2,1,0:T(4,128)} %param.13) | copy-start | bytes 2596
  3.0 13.2 %all-to-all-start = ((f32[4,64,384]{2,1,0:T(8,128)}), f32[4,64,384]{2,1,0:T(8,128)S(1)}, u32[]{:S(2)}, u32[]{:S(2)}) async-start(f32[4,64,384]{2,1,0:T(8,128)} %broadcast_in_dim.10), calls=%async_computation | async-start | bytes 786432 | tf_op jit(solution)/shard_map/all_to_all | solution.py:13
  17.9 5.6 %collective-permute-start = (f32[64,768]{1,0:T(8,128)S(1)}, f32[64,768]{1,0:T(8,128)S(1)}, u32[]{:S(2)}, u32[]{:S(2)}) collective-permute-start(f32[64,768]{1,0:T(8,128)S(1)} %fusion.11), channel_id=1, source_target_pairs={{0,1},{1,0},{2,3},{3,2},{4,5},{5,4},{6,7},{7,6},{8,9},{9,8},{10,11... | collective-permute-start | bytes 589832 | tf_op jit(solution)/shard_map/ppermute | solution.py:23
  23.6 6.1 %collective-permute-start.1 = (f32[64,768]{1,0:T(8,128)S(1)}, f32[64,768]{1,0:T(8,128)S(1)}, u32[]{:S(2)}, u32[]{:S(2)}) collective-permute-start(f32[64,768]{1,0:T(8,128)S(1)} %add.57), channel_id=1, source_target_pairs={{0,2},{1,3},{2,0},{3,1},{4,6},{5,7},{6,4},{7,5},{8,10},{9,11},{10,... | collective-permute-start | bytes 589832 | tf_op jit(solution)/shard_map/ppermute | solution.py:23
  29.7 4.6 %collective-permute-start.2 = (f32[64,768]{1,0:T(8,128)S(1)}, f32[64,768]{1,0:T(8,128)S(1)}, u32[]{:S(2)}, u32[]{:S(2)}) collective-permute-start(f32[64,768]{1,0:T(8,128)S(1)} %add.58), channel_id=1, source_target_pairs={{0,4},{1,5},{2,6},{3,7},{4,0},{5,1},{6,2},{7,3},{8,12},{9,13},{10,... | collective-permute-start | bytes 589832 | tf_op jit(solution)/shard_map/ppermute | solution.py:23
  36.5 17.9 %copy-start.3 = (s32[3,3,24]{2,1,0:T(4,128)S(1)}, s32[3,3,24]{2,1,0:T(4,128)}, u32[]{:S(2)}) copy-start(s32[3,3,24]{2,1,0:T(4,128)} %param.15) | copy-start | bytes 2596
  36.5 14.2 %all-to-all-start.1 = ((f32[4,64,384]{2,1,0:T(8,128)}), f32[4,64,384]{2,1,0:T(8,128)S(1)}, u32[]{:S(2)}, u32[]{:S(2)}) async-start(f32[4,64,384]{2,1,0:T(8,128)} %broadcast_in_dim.11), calls=%async_computation.1 | async-start | bytes 786432 | tf_op jit(solution)/shard_map/all_to_all | solution.py:13
  54.1 5.6 %collective-permute-start.3 = (f32[64,768]{1,0:T(8,128)S(1)}, f32[64,768]{1,0:T(8,128)S(1)}, u32[]{:S(2)}, u32[]{:S(2)}) collective-permute-start(f32[64,768]{1,0:T(8,128)S(1)} %fusion.12), channel_id=1, source_target_pairs={{0,1},{1,0},{2,3},{3,2},{4,5},{5,4},{6,7},{7,6},{8,9},{9,8},{10,11... | collective-permute-start | bytes 589832 | tf_op jit(solution)/shard_map/ppermute | solution.py:23
  59.8 6.1 %collective-permute-start.4 = (f32[64,768]{1,0:T(8,128)S(1)}, f32[64,768]{1,0:T(8,128)S(1)}, u32[]{:S(2)}, u32[]{:S(2)}) collective-permute-start(f32[64,768]{1,0:T(8,128)S(1)} %add.61), channel_id=1, source_target_pairs={{0,2},{1,3},{2,0},{3,1},{4,6},{5,7},{6,4},{7,5},{8,10},{9,11},{10,... | collective-permute-start | bytes 589832 | tf_op jit(solution)/shard_map/ppermute | solution.py:23
  65.9 4.6 %collective-permute-start.5 = (f32[64,768]{1,0:T(8,128)S(1)}, f32[64,768]{1,0:T(8,128)S(1)}, u32[]{:S(2)}, u32[]{:S(2)}) collective-permute-start(f32[64,768]{1,0:T(8,128)S(1)} %add.62), channel_id=1, source_target_pairs={{0,4},{1,5},{2,6},{3,7},{4,0},{5,1},{6,2},{7,3},{8,12},{9,13},{10,... | collective-permute-start | bytes 589832 | tf_op jit(solution)/shard_map/ppermute | solution.py:23
  72.7 14.1 %all-to-all-start.2 = ((f32[4,64,384]{2,1,0:T(8,128)}), f32[4,64,384]{2,1,0:T(8,128)S(1)}, u32[]{:S(2)}, u32[]{:S(2)}) async-start(f32[4,64,384]{2,1,0:T(8,128)} %broadcast_in_dim.12), calls=%async_computation.2 | async-start | bytes 786432 | tf_op jit(solution)/shard_map/all_to_all | solution.py:13
  83.5 47.0 %copy-start.1 = (f32[64,768]{1,0:T(8,128)S(1)}, f32[64,768]{1,0:T(8,128)}, u32[]{:S(2)}) copy-start(f32[64,768]{1,0:T(8,128)} %param.9) | copy-start | bytes 589828
  132.4 26.5 %all-to-all-start.5 = ((f32[4,64,1536]{2,1,0:T(8,128)}), f32[4,64,1536]{2,1,0:T(8,128)}, u32[]{:S(2)}, u32[]{:S(2)}) async-start(f32[4,64,1536]{2,1,0:T(8,128)} %broadcast_in_dim.14), calls=%async_computation.5 | async-start | bytes 3145728 | tf_op jit(solution)/shard_map/all_to_all | solution.py:13
where the time goes:
time: 162 us; the launch traced here: 161 us
  waiting for transfers between devices  63 us (39%)
  blocking collectives  41.5 us (26%)
  starting transfers between devices  32.1 us (20%)
  matrix products  16.4 us (10%)
  local copies, waits for them, and re-layouts  4 us (2%)
  other arithmetic  3.35 us (2%)
    all_to_all x4, waiting for transfers between devices, from_everyone(): lax.all_to_all(jnp.broadcast_to(shard[None], (count, *shard.shape)), axis...  34.2 us
    all_to_all x4, starting transfers between devices, from_everyone(): lax.all_to_all(jnp.broadcast_to(shard[None], (count, *shard.shape)), axis...  29 us
    ppermute x6, waiting for transfers between devices, from_partner(): lax.ppermute(shard, axis, [(i, i ^ 1 << bit) for i in range(lax.axis_size...  28.9 us
    all_to_all x1, blocking collectives, summed_on_arrival(): lax.all_to_all(blocks, axis, split_axis=0, concat_axis=0, tiled=True)  24.2 us
    all_to_all x1, blocking collectives, from_everyone(): lax.all_to_all(jnp.broadcast_to(shard[None], (count, *shard.shape)), axis...  17.4 us
    dot_general x6, matrix products, shards(): jnp.dot(kept[source], factor_tile, preferred_element_type=jnp.float32)  10 us
    dot_general x4, matrix products, solve_block(): jnp.dot(residual.astype(jnp.bfloat16), inverse, preferred_element_type=jn...  4.85 us
    broadcast_in_dim x5, local copies, waits for them, and re-layouts, from_everyone(): jnp.broadcast_to(shard[None], (count, *shard.shape))  3.78 us
  transfers between devices with their start and end apart: 10, of which 10 were waited for; matrix products, arithmetic and copies ran while one was open for 3% of the time, Pallas kernels for 0%

commit v1 on v0

v1 whole, which is shorter than its diff:
```python
import jax
import jax.numpy as jnp
from jax import lax
from jax.sharding import Mesh
from jax.sharding import PartitionSpec as P

LEVELS = 3
TILE = 128
PROW = ("xl", "core")
OWN = ("zl", "y")
TREES = ("grid", "zt")


def partner(shard, axis, bit=1):
    return lax.ppermute(shard, axis, [(i, i ^ bit) for i in range(lax.axis_size(axis))])


def to_everyone(shard, axis):
    count = lax.axis_size(axis)
    return lax.all_to_all(
        jnp.broadcast_to(shard[None], (count, *shard.shape)), axis, 0, 0, tiled=True
    )


def prow_sum(partial_sum):
    pair = partial_sum + partner(partial_sum, "core")
    return pair + partner(pair, "xl")


def owner_sum(partial_sum):
    total = partial_sum + partner(partial_sum, "zl")
    total = total + partner(total, "y", 1)
    return total + partner(total, "y", 2)


def product(left, right):
    return jnp.dot(left, right, preferred_element_type=jnp.float32)


def selector(positions, count):
    return (positions[:, None] // TILE == jnp.arange(count)[None, :]).astype(jnp.float32)


def masked(factor, mask, row_select, col_select):
    expanded = jnp.dot(jnp.dot(row_select, mask.astype(jnp.float32)), col_select.T)
    return factor * expanded.astype(jnp.bfloat16)


def shards(
    sub_rhs, root_rhs, diag_inverse, root_inverse, inner_factor, inner_mask, root_factor, root_mask
):
    rows_here = inner_factor.shape[1]
    out_cols = inner_factor.shape[2]
    rhs_count = root_rhs.shape[0]
    col_positions = lax.axis_index(PROW) * out_cols + jnp.arange(out_cols)
    row_select = selector(jnp.arange(rows_here), inner_mask.shape[1])
    col_select = selector(col_positions, inner_mask.shape[2])
    own_rhs = lax.dynamic_index_in_dim(sub_rhs, lax.axis_index("zt"), 0, keepdims=False)

    kept = []
    solved_all = []
    pair = 0
    for level in range(LEVELS):
        residual = own_rhs[level]
        if level > 0:
            local_update = jnp.zeros(residual.shape, jnp.float32)
            for source in range(level):
                tile = masked(inner_factor[pair], inner_mask[pair], row_select, col_select)
                local_update = local_update + product(kept[source], tile)
                pair += 1
            residual = residual - owner_sum(local_update)
        solved = prow_sum(product(residual.astype(jnp.bfloat16), diag_inverse[level]))
        solved_all.append(solved)
        kept.append(solved.astype(jnp.bfloat16))

    root_local = jnp.zeros(root_rhs.shape, jnp.float32)
    for source in range(LEVELS):
        tile = masked(root_factor[source], root_mask[source], row_select, col_select)
        root_local = root_local + product(kept[source], tile)

    owners = lax.axis_size(OWN)
    few = rhs_count // owners
    own_rows = lax.all_to_all(
        root_local.reshape(owners, few, out_cols), OWN, 0, 0, tiled=True
    ).sum(axis=0)
    root_update = to_everyone(own_rows, TREES).sum(axis=0)
    rhs_rows = lax.dynamic_slice_in_dim(root_rhs, lax.axis_index(OWN) * few, few, 0)
    root_residual = (rhs_rows - root_update).astype(jnp.bfloat16)
    part = product(root_residual, root_inverse)
    half = part.shape[1] // 2
    first = lax.axis_index("core") == 0
    low, high = part[:, :half], part[:, half:]
    mine = jnp.where(first, low, high) + partner(jnp.where(first, high, low), "core")
    mine = mine + partner(mine, "xl")
    columns = to_everyone(mine, OWN).reshape(rhs_count, half)
    others = partner(columns, "core")
    root_solution = jnp.concatenate(
        [jnp.where(first, columns, others), jnp.where(first, others, columns)], axis=1
    )
    return (jnp.stack(solved_all), root_solution)


def solution(mesh):
    prow, pcol = mesh.shape["prow"], mesh.shape["pcol"]
    cores, y = 2, 4
    trees = 8 // mesh.shape["grid"]
    fine = Mesh(
        mesh.devices.reshape(
            mesh.shape["grid"], prow // cores, cores, trees, pcol // (trees * y), y
        ),
        ("grid", "xl", "core", "zt", "zl", "y"),
    )
    columns = ("grid", "zt", "zl", "y")
    return jax.shard_map(
        shards,
        mesh=fine,
        in_specs=(
            P("grid", None, None, PROW),
            P(None, PROW),
            P(None, PROW, columns),
            P(PROW, "grid"),
            P(None, columns, PROW),
            P(None, columns, None),
            P(None, columns, PROW),
            P(None, columns, None),
        ),
        out_specs=(P(None, None, columns), P(None, "grid")),
        check_vma=False,
    )
```

time: 162 us -> 127 us (0.78)
  blocking collectives: 41.5 us -> 19.9 us
  waiting for transfers between devices: 63 us -> 51.3 us
  local copies, waits for them, and re-layouts: 4 us -> 0.73 us
  starting transfers between devices: 32.1 us -> 34.9 us
    all_to_all x4 -> x1, waiting for transfers between devices: 34.2 us -> 9.51 us  [to_everyone(): lax.all_to_all(jnp.broadcast_to(shard[None], (count, *shard.shape)), axis...]
    ppermute x6 -> x15, starting transfers between devices: 3.07 us -> 24.9 us  [partner(): lax.ppermute(shard, axis, [(i, i ^ bit) for i in range(lax.axis_size(axis...]
    all_to_all x2, blocking collectives: 41.5 us -> 19.9 us  [the longest x1 11.5 us: shards(): lax.all_to_all(root_local.reshape(owners, few, out_cols), OWN, 0, 0, tile...]
    all_to_all x4 -> x1, starting transfers between devices: 29 us -> 9.99 us  [to_everyone(): lax.all_to_all(jnp.broadcast_to(shard[None], (count, *shard.shape)), axis...]
    ppermute x6 -> x15, waiting for transfers between devices: 28.9 us -> 41.8 us  [partner(): lax.ppermute(shard, axis, [(i, i ^ bit) for i in range(lax.axis_size(axis...]
    broadcast_in_dim x5 -> x2, local copies, waits for them, and re-layouts: 3.78 us -> 0.71 us  [to_everyone(): jnp.broadcast_to(shard[None], (count, *shard.shape))]
    reduce_sum x5 -> x2, other arithmetic: 2.49 us -> 0.03 us  [the longest x1 0.02 us: shards(): own_rows = lax.all_to_all(root_local.reshape(owners, few, out_cols), OWN,...]
  transfers between devices with their start and end apart: 10 -> 16, of which waited for: 10 -> 15; matrix products, arithmetic and copies ran while one was open for 3% -> 4% of each run, Pallas kernels for 0% -> 0%
where the time goes in v1:
time: 127 us
  waiting for transfers between devices  51.3 us (40%)
  starting transfers between devices  34.9 us (27%)
  blocking collectives  19.9 us (16%)
  matrix products  17.4 us (14%)
  other arithmetic  1.78 us (1%)
    ppermute x15, waiting for transfers between devices, partner(): lax.ppermute(shard, axis, [(i, i ^ bit) for i in range(lax.axis_size(axis...  41.8 us
    ppermute x15, starting transfers between devices, partner(): lax.ppermute(shard, axis, [(i, i ^ bit) for i in range(lax.axis_size(axis...  24.9 us
    dot_general x10, matrix products, product(): return jnp.dot(left, right, preferred_element_type=jnp.float32)  15.3 us
    all_to_all x1, blocking collectives, shards(): lax.all_to_all(root_local.reshape(owners, few, out_cols), OWN, 0, 0, tile...  11.5 us
    all_to_all x1, starting transfers between devices, to_everyone(): lax.all_to_all(jnp.broadcast_to(shard[None], (count, *shard.shape)), axis...  9.99 us
    all_to_all x1, waiting for transfers between devices, to_everyone(): lax.all_to_all(jnp.broadcast_to(shard[None], (count, *shard.shape)), axis...  9.51 us
    all_to_all x1, blocking collectives, to_everyone(): lax.all_to_all(jnp.broadcast_to(shard[None], (count, *shard.shape)), axis...  8.38 us
  transfers between devices with their start and end apart: 16, of which 15 were waited for; matrix products, arithmetic and copies ran while one was open for 4% of the time, Pallas kernels for 0%

profile of v1, /device:TPU:1, one launch (start us, length us, event | category | flops | bytes accessed | tf_op | source)
XLA Modules:
  0.0 126.8 jit_solution(6458977860544869936)
XLA Ops:
  0.6 0.0 copy-start
  0.7 1.5 %fusion.26 = f32[64,384]{1,0:T(8,128)S(1)} fusion(bf16[3,768,384]{2,1,0:T(8,128)(2,1)} %param.10, f32[4,3,64,768]{3,2,1,0:T(8,128)} %param.8, s32[]{:T(128)S(6)} %select_n.61), kind=kOutput, calls=%fused_computation.32 | convolution fusion | flops 37748736 | bytes 786436 | tf_op jit(solution)/shard_map/dot_general | solution.py:37
  2.2 3.3 %collective-permute-start = (f32[64,384]{1,0:T(8,128)S(1)}, f32[64,384]{1,0:T(8,128)S(1)}, u32[]{:S(2)}, u32[]{:S(2)}) collective-permute-start(f32[64,384]{1,0:T(8,128)S(1)} %fusion.26), channel_id=1, source_target_pairs={{0,32},{32,0},{1,33},{33,1},{2,34},{34,2},{3,35},{35,3},{4,36},{36... | collective-permute-start | bytes 294920 | tf_op jit(solution)/shard_map/ppermute | solution.py:15
  5.5 0.9 fusion.58
  6.4 0.0 collective-permute-done
  6.5 0.1 collective-permute-start.1
  6.6 4.0 %collective-permute-done.1 = f32[64,384]{1,0:T(8,128)S(1)} collective-permute-done((f32[64,384]{1,0:T(8,128)S(1)}, f32[64,384]{1,0:T(8,128)S(1)}, u32[]{:S(2)}, u32[]{:S(2)}) %collective-permute-start.1) | collective-permute-done | bytes 98336 | tf_op jit(solution)/shard_map/ppermute | solution.py:15
  10.6 0.0 copy-start.1
  10.6 1.6 %fusion.11 = f32[64,768]{1,0:T(8,128)S(1)} fusion(bf16[64,384]{1,0:T(8,128)(2,1)S(1)} %get-tuple-element.5, bf16[384,24]{1,0:T(8,128)(2,1)S(1)} %fusion.58, bf16[3,384,768]{2,1,0:T(8,128)(2,1)} %param.12, s32[768]{0:T(1024)S(1)} %add_select_fusion), kind=kOutput, calls=%fused_computation.17 | convolution fusion | flops 52217856 | bytes 857088 | tf_op jit(solution)/shard_map/dot_general | solution.py:37
  12.3 0.1 collective-permute-start.2
  12.4 5.2 %collective-permute-done.2 = f32[64,768]{1,0:T(8,128)S(1)} collective-permute-done((f32[64,768]{1,0:T(8,128)S(1)}, f32[64,768]{1,0:T(8,128)S(1)}, u32[]{:S(2)}, u32[]{:S(2)}) %collective-permute-start.2) | collective-permute-done | bytes 196640 | tf_op jit(solution)/shard_map/ppermute | solution.py:15
  17.6 0.1 collective-permute-start.3
  17.7 4.5 %collective-permute-done.3 = f32[64,768]{1,0:T(8,128)S(1)} collective-permute-done((f32[64,768]{1,0:T(8,128)S(1)}, f32[64,768]{1,0:T(8,128)S(1)}, u32[]{:S(2)}, u32[]{:S(2)}) %collective-permute-start.3) | collective-permute-done | bytes 196640 | tf_op jit(solution)/shard_map/ppermute | solution.py:15
  22.2 1.6 %collective-permute-start.4 = (f32[64,768]{1,0:T(8,128)S(1)}, f32[64,768]{1,0:T(8,128)S(1)}, u32[]{:S(2)}, u32[]{:S(2)}) collective-permute-start(f32[64,768]{1,0:T(8,128)S(1)} %add.93), channel_id=1, source_target_pairs={{0,2},{1,3},{2,0},{3,1},{4,6},{5,7},{6,4},{7,5},{8,10},{9,11},{10,... | collective-permute-start | bytes 589832 | tf_op jit(solution)/shard_map/ppermute | solution.py:15
  23.8 4.5 %collective-permute-done.4 = f32[64,768]{1,0:T(8,128)S(1)} collective-permute-done((f32[64,768]{1,0:T(8,128)S(1)}, f32[64,768]{1,0:T(8,128)S(1)}, u32[]{:S(2)}, u32[]{:S(2)}) %collective-permute-start.4) | collective-permute-done | bytes 196640 | tf_op jit(solution)/shard_map/ppermute | solution.py:15
  28.3 1.4 %fusion.23 = f32[64,384]{1,0:T(8,128)S(1)} fusion(bf16[3,768,384]{2,1,0:T(8,128)(2,1)} %param.10, f32[4,3,64,768]{3,2,1,0:T(8,128)} %param.8, s32[]{:T(128)S(6)} %select_n.61, s32[]{:T(128)S(6)} %add.109, f32[64,768]{1,0:T(8,128)S(1)} %add.93, f32[64,768]{1,0:T(8,128)S(1)} %collective-permute-done.4), kind=kOutput, calls=%fused_computation.29 | convolution fusion | flops 37896192 | bytes 1277960 | tf_op jit(solution)/shard_map/dot_general | solution.py:37
  29.7 4.5 %collective-permute-start.5 = (f32[64,384]{1,0:T(8,128)S(1)}, f32[64,384]{1,0:T(8,128)S(1)}, u32[]{:S(2)}, u32[]{:S(2)}) collective-permute-start(f32[64,384]{1,0:T(8,128)S(1)} %fusion.23), channel_id=1, source_target_pairs={{0,32},{32,0},{1,33},{33,1},{2,34},{34,2},{3,35},{35,3},{4,36},{36... | collective-permute-start | bytes 294920 | tf_op jit(solution)/shard_map/ppermute | solution.py:15
  34.2 0.0 copy-done.1
  34.2 0.2 fusion.56
  34.5 0.0 copy-start.2
  34.5 0.7 collective-permute-done.5
  35.2 0.4 collective-permute-start.6
  35.6 0.2 fusion.57
  35.8 3.5 %collective-permute-done.6 = f32[64,384]{1,0:T(8,128)S(1)} collective-permute-done((f32[64,384]{1,0:T(8,128)S(1)}, f32[64,384]{1,0:T(8,128)S(1)}, u32[]{:S(2)}, u32[]{:S(2)}) %collective-permute-start.6) | collective-permute-done | bytes 98336 | tf_op jit(solution)/shard_map/ppermute | solution.py:15
  39.3 1.6 %fusion.9 = f32[64,768]{1,0:T(8,128)S(1)} fusion(bf16[64,384]{1,0:T(8,128)(2,1)S(1)} %get-tuple-element.7, bf16[384,24]{1,0:T(8,128)(2,1)S(1)} %fusion.56, bf16[3,384,768]{2,1,0:T(8,128)(2,1)} %param.12, s32[768]{0:T(1024)S(1)} %add_select_fusion), kind=kOutput, calls=%fused_computation.15 | convolution fusion | flops 52217856 | bytes 857088 | tf_op jit(solution)/shard_map/dot_general | solution.py:37
  41.0 1.6 %fusion.12 = f32[64,768]{1,0:T(8,128)S(1)} fusion(f32[64,768]{1,0:T(8,128)S(1)} %fusion.9, bf16[64,384]{1,0:T(8,128)(2,1)S(1)} %get-tuple-element.5, bf16[384,24]{1,0:T(8,128)(2,1)S(1)} %fusion.57, bf16[3,384,768]{2,1,0:T(8,128)(2,1)} %param.12, s32[768]{0:T(1024)S(1)} %add_select_fusion), kind=kOutput, calls=%fused_computation.18 | convolution fusion | flops 52267008 | bytes 1053696 | tf_op jit(solution)/shard_map/dot_general | solution.py:37
  42.6 0.1 collective-permute-start.7
  42.7 5.2 %collective-permute-done.7 = f32[64,768]{1,0:T(8,128)S(1)} collective-permute-done((f32[64,768]{1,0:T(8,128)S(1)}, f32[64,768]{1,0:T(8,128)S(1)}, u32[]{:S(2)}, u32[]{:S(2)}) %collective-permute-start.7) | collective-permute-done | bytes 196640 | tf_op jit(solution)/shard_map/ppermute | solution.py:15
  47.9 0.1 collective-permute-start.8
  48.0 0.0 copy-done.2
  48.0 0.2 fusion.53
  48.3 4.3 %collective-permute-done.8 = f32[64,768]{1,0:T(8,128)S(1)} collective-permute-done((f32[64,768]{1,0:T(8,128)S(1)}, f32[64,768]{1,0:T(8,128)S(1)}, u32[]{:S(2)}, u32[]{:S(2)}) %collective-permute-start.8) | collective-permute-done | bytes 196640 | tf_op jit(solution)/shard_map/ppermute | solution.py:15
  52.6 2.3 %collective-permute-start.9 = (f32[64,768]{1,0:T(8,128)S(1)}, f32[64,768]{1,0:T(8,128)S(1)}, u32[]{:S(2)}, u32[]{:S(2)}) collective-permute-start(f32[64,768]{1,0:T(8,128)S(1)} %add.99), channel_id=1, source_target_pairs={{0,2},{1,3},{2,0},{3,1},{4,6},{5,7},{6,4},{7,5},{8,10},{9,11},{10,... | collective-permute-start | bytes 589832 | tf_op jit(solution)/shard_map/ppermute | solution.py:15
  54.9 0.2 fusion.54
  55.2 3.7 %collective-permute-done.9 = f32[64,768]{1,0:T(8,128)S(1)} collective-permute-done((f32[64,768]{1,0:T(8,128)S(1)}, f32[64,768]{1,0:T(8,128)S(1)}, u32[]{:S(2)}, u32[]{:S(2)}) %collective-permute-start.9) | collective-permute-done | bytes 196640 | tf_op jit(solution)/shard_map/ppermute | solution.py:15
  58.8 1.4 %fusion.19 = f32[64,384]{1,0:T(8,128)S(1)} fusion(bf16[3,768,384]{2,1,0:T(8,128)(2,1)} %param.10, f32[4,3,64,768]{3,2,1,0:T(8,128)} %param.8, s32[]{:T(128)S(6)} %select_n.61, s32[]{:T(128)S(6)} %add.110, f32[64,768]{1,0:T(8,128)S(1)} %add.99, f32[64,768]{1,0:T(8,128)S(1)} %collective-permute-done.9), kind=kOutput, calls=%fused_computation.25 | convolution fusion | flops 37896192 | bytes 1277960 | tf_op jit(solution)/shard_map/dot_general | solution.py:37
  60.2 4.3 %collective-permute-start.10 = (f32[64,384]{1,0:T(8,128)S(1)}, f32[64,384]{1,0:T(8,128)S(1)}, u32[]{:S(2)}, u32[]{:S(2)}) collective-permute-start(f32[64,384]{1,0:T(8,128)S(1)} %fusion.19), channel_id=1, source_target_pairs={{0,32},{32,0},{1,33},{33,1},{2,34},{34,2},{3,35},{35,3},{4,36},{36... | collective-permute-start | bytes 294920 | tf_op jit(solution)/shard_map/ppermute | solution.py:15
  64.6 0.2 fusion.55
  64.8 0.7 collective-permute-done.10
  65.5 0.4 collective-permute-start.11
  66.0 1.6 %fusion.7 = f32[64,768]{1,0:T(8,128)S(1)} fusion(bf16[64,384]{1,0:T(8,128)(2,1)S(1)} %get-tuple-element.7, bf16[384,24]{1,0:T(8,128)(2,1)S(1)} %fusion.54, bf16[3,384,768]{2,1,0:T(8,128)(2,1)} %param.14, s32[768]{0:T(1024)S(1)} %add_select_fusion), kind=kOutput, calls=%fused_computation.13 | convolution fusion | flops 52217856 | bytes 857088 | tf_op jit(solution)/shard_map/dot_general | solution.py:37
  67.6 2.1 %collective-permute-done.11 = f32[64,384]{1,0:T(8,128)S(1)} collective-permute-done((f32[64,384]{1,0:T(8,128)S(1)}, f32[64,384]{1,0:T(8,128)S(1)}, u32[]{:S(2)}, u32[]{:S(2)}) %collective-permute-start.11) | collective-permute-done | bytes 98336 | tf_op jit(solution)/shard_map/ppermute | solution.py:15
  69.7 1.6 %fusion.6 = f32[64,768]{1,0:T(8,128)S(1)} fusion(bf16[384,24]{1,0:T(8,128)(2,1)S(1)} %fusion.53, bf16[3,384,768]{2,1,0:T(8,128)(2,1)} %param.14, s32[768]{0:T(1024)S(1)} %add_select_fusion, f32[64,384]{1,0:T(8,128)S(1)} %add.101, f32[64,384]{1,0:T(8,128)S(1)} %collective-permute-done.11), kind=kOutput, calls=%fused_computation.12 | convolution fusion | flops 52267008 | bytes 1004544 | tf_op jit(solution)/shard_map/dot_general | solution.py:37
  71.3 1.6 %fusion.15 = f32[8,8,768]{2,1,0:T(8,128)S(1)} fusion(f32[64,768]{1,0:T(8,128)S(1)} %fusion.6, f32[64,768]{1,0:T(8,128)S(1)} %fusion.7, bf16[64,384]{1,0:T(8,128)(2,1)S(1)} %get-tuple-element.5, bf16[384,24]{1,0:T(8,128)(2,1)S(1)} %fusion.55, bf16[3,384,768]{2,1,0:T(8,128)(2,1)} %param.14, s32[768]{0:T(1024)S(1)} %add_select_fusion), kind=kOutput, calls=%fused_computation.21 | convolution fusion | flops 52316160 | bytes 1250304 | tf_op jit(solution)/shard_map/dot_general | solution.py:37
  72.9 11.5 %all_to_all.15 = f32[8,8,768]{2,1,0:T(8,128)S(1)} all-to-all(f32[8,8,768]{2,1,0:T(8,128)S(1)} %fusion.15), channel_id=1, replica_groups=mesh['grid'=2,'xl'=2,'core'=2,'zt'=4,'zl'=2,'y'=4] {'zl','y'}, dimensions={0} | all-to-all | bytes 393216 | tf_op jit(solution)/shard_map/all_to_all | solution.py:83
  84.4 0.7 broadcast_in_dim.4
  85.1 10.0 %all-to-all-start.1 = ((f32[8,8,768]{2,1,0:T(8,128)}), f32[8,8,768]{2,1,0:T(8,128)S(1)}, u32[]{:S(2)}, u32[]{:S(2)}) async-start(f32[8,8,768]{2,1,0:T(8,128)} %broadcast_in_dim.4), calls=%async_computation.1 | async-start | bytes 393216 | tf_op jit(solution)/shard_map/all_to_all | solution.py:20
  95.1 9.5 %all-to-all-done.1 = f32[8,8,768]{2,1,0:T(8,128)S(1)} async-done(((f32[8,8,768]{2,1,0:T(8,128)}), f32[8,8,768]{2,1,0:T(8,128)S(1)}, u32[]{:S(2)}, u32[]{:S(2)}) %all-to-all-start.1) | async-done | bytes 196640 | tf_op jit(solution)/shard_map/all_to_all | solution.py:20
  104.7 0.0 copy-done
  104.7 1.1 fusion.71
  105.8 4.3 %collective-permute-start.12 = (f32[8,768]{1,0:T(8,128)S(1)}, f32[8,768]{1,0:T(8,128)S(1)}, u32[]{:S(2)}, u32[]{:S(2)}) collective-permute-start(f32[8,768]{1,0:T(8,128)S(1)} %slice_select_fusion), channel_id=1, source_target_pairs={{0,32},{32,0},{1,33},{33,1},{2,34},{34,2},{3,35},{35,3},{4,36},{36... | collective-permute-start | bytes 73736 | tf_op jit(solution)/shard_map/ppermute | solution.py:15
  110.1 0.8 collective-permute-done.12
  111.0 0.3 collective-permute-start.13
  111.3 2.4 %collective-permute-done.13 = f32[8,768]{1,0:T(8,128)S(1)} collective-permute-done((f32[8,768]{1,0:T(8,128)S(1)}, f32[8,768]{1,0:T(8,128)S(1)}, u32[]{:S(2)}, u32[]{:S(2)}) %collective-permute-start.13) | collective-permute-done | bytes 24608 | tf_op jit(solution)/shard_map/ppermute | solution.py:15
  113.7 8.4 %all_to_all.16 = f32[8,8,768]{2,1,0:T(8,128)S(1)} all-to-all(f32[8,8,768]{2,1,0:T(8,128)S(1)} %broadcast_in_dim.5), channel_id=1, replica_groups=mesh['grid'=2,'xl'=2,'core'=2,'zt'=4,'zl'=2,'y'=4] {'zl','y'}, dimensions={0} | all-to-all | bytes 393216 | tf_op jit(solution)/shard_map/all_to_all | solution.py:20
  122.0 2.9 %collective-permute-start.14 = (f32[64,768]{1,0:T(8,128)S(1)}, f32[64,768]{1,0:T(8,128)S(1)}, u32[]{:S(2)}, u32[]{:S(2)}) collective-permute-start(f32[64,768]{1,0:T(8,128)S(1)} %bitcast.97), channel_id=1, source_target_pairs={{0,32},{32,0},{1,33},{33,1},{2,34},{34,2},{3,35},{35,3},{4,36},{36... | collective-permute-start | bytes 589832 | tf_op jit(solution)/shard_map/ppermute | solution.py:15
  125.0 0.7 pad_maximum_fusion.1
  125.7 0.3 collective-permute-done.14
  126.1 0.8 pad_maximum_fusion
  (19 shorter events, 0.3 us)
Async XLA Ops:
  0.6 104.0 %copy-start = (bf16[768,1536]{1,0:T(8,128)(2,1)S(1)}, bf16[768,1536]{1,0:T(8,128)(2,1)}, u32[]{:S(2)}) copy-start(bf16[768,1536]{1,0:T(8,128)(2,1)} %param.11) | copy-start | bytes 7077892
  2.2 4.3 %collective-permute-start = (f32[64,384]{1,0:T(8,128)S(1)}, f32[64,384]{1,0:T(8,128)S(1)}, u32[]{:S(2)}, u32[]{:S(2)}) collective-permute-start(f32[64,384]{1,0:T(8,128)S(1)} %fusion.26), channel_id=1, source_target_pairs={{0,32},{32,0},{1,33},{33,1},{2,34},{34,2},{3,35},{35,3},{4,36},{36... | collective-permute-start | bytes 294920 | tf_op jit(solution)/shard_map/ppermute | solution.py:15
  6.5 4.1 %collective-permute-start.1 = (f32[64,384]{1,0:T(8,128)S(1)}, f32[64,384]{1,0:T(8,128)S(1)}, u32[]{:S(2)}, u32[]{:S(2)}) collective-permute-start(f32[64,384]{1,0:T(8,128)S(1)} %add.87), channel_id=1, source_target_pairs={{0,64},{64,0},{1,65},{65,1},{2,66},{66,2},{3,67},{67,3},{4,68},{68... | collective-permute-start | bytes 294920 | tf_op jit(solution)/shard_map/ppermute | solution.py:15
  10.6 23.6 %copy-start.1 = (s32[3,3,24]{2,1,0:T(4,128)S(1)}, s32[3,3,24]{2,1,0:T(4,128)}, u32[]{:S(2)}) copy-start(s32[3,3,24]{2,1,0:T(4,128)} %param.13) | copy-start | bytes 2596
  12.3 5.3 %collective-permute-start.2 = (f32[64,768]{1,0:T(8,128)S(1)}, f32[64,768]{1,0:T(8,128)S(1)}, u32[]{:S(2)}, u32[]{:S(2)}) collective-permute-start(f32[64,768]{1,0:T(8,128)S(1)} %fusion.11), channel_id=1, source_target_pairs={{0,4},{4,0},{1,5},{5,1},{2,6},{6,2},{3,7},{7,3},{8,12},{12,8},{9,1... | collective-permute-start | bytes 589832 | tf_op jit(solution)/shard_map/ppermute | solution.py:15
  17.6 4.6 %collective-permute-start.3 = (f32[64,768]{1,0:T(8,128)S(1)}, f32[64,768]{1,0:T(8,128)S(1)}, u32[]{:S(2)}, u32[]{:S(2)}) collective-permute-start(f32[64,768]{1,0:T(8,128)S(1)} %add.92), channel_id=1, source_target_pairs={{0,1},{1,0},{2,3},{3,2},{4,5},{5,4},{6,7},{7,6},{8,9},{9,8},{10,11... | collective-permute-start | bytes 589832 | tf_op jit(solution)/shard_map/ppermute | solution.py:15
  22.2 6.1 %collective-permute-start.4 = (f32[64,768]{1,0:T(8,128)S(1)}, f32[64,768]{1,0:T(8,128)S(1)}, u32[]{:S(2)}, u32[]{:S(2)}) collective-permute-start(f32[64,768]{1,0:T(8,128)S(1)} %add.93), channel_id=1, source_target_pairs={{0,2},{1,3},{2,0},{3,1},{4,6},{5,7},{6,4},{7,5},{8,10},{9,11},{10,... | collective-permute-start | bytes 589832 | tf_op jit(solution)/shard_map/ppermute | solution.py:15
  29.7 5.4 %collective-permute-start.5 = (f32[64,384]{1,0:T(8,128)S(1)}, f32[64,384]{1,0:T(8,128)S(1)}, u32[]{:S(2)}, u32[]{:S(2)}) collective-permute-start(f32[64,384]{1,0:T(8,128)S(1)} %fusion.23), channel_id=1, source_target_pairs={{0,32},{32,0},{1,33},{33,1},{2,34},{34,2},{3,35},{35,3},{4,36},{36... | collective-permute-start | bytes 294920 | tf_op jit(solution)/shard_map/ppermute | solution.py:15
  34.5 13.6 %copy-start.2 = (s32[3,3,24]{2,1,0:T(4,128)S(1)}, s32[3,3,24]{2,1,0:T(4,128)}, u32[]{:S(2)}) copy-start(s32[3,3,24]{2,1,0:T(4,128)} %param.15) | copy-start | bytes 2596
  35.2 4.1 %collective-permute-start.6 = (f32[64,384]{1,0:T(8,128)S(1)}, f32[64,384]{1,0:T(8,128)S(1)}, u32[]{:S(2)}, u32[]{:S(2)}) collective-permute-start(f32[64,384]{1,0:T(8,128)S(1)} %add.95), channel_id=1, source_target_pairs={{0,64},{64,0},{1,65},{65,1},{2,66},{66,2},{3,67},{67,3},{4,68},{68... | collective-permute-start | bytes 294920 | tf_op jit(solution)/shard_map/ppermute | solution.py:15
  42.6 5.3 %collective-permute-start.7 = (f32[64,768]{1,0:T(8,128)S(1)}, f32[64,768]{1,0:T(8,128)S(1)}, u32[]{:S(2)}, u32[]{:S(2)}) collective-permute-start(f32[64,768]{1,0:T(8,128)S(1)} %fusion.12), channel_id=1, source_target_pairs={{0,4},{4,0},{1,5},{5,1},{2,6},{6,2},{3,7},{7,3},{8,12},{12,8},{9,1... | collective-permute-start | bytes 589832 | tf_op jit(solution)/shard_map/ppermute | solution.py:15
  47.9 4.6 %collective-permute-start.8 = (f32[64,768]{1,0:T(8,128)S(1)}, f32[64,768]{1,0:T(8,128)S(1)}, u32[]{:S(2)}, u32[]{:S(2)}) collective-permute-start(f32[64,768]{1,0:T(8,128)S(1)} %add.98), channel_id=1, source_target_pairs={{0,1},{1,0},{2,3},{3,2},{4,5},{5,4},{6,7},{7,6},{8,9},{9,8},{10,11... | collective-permute-start | bytes 589832 | tf_op jit(solution)/shard_map/ppermute | solution.py:15
  52.6 6.3 %collective-permute-start.9 = (f32[64,768]{1,0:T(8,128)S(1)}, f32[64,768]{1,0:T(8,128)S(1)}, u32[]{:S(2)}, u32[]{:S(2)}) collective-permute-start(f32[64,768]{1,0:T(8,128)S(1)} %add.99), channel_id=1, source_target_pairs={{0,2},{1,3},{2,0},{3,1},{4,6},{5,7},{6,4},{7,5},{8,10},{9,11},{10,... | collective-permute-start | bytes 589832 | tf_op jit(solution)/shard_map/ppermute | solution.py:15
  60.2 5.3 %collective-permute-start.10 = (f32[64,384]{1,0:T(8,128)S(1)}, f32[64,384]{1,0:T(8,128)S(1)}, u32[]{:S(2)}, u32[]{:S(2)}) collective-permute-start(f32[64,384]{1,0:T(8,128)S(1)} %fusion.19), channel_id=1, source_target_pairs={{0,32},{32,0},{1,33},{33,1},{2,34},{34,2},{3,35},{35,3},{4,36},{36... | collective-permute-start | bytes 294920 | tf_op jit(solution)/shard_map/ppermute | solution.py:15
  65.5 4.1 %collective-permute-start.11 = (f32[64,384]{1,0:T(8,128)S(1)}, f32[64,384]{1,0:T(8,128)S(1)}, u32[]{:S(2)}, u32[]{:S(2)}) collective-permute-start(f32[64,384]{1,0:T(8,128)S(1)} %add.101), channel_id=1, source_target_pairs={{0,64},{64,0},{1,65},{65,1},{2,66},{66,2},{3,67},{67,3},{4,68},{68... | collective-permute-start | bytes 294920 | tf_op jit(solution)/shard_map/ppermute | solution.py:15
  85.1 19.5 %all-to-all-start.1 = ((f32[8,8,768]{2,1,0:T(8,128)}), f32[8,8,768]{2,1,0:T(8,128)S(1)}, u32[]{:S(2)}, u32[]{:S(2)}) async-start(f32[8,8,768]{2,1,0:T(8,128)} %broadcast_in_dim.4), calls=%async_computation.1 | async-start | bytes 393216 | tf_op jit(solution)/shard_map/all_to_all | solution.py:20
  105.8 5.1 %collective-permute-start.12 = (f32[8,768]{1,0:T(8,128)S(1)}, f32[8,768]{1,0:T(8,128)S(1)}, u32[]{:S(2)}, u32[]{:S(2)}) collective-permute-start(f32[8,768]{1,0:T(8,128)S(1)} %slice_select_fusion), channel_id=1, source_target_pairs={{0,32},{32,0},{1,33},{33,1},{2,34},{34,2},{3,35},{35,3},{4,36},{36... | collective-permute-start | bytes 73736 | tf_op jit(solution)/shard_map/ppermute | solution.py:15
  111.0 2.7 %collective-permute-start.13 = (f32[8,768]{1,0:T(8,128)S(1)}, f32[8,768]{1,0:T(8,128)S(1)}, u32[]{:S(2)}, u32[]{:S(2)}) collective-permute-start(f32[8,768]{1,0:T(8,128)S(1)} %select_add_fusion), channel_id=1, source_target_pairs={{0,64},{64,0},{1,65},{65,1},{2,66},{66,2},{3,67},{67,3},{4,68},{68... | collective-permute-start | bytes 73736 | tf_op jit(solution)/shard_map/ppermute | solution.py:15
  122.0 4.0 %collective-permute-start.14 = (f32[64,768]{1,0:T(8,128)S(1)}, f32[64,768]{1,0:T(8,128)S(1)}, u32[]{:S(2)}, u32[]{:S(2)}) collective-permute-start(f32[64,768]{1,0:T(8,128)S(1)} %bitcast.97), channel_id=1, source_target_pairs={{0,32},{32,0},{1,33},{33,1},{2,34},{34,2},{3,35},{35,3},{4,36},{36... | collective-permute-start | bytes 589832 | tf_op jit(solution)/shard_map/ppermute | solution.py:15

commit v2 on v1

v2 whole, which is shorter than its diff:
```python
import jax
import jax.numpy as jnp
from jax import lax
from jax.experimental import pallas as pl
from jax.experimental.pallas import tpu as pltpu
from jax.sharding import Mesh
from jax.sharding import PartitionSpec as P

LEVELS = 3
TILE = 128
PROW = ("xl", "core")
OWN = ("zl", "y")
SCOPED_BYTES = 4 << 20
F32 = jnp.float32
BF16 = jnp.bfloat16

ON_CHIP = pl.BlockSpec(memory_space=pltpu.VMEM)
SCALARS = pl.BlockSpec(memory_space=pltpu.SMEM)
IN_PLACE = pl.BlockSpec(memory_space=pltpu.HBM)


def partner(shard, axis, bit=1):
    return lax.ppermute(shard, axis, [(i, i ^ bit) for i in range(lax.axis_size(axis))])


def to_everyone(shard, axis):
    count = lax.axis_size(axis)
    return lax.all_to_all(
        jnp.broadcast_to(shard[None], (count, *shard.shape)), axis, 0, 0, tiled=True
    )


def call(body, outs, args, specs=None, scratch=(), name=None):
    specs = specs or [ON_CHIP] * len(args)
    args = [
        arg if spec is SCALARS else pltpu.with_memory_space_constraint(arg, spec.memory_space)
        for arg, spec in zip(args, specs)
    ]
    return pl.pallas_call(
        body,
        out_shape=[pltpu.VMEM(shape, kind) for shape, kind in outs],
        in_specs=specs,
        out_specs=[ON_CHIP] * len(outs),
        scratch_shapes=list(scratch),
        compiler_params=pltpu.CompilerParams(vmem_limit_bytes=SCOPED_BYTES),
        name=name,
    )(*args)


def product(left, right):
    return jnp.dot(left, right, preferred_element_type=F32)


def first_solve(tree, sub_rhs, diag_inverse):
    rhs_count, depth = sub_rhs.shape[2:]
    cols = diag_inverse.shape[2]
    pieces = 3
    step = depth // pieces

    def body(tree_ref, rhs_hbm, inverse_hbm, out_ref, rhs, inverse, rhs_sem, inverse_sem):
        rhs_copy = pltpu.make_async_copy(rhs_hbm.at[tree_ref[0], 0], rhs, rhs_sem)
        rhs_copy.start()
        copies = []
        for piece in range(pieces):
            part = pl.ds(piece * step, step)
            copies.append(
                pltpu.make_async_copy(
                    inverse_hbm.at[0, part], inverse.at[part], inverse_sem.at[piece]
                )
            )
            copies[-1].start()
        rhs_copy.wait()
        total = jnp.zeros((rhs_count, cols), F32)
        for piece in range(pieces):
            copies[piece].wait()
            part = slice(piece * step, (piece + 1) * step)
            total = total + product(rhs[:, part].astype(BF16), inverse[part, :])
        out_ref[...] = total

    return call(
        body,
        [((rhs_count, cols), F32)],
        (tree, sub_rhs, diag_inverse),
        [SCALARS, IN_PLACE, IN_PLACE],
        [
            pltpu.VMEM((rhs_count, depth), F32),
            pltpu.VMEM((depth, cols), BF16),
            pltpu.SemaphoreType.DMA,
            pltpu.SemaphoreType.DMA((pieces,)),
        ],
        "first_solve",
    )[0]


def next_solve(place, rhs, sums, diag_inverse):
    def body(rhs_ref, *refs):
        *sum_refs, inverse_ref, out_ref = refs
        update = sum_refs[0][...]
        for ref in sum_refs[1:]:
            update = update + ref[...]
        residual = (rhs_ref[place] - update).astype(BF16)
        out_ref[...] = product(residual, inverse_ref[place])

    shape = (rhs.shape[1], diag_inverse.shape[2])
    return call(body, [(shape, F32)], (rhs, *sums, diag_inverse), name="next_solve")[0]


def mask_tiles(mask_ref, block, source, target):
    rows, cols = source.shape[1:]
    for i in range(rows // TILE):
        for j in range(cols // TILE):
            there = (
                block,
                slice(i * TILE, (i + 1) * TILE),
                slice(j * TILE, (j + 1) * TILE),
            )
            keep = jnp.full((TILE, TILE), mask_ref[block, i, j], F32).astype(BF16)
            target[there] = source[there] * keep


def stage(tree, mask, sub_rhs, diag_inverse, factor):
    levels, rhs_count, depth = sub_rhs.shape[1:]
    later = levels - 1
    cols = diag_inverse.shape[2]

    def body(
        tree_ref, mask_ref, rhs_hbm, inverse_hbm, factor_hbm, out_ref, inverse_ref, rhs_ref, landed, sems, other_sems
    ):
        blocks = factor_hbm.shape[0]
        copies = [
            pltpu.make_async_copy(factor_hbm.at[block], landed.at[block], sems.at[block])
            for block in range(blocks)
        ]
        others = [
            pltpu.make_async_copy(inverse_hbm.at[pl.ds(1, later)], inverse_ref, other_sems.at[0]),
            pltpu.make_async_copy(
                rhs_hbm.at[tree_ref[0], pl.ds(1, later)], rhs_ref, other_sems.at[1]
            ),
        ]
        for copy in copies + others:
            copy.start()
        for block, copy in enumerate(copies):
            copy.wait()
            mask_tiles(mask_ref, block, landed, out_ref)
        for copy in others:
            copy.wait()

    return call(
        body,
        [
            (factor.shape, BF16),
            ((later, depth, cols), BF16),
            ((later, rhs_count, depth), F32),
        ],
        (tree, mask, sub_rhs, diag_inverse, factor),
        [SCALARS, SCALARS, IN_PLACE, IN_PLACE, IN_PLACE],
        [
            pltpu.VMEM(factor.shape, BF16),
            pltpu.SemaphoreType.DMA((factor.shape[0],)),
            pltpu.SemaphoreType.DMA((2,)),
        ],
        "stage",
    )


def masked(mask, factor):
    def body(mask_ref, factor_ref, out_ref):
        for block in range(factor.shape[0]):
            mask_tiles(mask_ref, block, factor_ref, out_ref)

    return call(
        body, [(factor.shape, BF16)], (mask, factor), [SCALARS, ON_CHIP], name="masked"
    )[0]


def stacked(parts):
    def body(*refs):
        *part_refs, out_hbm, sems = refs
        copies = [
            pltpu.make_async_copy(ref, out_hbm.at[k], sems.at[k])
            for k, ref in enumerate(part_refs)
        ]
        for copy in copies:
            copy.start()
        for copy in copies:
            copy.wait()

    args = [pltpu.with_memory_space_constraint(part, pltpu.VMEM) for part in parts]
    return pl.pallas_call(
        body,
        out_shape=jax.ShapeDtypeStruct((len(parts), *parts[0].shape), F32),
        in_specs=[ON_CHIP] * len(parts),
        out_specs=IN_PLACE,
        scratch_shapes=[pltpu.SemaphoreType.DMA((len(parts),))],
        compiler_params=pltpu.CompilerParams(vmem_limit_bytes=SCOPED_BYTES),
        name="stacked",
    )(*args)


def kept_update(halves, factor, block, before):
    rows, cols = halves[0].shape
    out_cols = factor.shape[2]

    def body(one_ref, other_ref, factor_ref, *refs):
        *before_ref, solved_ref, kept_ref, out_ref = refs
        solved = one_ref[...] + other_ref[...]
        kept = solved.astype(BF16)
        solved_ref[...] = solved
        kept_ref[...] = kept
        update = product(kept, factor_ref[block])
        for ref in before_ref:
            update = update + ref[...]
        out_ref[...] = update

    return call(
        body,
        [((rows, cols), F32), ((rows, cols), BF16), ((rows, out_cols), F32)],
        (*halves, factor, *before),
        name="kept_update",
    )


def early_update(kept, factor, blocks):
    def body(*refs):
        *kept_refs, factor_ref, out_ref = refs
        update = product(kept_refs[0][...], factor_ref[blocks[0]])
        for ref, block in zip(kept_refs[1:], blocks[1:]):
            update = update + product(ref[...], factor_ref[block])
        out_ref[...] = update

    shape = (kept[0].shape[0], factor.shape[2])
    return call(body, [(shape, F32)], (*kept, factor), name="early_update")[0]


def root_part(rhs_rows, update_parts, root_inverse):
    def body(rhs_ref, one_ref, other_ref, inverse_ref, out_ref):
        residual = rhs_ref[...] - (one_ref[...] + other_ref[...])
        out_ref[...] = product(residual.astype(BF16), inverse_ref[...])

    shape = (rhs_rows.shape[0], root_inverse.shape[1])
    return call(
        body, [(shape, F32)], (rhs_rows, *update_parts, root_inverse), name="root_part"
    )[0]


def prow_halves(partial_sum):
    pair = partial_sum + partner(partial_sum, "core")
    return pair, partner(pair, "xl")


def owner_sums(partial_sum):
    pair = partial_sum + partner(partial_sum, "zl")
    return [pair] + [partner(pair, "y", bit) for bit in (2, 3, 1)]


def shards(
    sub_rhs, root_rhs, diag_inverse, root_inverse, inner_factor, inner_mask, root_factor, root_mask
):
    out_cols = inner_factor.shape[2]
    rhs_count = root_rhs.shape[0]
    tiles = out_cols // TILE
    tree = lax.axis_index("zt")
    first_tile = lax.axis_index(PROW) * tiles
    inner_tiles = lax.dynamic_slice_in_dim(inner_mask, first_tile, tiles, 2)
    root_tiles = lax.dynamic_slice_in_dim(root_mask, first_tile, tiles, 2)
    tree = tree.reshape(1)

    halves = prow_halves(first_solve(tree, sub_rhs, diag_inverse))
    inner, inverse, rhs = stage(tree, inner_tiles, sub_rhs, diag_inverse, inner_factor)
    root = masked(root_tiles, root_factor)
    solved0, kept0, update1 = kept_update(halves, inner, 0, ())
    halves = prow_halves(next_solve(0, rhs, owner_sums(update1), inverse))
    early = early_update((kept0,), inner, (1,))
    solved1, kept1, update2 = kept_update(halves, inner, 2, (early,))
    halves = prow_halves(next_solve(1, rhs, owner_sums(update2), inverse))
    early = early_update((kept0, kept1), root, (0, 1))
    solved2, _, root_local = kept_update(halves, root, 2, (early,))

    owners = lax.axis_size(OWN)
    few = rhs_count // owners
    own_rows = lax.all_to_all(
        root_local.reshape(owners, few, out_cols), OWN, 0, 0, tiled=True
    ).sum(axis=0)
    sub_solution, across = lax.optimization_barrier(
        (stacked([solved0, solved1, solved2]), partner(own_rows, "grid"))
    )
    total = own_rows + across
    total = total + partner(total, "zt", 1)
    rhs_rows = lax.dynamic_slice_in_dim(root_rhs, lax.axis_index(OWN) * few, few, 0)
    part = root_part(rhs_rows, (total, partner(total, "zt", 3)), root_inverse)
    pair, other = prow_halves(part)
    root_solution = to_everyone(pair + other, OWN).reshape(rhs_count, part.shape[1])
    return (sub_solution, root_solution)


def solution(mesh):
    prow, pcol = mesh.shape["prow"], mesh.shape["pcol"]
    cores, y = 2, 4
    trees = 8 // mesh.shape["grid"]
    fine = Mesh(
        mesh.devices.reshape(
            mesh.shape["grid"], prow // cores, cores, trees, pcol // (trees * y), y
        ),
        ("grid", "xl", "core", "zt", "zl", "y"),
    )
    columns = ("grid", "zt", "zl", "y")
    return jax.shard_map(
        shards,
        mesh=fine,
        in_specs=(
            P("grid", None, None, PROW),
            P(None, PROW),
            P(None, PROW, columns),
            P(PROW, "grid"),
            P(None, columns, PROW),
            P(None, columns, None),
            P(None, columns, PROW),
            P(None, columns, None),
        ),
        out_specs=(P(None, None, columns), P(None, "grid")),
        check_vma=False,
    )
```

time: 127 us -> 105 us (0.83); the launches traced: 127 us -> 103 us
  matrix products: 17.4 us -> 0 us
  waiting for transfers between devices: 51.3 us -> 42.8 us
  Pallas kernels: 0 us -> 8.39 us
  starting transfers between devices: 34.9 us -> 31.5 us
  other arithmetic: 1.78 us -> 0.14 us
  blocking collectives: 19.9 us -> 18.6 us
    dot_general x16 -> x0, matrix products: 17.4 us -> none  [the longest x10 15.3 us: product(): return jnp.dot(left, right, preferred_element_type=jnp.float32)]
    all_to_all x1 -> x0, starting transfers between devices: 9.99 us -> none  [to_everyone(): lax.all_to_all(jnp.broadcast_to(shard[None], (count, *shard.shape)), axis...]
    all_to_all x1 -> x0, waiting for transfers between devices: 9.51 us -> none  [to_everyone(): lax.all_to_all(jnp.broadcast_to(shard[None], (count, *shard.shape)), axis...]
    pallas_call x0 -> x12, Pallas kernels: none -> 8.39 us  [the longest x11 7.66 us: call(): pl.pallas_call(body, out_shape=[pltpu.VMEM(shape, kind) for shape, kind i...]
    ppermute x15 -> x19, starting transfers between devices: 24.9 us -> 31.5 us  [partner(): lax.ppermute(shard, axis, [(i, i ^ bit) for i in range(lax.axis_size(axis...]
    all_to_all x1, blocking collectives: 11.5 us -> 9.2 us  [shards(): lax.all_to_all(root_local.reshape(owners, few, out_cols), OWN, 0, 0, tile...]
    ppermute x15 -> x19, waiting for transfers between devices: 41.8 us -> 42.8 us  [partner(): lax.ppermute(shard, axis, [(i, i ^ bit) for i in range(lax.axis_size(axis...]
  transfers between devices with their start and end apart: 16 -> 19, of which waited for: 15 -> 17; matrix products, arithmetic and copies ran while one was open for 4% -> 0% of each run, Pallas kernels for 0% -> 5%
where the time goes in v2:
time: 105 us; the launch traced here: 103 us
  waiting for transfers between devices  42.8 us (41%)
  starting transfers between devices  31.5 us (30%)
  blocking collectives  18.6 us (18%)
  Pallas kernels  8.39 us (8%)
    ppermute x19, waiting for transfers between devices, partner(): lax.ppermute(shard, axis, [(i, i ^ bit) for i in range(lax.axis_size(axis...  42.8 us
    ppermute x19, starting transfers between devices, partner(): lax.ppermute(shard, axis, [(i, i ^ bit) for i in range(lax.axis_size(axis...  31.5 us
    all_to_all x1, blocking collectives, to_everyone(): lax.all_to_all(jnp.broadcast_to(shard[None], (count, *shard.shape)), axis...  9.42 us
    all_to_all x1, blocking collectives, shards(): lax.all_to_all(root_local.reshape(owners, few, out_cols), OWN, 0, 0, tile...  9.2 us
    pallas_call x11, Pallas kernels, call(): pl.pallas_call(body, out_shape=[pltpu.VMEM(shape, kind) for shape, kind i...  7.66 us
  transfers between devices with their start and end apart: 19, of which 17 were waited for; matrix products, arithmetic and copies ran while one was open for 0% of the time, Pallas kernels for 5%

profile of v2, /device:TPU:1, one launch (start us, length us, event | category | flops | bytes accessed | tf_op | source)
XLA Modules:
  0.0 103.2 jit_solution(14989147126520784405)
XLA Ops:
  0.6 0.0 copy-start
  0.7 0.0 copy-start.3
  0.7 1.6 %first_solve.1 = f32[64,384]{1,0:T(8,128)S(1)} custom-call(s32[1]{0:T(128)} %bitcast.tree_ref, f32[4,3,64,768]{3,2,1,0:T(8,128)} %rhs_hbm.3, bf16[3,768,384]{2,1,0:T(8,128)(2,1)} %inverse_hbm.3), custom_call_target="tpu_custom_call" | custom-call | tf_op jit(solution)/shard_map/first_solve/pallas_call | solution.py:39
  2.3 3.3 %collective-permute-start = (f32[64,384]{1,0:T(8,128)S(1)}, f32[64,384]{1,0:T(8,128)S(1)}, u32[]{:S(2)}, u32[]{:S(2)}) collective-permute-start(f32[64,384]{1,0:T(8,128)S(1)} %first_solve.1), channel_id=1, source_target_pairs={{0,32},{32,0},{1,33},{33,1},{2,34},{34,2},{3,35},{35,3},{4,36},{36... | collective-permute-start | bytes 294920 | tf_op jit(solution)/shard_map/ppermute | solution.py:23
  5.6 0.9 collective-permute-done
  6.5 0.1 collective-permute-start.1
  6.6 0.0 copy-done.3
  6.7 0.1 constant_dynamic-slice_fusion.2.mask_ref
  6.7 2.6 %stage.1 = (bf16[3,384,768]{2,1,0:T(8,128)(2,1)S(1)}, bf16[2,768,384]{2,1,0:T(8,128)(2,1)S(1)}, f32[2,64,768]{2,1,0:T(8,128)S(1)}) custom-call(s32[1]{0:T(128)} %bitcast.tree_ref, s32[3,3,6]{2,1,0:T(4,128)S(1)} %constant_dynamic-slice_fusion.2.mask_ref, f32[4,3,64,768]{3,2,1,0:T(8,128)} %rhs_hbm.3, bf16[3,768,384]{2,1,0:T(8,128)(2,1)} %inverse_hbm.3, ...), custom_call_target="tpu_custom_call" | custom-call | tf_op jit(solution)/shard_map/stage/pallas_call | solution.py:39
  9.3 1.4 %collective-permute-done.1.other_ref = f32[64,384]{1,0:T(8,128)S(1)} collective-permute-done((f32[64,384]{1,0:T(8,128)S(1)}, f32[64,384]{1,0:T(8,128)S(1)}, u32[]{:S(2)}, u32[]{:S(2)}) %collective-permute-start.1) | collective-permute-done | bytes 98336 | tf_op jit(solution)/shard_map/ppermute | solution.py:23
  10.7 0.2 kept_update.3
  10.9 0.1 collective-permute-start.2
  11.0 5.2 %collective-permute-done.2 = f32[64,768]{1,0:T(8,128)S(1)} collective-permute-done((f32[64,768]{1,0:T(8,128)S(1)}, f32[64,768]{1,0:T(8,128)S(1)}, u32[]{:S(2)}, u32[]{:S(2)}) %collective-permute-start.2) | collective-permute-done | bytes 196640 | tf_op jit(solution)/shard_map/ppermute | solution.py:23
  16.2 1.6 %collective-permute-start.3 = (f32[64,768]{1,0:T(8,128)S(1)}, f32[64,768]{1,0:T(8,128)S(1)}, u32[]{:S(2)}, u32[]{:S(2)}) collective-permute-start(f32[64,768]{1,0:T(8,128)S(1)} %add.43.refs_0_), channel_id=1, source_target_pairs={{0,2},{1,3},{2,0},{3,1},{4,6},{5,7},{6,4},{7,5},{8,10},{9,11},{10,... | collective-permute-start | bytes 589832 | tf_op jit(solution)/shard_map/ppermute | solution.py:23
  17.8 0.8 collective-permute-start.4
  18.6 0.3 collective-permute-start.5
  18.9 3.5 %collective-permute-done.3.refs_1_ = f32[64,768]{1,0:T(8,128)S(1)} collective-permute-done((f32[64,768]{1,0:T(8,128)S(1)}, f32[64,768]{1,0:T(8,128)S(1)}, u32[]{:S(2)}, u32[]{:S(2)}) %collective-permute-start.3) | collective-permute-done | bytes 196640 | tf_op jit(solution)/shard_map/ppermute | solution.py:23
  22.4 5.3 %collective-permute-done.4.refs_2_ = f32[64,768]{1,0:T(8,128)S(1)} collective-permute-done((f32[64,768]{1,0:T(8,128)S(1)}, f32[64,768]{1,0:T(8,128)S(1)}, u32[]{:S(2)}, u32[]{:S(2)}) %collective-permute-start.4) | collective-permute-done | bytes 196640 | tf_op jit(solution)/shard_map/ppermute | solution.py:23
  27.7 0.0 collective-permute-done.5.refs_3_
  27.7 0.2 next_solve.2
  28.0 1.7 %collective-permute-start.6 = (f32[64,384]{1,0:T(8,128)S(1)}, f32[64,384]{1,0:T(8,128)S(1)}, u32[]{:S(2)}, u32[]{:S(2)}) collective-permute-start(f32[64,384]{1,0:T(8,128)S(1)} %next_solve.2), channel_id=1, source_target_pairs={{0,32},{32,0},{1,33},{33,1},{2,34},{34,2},{3,35},{35,3},{4,36},{36... | collective-permute-start | bytes 294920 | tf_op jit(solution)/shard_map/ppermute | solution.py:23
  29.7 0.9 collective-permute-done.6
  30.6 0.8 collective-permute-start.7
  31.4 0.2 early_update.2.refs_0_
  31.6 3.1 %collective-permute-done.7.other_ref = f32[64,384]{1,0:T(8,128)S(1)} collective-permute-done((f32[64,384]{1,0:T(8,128)S(1)}, f32[64,384]{1,0:T(8,128)S(1)}, u32[]{:S(2)}, u32[]{:S(2)}) %collective-permute-start.7) | collective-permute-done | bytes 98336 | tf_op jit(solution)/shard_map/ppermute | solution.py:23
  34.7 0.2 kept_update.4
  35.0 0.0 copy-start.4
  35.0 0.0 copy-start.2
  35.0 0.5 collective-permute-start.8
  35.5 4.8 %collective-permute-done.8 = f32[64,768]{1,0:T(8,128)S(1)} collective-permute-done((f32[64,768]{1,0:T(8,128)S(1)}, f32[64,768]{1,0:T(8,128)S(1)}, u32[]{:S(2)}, u32[]{:S(2)}) %collective-permute-start.8) | collective-permute-done | bytes 196640 | tf_op jit(solution)/shard_map/ppermute | solution.py:23
  40.3 1.6 %collective-permute-start.9 = (f32[64,768]{1,0:T(8,128)S(1)}, f32[64,768]{1,0:T(8,128)S(1)}, u32[]{:S(2)}, u32[]{:S(2)}) collective-permute-start(f32[64,768]{1,0:T(8,128)S(1)} %add.45.refs_0_), channel_id=1, source_target_pairs={{0,2},{1,3},{2,0},{3,1},{4,6},{5,7},{6,4},{7,5},{8,10},{9,11},{10,... | collective-permute-start | bytes 589832 | tf_op jit(solution)/shard_map/ppermute | solution.py:23
  41.9 1.0 collective-permute-start.10
  42.9 0.2 collective-permute-start.11
  43.0 3.5 %collective-permute-done.9.refs_1_ = f32[64,768]{1,0:T(8,128)S(1)} collective-permute-done((f32[64,768]{1,0:T(8,128)S(1)}, f32[64,768]{1,0:T(8,128)S(1)}, u32[]{:S(2)}, u32[]{:S(2)}) %collective-permute-start.9) | collective-permute-done | bytes 196640 | tf_op jit(solution)/shard_map/ppermute | solution.py:23
  46.5 5.3 %collective-permute-done.10.refs_2_ = f32[64,768]{1,0:T(8,128)S(1)} collective-permute-done((f32[64,768]{1,0:T(8,128)S(1)}, f32[64,768]{1,0:T(8,128)S(1)}, u32[]{:S(2)}, u32[]{:S(2)}) %collective-permute-start.10) | collective-permute-done | bytes 196640 | tf_op jit(solution)/shard_map/ppermute | solution.py:23
  51.8 0.0 collective-permute-done.11.refs_3_
  51.8 0.2 next_solve.3
  52.0 1.7 %collective-permute-start.12 = (f32[64,384]{1,0:T(8,128)S(1)}, f32[64,384]{1,0:T(8,128)S(1)}, u32[]{:S(2)}, u32[]{:S(2)}) collective-permute-start(f32[64,384]{1,0:T(8,128)S(1)} %next_solve.3), channel_id=1, source_target_pairs={{0,32},{32,0},{1,33},{33,1},{2,34},{34,2},{3,35},{35,3},{4,36},{36... | collective-permute-start | bytes 294920 | tf_op jit(solution)/shard_map/ppermute | solution.py:23
  53.8 0.9 collective-permute-done.12
  54.7 0.8 collective-permute-start.13
  55.5 0.0 copy-done.4
  55.5 0.1 constant_dynamic-slice_fusion.1.mask_ref
  55.6 0.0 copy-done.2
  55.6 0.9 masked.1.refs_2_.factor_ref
  56.5 0.3 early_update.3.refs_0_
  56.8 0.0 copy-start.1
  56.9 2.0 %collective-permute-done.13.other_ref = f32[64,384]{1,0:T(8,128)S(1)} collective-permute-done((f32[64,384]{1,0:T(8,128)S(1)}, f32[64,384]{1,0:T(8,128)S(1)}, u32[]{:S(2)}, u32[]{:S(2)}) %collective-permute-start.13) | collective-permute-done | bytes 98336 | tf_op jit(solution)/shard_map/ppermute | solution.py:23
  58.8 0.7 kept_update.5
  59.5 9.2 %all_to_all.10 = f32[8,8,768]{2,1,0:T(8,128)S(1)} all-to-all(f32[8,8,768]{2,1,0:T(8,128)S(1)} %bitcast.3), channel_id=1, replica_groups=mesh['grid'=2,'xl'=2,'core'=2,'zt'=4,'zl'=2,'y'=4] {'zl','y'}, dimensions={0} | all-to-all | bytes 393216 | tf_op jit(solution)/shard_map/all_to_all | solution.py:281
  68.8 2.8 %collective-permute-start.14 = (f32[8,768]{1,0:T(8,128)S(1)}, f32[8,768]{1,0:T(8,128)S(1)}, u32[]{:S(2)}, u32[]{:S(2)}) collective-permute-start(f32[8,768]{1,0:T(8,128)S(1)} %reduce_sum.9), channel_id=1, source_target_pairs={{0,128},{128,0},{1,129},{129,1},{2,130},{130,2},{3,131},{131,3},{4... | collective-permute-start | bytes 73736 | tf_op jit(solution)/shard_map/ppermute | solution.py:23
  71.6 0.7 stacked.1
  72.3 0.7 collective-permute-done.14
  73.0 3.0 %collective-permute-start.15 = (f32[8,768]{1,0:T(8,128)S(1)}, f32[8,768]{1,0:T(8,128)S(1)}, u32[]{:S(2)}, u32[]{:S(2)}) collective-permute-start(f32[8,768]{1,0:T(8,128)S(1)} %add.49), channel_id=1, source_target_pairs={{0,8},{8,0},{16,24},{24,16},{1,9},{9,1},{17,25},{25,17},{2,10},{10... | collective-permute-start | bytes 73736 | tf_op jit(solution)/shard_map/ppermute | solution.py:23
  76.0 1.5 %collective-permute-done.15 = f32[8,768]{1,0:T(8,128)S(1)} collective-permute-done((f32[8,768]{1,0:T(8,128)S(1)}, f32[8,768]{1,0:T(8,128)S(1)}, u32[]{:S(2)}, u32[]{:S(2)}) %collective-permute-start.15) | collective-permute-done | bytes 24608 | tf_op jit(solution)/shard_map/ppermute | solution.py:23
  77.5 4.2 %collective-permute-start.16 = (f32[8,768]{1,0:T(8,128)S(1)}, f32[8,768]{1,0:T(8,128)S(1)}, u32[]{:S(2)}, u32[]{:S(2)}) collective-permute-start(f32[8,768]{1,0:T(8,128)S(1)} %add.50.one_ref), channel_id=1, source_target_pairs={{0,24},{8,16},{16,8},{24,0},{1,25},{9,17},{17,9},{25,1},{2,26},{10... | collective-permute-start | bytes 73736 | tf_op jit(solution)/shard_map/ppermute | solution.py:23
  81.7 0.0 copy-done
  81.7 1.2 %collective-permute-done.16.other_ref = f32[8,768]{1,0:T(8,128)S(1)} collective-permute-done((f32[8,768]{1,0:T(8,128)S(1)}, f32[8,768]{1,0:T(8,128)S(1)}, u32[]{:S(2)}, u32[]{:S(2)}) %collective-permute-start.16) | collective-permute-done | bytes 24608 | tf_op jit(solution)/shard_map/ppermute | solution.py:23
  83.0 0.4 root_part.1
  83.4 5.8 %collective-permute-start.17 = (f32[8,1536]{1,0:T(8,128)S(1)}, f32[8,1536]{1,0:T(8,128)S(1)}, u32[]{:S(2)}, u32[]{:S(2)}) collective-permute-start(f32[8,1536]{1,0:T(8,128)S(1)} %root_part.1), channel_id=1, source_target_pairs={{0,32},{32,0},{1,33},{33,1},{2,34},{34,2},{3,35},{35,3},{4,36},{36... | collective-permute-start | bytes 147464 | tf_op jit(solution)/shard_map/ppermute | solution.py:23
  89.2 0.9 collective-permute-done.17
  90.0 1.2 %collective-permute-start.18 = (f32[8,1536]{1,0:T(8,128)S(1)}, f32[8,1536]{1,0:T(8,128)S(1)}, u32[]{:S(2)}, u32[]{:S(2)}) collective-permute-start(f32[8,1536]{1,0:T(8,128)S(1)} %add.51), channel_id=1, source_target_pairs={{0,64},{64,0},{1,65},{65,1},{2,66},{66,2},{3,67},{67,3},{4,68},{68... | collective-permute-start | bytes 147464 | tf_op jit(solution)/shard_map/ppermute | solution.py:23
  91.3 1.7 %collective-permute-done.18 = f32[8,1536]{1,0:T(8,128)S(1)} collective-permute-done((f32[8,1536]{1,0:T(8,128)S(1)}, f32[8,1536]{1,0:T(8,128)S(1)}, u32[]{:S(2)}, u32[]{:S(2)}) %collective-permute-start.18) | collective-permute-done | bytes 49184 | tf_op jit(solution)/shard_map/ppermute | solution.py:23
  93.0 9.4 %all_to_all.11 = f32[8,8,1536]{2,1,0:T(8,128)S(1)} all-to-all(f32[8,8,1536]{2,1,0:T(8,128)S(1)} %broadcast_in_dim.2), channel_id=1, replica_groups=mesh['grid'=2,'xl'=2,'core'=2,'zt'=4,'zl'=2,'y'=4] {'zl','y'}, dimensions={0} | all-to-all | bytes 786432 | tf_op jit(solution)/shard_map/all_to_all | solution.py:28
  102.5 0.7 copy.11
  (13 shorter events, 0.2 us)
Async XLA Ops:
  0.6 81.1 %copy-start = (f32[64,768]{1,0:T(8,128)S(1)}, f32[64,768]{1,0:T(8,128)}, u32[]{:S(2)}) copy-start(f32[64,768]{1,0:T(8,128)} %param.9) | copy-start | bytes 589828
  0.7 6.0 %copy-start.3 = (s32[3,3,24]{2,1,0:T(4,128)S(1)}, s32[3,3,24]{2,1,0:T(4,128)}, u32[]{:S(2)}) copy-start(s32[3,3,24]{2,1,0:T(4,128)} %param.13) | copy-start | bytes 2596
  2.3 4.3 %collective-permute-start = (f32[64,384]{1,0:T(8,128)S(1)}, f32[64,384]{1,0:T(8,128)S(1)}, u32[]{:S(2)}, u32[]{:S(2)}) collective-permute-start(f32[64,384]{1,0:T(8,128)S(1)} %first_solve.1), channel_id=1, source_target_pairs={{0,32},{32,0},{1,33},{33,1},{2,34},{34,2},{3,35},{35,3},{4,36},{36... | collective-permute-start | bytes 294920 | tf_op jit(solution)/shard_map/ppermute | solution.py:23
  6.5 4.1 %collective-permute-start.1 = (f32[64,384]{1,0:T(8,128)S(1)}, f32[64,384]{1,0:T(8,128)S(1)}, u32[]{:S(2)}, u32[]{:S(2)}) collective-permute-start(f32[64,384]{1,0:T(8,128)S(1)} %add.40.one_ref), channel_id=1, source_target_pairs={{0,64},{64,0},{1,65},{65,1},{2,66},{66,2},{3,67},{67,3},{4,68},{68... | collective-permute-start | bytes 294920 | tf_op jit(solution)/shard_map/ppermute | solution.py:23
  10.9 5.3 %collective-permute-start.2 = (f32[64,768]{1,0:T(8,128)S(1)}, f32[64,768]{1,0:T(8,128)S(1)}, u32[]{:S(2)}, u32[]{:S(2)}) collective-permute-start(f32[64,768]{1,0:T(8,128)S(1)} %get-tuple-element.18), channel_id=1, source_target_pairs={{0,4},{4,0},{1,5},{5,1},{2,6},{6,2},{3,7},{7,3},{8,12},{12,8},{9,1... | collective-permute-start | bytes 589832 | tf_op jit(solution)/shard_map/ppermute | solution.py:23
  16.2 6.2 %collective-permute-start.3 = (f32[64,768]{1,0:T(8,128)S(1)}, f32[64,768]{1,0:T(8,128)S(1)}, u32[]{:S(2)}, u32[]{:S(2)}) collective-permute-start(f32[64,768]{1,0:T(8,128)S(1)} %add.43.refs_0_), channel_id=1, source_target_pairs={{0,2},{1,3},{2,0},{3,1},{4,6},{5,7},{6,4},{7,5},{8,10},{9,11},{10,... | collective-permute-start | bytes 589832 | tf_op jit(solution)/shard_map/ppermute | solution.py:23
  17.8 9.9 %collective-permute-start.4 = (f32[64,768]{1,0:T(8,128)S(1)}, f32[64,768]{1,0:T(8,128)S(1)}, u32[]{:S(2)}, u32[]{:S(2)}) collective-permute-start(f32[64,768]{1,0:T(8,128)S(1)} %add.43.refs_0_), channel_id=1, source_target_pairs={{0,3},{1,2},{2,1},{3,0},{4,7},{5,6},{6,5},{7,4},{8,11},{9,10},{10,... | collective-permute-start | bytes 589832 | tf_op jit(solution)/shard_map/ppermute | solution.py:23
  18.6 9.1 %collective-permute-start.5 = (f32[64,768]{1,0:T(8,128)S(1)}, f32[64,768]{1,0:T(8,128)S(1)}, u32[]{:S(2)}, u32[]{:S(2)}) collective-permute-start(f32[64,768]{1,0:T(8,128)S(1)} %add.43.refs_0_), channel_id=1, source_target_pairs={{0,1},{1,0},{2,3},{3,2},{4,5},{5,4},{6,7},{7,6},{8,9},{9,8},{10,11... | collective-permute-start | bytes 589832 | tf_op jit(solution)/shard_map/ppermute | solution.py:23
  28.0 2.6 %collective-permute-start.6 = (f32[64,384]{1,0:T(8,128)S(1)}, f32[64,384]{1,0:T(8,128)S(1)}, u32[]{:S(2)}, u32[]{:S(2)}) collective-permute-start(f32[64,384]{1,0:T(8,128)S(1)} %next_solve.2), channel_id=1, source_target_pairs={{0,32},{32,0},{1,33},{33,1},{2,34},{34,2},{3,35},{35,3},{4,36},{36... | collective-permute-start | bytes 294920 | tf_op jit(solution)/shard_map/ppermute | solution.py:23
  30.6 4.1 %collective-permute-start.7 = (f32[64,384]{1,0:T(8,128)S(1)}, f32[64,384]{1,0:T(8,128)S(1)}, u32[]{:S(2)}, u32[]{:S(2)}) collective-permute-start(f32[64,384]{1,0:T(8,128)S(1)} %add.44.one_ref), channel_id=1, source_target_pairs={{0,64},{64,0},{1,65},{65,1},{2,66},{66,2},{3,67},{67,3},{4,68},{68... | collective-permute-start | bytes 294920 | tf_op jit(solution)/shard_map/ppermute | solution.py:23
  35.0 20.5 %copy-start.4 = (s32[3,3,24]{2,1,0:T(4,128)S(1)}, s32[3,3,24]{2,1,0:T(4,128)}, u32[]{:S(2)}) copy-start(s32[3,3,24]{2,1,0:T(4,128)} %param.15) | copy-start | bytes 2596
  35.0 20.6 %copy-start.2 = (bf16[3,384,768]{2,1,0:T(8,128)(2,1)S(1)}, bf16[3,384,768]{2,1,0:T(8,128)(2,1)}, u32[]{:S(2)}) copy-start(bf16[3,384,768]{2,1,0:T(8,128)(2,1)} %factor_ref.1) | copy-start | bytes 5308420
  35.0 5.3 %collective-permute-start.8 = (f32[64,768]{1,0:T(8,128)S(1)}, f32[64,768]{1,0:T(8,128)S(1)}, u32[]{:S(2)}, u32[]{:S(2)}) collective-permute-start(f32[64,768]{1,0:T(8,128)S(1)} %get-tuple-element.22), channel_id=1, source_target_pairs={{0,4},{4,0},{1,5},{5,1},{2,6},{6,2},{3,7},{7,3},{8,12},{12,8},{9,1... | collective-permute-start | bytes 589832 | tf_op jit(solution)/shard_map/ppermute | solution.py:23
  40.3 6.2 %collective-permute-start.9 = (f32[64,768]{1,0:T(8,128)S(1)}, f32[64,768]{1,0:T(8,128)S(1)}, u32[]{:S(2)}, u32[]{:S(2)}) collective-permute-start(f32[64,768]{1,0:T(8,128)S(1)} %add.45.refs_0_), channel_id=1, source_target_pairs={{0,2},{1,3},{2,0},{3,1},{4,6},{5,7},{6,4},{7,5},{8,10},{9,11},{10,... | collective-permute-start | bytes 589832 | tf_op jit(solution)/shard_map/ppermute | solution.py:23
  41.9 9.9 %collective-permute-start.10 = (f32[64,768]{1,0:T(8,128)S(1)}, f32[64,768]{1,0:T(8,128)S(1)}, u32[]{:S(2)}, u32[]{:S(2)}) collective-permute-start(f32[64,768]{1,0:T(8,128)S(1)} %add.45.refs_0_), channel_id=1, source_target_pairs={{0,3},{1,2},{2,1},{3,0},{4,7},{5,6},{6,5},{7,4},{8,11},{9,10},{10,... | collective-permute-start | bytes 589832 | tf_op jit(solution)/shard_map/ppermute | solution.py:23
  42.9 8.9 %collective-permute-start.11 = (f32[64,768]{1,0:T(8,128)S(1)}, f32[64,768]{1,0:T(8,128)S(1)}, u32[]{:S(2)}, u32[]{:S(2)}) collective-permute-start(f32[64,768]{1,0:T(8,128)S(1)} %add.45.refs_0_), channel_id=1, source_target_pairs={{0,1},{1,0},{2,3},{3,2},{4,5},{5,4},{6,7},{7,6},{8,9},{9,8},{10,11... | collective-permute-start | bytes 589832 | tf_op jit(solution)/shard_map/ppermute | solution.py:23
  52.0 2.7 %collective-permute-start.12 = (f32[64,384]{1,0:T(8,128)S(1)}, f32[64,384]{1,0:T(8,128)S(1)}, u32[]{:S(2)}, u32[]{:S(2)}) collective-permute-start(f32[64,384]{1,0:T(8,128)S(1)} %next_solve.3), channel_id=1, source_target_pairs={{0,32},{32,0},{1,33},{33,1},{2,34},{34,2},{3,35},{35,3},{4,36},{36... | collective-permute-start | bytes 294920 | tf_op jit(solution)/shard_map/ppermute | solution.py:23
  54.7 4.1 %collective-permute-start.13 = (f32[64,384]{1,0:T(8,128)S(1)}, f32[64,384]{1,0:T(8,128)S(1)}, u32[]{:S(2)}, u32[]{:S(2)}) collective-permute-start(f32[64,384]{1,0:T(8,128)S(1)} %add.46.one_ref), channel_id=1, source_target_pairs={{0,64},{64,0},{1,65},{65,1},{2,66},{66,2},{3,67},{67,3},{4,68},{68... | collective-permute-start | bytes 294920 | tf_op jit(solution)/shard_map/ppermute | solution.py:23
  56.8 26.1 %copy-start.1 = (bf16[768,1536]{1,0:T(8,128)(2,1)S(1)}, bf16[768,1536]{1,0:T(8,128)(2,1)}, u32[]{:S(2)}) copy-start(bf16[768,1536]{1,0:T(8,128)(2,1)} %inverse_ref.1) | copy-start | bytes 7077892
  68.8 4.3 %collective-permute-start.14 = (f32[8,768]{1,0:T(8,128)S(1)}, f32[8,768]{1,0:T(8,128)S(1)}, u32[]{:S(2)}, u32[]{:S(2)}) collective-permute-start(f32[8,768]{1,0:T(8,128)S(1)} %reduce_sum.9), channel_id=1, source_target_pairs={{0,128},{128,0},{1,129},{129,1},{2,130},{130,2},{3,131},{131,3},{4... | collective-permute-start | bytes 73736 | tf_op jit(solution)/shard_map/ppermute | solution.py:23
  73.0 4.5 %collective-permute-start.15 = (f32[8,768]{1,0:T(8,128)S(1)}, f32[8,768]{1,0:T(8,128)S(1)}, u32[]{:S(2)}, u32[]{:S(2)}) collective-permute-start(f32[8,768]{1,0:T(8,128)S(1)} %add.49), channel_id=1, source_target_pairs={{0,8},{8,0},{16,24},{24,16},{1,9},{9,1},{17,25},{25,17},{2,10},{10... | collective-permute-start | bytes 73736 | tf_op jit(solution)/shard_map/ppermute | solution.py:23
  77.5 5.4 %collective-permute-start.16 = (f32[8,768]{1,0:T(8,128)S(1)}, f32[8,768]{1,0:T(8,128)S(1)}, u32[]{:S(2)}, u32[]{:S(2)}) collective-permute-start(f32[8,768]{1,0:T(8,128)S(1)} %add.50.one_ref), channel_id=1, source_target_pairs={{0,24},{8,16},{16,8},{24,0},{1,25},{9,17},{17,9},{25,1},{2,26},{10... | collective-permute-start | bytes 73736 | tf_op jit(solution)/shard_map/ppermute | solution.py:23
  83.4 6.7 %collective-permute-start.17 = (f32[8,1536]{1,0:T(8,128)S(1)}, f32[8,1536]{1,0:T(8,128)S(1)}, u32[]{:S(2)}, u32[]{:S(2)}) collective-permute-start(f32[8,1536]{1,0:T(8,128)S(1)} %root_part.1), channel_id=1, source_target_pairs={{0,32},{32,0},{1,33},{33,1},{2,34},{34,2},{3,35},{35,3},{4,36},{36... | collective-permute-start | bytes 147464 | tf_op jit(solution)/shard_map/ppermute | solution.py:23
  90.0 2.9 %collective-permute-start.18 = (f32[8,1536]{1,0:T(8,128)S(1)}, f32[8,1536]{1,0:T(8,128)S(1)}, u32[]{:S(2)}, u32[]{:S(2)}) collective-permute-start(f32[8,1536]{1,0:T(8,128)S(1)} %add.51), channel_id=1, source_target_pairs={{0,64},{64,0},{1,65},{65,1},{2,66},{66,2},{3,67},{67,3},{4,68},{68... | collective-permute-start | bytes 147464 | tf_op jit(solution)/shard_map/ppermute | solution.py:23

commit v3 on v2

--- a/solution.py
+++ b/solution.py
@@ -10,6 +10,7 @@
 TILE = 128
 PROW = ("xl", "core")
 OWN = ("zl", "y")
+TREES = ("grid", "zt")
 SCOPED_BYTES = 4 << 20
 F32 = jnp.float32
 BF16 = jnp.bfloat16
@@ -197,16 +198,17 @@
     )(*args)
 
 
-def kept_update(halves, factor, block, before):
+def kept_update(halves, factor, block, before, last=False):
     rows, cols = halves[0].shape
     out_cols = factor.shape[2]
 
     def body(one_ref, other_ref, factor_ref, *refs):
-        *before_ref, solved_ref, kept_ref, out_ref = refs
+        before_ref, (out_ref, solved_ref, *kept_ref) = refs[: len(before)], refs[len(before) :]
         solved = one_ref[...] + other_ref[...]
         kept = solved.astype(BF16)
         solved_ref[...] = solved
-        kept_ref[...] = kept
+        for ref in kept_ref:
+            ref[...] = kept
         update = product(kept, factor_ref[block])
         for ref in before_ref:
             update = update + ref[...]
@@ -214,7 +216,7 @@
 
     return call(
         body,
-        [((rows, cols), F32), ((rows, cols), BF16), ((rows, out_cols), F32)],
+        [((rows, out_cols), F32), ((rows, cols), F32), ((rows, cols), BF16)][: 2 if last else 3],
         (*halves, factor, *before),
         name="kept_update",
     )
@@ -250,7 +252,7 @@
 
 def owner_sums(partial_sum):
     pair = partial_sum + partner(partial_sum, "zl")
-    return [pair] + [partner(pair, "y", bit) for bit in (2, 3, 1)]
+    return [pair] + [partner(pair, "y", bit) for bit in (1, 3, 2)]
 
 
 def shards(
@@ -268,24 +270,26 @@
     halves = prow_halves(first_solve(tree, sub_rhs, diag_inverse))
     inner, inverse, rhs = stage(tree, inner_tiles, sub_rhs, diag_inverse, inner_factor)
     root = masked(root_tiles, root_factor)
-    solved0, kept0, update1 = kept_update(halves, inner, 0, ())
+    update1, solved0, kept0 = kept_update(halves, inner, 0, ())
     halves = prow_halves(next_solve(0, rhs, owner_sums(update1), inverse))
     early = early_update((kept0,), inner, (1,))
-    solved1, kept1, update2 = kept_update(halves, inner, 2, (early,))
+    update2, solved1, kept1 = kept_update(halves, inner, 2, (early,))
     halves = prow_halves(next_solve(1, rhs, owner_sums(update2), inverse))
     early = early_update((kept0, kept1), root, (0, 1))
-    solved2, _, root_local = kept_update(halves, root, 2, (early,))
+    root_local, solved2 = kept_update(halves, root, 2, (early,), last=True)
 
     owners = lax.axis_size(OWN)
     few = rhs_count // owners
     own_rows = lax.all_to_all(
         root_local.reshape(owners, few, out_cols), OWN, 0, 0, tiled=True
     ).sum(axis=0)
-    sub_solution, across = lax.optimization_barrier(
-        (stacked([solved0, solved1, solved2]), partner(own_rows, "grid"))
-    )
-    total = own_rows + across
-    total = total + partner(total, "zt", 1)
+    sub_solution, *arrived = lax.optimization_barrier(
+        (
+            stacked([solved0, solved1, solved2]),
+            *[partner(own_rows, TREES, bit) for bit in (4, 1, 5)],
+        )
+    )
+    total = own_rows + arrived[0] + (arrived[1] + arrived[2])
     rhs_rows = lax.dynamic_slice_in_dim(root_rhs, lax.axis_index(OWN) * few, few, 0)
     part = root_part(rhs_rows, (total, partner(total, "zt", 3)), root_inverse)
     pair, other = prow_halves(part)

time: 105 us -> 106 us (level)
  starting transfers between devices: 31.5 us -> 35.5 us
  waiting for transfers between devices: 42.8 us -> 41.3 us
    ppermute x19 -> x20, starting transfers between devices: 31.5 us -> 35.5 us  [partner(): lax.ppermute(shard, axis, [(i, i ^ bit) for i in range(lax.axis_size(axis...]
    ppermute x19 -> x20, waiting for transfers between devices: 42.8 us -> 41.3 us  [partner(): lax.ppermute(shard, axis, [(i, i ^ bit) for i in range(lax.axis_size(axis...]
  transfers between devices with their start and end apart: 19 -> 20, of which waited for: 17 -> 19; matrix products, arithmetic and copies ran while one was open for 0% -> 0% of each run, Pallas kernels for 5% -> 5%
where the time goes in v3:
time: 106 us; the launch traced here: 105 us
  waiting for transfers between devices  41.3 us (39%)
  starting transfers between devices  35.5 us (33%)
  blocking collectives  18.6 us (18%)
  Pallas kernels  7.9 us (7%)
    ppermute x20, waiting for transfers between devices, partner(): lax.ppermute(shard, axis, [(i, i ^ bit) for i in range(lax.axis_size(axis...  41.3 us
    ppermute x20, starting transfers between devices, partner(): lax.ppermute(shard, axis, [(i, i ^ bit) for i in range(lax.axis_size(axis...  35.5 us
    all_to_all x1, blocking collectives, to_everyone(): lax.all_to_all(jnp.broadcast_to(shard[None], (count, *shard.shape)), axis...  9.31 us
    all_to_all x1, blocking collectives, shards(): lax.all_to_all(root_local.reshape(owners, few, out_cols), OWN, 0, 0, tile...  9.25 us
    pallas_call x11, Pallas kernels, call(): pl.pallas_call(body, out_shape=[pltpu.VMEM(shape, kind) for shape, kind i...  7.17 us
  transfers between devices with their start and end apart: 20, of which 19 were waited for; matrix products, arithmetic and copies ran while one was open for 0% of the time, Pallas kernels for 5%

profile of v3, /device:TPU:1, one launch (start us, length us, event | category | flops | bytes accessed | tf_op | source)
XLA Modules:
  0.0 105.2 jit_solution(3724324368267844531)
XLA Ops:
  0.6 0.0 copy-start
  0.7 1.6 %first_solve.1 = f32[64,384]{1,0:T(8,128)S(1)} custom-call(s32[1]{0:T(128)} %bitcast.tree_ref, f32[4,3,64,768]{3,2,1,0:T(8,128)} %rhs_hbm.3, bf16[3,768,384]{2,1,0:T(8,128)(2,1)} %inverse_hbm.3), custom_call_target="tpu_custom_call" | custom-call | tf_op jit(solution)/shard_map/first_solve/pallas_call | solution.py:40
  2.3 3.3 %collective-permute-start = (f32[64,384]{1,0:T(8,128)S(1)}, f32[64,384]{1,0:T(8,128)S(1)}, u32[]{:S(2)}, u32[]{:S(2)}) collective-permute-start(f32[64,384]{1,0:T(8,128)S(1)} %first_solve.1), channel_id=1, source_target_pairs={{0,32},{32,0},{1,33},{33,1},{2,34},{34,2},{3,35},{35,3},{4,36},{36... | collective-permute-start | bytes 294920 | tf_op jit(solution)/shard_map/ppermute | solution.py:24
  5.6 0.9 collective-permute-done
  6.5 0.1 collective-permute-start.1
  6.6 0.0 copy-done.3
  6.7 0.1 constant_dynamic-slice_fusion.2.mask_ref
  6.7 2.6 %stage.1 = (bf16[3,384,768]{2,1,0:T(8,128)(2,1)S(1)}, bf16[2,768,384]{2,1,0:T(8,128)(2,1)S(1)}, f32[2,64,768]{2,1,0:T(8,128)S(1)}) custom-call(s32[1]{0:T(128)} %bitcast.tree_ref, s32[3,3,6]{2,1,0:T(4,128)S(1)} %constant_dynamic-slice_fusion.2.mask_ref, f32[4,3,64,768]{3,2,1,0:T(8,128)} %rhs_hbm.3, bf16[3,768,384]{2,1,0:T(8,128)(2,1)} %inverse_hbm.3, ...), custom_call_target="tpu_custom_call" | custom-call | tf_op jit(solution)/shard_map/stage/pallas_call | solution.py:40
  9.3 1.4 %collective-permute-done.1.other_ref = f32[64,384]{1,0:T(8,128)S(1)} collective-permute-done((f32[64,384]{1,0:T(8,128)S(1)}, f32[64,384]{1,0:T(8,128)S(1)}, u32[]{:S(2)}, u32[]{:S(2)}) %collective-permute-start.1) | collective-permute-done | bytes 98336 | tf_op jit(solution)/shard_map/ppermute | solution.py:24
  10.7 0.2 kept_update.3
  10.9 0.1 collective-permute-start.2
  11.0 5.2 %collective-permute-done.2 = f32[64,768]{1,0:T(8,128)S(1)} collective-permute-done((f32[64,768]{1,0:T(8,128)S(1)}, f32[64,768]{1,0:T(8,128)S(1)}, u32[]{:S(2)}, u32[]{:S(2)}) %collective-permute-start.2) | collective-permute-done | bytes 196640 | tf_op jit(solution)/shard_map/ppermute | solution.py:24
  16.2 0.1 collective-permute-start.3
  16.3 1.8 %collective-permute-start.4 = (f32[64,768]{1,0:T(8,128)S(1)}, f32[64,768]{1,0:T(8,128)S(1)}, u32[]{:S(2)}, u32[]{:S(2)}) collective-permute-start(f32[64,768]{1,0:T(8,128)S(1)} %add.46.refs_0_), channel_id=1, source_target_pairs={{0,3},{1,2},{2,1},{3,0},{4,7},{5,6},{6,5},{7,4},{8,11},{9,10},{10,... | collective-permute-start | bytes 589832 | tf_op jit(solution)/shard_map/ppermute | solution.py:24
  18.1 1.4 %collective-permute-start.5 = (f32[64,768]{1,0:T(8,128)S(1)}, f32[64,768]{1,0:T(8,128)S(1)}, u32[]{:S(2)}, u32[]{:S(2)}) collective-permute-start(f32[64,768]{1,0:T(8,128)S(1)} %add.46.refs_0_), channel_id=1, source_target_pairs={{0,2},{1,3},{2,0},{3,1},{4,6},{5,7},{6,4},{7,5},{8,10},{9,11},{10,... | collective-permute-start | bytes 589832 | tf_op jit(solution)/shard_map/ppermute | solution.py:24
  19.5 1.3 %collective-permute-done.3.refs_1_ = f32[64,768]{1,0:T(8,128)S(1)} collective-permute-done((f32[64,768]{1,0:T(8,128)S(1)}, f32[64,768]{1,0:T(8,128)S(1)}, u32[]{:S(2)}, u32[]{:S(2)}) %collective-permute-start.3) | collective-permute-done | bytes 196640 | tf_op jit(solution)/shard_map/ppermute | solution.py:24
  20.8 1.3 %collective-permute-done.4.refs_2_ = f32[64,768]{1,0:T(8,128)S(1)} collective-permute-done((f32[64,768]{1,0:T(8,128)S(1)}, f32[64,768]{1,0:T(8,128)S(1)}, u32[]{:S(2)}, u32[]{:S(2)}) %collective-permute-start.4) | collective-permute-done | bytes 196640 | tf_op jit(solution)/shard_map/ppermute | solution.py:24
  22.1 4.0 %collective-permute-done.5.refs_3_ = f32[64,768]{1,0:T(8,128)S(1)} collective-permute-done((f32[64,768]{1,0:T(8,128)S(1)}, f32[64,768]{1,0:T(8,128)S(1)}, u32[]{:S(2)}, u32[]{:S(2)}) %collective-permute-start.5) | collective-permute-done | bytes 196640 | tf_op jit(solution)/shard_map/ppermute | solution.py:24
  26.1 0.2 next_solve.2
  26.3 3.2 %collective-permute-start.6 = (f32[64,384]{1,0:T(8,128)S(1)}, f32[64,384]{1,0:T(8,128)S(1)}, u32[]{:S(2)}, u32[]{:S(2)}) collective-permute-start(f32[64,384]{1,0:T(8,128)S(1)} %next_solve.2), channel_id=1, source_target_pairs={{0,32},{32,0},{1,33},{33,1},{2,34},{34,2},{3,35},{35,3},{4,36},{36... | collective-permute-start | bytes 294920 | tf_op jit(solution)/shard_map/ppermute | solution.py:24
  29.6 0.9 collective-permute-done.6
  30.5 1.3 %collective-permute-start.7 = (f32[64,384]{1,0:T(8,128)S(1)}, f32[64,384]{1,0:T(8,128)S(1)}, u32[]{:S(2)}, u32[]{:S(2)}) collective-permute-start(f32[64,384]{1,0:T(8,128)S(1)} %add.47.one_ref), channel_id=1, source_target_pairs={{0,64},{64,0},{1,65},{65,1},{2,66},{66,2},{3,67},{67,3},{4,68},{68... | collective-permute-start | bytes 294920 | tf_op jit(solution)/shard_map/ppermute | solution.py:24
  31.8 0.2 early_update.2.refs_0_
  32.0 2.6 %collective-permute-done.7.other_ref = f32[64,384]{1,0:T(8,128)S(1)} collective-permute-done((f32[64,384]{1,0:T(8,128)S(1)}, f32[64,384]{1,0:T(8,128)S(1)}, u32[]{:S(2)}, u32[]{:S(2)}) %collective-permute-start.7) | collective-permute-done | bytes 98336 | tf_op jit(solution)/shard_map/ppermute | solution.py:24
  34.6 0.2 kept_update.4
  34.9 0.0 copy-start.4
  34.9 0.0 copy-start.2
  34.9 1.3 %collective-permute-start.8 = (f32[64,768]{1,0:T(8,128)S(1)}, f32[64,768]{1,0:T(8,128)S(1)}, u32[]{:S(2)}, u32[]{:S(2)}) collective-permute-start(f32[64,768]{1,0:T(8,128)S(1)} %get-tuple-element.24), channel_id=1, source_target_pairs={{0,4},{4,0},{1,5},{5,1},{2,6},{6,2},{3,7},{7,3},{8,12},{12,8},{9,1... | collective-permute-start | bytes 589832 | tf_op jit(solution)/shard_map/ppermute | solution.py:24
  36.2 4.0 %collective-permute-done.8 = f32[64,768]{1,0:T(8,128)S(1)} collective-permute-done((f32[64,768]{1,0:T(8,128)S(1)}, f32[64,768]{1,0:T(8,128)S(1)}, u32[]{:S(2)}, u32[]{:S(2)}) %collective-permute-start.8) | collective-permute-done | bytes 196640 | tf_op jit(solution)/shard_map/ppermute | solution.py:24
  40.2 0.5 collective-permute-start.9
  40.8 1.3 %collective-permute-start.10 = (f32[64,768]{1,0:T(8,128)S(1)}, f32[64,768]{1,0:T(8,128)S(1)}, u32[]{:S(2)}, u32[]{:S(2)}) collective-permute-start(f32[64,768]{1,0:T(8,128)S(1)} %add.48.refs_0_), channel_id=1, source_target_pairs={{0,3},{1,2},{2,1},{3,0},{4,7},{5,6},{6,5},{7,4},{8,11},{9,10},{10,... | collective-permute-start | bytes 589832 | tf_op jit(solution)/shard_map/ppermute | solution.py:24
  42.0 1.5 %collective-permute-start.11 = (f32[64,768]{1,0:T(8,128)S(1)}, f32[64,768]{1,0:T(8,128)S(1)}, u32[]{:S(2)}, u32[]{:S(2)}) collective-permute-start(f32[64,768]{1,0:T(8,128)S(1)} %add.48.refs_0_), channel_id=1, source_target_pairs={{0,2},{1,3},{2,0},{3,1},{4,6},{5,7},{6,4},{7,5},{8,10},{9,11},{10,... | collective-permute-start | bytes 589832 | tf_op jit(solution)/shard_map/ppermute | solution.py:24
  43.6 1.3 %collective-permute-done.9.refs_1_ = f32[64,768]{1,0:T(8,128)S(1)} collective-permute-done((f32[64,768]{1,0:T(8,128)S(1)}, f32[64,768]{1,0:T(8,128)S(1)}, u32[]{:S(2)}, u32[]{:S(2)}) %collective-permute-start.9) | collective-permute-done | bytes 196640 | tf_op jit(solution)/shard_map/ppermute | solution.py:24
  44.8 2.5 %collective-permute-done.10.refs_2_ = f32[64,768]{1,0:T(8,128)S(1)} collective-permute-done((f32[64,768]{1,0:T(8,128)S(1)}, f32[64,768]{1,0:T(8,128)S(1)}, u32[]{:S(2)}, u32[]{:S(2)}) %collective-permute-start.10) | collective-permute-done | bytes 196640 | tf_op jit(solution)/shard_map/ppermute | solution.py:24
  47.3 2.5 %collective-permute-done.11.refs_3_ = f32[64,768]{1,0:T(8,128)S(1)} collective-permute-done((f32[64,768]{1,0:T(8,128)S(1)}, f32[64,768]{1,0:T(8,128)S(1)}, u32[]{:S(2)}, u32[]{:S(2)}) %collective-permute-start.11) | collective-permute-done | bytes 196640 | tf_op jit(solution)/shard_map/ppermute | solution.py:24
  49.8 0.2 next_solve.3
  50.1 3.7 %collective-permute-start.12 = (f32[64,384]{1,0:T(8,128)S(1)}, f32[64,384]{1,0:T(8,128)S(1)}, u32[]{:S(2)}, u32[]{:S(2)}) collective-permute-start(f32[64,384]{1,0:T(8,128)S(1)} %next_solve.3), channel_id=1, source_target_pairs={{0,32},{32,0},{1,33},{33,1},{2,34},{34,2},{3,35},{35,3},{4,36},{36... | collective-permute-start | bytes 294920 | tf_op jit(solution)/shard_map/ppermute | solution.py:24
  53.8 0.9 collective-permute-done.12
  54.8 1.0 collective-permute-start.13
  55.8 0.0 copy-done.4
  55.8 0.1 constant_dynamic-slice_fusion.1.mask_ref
  55.8 0.9 masked.1.refs_2_.factor_ref
  56.8 0.3 early_update.3.refs_0_
  57.1 0.0 copy-start.1
  57.1 1.8 %collective-permute-done.13.other_ref = f32[64,384]{1,0:T(8,128)S(1)} collective-permute-done((f32[64,384]{1,0:T(8,128)S(1)}, f32[64,384]{1,0:T(8,128)S(1)}, u32[]{:S(2)}, u32[]{:S(2)}) %collective-permute-start.13) | collective-permute-done | bytes 98336 | tf_op jit(solution)/shard_map/ppermute | solution.py:24
  58.9 0.2 kept_update.5
  59.1 9.2 %all_to_all.10 = f32[8,8,768]{2,1,0:T(8,128)S(1)} all-to-all(f32[8,8,768]{2,1,0:T(8,128)S(1)} %bitcast.3), channel_id=1, replica_groups=mesh['grid'=2,'xl'=2,'core'=2,'zt'=4,'zl'=2,'y'=4] {'zl','y'}, dimensions={0} | all-to-all | bytes 393216 | tf_op jit(solution)/shard_map/all_to_all | solution.py:283
  68.4 2.8 %collective-permute-start.14 = (f32[8,768]{1,0:T(8,128)S(1)}, f32[8,768]{1,0:T(8,128)S(1)}, u32[]{:S(2)}, u32[]{:S(2)}) collective-permute-start(f32[8,768]{1,0:T(8,128)S(1)} %reduce_sum.9), channel_id=1, source_target_pairs={{0,128},{8,136},{16,144},{24,152},{128,0},{136,8},{144,16},{152,24... | collective-permute-start | bytes 73736 | tf_op jit(solution)/shard_map/ppermute | solution.py:24
  71.2 3.0 %collective-permute-start.15 = (f32[8,768]{1,0:T(8,128)S(1)}, f32[8,768]{1,0:T(8,128)S(1)}, u32[]{:S(2)}, u32[]{:S(2)}) collective-permute-start(f32[8,768]{1,0:T(8,128)S(1)} %reduce_sum.9), channel_id=1, source_target_pairs={{0,8},{8,0},{16,24},{24,16},{128,136},{136,128},{144,152},{152,144... | collective-permute-start | bytes 73736 | tf_op jit(solution)/shard_map/ppermute | solution.py:24
  74.2 0.0 collective-permute-start.16
  74.2 0.7 stacked.1
  75.0 0.0 collective-permute-done.14
  75.0 1.0 collective-permute-done.15
  76.0 4.5 %collective-permute-done.16 = f32[8,768]{1,0:T(8,128)S(1)} collective-permute-done((f32[8,768]{1,0:T(8,128)S(1)}, f32[8,768]{1,0:T(8,128)S(1)}, u32[]{:S(2)}, u32[]{:S(2)}) %collective-permute-start.16) | collective-permute-done | bytes 24608 | tf_op jit(solution)/shard_map/ppermute | solution.py:24
  80.5 3.1 %collective-permute-start.17 = (f32[8,768]{1,0:T(8,128)S(1)}, f32[8,768]{1,0:T(8,128)S(1)}, u32[]{:S(2)}, u32[]{:S(2)}) collective-permute-start(f32[8,768]{1,0:T(8,128)S(1)} %add_add_fusion.one_ref), channel_id=1, source_target_pairs={{0,24},{8,16},{16,8},{24,0},{1,25},{9,17},{17,9},{25,1},{2,26},{10... | collective-permute-start | bytes 73736 | tf_op jit(solution)/shard_map/ppermute | solution.py:24
  83.6 0.0 copy-done
  83.6 1.7 %collective-permute-done.17.other_ref = f32[8,768]{1,0:T(8,128)S(1)} collective-permute-done((f32[8,768]{1,0:T(8,128)S(1)}, f32[8,768]{1,0:T(8,128)S(1)}, u32[]{:S(2)}, u32[]{:S(2)}) %collective-permute-start.17) | collective-permute-done | bytes 24608 | tf_op jit(solution)/shard_map/ppermute | solution.py:24
  85.4 0.4 root_part.1
  85.8 5.5 %collective-permute-start.18 = (f32[8,1536]{1,0:T(8,128)S(1)}, f32[8,1536]{1,0:T(8,128)S(1)}, u32[]{:S(2)}, u32[]{:S(2)}) collective-permute-start(f32[8,1536]{1,0:T(8,128)S(1)} %root_part.1), channel_id=1, source_target_pairs={{0,32},{32,0},{1,33},{33,1},{2,34},{34,2},{3,35},{35,3},{4,36},{36... | collective-permute-start | bytes 147464 | tf_op jit(solution)/shard_map/ppermute | solution.py:24
  91.2 0.9 collective-permute-done.18
  92.1 0.3 collective-permute-start.19
  92.5 2.6 %collective-permute-done.19 = f32[8,1536]{1,0:T(8,128)S(1)} collective-permute-done((f32[8,1536]{1,0:T(8,128)S(1)}, f32[8,1536]{1,0:T(8,128)S(1)}, u32[]{:S(2)}, u32[]{:S(2)}) %collective-permute-start.19) | collective-permute-done | bytes 49184 | tf_op jit(solution)/shard_map/ppermute | solution.py:24
  95.1 9.3 %all_to_all.11 = f32[8,8,1536]{2,1,0:T(8,128)S(1)} all-to-all(f32[8,8,1536]{2,1,0:T(8,128)S(1)} %broadcast_in_dim.2), channel_id=1, replica_groups=mesh['grid'=2,'xl'=2,'core'=2,'zt'=4,'zl'=2,'y'=4] {'zl','y'}, dimensions={0} | all-to-all | bytes 786432 | tf_op jit(solution)/shard_map/all_to_all | solution.py:29
  104.4 0.7 copy.11
  (14 shorter events, 0.2 us)
Async XLA Ops:
  0.6 83.0 %copy-start = (f32[64,768]{1,0:T(8,128)S(1)}, f32[64,768]{1,0:T(8,128)}, u32[]{:S(2)}) copy-start(f32[64,768]{1,0:T(8,128)} %param.9) | copy-start | bytes 589828
  0.7 6.0 %copy-start.3 = (s32[3,3,24]{2,1,0:T(4,128)S(1)}, s32[3,3,24]{2,1,0:T(4,128)}, u32[]{:S(2)}) copy-start(s32[3,3,24]{2,1,0:T(4,128)} %param.13) | copy-start | bytes 2596
  2.3 4.3 %collective-permute-start = (f32[64,384]{1,0:T(8,128)S(1)}, f32[64,384]{1,0:T(8,128)S(1)}, u32[]{:S(2)}, u32[]{:S(2)}) collective-permute-start(f32[64,384]{1,0:T(8,128)S(1)} %first_solve.1), channel_id=1, source_target_pairs={{0,32},{32,0},{1,33},{33,1},{2,34},{34,2},{3,35},{35,3},{4,36},{36... | collective-permute-start | bytes 294920 | tf_op jit(solution)/shard_map/ppermute | solution.py:24
  6.5 4.1 %collective-permute-start.1 = (f32[64,384]{1,0:T(8,128)S(1)}, f32[64,384]{1,0:T(8,128)S(1)}, u32[]{:S(2)}, u32[]{:S(2)}) collective-permute-start(f32[64,384]{1,0:T(8,128)S(1)} %add.43.one_ref), channel_id=1, source_target_pairs={{0,64},{64,0},{1,65},{65,1},{2,66},{66,2},{3,67},{67,3},{4,68},{68... | collective-permute-start | bytes 294920 | tf_op jit(solution)/shard_map/ppermute | solution.py:24
  10.9 5.3 %collective-permute-start.2 = (f32[64,768]{1,0:T(8,128)S(1)}, f32[64,768]{1,0:T(8,128)S(1)}, u32[]{:S(2)}, u32[]{:S(2)}) collective-permute-start(f32[64,768]{1,0:T(8,128)S(1)} %get-tuple-element.20), channel_id=1, source_target_pairs={{0,4},{4,0},{1,5},{5,1},{2,6},{6,2},{3,7},{7,3},{8,12},{12,8},{9,1... | collective-permute-start | bytes 589832 | tf_op jit(solution)/shard_map/ppermute | solution.py:24
  16.2 4.6 %collective-permute-start.3 = (f32[64,768]{1,0:T(8,128)S(1)}, f32[64,768]{1,0:T(8,128)S(1)}, u32[]{:S(2)}, u32[]{:S(2)}) collective-permute-start(f32[64,768]{1,0:T(8,128)S(1)} %add.46.refs_0_), channel_id=1, source_target_pairs={{0,1},{1,0},{2,3},{3,2},{4,5},{5,4},{6,7},{7,6},{8,9},{9,8},{10,11... | collective-permute-start | bytes 589832 | tf_op jit(solution)/shard_map/ppermute | solution.py:24
  16.3 5.8 %collective-permute-start.4 = (f32[64,768]{1,0:T(8,128)S(1)}, f32[64,768]{1,0:T(8,128)S(1)}, u32[]{:S(2)}, u32[]{:S(2)}) collective-permute-start(f32[64,768]{1,0:T(8,128)S(1)} %add.46.refs_0_), channel_id=1, source_target_pairs={{0,3},{1,2},{2,1},{3,0},{4,7},{5,6},{6,5},{7,4},{8,11},{9,10},{10,... | collective-permute-start | bytes 589832 | tf_op jit(solution)/shard_map/ppermute | solution.py:24
  18.1 8.0 %collective-permute-start.5 = (f32[64,768]{1,0:T(8,128)S(1)}, f32[64,768]{1,0:T(8,128)S(1)}, u32[]{:S(2)}, u32[]{:S(2)}) collective-permute-start(f32[64,768]{1,0:T(8,128)S(1)} %add.46.refs_0_), channel_id=1, source_target_pairs={{0,2},{1,3},{2,0},{3,1},{4,6},{5,7},{6,4},{7,5},{8,10},{9,11},{10,... | collective-permute-start | bytes 589832 | tf_op jit(solution)/shard_map/ppermute | solution.py:24
  26.3 4.2 %collective-permute-start.6 = (f32[64,384]{1,0:T(8,128)S(1)}, f32[64,384]{1,0:T(8,128)S(1)}, u32[]{:S(2)}, u32[]{:S(2)}) collective-permute-start(f32[64,384]{1,0:T(8,128)S(1)} %next_solve.2), channel_id=1, source_target_pairs={{0,32},{32,0},{1,33},{33,1},{2,34},{34,2},{3,35},{35,3},{4,36},{36... | collective-permute-start | bytes 294920 | tf_op jit(solution)/shard_map/ppermute | solution.py:24
  30.5 4.1 %collective-permute-start.7 = (f32[64,384]{1,0:T(8,128)S(1)}, f32[64,384]{1,0:T(8,128)S(1)}, u32[]{:S(2)}, u32[]{:S(2)}) collective-permute-start(f32[64,384]{1,0:T(8,128)S(1)} %add.47.one_ref), channel_id=1, source_target_pairs={{0,64},{64,0},{1,65},{65,1},{2,66},{66,2},{3,67},{67,3},{4,68},{68... | collective-permute-start | bytes 294920 | tf_op jit(solution)/shard_map/ppermute | solution.py:24
  34.9 20.9 %copy-start.4 = (s32[3,3,24]{2,1,0:T(4,128)S(1)}, s32[3,3,24]{2,1,0:T(4,128)}, u32[]{:S(2)}) copy-start(s32[3,3,24]{2,1,0:T(4,128)} %param.15) | copy-start | bytes 2596
  34.9 21.0 %copy-start.2 = (bf16[3,384,768]{2,1,0:T(8,128)(2,1)S(1)}, bf16[3,384,768]{2,1,0:T(8,128)(2,1)}, u32[]{:S(2)}) copy-start(bf16[3,384,768]{2,1,0:T(8,128)(2,1)} %factor_ref.1) | copy-start | bytes 5308420
  34.9 5.3 %collective-permute-start.8 = (f32[64,768]{1,0:T(8,128)S(1)}, f32[64,768]{1,0:T(8,128)S(1)}, u32[]{:S(2)}, u32[]{:S(2)}) collective-permute-start(f32[64,768]{1,0:T(8,128)S(1)} %get-tuple-element.24), channel_id=1, source_target_pairs={{0,4},{4,0},{1,5},{5,1},{2,6},{6,2},{3,7},{7,3},{8,12},{12,8},{9,1... | collective-permute-start | bytes 589832 | tf_op jit(solution)/shard_map/ppermute | solution.py:24
  40.2 4.6 %collective-permute-start.9 = (f32[64,768]{1,0:T(8,128)S(1)}, f32[64,768]{1,0:T(8,128)S(1)}, u32[]{:S(2)}, u32[]{:S(2)}) collective-permute-start(f32[64,768]{1,0:T(8,128)S(1)} %add.48.refs_0_), channel_id=1, source_target_pairs={{0,1},{1,0},{2,3},{3,2},{4,5},{5,4},{6,7},{7,6},{8,9},{9,8},{10,11... | collective-permute-start | bytes 589832 | tf_op jit(solution)/shard_map/ppermute | solution.py:24
  40.8 6.6 %collective-permute-start.10 = (f32[64,768]{1,0:T(8,128)S(1)}, f32[64,768]{1,0:T(8,128)S(1)}, u32[]{:S(2)}, u32[]{:S(2)}) collective-permute-start(f32[64,768]{1,0:T(8,128)S(1)} %add.48.refs_0_), channel_id=1, source_target_pairs={{0,3},{1,2},{2,1},{3,0},{4,7},{5,6},{6,5},{7,4},{8,11},{9,10},{10,... | collective-permute-start | bytes 589832 | tf_op jit(solution)/shard_map/ppermute | solution.py:24
  42.0 7.8 %collective-permute-start.11 = (f32[64,768]{1,0:T(8,128)S(1)}, f32[64,768]{1,0:T(8,128)S(1)}, u32[]{:S(2)}, u32[]{:S(2)}) collective-permute-start(f32[64,768]{1,0:T(8,128)S(1)} %add.48.refs_0_), channel_id=1, source_target_pairs={{0,2},{1,3},{2,0},{3,1},{4,6},{5,7},{6,4},{7,5},{8,10},{9,11},{10,... | collective-permute-start | bytes 589832 | tf_op jit(solution)/shard_map/ppermute | solution.py:24
  50.1 4.7 %collective-permute-start.12 = (f32[64,384]{1,0:T(8,128)S(1)}, f32[64,384]{1,0:T(8,128)S(1)}, u32[]{:S(2)}, u32[]{:S(2)}) collective-permute-start(f32[64,384]{1,0:T(8,128)S(1)} %next_solve.3), channel_id=1, source_target_pairs={{0,32},{32,0},{1,33},{33,1},{2,34},{34,2},{3,35},{35,3},{4,36},{36... | collective-permute-start | bytes 294920 | tf_op jit(solution)/shard_map/ppermute | solution.py:24
  54.8 4.1 %collective-permute-start.13 = (f32[64,384]{1,0:T(8,128)S(1)}, f32[64,384]{1,0:T(8,128)S(1)}, u32[]{:S(2)}, u32[]{:S(2)}) collective-permute-start(f32[64,384]{1,0:T(8,128)S(1)} %add.49.one_ref), channel_id=1, source_target_pairs={{0,64},{64,0},{1,65},{65,1},{2,66},{66,2},{3,67},{67,3},{4,68},{68... | collective-permute-start | bytes 294920 | tf_op jit(solution)/shard_map/ppermute | solution.py:24
  57.1 28.2 %copy-start.1 = (bf16[768,1536]{1,0:T(8,128)(2,1)S(1)}, bf16[768,1536]{1,0:T(8,128)(2,1)}, u32[]{:S(2)}) copy-start(bf16[768,1536]{1,0:T(8,128)(2,1)} %inverse_ref.1) | copy-start | bytes 7077892
  68.4 6.6 %collective-permute-start.14 = (f32[8,768]{1,0:T(8,128)S(1)}, f32[8,768]{1,0:T(8,128)S(1)}, u32[]{:S(2)}, u32[]{:S(2)}) collective-permute-start(f32[8,768]{1,0:T(8,128)S(1)} %reduce_sum.9), channel_id=1, source_target_pairs={{0,128},{8,136},{16,144},{24,152},{128,0},{136,8},{144,16},{152,24... | collective-permute-start | bytes 73736 | tf_op jit(solution)/shard_map/ppermute | solution.py:24
  71.2 4.8 %collective-permute-start.15 = (f32[8,768]{1,0:T(8,128)S(1)}, f32[8,768]{1,0:T(8,128)S(1)}, u32[]{:S(2)}, u32[]{:S(2)}) collective-permute-start(f32[8,768]{1,0:T(8,128)S(1)} %reduce_sum.9), channel_id=1, source_target_pairs={{0,8},{8,0},{16,24},{24,16},{128,136},{136,128},{144,152},{152,144... | collective-permute-start | bytes 73736 | tf_op jit(solution)/shard_map/ppermute | solution.py:24
  74.2 6.2 %collective-permute-start.16 = (f32[8,768]{1,0:T(8,128)S(1)}, f32[8,768]{1,0:T(8,128)S(1)}, u32[]{:S(2)}, u32[]{:S(2)}) collective-permute-start(f32[8,768]{1,0:T(8,128)S(1)} %reduce_sum.9), channel_id=1, source_target_pairs={{0,136},{8,128},{16,152},{24,144},{128,8},{136,0},{144,24},{152,16... | collective-permute-start | bytes 73736 | tf_op jit(solution)/shard_map/ppermute | solution.py:24
  80.5 4.9 %collective-permute-start.17 = (f32[8,768]{1,0:T(8,128)S(1)}, f32[8,768]{1,0:T(8,128)S(1)}, u32[]{:S(2)}, u32[]{:S(2)}) collective-permute-start(f32[8,768]{1,0:T(8,128)S(1)} %add_add_fusion.one_ref), channel_id=1, source_target_pairs={{0,24},{8,16},{16,8},{24,0},{1,25},{9,17},{17,9},{25,1},{2,26},{10... | collective-permute-start | bytes 73736 | tf_op jit(solution)/shard_map/ppermute | solution.py:24
  85.8 6.4 %collective-permute-start.18 = (f32[8,1536]{1,0:T(8,128)S(1)}, f32[8,1536]{1,0:T(8,128)S(1)}, u32[]{:S(2)}, u32[]{:S(2)}) collective-permute-start(f32[8,1536]{1,0:T(8,128)S(1)} %root_part.1), channel_id=1, source_target_pairs={{0,32},{32,0},{1,33},{33,1},{2,34},{34,2},{3,35},{35,3},{4,36},{36... | collective-permute-start | bytes 147464 | tf_op jit(solution)/shard_map/ppermute | solution.py:24
  92.1 2.9 %collective-permute-start.19 = (f32[8,1536]{1,0:T(8,128)S(1)}, f32[8,1536]{1,0:T(8,128)S(1)}, u32[]{:S(2)}, u32[]{:S(2)}) collective-permute-start(f32[8,1536]{1,0:T(8,128)S(1)} %add.55), channel_id=1, source_target_pairs={{0,64},{64,0},{1,65},{65,1},{2,66},{66,2},{3,67},{67,3},{4,68},{68... | collective-permute-start | bytes 147464 | tf_op jit(solution)/shard_map/ppermute | solution.py:24

commit v4 on v3

--- a/solution.py
+++ b/solution.py
@@ -8,6 +8,7 @@
 
 LEVELS = 3
 TILE = 128
+PARTS = 2
 PROW = ("xl", "core")
 OWN = ("zl", "y")
 TREES = ("grid", "zt")
@@ -52,13 +53,16 @@
     return jnp.dot(left, right, preferred_element_type=F32)
 
 
-def first_solve(tree, sub_rhs, diag_inverse):
+def first_solve(tree, sub_rhs, diag_inverse, parts):
     rhs_count, depth = sub_rhs.shape[2:]
     cols = diag_inverse.shape[2]
     pieces = 3
     step = depth // pieces
 
-    def body(tree_ref, rhs_hbm, inverse_hbm, out_ref, rhs, inverse, rhs_sem, inverse_sem):
+    few = rhs_count // parts
+
+    def body(tree_ref, rhs_hbm, inverse_hbm, *refs):
+        *out_refs, rhs, inverse, rhs_sem, inverse_sem = refs
         rhs_copy = pltpu.make_async_copy(rhs_hbm.at[tree_ref[0], 0], rhs, rhs_sem)
         rhs_copy.start()
         copies = []
@@ -76,11 +80,12 @@
             copies[piece].wait()
             part = slice(piece * step, (piece + 1) * step)
             total = total + product(rhs[:, part].astype(BF16), inverse[part, :])
-        out_ref[...] = total
-
-    return call(
-        body,
-        [((rhs_count, cols), F32)],
+        for k, ref in enumerate(out_refs):
+            ref[...] = total[k * few : (k + 1) * few]
+
+    return call(
+        body,
+        [((few, cols), F32)] * parts,
         (tree, sub_rhs, diag_inverse),
         [SCALARS, IN_PLACE, IN_PLACE],
         [
@@ -90,19 +95,22 @@
             pltpu.SemaphoreType.DMA((pieces,)),
         ],
         "first_solve",
-    )[0]
-
-
-def next_solve(place, rhs, sums, diag_inverse):
+    )
+
+
+def next_solve(place, part, rhs, sums, diag_inverse):
+    few = sums[0].shape[0]
+    rows = slice(part * few, (part + 1) * few)
+
     def body(rhs_ref, *refs):
         *sum_refs, inverse_ref, out_ref = refs
         update = sum_refs[0][...]
         for ref in sum_refs[1:]:
             update = update + ref[...]
-        residual = (rhs_ref[place] - update).astype(BF16)
+        residual = (rhs_ref[place, rows] - update).astype(BF16)
         out_ref[...] = product(residual, inverse_ref[place])
 
-    shape = (rhs.shape[1], diag_inverse.shape[2])
+    shape = (few, diag_inverse.shape[2])
     return call(body, [(shape, F32)], (rhs, *sums, diag_inverse), name="next_solve")[0]
 
 
@@ -175,10 +183,15 @@
 
 
 def stacked(parts):
+    levels, count = len(parts), len(parts[0])
+    rows, cols = parts[0][0].shape
+
     def body(*refs):
         *part_refs, out_hbm, sems = refs
         copies = [
-            pltpu.make_async_copy(ref, out_hbm.at[k], sems.at[k])
+            pltpu.make_async_copy(
+                ref, out_hbm.at[k // count, pl.ds(k % count * rows, rows)], sems.at[k]
+            )
             for k, ref in enumerate(part_refs)
         ]
         for copy in copies:
@@ -186,13 +199,13 @@
         for copy in copies:
             copy.wait()
 
-    args = [pltpu.with_memory_space_constraint(part, pltpu.VMEM) for part in parts]
+    args = [pltpu.with_memory_space_constraint(part, pltpu.VMEM) for one in parts for part in one]
     return pl.pallas_call(
         body,
-        out_shape=jax.ShapeDtypeStruct((len(parts), *parts[0].shape), F32),
-        in_specs=[ON_CHIP] * len(parts),
+        out_shape=jax.ShapeDtypeStruct((levels, count * rows, cols), F32),
+        in_specs=[ON_CHIP] * len(args),
         out_specs=IN_PLACE,
-        scratch_shapes=[pltpu.SemaphoreType.DMA((len(parts),))],
+        scratch_shapes=[pltpu.SemaphoreType.DMA((len(args),))],
         compiler_params=pltpu.CompilerParams(vmem_limit_bytes=SCOPED_BYTES),
         name="stacked",
     )(*args)
@@ -267,16 +280,21 @@
     root_tiles = lax.dynamic_slice_in_dim(root_mask, first_tile, tiles, 2)
     tree = tree.reshape(1)
 
-    halves = prow_halves(first_solve(tree, sub_rhs, diag_inverse))
+    firsts = first_solve(tree, sub_rhs, diag_inverse, PARTS)
     inner, inverse, rhs = stage(tree, inner_tiles, sub_rhs, diag_inverse, inner_factor)
     root = masked(root_tiles, root_factor)
-    update1, solved0, kept0 = kept_update(halves, inner, 0, ())
-    halves = prow_halves(next_solve(0, rhs, owner_sums(update1), inverse))
-    early = early_update((kept0,), inner, (1,))
-    update2, solved1, kept1 = kept_update(halves, inner, 2, (early,))
-    halves = prow_halves(next_solve(1, rhs, owner_sums(update2), inverse))
-    early = early_update((kept0, kept1), root, (0, 1))
-    root_local, solved2 = kept_update(halves, root, 2, (early,), last=True)
+    solved, locals_ = [], []
+    for part, first in enumerate(firsts):
+        update, solved0, kept0 = kept_update(prow_halves(first), inner, 0, ())
+        halves = prow_halves(next_solve(0, part, rhs, owner_sums(update), inverse))
+        early = early_update((kept0,), inner, (1,))
+        update, solved1, kept1 = kept_update(halves, inner, 2, (early,))
+        halves = prow_halves(next_solve(1, part, rhs, owner_sums(update), inverse))
+        early = early_update((kept0, kept1), root, (0, 1))
+        root_local, solved2 = kept_update(halves, root, 2, (early,), last=True)
+        solved.append((solved0, solved1, solved2))
+        locals_.append(root_local)
+    root_local = jnp.concatenate(locals_)
 
     owners = lax.axis_size(OWN)
     few = rhs_count // owners
@@ -285,7 +303,7 @@
     ).sum(axis=0)
     sub_solution, *arrived = lax.optimization_barrier(
         (
-            stacked([solved0, solved1, solved2]),
+            stacked(list(zip(*solved))),
             *[partner(own_rows, TREES, bit) for bit in (4, 1, 5)],
         )
     )

time: 106 us -> 104 us (0.981)
  waiting for transfers between devices: 41.3 us -> 20.4 us
  starting transfers between devices: 35.5 us -> 53.2 us
  Pallas kernels: 7.9 us -> 9.21 us
    ppermute x20 -> x34, waiting for transfers between devices: 41.3 us -> 20.4 us  [partner(): lax.ppermute(shard, axis, [(i, i ^ bit) for i in range(lax.axis_size(axis...]
    ppermute x20 -> x34, starting transfers between devices: 35.5 us -> 53.2 us  [partner(): lax.ppermute(shard, axis, [(i, i ^ bit) for i in range(lax.axis_size(axis...]
    pallas_call x11 -> x18, Pallas kernels: 7.17 us -> 8.46 us  [call(): pl.pallas_call(body, out_shape=[pltpu.VMEM(shape, kind) for shape, kind i...]
  transfers between devices with their start and end apart: 20 -> 34, of which waited for: 19 -> 14; matrix products, arithmetic and copies ran while one was open for 0% -> 0% of each run, Pallas kernels for 5% -> 7%
where the time goes in v4:
time: 104 us
  starting transfers between devices  53.2 us (51%)
  waiting for transfers between devices  20.4 us (20%)
  blocking collectives  18.9 us (18%)
  Pallas kernels  9.21 us (9%)
    ppermute x34, starting transfers between devices, partner(): lax.ppermute(shard, axis, [(i, i ^ bit) for i in range(lax.axis_size(axis...  53.2 us
    ppermute x34, waiting for transfers between devices, partner(): lax.ppermute(shard, axis, [(i, i ^ bit) for i in range(lax.axis_size(axis...  20.4 us
    all_to_all x1, blocking collectives, shards(): lax.all_to_all(root_local.reshape(owners, few, out_cols), OWN, 0, 0, tile...  9.56 us
    all_to_all x1, blocking collectives, to_everyone(): lax.all_to_all(jnp.broadcast_to(shard[None], (count, *shard.shape)), axis...  9.31 us
    pallas_call x18, Pallas kernels, call(): pl.pallas_call(body, out_shape=[pltpu.VMEM(shape, kind) for shape, kind i...  8.46 us
  transfers between devices with their start and end apart: 34, of which 14 were waited for; matrix products, arithmetic and copies ran while one was open for 0% of the time, Pallas kernels for 7%

profile of v4, /device:TPU:1, one launch (start us, length us, event | category | flops | bytes accessed | tf_op | source)
XLA Modules:
  0.0 103.7 jit_solution(17696403470870486693)
XLA Ops:
  0.7 1.6 %first_solve.1 = (f32[32,384]{1,0:T(8,128)S(1)}, f32[32,384]{1,0:T(8,128)S(1)}) custom-call(s32[1]{0:T(128)} %bitcast.tree_ref, f32[4,3,64,768]{3,2,1,0:T(8,128)} %rhs_hbm.3, bf16[3,768,384]{2,1,0:T(8,128)(2,1)} %inverse_hbm.3), custom_call_target="tpu_custom_call" | custom-call | tf_op jit(solution)/shard_map/first_solve/pallas_call | solution.py:41
  2.3 3.3 %collective-permute-start = (f32[32,384]{1,0:T(8,128)S(1)}, f32[32,384]{1,0:T(8,128)S(1)}, u32[]{:S(2)}, u32[]{:S(2)}) collective-permute-start(f32[32,384]{1,0:T(8,128)S(1)} %get-tuple-element.27), channel_id=1, source_target_pairs={{0,32},{32,0},{1,33},{33,1},{2,34},{34,2},{3,35},{35,3},{4,36},{36... | collective-permute-start | bytes 147464 | tf_op jit(solution)/shard_map/ppermute | solution.py:25
  5.7 0.8 collective-permute-done
  6.6 2.6 %stage.1 = (bf16[3,384,768]{2,1,0:T(8,128)(2,1)S(1)}, bf16[2,768,384]{2,1,0:T(8,128)(2,1)S(1)}, f32[2,64,768]{2,1,0:T(8,128)S(1)}) custom-call(s32[1]{0:T(128)} %bitcast.tree_ref, s32[3,3,6]{2,1,0:T(4,128)S(1)} %constant_dynamic-slice_fusion.2.mask_ref, f32[4,3,64,768]{3,2,1,0:T(8,128)} %rhs_hbm.3, bf16[3,768,384]{2,1,0:T(8,128)(2,1)} %inverse_hbm.3, ...), custom_call_target="tpu_custom_call" | custom-call | tf_op jit(solution)/shard_map/stage/pallas_call | solution.py:41
  9.2 0.3 collective-permute-done.1.other_ref
  9.5 0.2 kept_update.6
  9.7 0.9 collective-permute-start.4
  10.6 0.5 collective-permute-start.3
  11.0 2.6 %collective-permute-done.3.other_ref = f32[32,384]{1,0:T(8,128)S(1)} collective-permute-done((f32[32,384]{1,0:T(8,128)S(1)}, f32[32,384]{1,0:T(8,128)S(1)}, u32[]{:S(2)}, u32[]{:S(2)}) %collective-permute-start.3) | collective-permute-done | bytes 49184 | tf_op jit(solution)/shard_map/ppermute | solution.py:25
  13.6 0.2 kept_update.7
  13.8 1.0 collective-permute-start.10
  14.8 0.8 collective-permute-start.5
  15.6 1.9 %collective-permute-start.6 = (f32[32,768]{1,0:T(8,128)S(1)}, f32[32,768]{1,0:T(8,128)S(1)}, u32[]{:S(2)}, u32[]{:S(2)}) collective-permute-start(f32[32,768]{1,0:T(8,128)S(1)} %add.62.refs_0_), channel_id=1, source_target_pairs={{0,3},{1,2},{2,1},{3,0},{4,7},{5,6},{6,5},{7,4},{8,11},{9,10},{10,... | collective-permute-start | bytes 294920 | tf_op jit(solution)/shard_map/ppermute | solution.py:25
  17.5 0.7 collective-permute-start.7
  18.3 0.8 collective-permute-start.11
  19.1 1.9 %collective-permute-start.12 = (f32[32,768]{1,0:T(8,128)S(1)}, f32[32,768]{1,0:T(8,128)S(1)}, u32[]{:S(2)}, u32[]{:S(2)}) collective-permute-start(f32[32,768]{1,0:T(8,128)S(1)} %add.64.refs_0_), channel_id=1, source_target_pairs={{0,3},{1,2},{2,1},{3,0},{4,7},{5,6},{6,5},{7,4},{8,11},{9,10},{10,... | collective-permute-start | bytes 294920 | tf_op jit(solution)/shard_map/ppermute | solution.py:25
  21.0 0.7 collective-permute-start.13
  21.7 1.8 %collective-permute-done.7.refs_3_ = f32[32,768]{1,0:T(8,128)S(1)} collective-permute-done((f32[32,768]{1,0:T(8,128)S(1)}, f32[32,768]{1,0:T(8,128)S(1)}, u32[]{:S(2)}, u32[]{:S(2)}) %collective-permute-start.7) | collective-permute-done | bytes 98336 | tf_op jit(solution)/shard_map/ppermute | solution.py:25
  23.4 0.2 next_solve.4
  23.6 3.9 %collective-permute-start.8 = (f32[32,384]{1,0:T(8,128)S(1)}, f32[32,384]{1,0:T(8,128)S(1)}, u32[]{:S(2)}, u32[]{:S(2)}) collective-permute-start(f32[32,384]{1,0:T(8,128)S(1)} %next_solve.4), channel_id=1, source_target_pairs={{0,32},{32,0},{1,33},{33,1},{2,34},{34,2},{3,35},{35,3},{4,36},{36... | collective-permute-start | bytes 147464 | tf_op jit(solution)/shard_map/ppermute | solution.py:25
  27.5 0.9 collective-permute-done.8
  28.4 0.8 collective-permute-start.9
  29.2 0.2 next_solve.5
  29.4 1.5 %collective-permute-start.14 = (f32[32,384]{1,0:T(8,128)S(1)}, f32[32,384]{1,0:T(8,128)S(1)}, u32[]{:S(2)}, u32[]{:S(2)}) collective-permute-start(f32[32,384]{1,0:T(8,128)S(1)} %next_solve.5), channel_id=1, source_target_pairs={{0,32},{32,0},{1,33},{33,1},{2,34},{34,2},{3,35},{35,3},{4,36},{36... | collective-permute-start | bytes 147464 | tf_op jit(solution)/shard_map/ppermute | solution.py:25
  30.9 0.2 early_update.4.refs_0_
  31.1 0.3 collective-permute-done.9.other_ref
  31.4 0.2 kept_update.8
  31.6 1.6 %collective-permute-start.16 = (f32[32,768]{1,0:T(8,128)S(1)}, f32[32,768]{1,0:T(8,128)S(1)}, u32[]{:S(2)}, u32[]{:S(2)}) collective-permute-start(f32[32,768]{1,0:T(8,128)S(1)} %get-tuple-element.40), channel_id=1, source_target_pairs={{0,4},{4,0},{1,5},{5,1},{2,6},{6,2},{3,7},{7,3},{8,12},{12,8},{9,1... | collective-permute-start | bytes 294920 | tf_op jit(solution)/shard_map/ppermute | solution.py:25
  33.2 0.8 collective-permute-start.15
  34.0 0.2 early_update.5.refs_0_
  34.2 2.3 %collective-permute-done.15.other_ref = f32[32,384]{1,0:T(8,128)S(1)} collective-permute-done((f32[32,384]{1,0:T(8,128)S(1)}, f32[32,384]{1,0:T(8,128)S(1)}, u32[]{:S(2)}, u32[]{:S(2)}) %collective-permute-start.15) | collective-permute-done | bytes 49184 | tf_op jit(solution)/shard_map/ppermute | solution.py:25
  36.5 0.2 kept_update.9
  36.8 0.4 collective-permute-start.17
  37.3 1.2 %collective-permute-start.18 = (f32[32,768]{1,0:T(8,128)S(1)}, f32[32,768]{1,0:T(8,128)S(1)}, u32[]{:S(2)}, u32[]{:S(2)}) collective-permute-start(f32[32,768]{1,0:T(8,128)S(1)} %add.66.refs_0_), channel_id=1, source_target_pairs={{0,3},{1,2},{2,1},{3,0},{4,7},{5,6},{6,5},{7,4},{8,11},{9,10},{10,... | collective-permute-start | bytes 294920 | tf_op jit(solution)/shard_map/ppermute | solution.py:25
  38.4 1.7 %collective-permute-start.19 = (f32[32,768]{1,0:T(8,128)S(1)}, f32[32,768]{1,0:T(8,128)S(1)}, u32[]{:S(2)}, u32[]{:S(2)}) collective-permute-start(f32[32,768]{1,0:T(8,128)S(1)} %add.66.refs_0_), channel_id=1, source_target_pairs={{0,2},{1,3},{2,0},{3,1},{4,6},{5,7},{6,4},{7,5},{8,10},{9,11},{10,... | collective-permute-start | bytes 294920 | tf_op jit(solution)/shard_map/ppermute | solution.py:25
  40.3 0.4 collective-permute-start.23
  40.7 1.2 %collective-permute-start.24 = (f32[32,768]{1,0:T(8,128)S(1)}, f32[32,768]{1,0:T(8,128)S(1)}, u32[]{:S(2)}, u32[]{:S(2)}) collective-permute-start(f32[32,768]{1,0:T(8,128)S(1)} %add.68.refs_0_), channel_id=1, source_target_pairs={{0,3},{1,2},{2,1},{3,0},{4,7},{5,6},{6,5},{7,4},{8,11},{9,10},{10,... | collective-permute-start | bytes 294920 | tf_op jit(solution)/shard_map/ppermute | solution.py:25
  41.9 1.7 %collective-permute-start.25 = (f32[32,768]{1,0:T(8,128)S(1)}, f32[32,768]{1,0:T(8,128)S(1)}, u32[]{:S(2)}, u32[]{:S(2)}) collective-permute-start(f32[32,768]{1,0:T(8,128)S(1)} %add.68.refs_0_), channel_id=1, source_target_pairs={{0,2},{1,3},{2,0},{3,1},{4,6},{5,7},{6,4},{7,5},{8,10},{9,11},{10,... | collective-permute-start | bytes 294920 | tf_op jit(solution)/shard_map/ppermute | solution.py:25
  43.7 0.2 next_solve.6
  43.9 5.6 %collective-permute-start.20 = (f32[32,384]{1,0:T(8,128)S(1)}, f32[32,384]{1,0:T(8,128)S(1)}, u32[]{:S(2)}, u32[]{:S(2)}) collective-permute-start(f32[32,384]{1,0:T(8,128)S(1)} %next_solve.6), channel_id=1, source_target_pairs={{0,32},{32,0},{1,33},{33,1},{2,34},{34,2},{3,35},{35,3},{4,36},{36... | collective-permute-start | bytes 147464 | tf_op jit(solution)/shard_map/ppermute | solution.py:25
  49.5 0.2 next_solve.7
  49.7 3.0 %collective-permute-start.26 = (f32[32,384]{1,0:T(8,128)S(1)}, f32[32,384]{1,0:T(8,128)S(1)}, u32[]{:S(2)}, u32[]{:S(2)}) collective-permute-start(f32[32,384]{1,0:T(8,128)S(1)} %next_solve.7), channel_id=1, source_target_pairs={{0,32},{32,0},{1,33},{33,1},{2,34},{34,2},{3,35},{35,3},{4,36},{36... | collective-permute-start | bytes 147464 | tf_op jit(solution)/shard_map/ppermute | solution.py:25
  52.7 1.3 %collective-permute-start.21 = (f32[32,384]{1,0:T(8,128)S(1)}, f32[32,384]{1,0:T(8,128)S(1)}, u32[]{:S(2)}, u32[]{:S(2)}) collective-permute-start(f32[32,384]{1,0:T(8,128)S(1)} %add.67.one_ref), channel_id=1, source_target_pairs={{0,64},{64,0},{1,65},{65,1},{2,66},{66,2},{3,67},{67,3},{4,68},{68... | collective-permute-start | bytes 147464 | tf_op jit(solution)/shard_map/ppermute | solution.py:25
  54.0 0.8 collective-permute-start.27
  54.9 0.9 masked.1.refs_2_.factor_ref
  55.9 0.3 early_update.6.refs_0_
  56.2 0.3 early_update.7.refs_0_
  56.5 0.2 kept_update.10
  56.7 0.3 collective-permute-done.27.other_ref
  57.0 0.2 kept_update.11
  57.3 9.6 %all_to_all.10 = f32[8,8,768]{2,1,0:T(8,128)S(1)} all-to-all(f32[8,8,768]{2,1,0:T(8,128)S(1)} %maximum_bitcast_fusion), channel_id=1, replica_groups=mesh['grid'=2,'xl'=2,'core'=2,'zt'=4,'zl'=2,'y'=4] {'zl','y'}, dimensions={0} | all-to-all | bytes 393216 | tf_op jit(solution)/shard_map/all_to_all | solution.py:301
  66.9 2.9 %collective-permute-start.28 = (f32[8,768]{1,0:T(8,128)S(1)}, f32[8,768]{1,0:T(8,128)S(1)}, u32[]{:S(2)}, u32[]{:S(2)}) collective-permute-start(f32[8,768]{1,0:T(8,128)S(1)} %reduce_sum.9), channel_id=1, source_target_pairs={{0,128},{8,136},{16,144},{24,152},{128,0},{136,8},{144,16},{152,24... | collective-permute-start | bytes 73736 | tf_op jit(solution)/shard_map/ppermute | solution.py:25
  69.7 3.0 %collective-permute-start.29 = (f32[8,768]{1,0:T(8,128)S(1)}, f32[8,768]{1,0:T(8,128)S(1)}, u32[]{:S(2)}, u32[]{:S(2)}) collective-permute-start(f32[8,768]{1,0:T(8,128)S(1)} %reduce_sum.9), channel_id=1, source_target_pairs={{0,8},{8,0},{16,24},{24,16},{128,136},{136,128},{144,152},{152,144... | collective-permute-start | bytes 73736 | tf_op jit(solution)/shard_map/ppermute | solution.py:25
  72.7 0.8 stacked.1
  73.5 1.0 collective-permute-done.29
  74.5 4.5 %collective-permute-done.30 = f32[8,768]{1,0:T(8,128)S(1)} collective-permute-done((f32[8,768]{1,0:T(8,128)S(1)}, f32[8,768]{1,0:T(8,128)S(1)}, u32[]{:S(2)}, u32[]{:S(2)}) %collective-permute-start.30) | collective-permute-done | bytes 24608 | tf_op jit(solution)/shard_map/ppermute | solution.py:25
  79.0 3.1 %collective-permute-start.31 = (f32[8,768]{1,0:T(8,128)S(1)}, f32[8,768]{1,0:T(8,128)S(1)}, u32[]{:S(2)}, u32[]{:S(2)}) collective-permute-start(f32[8,768]{1,0:T(8,128)S(1)} %add_add_fusion.one_ref), channel_id=1, source_target_pairs={{0,24},{8,16},{16,8},{24,0},{1,25},{9,17},{17,9},{25,1},{2,26},{10... | collective-permute-start | bytes 73736 | tf_op jit(solution)/shard_map/ppermute | solution.py:25
  82.0 1.8 %collective-permute-done.31.other_ref = f32[8,768]{1,0:T(8,128)S(1)} collective-permute-done((f32[8,768]{1,0:T(8,128)S(1)}, f32[8,768]{1,0:T(8,128)S(1)}, u32[]{:S(2)}, u32[]{:S(2)}) %collective-permute-start.31) | collective-permute-done | bytes 24608 | tf_op jit(solution)/shard_map/ppermute | solution.py:25
  83.8 0.4 root_part.1
  84.2 5.5 %collective-permute-start.32 = (f32[8,1536]{1,0:T(8,128)S(1)}, f32[8,1536]{1,0:T(8,128)S(1)}, u32[]{:S(2)}, u32[]{:S(2)}) collective-permute-start(f32[8,1536]{1,0:T(8,128)S(1)} %root_part.1), channel_id=1, source_target_pairs={{0,32},{32,0},{1,33},{33,1},{2,34},{34,2},{3,35},{35,3},{4,36},{36... | collective-permute-start | bytes 147464 | tf_op jit(solution)/shard_map/ppermute | solution.py:25
  89.7 0.9 collective-permute-done.32
  90.7 2.9 %collective-permute-done.33 = f32[8,1536]{1,0:T(8,128)S(1)} collective-permute-done((f32[8,1536]{1,0:T(8,128)S(1)}, f32[8,1536]{1,0:T(8,128)S(1)}, u32[]{:S(2)}, u32[]{:S(2)}) %collective-permute-start.33) | collective-permute-done | bytes 49184 | tf_op jit(solution)/shard_map/ppermute | solution.py:25
  93.6 9.3 %all_to_all.11 = f32[8,8,1536]{2,1,0:T(8,128)S(1)} all-to-all(f32[8,8,1536]{2,1,0:T(8,128)S(1)} %broadcast_in_dim.2), channel_id=1, replica_groups=mesh['grid'=2,'xl'=2,'core'=2,'zt'=4,'zl'=2,'y'=4] {'zl','y'}, dimensions={0} | all-to-all | bytes 786432 | tf_op jit(solution)/shard_map/all_to_all | solution.py:30
  102.9 0.7 copy.11
  (55 shorter events, 0.8 us)
Async XLA Ops:
  0.6 81.4 %copy-start = (f32[64,768]{1,0:T(8,128)S(1)}, f32[64,768]{1,0:T(8,128)}, u32[]{:S(2)}) copy-start(f32[64,768]{1,0:T(8,128)} %param.9) | copy-start | bytes 589828
  0.7 5.9 %copy-start.3 = (s32[3,3,24]{2,1,0:T(4,128)S(1)}, s32[3,3,24]{2,1,0:T(4,128)}, u32[]{:S(2)}) copy-start(s32[3,3,24]{2,1,0:T(4,128)} %param.13) | copy-start | bytes 2596
  2.3 4.2 %collective-permute-start = (f32[32,384]{1,0:T(8,128)S(1)}, f32[32,384]{1,0:T(8,128)S(1)}, u32[]{:S(2)}, u32[]{:S(2)}) collective-permute-start(f32[32,384]{1,0:T(8,128)S(1)} %get-tuple-element.27), channel_id=1, source_target_pairs={{0,32},{32,0},{1,33},{33,1},{2,34},{34,2},{3,35},{35,3},{4,36},{36... | collective-permute-start | bytes 147464 | tf_op jit(solution)/shard_map/ppermute | solution.py:25
  5.6 5.0 %collective-permute-start.2 = (f32[32,384]{1,0:T(8,128)S(1)}, f32[32,384]{1,0:T(8,128)S(1)}, u32[]{:S(2)}, u32[]{:S(2)}) collective-permute-start(f32[32,384]{1,0:T(8,128)S(1)} %get-tuple-element.30), channel_id=1, source_target_pairs={{0,32},{32,0},{1,33},{33,1},{2,34},{34,2},{3,35},{35,3},{4,36},{36... | collective-permute-start | bytes 147464 | tf_op jit(solution)/shard_map/ppermute | solution.py:25
  6.5 3.0 %collective-permute-start.1 = (f32[32,384]{1,0:T(8,128)S(1)}, f32[32,384]{1,0:T(8,128)S(1)}, u32[]{:S(2)}, u32[]{:S(2)}) collective-permute-start(f32[32,384]{1,0:T(8,128)S(1)} %add.58.one_ref), channel_id=1, source_target_pairs={{0,64},{64,0},{1,65},{65,1},{2,66},{66,2},{3,67},{67,3},{4,68},{68... | collective-permute-start | bytes 147464 | tf_op jit(solution)/shard_map/ppermute | solution.py:25
  9.7 5.2 %collective-permute-start.4 = (f32[32,768]{1,0:T(8,128)S(1)}, f32[32,768]{1,0:T(8,128)S(1)}, u32[]{:S(2)}, u32[]{:S(2)}) collective-permute-start(f32[32,768]{1,0:T(8,128)S(1)} %get-tuple-element.33), channel_id=1, source_target_pairs={{0,4},{4,0},{1,5},{5,1},{2,6},{6,2},{3,7},{7,3},{8,12},{12,8},{9,1... | collective-permute-start | bytes 294920 | tf_op jit(solution)/shard_map/ppermute | solution.py:25
  10.6 3.0 %collective-permute-start.3 = (f32[32,384]{1,0:T(8,128)S(1)}, f32[32,384]{1,0:T(8,128)S(1)}, u32[]{:S(2)}, u32[]{:S(2)}) collective-permute-start(f32[32,384]{1,0:T(8,128)S(1)} %add.61.one_ref), channel_id=1, source_target_pairs={{0,64},{64,0},{1,65},{65,1},{2,66},{66,2},{3,67},{67,3},{4,68},{68... | collective-permute-start | bytes 147464 | tf_op jit(solution)/shard_map/ppermute | solution.py:25
  13.8 4.4 %collective-permute-start.10 = (f32[32,768]{1,0:T(8,128)S(1)}, f32[32,768]{1,0:T(8,128)S(1)}, u32[]{:S(2)}, u32[]{:S(2)}) collective-permute-start(f32[32,768]{1,0:T(8,128)S(1)} %get-tuple-element.37), channel_id=1, source_target_pairs={{0,4},{4,0},{1,5},{5,1},{2,6},{6,2},{3,7},{7,3},{8,12},{12,8},{9,1... | collective-permute-start | bytes 294920 | tf_op jit(solution)/shard_map/ppermute | solution.py:25
  14.8 6.1 %collective-permute-start.5 = (f32[32,768]{1,0:T(8,128)S(1)}, f32[32,768]{1,0:T(8,128)S(1)}, u32[]{:S(2)}, u32[]{:S(2)}) collective-permute-start(f32[32,768]{1,0:T(8,128)S(1)} %add.62.refs_0_), channel_id=1, source_target_pairs={{0,1},{1,0},{2,3},{3,2},{4,5},{5,4},{6,7},{7,6},{8,9},{9,8},{10,11... | collective-permute-start | bytes 294920 | tf_op jit(solution)/shard_map/ppermute | solution.py:25
  15.6 6.1 %collective-permute-start.6 = (f32[32,768]{1,0:T(8,128)S(1)}, f32[32,768]{1,0:T(8,128)S(1)}, u32[]{:S(2)}, u32[]{:S(2)}) collective-permute-start(f32[32,768]{1,0:T(8,128)S(1)} %add.62.refs_0_), channel_id=1, source_target_pairs={{0,3},{1,2},{2,1},{3,0},{4,7},{5,6},{6,5},{7,4},{8,11},{9,10},{10,... | collective-permute-start | bytes 294920 | tf_op jit(solution)/shard_map/ppermute | solution.py:25
  17.5 5.9 %collective-permute-start.7 = (f32[32,768]{1,0:T(8,128)S(1)}, f32[32,768]{1,0:T(8,128)S(1)}, u32[]{:S(2)}, u32[]{:S(2)}) collective-permute-start(f32[32,768]{1,0:T(8,128)S(1)} %add.62.refs_0_), channel_id=1, source_target_pairs={{0,2},{1,3},{2,0},{3,1},{4,6},{5,7},{6,4},{7,5},{8,10},{9,11},{10,... | collective-permute-start | bytes 294920 | tf_op jit(solution)/shard_map/ppermute | solution.py:25
  18.3 10.9 %collective-permute-start.11 = (f32[32,768]{1,0:T(8,128)S(1)}, f32[32,768]{1,0:T(8,128)S(1)}, u32[]{:S(2)}, u32[]{:S(2)}) collective-permute-start(f32[32,768]{1,0:T(8,128)S(1)} %add.64.refs_0_), channel_id=1, source_target_pairs={{0,1},{1,0},{2,3},{3,2},{4,5},{5,4},{6,7},{7,6},{8,9},{9,8},{10,11... | collective-permute-start | bytes 294920 | tf_op jit(solution)/shard_map/ppermute | solution.py:25
  19.1 10.1 %collective-permute-start.12 = (f32[32,768]{1,0:T(8,128)S(1)}, f32[32,768]{1,0:T(8,128)S(1)}, u32[]{:S(2)}, u32[]{:S(2)}) collective-permute-start(f32[32,768]{1,0:T(8,128)S(1)} %add.64.refs_0_), channel_id=1, source_target_pairs={{0,3},{1,2},{2,1},{3,0},{4,7},{5,6},{6,5},{7,4},{8,11},{9,10},{10,... | collective-permute-start | bytes 294920 | tf_op jit(solution)/shard_map/ppermute | solution.py:25
  21.0 8.2 %collective-permute-start.13 = (f32[32,768]{1,0:T(8,128)S(1)}, f32[32,768]{1,0:T(8,128)S(1)}, u32[]{:S(2)}, u32[]{:S(2)}) collective-permute-start(f32[32,768]{1,0:T(8,128)S(1)} %add.64.refs_0_), channel_id=1, source_target_pairs={{0,2},{1,3},{2,0},{3,1},{4,6},{5,7},{6,4},{7,5},{8,10},{9,11},{10,... | collective-permute-start | bytes 294920 | tf_op jit(solution)/shard_map/ppermute | solution.py:25
  23.6 4.7 %collective-permute-start.8 = (f32[32,384]{1,0:T(8,128)S(1)}, f32[32,384]{1,0:T(8,128)S(1)}, u32[]{:S(2)}, u32[]{:S(2)}) collective-permute-start(f32[32,384]{1,0:T(8,128)S(1)} %next_solve.4), channel_id=1, source_target_pairs={{0,32},{32,0},{1,33},{33,1},{2,34},{34,2},{3,35},{35,3},{4,36},{36... | collective-permute-start | bytes 147464 | tf_op jit(solution)/shard_map/ppermute | solution.py:25
  28.4 3.0 %collective-permute-start.9 = (f32[32,384]{1,0:T(8,128)S(1)}, f32[32,384]{1,0:T(8,128)S(1)}, u32[]{:S(2)}, u32[]{:S(2)}) collective-permute-start(f32[32,384]{1,0:T(8,128)S(1)} %add.63.one_ref), channel_id=1, source_target_pairs={{0,64},{64,0},{1,65},{65,1},{2,66},{66,2},{3,67},{67,3},{4,68},{68... | collective-permute-start | bytes 147464 | tf_op jit(solution)/shard_map/ppermute | solution.py:25
  29.4 3.8 %collective-permute-start.14 = (f32[32,384]{1,0:T(8,128)S(1)}, f32[32,384]{1,0:T(8,128)S(1)}, u32[]{:S(2)}, u32[]{:S(2)}) collective-permute-start(f32[32,384]{1,0:T(8,128)S(1)} %next_solve.5), channel_id=1, source_target_pairs={{0,32},{32,0},{1,33},{33,1},{2,34},{34,2},{3,35},{35,3},{4,36},{36... | collective-permute-start | bytes 147464 | tf_op jit(solution)/shard_map/ppermute | solution.py:25
  31.6 5.2 %collective-permute-start.16 = (f32[32,768]{1,0:T(8,128)S(1)}, f32[32,768]{1,0:T(8,128)S(1)}, u32[]{:S(2)}, u32[]{:S(2)}) collective-permute-start(f32[32,768]{1,0:T(8,128)S(1)} %get-tuple-element.40), channel_id=1, source_target_pairs={{0,4},{4,0},{1,5},{5,1},{2,6},{6,2},{3,7},{7,3},{8,12},{12,8},{9,1... | collective-permute-start | bytes 294920 | tf_op jit(solution)/shard_map/ppermute | solution.py:25
  33.2 3.3 %collective-permute-start.15 = (f32[32,384]{1,0:T(8,128)S(1)}, f32[32,384]{1,0:T(8,128)S(1)}, u32[]{:S(2)}, u32[]{:S(2)}) collective-permute-start(f32[32,384]{1,0:T(8,128)S(1)} %add.65.one_ref), channel_id=1, source_target_pairs={{0,64},{64,0},{1,65},{65,1},{2,66},{66,2},{3,67},{67,3},{4,68},{68... | collective-permute-start | bytes 147464 | tf_op jit(solution)/shard_map/ppermute | solution.py:25
  36.7 3.6 %collective-permute-start.22 = (f32[32,768]{1,0:T(8,128)S(1)}, f32[32,768]{1,0:T(8,128)S(1)}, u32[]{:S(2)}, u32[]{:S(2)}) collective-permute-start(f32[32,768]{1,0:T(8,128)S(1)} %get-tuple-element.43), channel_id=1, source_target_pairs={{0,4},{4,0},{1,5},{5,1},{2,6},{6,2},{3,7},{7,3},{8,12},{12,8},{9,1... | collective-permute-start | bytes 294920 | tf_op jit(solution)/shard_map/ppermute | solution.py:25
  36.8 5.1 %collective-permute-start.17 = (f32[32,768]{1,0:T(8,128)S(1)}, f32[32,768]{1,0:T(8,128)S(1)}, u32[]{:S(2)}, u32[]{:S(2)}) collective-permute-start(f32[32,768]{1,0:T(8,128)S(1)} %add.66.refs_0_), channel_id=1, source_target_pairs={{0,1},{1,0},{2,3},{3,2},{4,5},{5,4},{6,7},{7,6},{8,9},{9,8},{10,11... | collective-permute-start | bytes 294920 | tf_op jit(solution)/shard_map/ppermute | solution.py:25
  37.3 6.4 %collective-permute-start.18 = (f32[32,768]{1,0:T(8,128)S(1)}, f32[32,768]{1,0:T(8,128)S(1)}, u32[]{:S(2)}, u32[]{:S(2)}) collective-permute-start(f32[32,768]{1,0:T(8,128)S(1)} %add.66.refs_0_), channel_id=1, source_target_pairs={{0,3},{1,2},{2,1},{3,0},{4,7},{5,6},{6,5},{7,4},{8,11},{9,10},{10,... | collective-permute-start | bytes 294920 | tf_op jit(solution)/shard_map/ppermute | solution.py:25
  38.4 5.2 %collective-permute-start.19 = (f32[32,768]{1,0:T(8,128)S(1)}, f32[32,768]{1,0:T(8,128)S(1)}, u32[]{:S(2)}, u32[]{:S(2)}) collective-permute-start(f32[32,768]{1,0:T(8,128)S(1)} %add.66.refs_0_), channel_id=1, source_target_pairs={{0,2},{1,3},{2,0},{3,1},{4,6},{5,7},{6,4},{7,5},{8,10},{9,11},{10,... | collective-permute-start | bytes 294920 | tf_op jit(solution)/shard_map/ppermute | solution.py:25
  40.3 14.6 %copy-start.4 = (s32[3,3,24]{2,1,0:T(4,128)S(1)}, s32[3,3,24]{2,1,0:T(4,128)}, u32[]{:S(2)}) copy-start(s32[3,3,24]{2,1,0:T(4,128)} %param.15) | copy-start | bytes 2596
  40.3 14.6 %copy-start.2 = (bf16[3,384,768]{2,1,0:T(8,128)(2,1)S(1)}, bf16[3,384,768]{2,1,0:T(8,128)(2,1)}, u32[]{:S(2)}) copy-start(bf16[3,384,768]{2,1,0:T(8,128)(2,1)} %factor_ref.1) | copy-start | bytes 5308420
  40.3 9.2 %collective-permute-start.23 = (f32[32,768]{1,0:T(8,128)S(1)}, f32[32,768]{1,0:T(8,128)S(1)}, u32[]{:S(2)}, u32[]{:S(2)}) collective-permute-start(f32[32,768]{1,0:T(8,128)S(1)} %add.68.refs_0_), channel_id=1, source_target_pairs={{0,1},{1,0},{2,3},{3,2},{4,5},{5,4},{6,7},{7,6},{8,9},{9,8},{10,11... | collective-permute-start | bytes 294920 | tf_op jit(solution)/shard_map/ppermute | solution.py:25
  40.7 8.8 %collective-permute-start.24 = (f32[32,768]{1,0:T(8,128)S(1)}, f32[32,768]{1,0:T(8,128)S(1)}, u32[]{:S(2)}, u32[]{:S(2)}) collective-permute-start(f32[32,768]{1,0:T(8,128)S(1)} %add.68.refs_0_), channel_id=1, source_target_pairs={{0,3},{1,2},{2,1},{3,0},{4,7},{5,6},{6,5},{7,4},{8,11},{9,10},{10,... | collective-permute-start | bytes 294920 | tf_op jit(solution)/shard_map/ppermute | solution.py:25
  41.9 7.6 %collective-permute-start.25 = (f32[32,768]{1,0:T(8,128)S(1)}, f32[32,768]{1,0:T(8,128)S(1)}, u32[]{:S(2)}, u32[]{:S(2)}) collective-permute-start(f32[32,768]{1,0:T(8,128)S(1)} %add.68.refs_0_), channel_id=1, source_target_pairs={{0,2},{1,3},{2,0},{3,1},{4,6},{5,7},{6,4},{7,5},{8,10},{9,11},{10,... | collective-permute-start | bytes 294920 | tf_op jit(solution)/shard_map/ppermute | solution.py:25
  43.9 8.9 %collective-permute-start.20 = (f32[32,384]{1,0:T(8,128)S(1)}, f32[32,384]{1,0:T(8,128)S(1)}, u32[]{:S(2)}, u32[]{:S(2)}) collective-permute-start(f32[32,384]{1,0:T(8,128)S(1)} %next_solve.6), channel_id=1, source_target_pairs={{0,32},{32,0},{1,33},{33,1},{2,34},{34,2},{3,35},{35,3},{4,36},{36... | collective-permute-start | bytes 147464 | tf_op jit(solution)/shard_map/ppermute | solution.py:25
  49.7 4.3 %collective-permute-start.26 = (f32[32,384]{1,0:T(8,128)S(1)}, f32[32,384]{1,0:T(8,128)S(1)}, u32[]{:S(2)}, u32[]{:S(2)}) collective-permute-start(f32[32,384]{1,0:T(8,128)S(1)} %next_solve.7), channel_id=1, source_target_pairs={{0,32},{32,0},{1,33},{33,1},{2,34},{34,2},{3,35},{35,3},{4,36},{36... | collective-permute-start | bytes 147464 | tf_op jit(solution)/shard_map/ppermute | solution.py:25
  52.7 3.8 %collective-permute-start.21 = (f32[32,384]{1,0:T(8,128)S(1)}, f32[32,384]{1,0:T(8,128)S(1)}, u32[]{:S(2)}, u32[]{:S(2)}) collective-permute-start(f32[32,384]{1,0:T(8,128)S(1)} %add.67.one_ref), channel_id=1, source_target_pairs={{0,64},{64,0},{1,65},{65,1},{2,66},{66,2},{3,67},{67,3},{4,68},{68... | collective-permute-start | bytes 147464 | tf_op jit(solution)/shard_map/ppermute | solution.py:25
  54.0 3.0 %collective-permute-start.27 = (f32[32,384]{1,0:T(8,128)S(1)}, f32[32,384]{1,0:T(8,128)S(1)}, u32[]{:S(2)}, u32[]{:S(2)}) collective-permute-start(f32[32,384]{1,0:T(8,128)S(1)} %add.69.one_ref), channel_id=1, source_target_pairs={{0,64},{64,0},{1,65},{65,1},{2,66},{66,2},{3,67},{67,3},{4,68},{68... | collective-permute-start | bytes 147464 | tf_op jit(solution)/shard_map/ppermute | solution.py:25
  56.7 27.1 %copy-start.1 = (bf16[768,1536]{1,0:T(8,128)(2,1)S(1)}, bf16[768,1536]{1,0:T(8,128)(2,1)}, u32[]{:S(2)}) copy-start(bf16[768,1536]{1,0:T(8,128)(2,1)} %inverse_ref.1) | copy-start | bytes 7077892
  66.9 6.6 %collective-permute-start.28 = (f32[8,768]{1,0:T(8,128)S(1)}, f32[8,768]{1,0:T(8,128)S(1)}, u32[]{:S(2)}, u32[]{:S(2)}) collective-permute-start(f32[8,768]{1,0:T(8,128)S(1)} %reduce_sum.9), channel_id=1, source_target_pairs={{0,128},{8,136},{16,144},{24,152},{128,0},{136,8},{144,16},{152,24... | collective-permute-start | bytes 73736 | tf_op jit(solution)/shard_map/ppermute | solution.py:25
  69.7 4.8 %collective-permute-start.29 = (f32[8,768]{1,0:T(8,128)S(1)}, f32[8,768]{1,0:T(8,128)S(1)}, u32[]{:S(2)}, u32[]{:S(2)}) collective-permute-start(f32[8,768]{1,0:T(8,128)S(1)} %reduce_sum.9), channel_id=1, source_target_pairs={{0,8},{8,0},{16,24},{24,16},{128,136},{136,128},{144,152},{152,144... | collective-permute-start | bytes 73736 | tf_op jit(solution)/shard_map/ppermute | solution.py:25
  72.7 6.2 %collective-permute-start.30 = (f32[8,768]{1,0:T(8,128)S(1)}, f32[8,768]{1,0:T(8,128)S(1)}, u32[]{:S(2)}, u32[]{:S(2)}) collective-permute-start(f32[8,768]{1,0:T(8,128)S(1)} %reduce_sum.9), channel_id=1, source_target_pairs={{0,136},{8,128},{16,152},{24,144},{128,8},{136,0},{144,24},{152,16... | collective-permute-start | bytes 73736 | tf_op jit(solution)/shard_map/ppermute | solution.py:25
  79.0 4.9 %collective-permute-start.31 = (f32[8,768]{1,0:T(8,128)S(1)}, f32[8,768]{1,0:T(8,128)S(1)}, u32[]{:S(2)}, u32[]{:S(2)}) collective-permute-start(f32[8,768]{1,0:T(8,128)S(1)} %add_add_fusion.one_ref), channel_id=1, source_target_pairs={{0,24},{8,16},{16,8},{24,0},{1,25},{9,17},{17,9},{25,1},{2,26},{10... | collective-permute-start | bytes 73736 | tf_op jit(solution)/shard_map/ppermute | solution.py:25
  84.2 6.4 %collective-permute-start.32 = (f32[8,1536]{1,0:T(8,128)S(1)}, f32[8,1536]{1,0:T(8,128)S(1)}, u32[]{:S(2)}, u32[]{:S(2)}) collective-permute-start(f32[8,1536]{1,0:T(8,128)S(1)} %root_part.1), channel_id=1, source_target_pairs={{0,32},{32,0},{1,33},{33,1},{2,34},{34,2},{3,35},{35,3},{4,36},{36... | collective-permute-start | bytes 147464 | tf_op jit(solution)/shard_map/ppermute | solution.py:25
  90.6 2.9 %collective-permute-start.33 = (f32[8,1536]{1,0:T(8,128)S(1)}, f32[8,1536]{1,0:T(8,128)S(1)}, u32[]{:S(2)}, u32[]{:S(2)}) collective-permute-start(f32[8,1536]{1,0:T(8,128)S(1)} %add.75), channel_id=1, source_target_pairs={{0,64},{64,0},{1,65},{65,1},{2,66},{66,2},{3,67},{67,3},{4,68},{68... | collective-permute-start | bytes 147464 | tf_op jit(solution)/shard_map/ppermute | solution.py:25

commit v5 on v4

--- a/solution.py
+++ b/solution.py
@@ -248,9 +248,10 @@
 
 
 def root_part(rhs_rows, update_parts, root_inverse):
-    def body(rhs_ref, one_ref, other_ref, inverse_ref, out_ref):
-        residual = rhs_ref[...] - (one_ref[...] + other_ref[...])
-        out_ref[...] = product(residual.astype(BF16), inverse_ref[...])
+    def body(rhs_ref, own_ref, one_ref, two_ref, both_ref, inverse_ref, out_ref):
+        update = own_ref[...] + one_ref[...] + (two_ref[...] + both_ref[...])
+        residual = (rhs_ref[...] - update).astype(BF16)
+        out_ref[...] = product(residual, inverse_ref[...])
 
     shape = (rhs_rows.shape[0], root_inverse.shape[1])
     return call(
@@ -298,6 +299,9 @@
 
     owners = lax.axis_size(OWN)
     few = rhs_count // owners
+    rhs_rows = lax.dynamic_slice_in_dim(root_rhs, lax.axis_index(OWN) * few, few, 0)
+    rhs_rows = jnp.where(lax.axis_index("zt") < lax.axis_size("zt") // 2, rhs_rows, 0.0)
+    rhs_rows, root_local = lax.optimization_barrier((rhs_rows, root_local))
     own_rows = lax.all_to_all(
         root_local.reshape(owners, few, out_cols), OWN, 0, 0, tiled=True
     ).sum(axis=0)
@@ -307,11 +311,14 @@
             *[partner(own_rows, TREES, bit) for bit in (4, 1, 5)],
         )
     )
-    total = own_rows + arrived[0] + (arrived[1] + arrived[2])
-    rhs_rows = lax.dynamic_slice_in_dim(root_rhs, lax.axis_index(OWN) * few, few, 0)
-    part = root_part(rhs_rows, (total, partner(total, "zt", 3)), root_inverse)
-    pair, other = prow_halves(part)
-    root_solution = to_everyone(pair + other, OWN).reshape(rhs_count, part.shape[1])
+    part = root_part(rhs_rows, (own_rows, *arrived), root_inverse)
+    pair = part + partner(part, "core")
+    trees = lax.axis_size("zt")
+    across, far, both = [
+        partner(pair, ("xl", "zt"), bit) for bit in (trees, trees - 1, 2 * trees - 1)
+    ]
+    own_solution = pair + across + (far + both)
+    root_solution = to_everyone(own_solution, OWN).reshape(rhs_count, part.shape[1])
     return (sub_solution, root_solution)
 
 

time: 104 us -> 105 us (level)
    ppermute x34 -> x35, starting transfers between devices: 53.2 us -> 52.9 us  [partner(): lax.ppermute(shard, axis, [(i, i ^ bit) for i in range(lax.axis_size(axis...]
    ppermute x34 -> x35, waiting for transfers between devices: 20.4 us -> 20.1 us  [partner(): lax.ppermute(shard, axis, [(i, i ^ bit) for i in range(lax.axis_size(axis...]
  transfers between devices with their start and end apart: 34 -> 35, of which waited for: 14 -> 15; matrix products, arithmetic and copies ran while one was open for 0% -> 1% of each run, Pallas kernels for 7% -> 7%
where the time goes in v5:
time: 105 us; the launch traced here: 104 us
  starting transfers between devices  52.9 us (50%)
  waiting for transfers between devices  20.1 us (19%)
  blocking collectives  19.5 us (19%)
  Pallas kernels  9.17 us (9%)
    ppermute x35, starting transfers between devices, partner(): lax.ppermute(shard, axis, [(i, i ^ bit) for i in range(lax.axis_size(axis...  52.9 us
    ppermute x35, waiting for transfers between devices, partner(): lax.ppermute(shard, axis, [(i, i ^ bit) for i in range(lax.axis_size(axis...  20.1 us
    all_to_all x1, blocking collectives, shards(): lax.all_to_all(root_local.reshape(owners, few, out_cols), OWN, 0, 0, tile...  9.92 us
    all_to_all x1, blocking collectives, to_everyone(): lax.all_to_all(jnp.broadcast_to(shard[None], (count, *shard.shape)), axis...  9.6 us
    pallas_call x18, Pallas kernels, call(): pl.pallas_call(body, out_shape=[pltpu.VMEM(shape, kind) for shape, kind i...  8.42 us
  transfers between devices with their start and end apart: 35, of which 15 were waited for; matrix products, arithmetic and copies ran while one was open for 1% of the time, Pallas kernels for 7%

profile of v5, /device:TPU:1, one launch (start us, length us, event | category | flops | bytes accessed | tf_op | source)
XLA Modules:
  0.0 104.4 jit_solution(159786199060555817)
XLA Ops:
  0.7 1.5 %first_solve.1 = (f32[32,384]{1,0:T(8,128)S(1)}, f32[32,384]{1,0:T(8,128)S(1)}) custom-call(s32[1]{0:T(128)} %bitcast.tree_ref, f32[4,3,64,768]{3,2,1,0:T(8,128)} %rhs_hbm.3, bf16[3,768,384]{2,1,0:T(8,128)(2,1)} %inverse_hbm.3), custom_call_target="tpu_custom_call" | custom-call | tf_op jit(solution)/shard_map/first_solve/pallas_call | solution.py:41
  2.2 3.3 %collective-permute-start = (f32[32,384]{1,0:T(8,128)S(1)}, f32[32,384]{1,0:T(8,128)S(1)}, u32[]{:S(2)}, u32[]{:S(2)}) collective-permute-start(f32[32,384]{1,0:T(8,128)S(1)} %get-tuple-element.29), channel_id=1, source_target_pairs={{0,32},{32,0},{1,33},{33,1},{2,34},{34,2},{3,35},{35,3},{4,36},{36... | collective-permute-start | bytes 147464 | tf_op jit(solution)/shard_map/ppermute | solution.py:25
  5.6 0.8 collective-permute-done
  6.6 2.6 %stage.1 = (bf16[3,384,768]{2,1,0:T(8,128)(2,1)S(1)}, bf16[2,768,384]{2,1,0:T(8,128)(2,1)S(1)}, f32[2,64,768]{2,1,0:T(8,128)S(1)}) custom-call(s32[1]{0:T(128)} %bitcast.tree_ref, s32[3,3,6]{2,1,0:T(4,128)S(1)} %constant_dynamic-slice_fusion.1.mask_ref, f32[4,3,64,768]{3,2,1,0:T(8,128)} %rhs_hbm.3, bf16[3,768,384]{2,1,0:T(8,128)(2,1)} %inverse_hbm.3, ...), custom_call_target="tpu_custom_call" | custom-call | tf_op jit(solution)/shard_map/stage/pallas_call | solution.py:41
  9.1 0.3 collective-permute-done.1.other_ref
  9.6 0.9 collective-permute-start.4
  10.5 0.5 collective-permute-start.3
  11.0 2.6 %collective-permute-done.3.other_ref = f32[32,384]{1,0:T(8,128)S(1)} collective-permute-done((f32[32,384]{1,0:T(8,128)S(1)}, f32[32,384]{1,0:T(8,128)S(1)}, u32[]{:S(2)}, u32[]{:S(2)}) %collective-permute-start.3) | collective-permute-done | bytes 49184 | tf_op jit(solution)/shard_map/ppermute | solution.py:25
  13.8 1.0 collective-permute-start.10
  14.8 0.8 collective-permute-start.5
  15.6 1.9 %collective-permute-start.6 = (f32[32,768]{1,0:T(8,128)S(1)}, f32[32,768]{1,0:T(8,128)S(1)}, u32[]{:S(2)}, u32[]{:S(2)}) collective-permute-start(f32[32,768]{1,0:T(8,128)S(1)} %add.59.refs_0_), channel_id=1, source_target_pairs={{0,3},{1,2},{2,1},{3,0},{4,7},{5,6},{6,5},{7,4},{8,11},{9,10},{10,... | collective-permute-start | bytes 294920 | tf_op jit(solution)/shard_map/ppermute | solution.py:25
  17.5 0.7 collective-permute-start.7
  18.2 0.8 collective-permute-start.11
  19.0 1.9 %collective-permute-start.12 = (f32[32,768]{1,0:T(8,128)S(1)}, f32[32,768]{1,0:T(8,128)S(1)}, u32[]{:S(2)}, u32[]{:S(2)}) collective-permute-start(f32[32,768]{1,0:T(8,128)S(1)} %add.61.refs_0_), channel_id=1, source_target_pairs={{0,3},{1,2},{2,1},{3,0},{4,7},{5,6},{6,5},{7,4},{8,11},{9,10},{10,... | collective-permute-start | bytes 294920 | tf_op jit(solution)/shard_map/ppermute | solution.py:25
  20.9 0.7 collective-permute-start.13
  21.6 1.8 %collective-permute-done.7.refs_3_ = f32[32,768]{1,0:T(8,128)S(1)} collective-permute-done((f32[32,768]{1,0:T(8,128)S(1)}, f32[32,768]{1,0:T(8,128)S(1)}, u32[]{:S(2)}, u32[]{:S(2)}) %collective-permute-start.7) | collective-permute-done | bytes 98336 | tf_op jit(solution)/shard_map/ppermute | solution.py:25
  23.4 0.2 next_solve.4
  23.6 3.9 %collective-permute-start.8 = (f32[32,384]{1,0:T(8,128)S(1)}, f32[32,384]{1,0:T(8,128)S(1)}, u32[]{:S(2)}, u32[]{:S(2)}) collective-permute-start(f32[32,384]{1,0:T(8,128)S(1)} %next_solve.4), channel_id=1, source_target_pairs={{0,32},{32,0},{1,33},{33,1},{2,34},{34,2},{3,35},{35,3},{4,36},{36... | collective-permute-start | bytes 147464 | tf_op jit(solution)/shard_map/ppermute | solution.py:25
  27.5 0.9 collective-permute-done.8
  28.3 0.8 collective-permute-start.9
  29.2 0.2 next_solve.5
  29.4 1.5 %collective-permute-start.14 = (f32[32,384]{1,0:T(8,128)S(1)}, f32[32,384]{1,0:T(8,128)S(1)}, u32[]{:S(2)}, u32[]{:S(2)}) collective-permute-start(f32[32,384]{1,0:T(8,128)S(1)} %next_solve.5), channel_id=1, source_target_pairs={{0,32},{32,0},{1,33},{33,1},{2,34},{34,2},{3,35},{35,3},{4,36},{36... | collective-permute-start | bytes 147464 | tf_op jit(solution)/shard_map/ppermute | solution.py:25
  30.9 0.2 early_update.4.refs_0_
  31.1 0.3 collective-permute-done.9.other_ref
  31.3 0.2 kept_update.8
  31.5 1.6 %collective-permute-start.16 = (f32[32,768]{1,0:T(8,128)S(1)}, f32[32,768]{1,0:T(8,128)S(1)}, u32[]{:S(2)}, u32[]{:S(2)}) collective-permute-start(f32[32,768]{1,0:T(8,128)S(1)} %get-tuple-element.42), channel_id=1, source_target_pairs={{0,4},{4,0},{1,5},{5,1},{2,6},{6,2},{3,7},{7,3},{8,12},{12,8},{9,1... | collective-permute-start | bytes 294920 | tf_op jit(solution)/shard_map/ppermute | solution.py:25
  33.1 0.8 collective-permute-start.15
  34.1 2.3 %collective-permute-done.15.other_ref = f32[32,384]{1,0:T(8,128)S(1)} collective-permute-done((f32[32,384]{1,0:T(8,128)S(1)}, f32[32,384]{1,0:T(8,128)S(1)}, u32[]{:S(2)}, u32[]{:S(2)}) %collective-permute-start.15) | collective-permute-done | bytes 49184 | tf_op jit(solution)/shard_map/ppermute | solution.py:25
  36.5 0.2 kept_update.9
  36.8 0.4 collective-permute-start.17
  37.2 1.2 %collective-permute-start.18 = (f32[32,768]{1,0:T(8,128)S(1)}, f32[32,768]{1,0:T(8,128)S(1)}, u32[]{:S(2)}, u32[]{:S(2)}) collective-permute-start(f32[32,768]{1,0:T(8,128)S(1)} %add.63.refs_0_), channel_id=1, source_target_pairs={{0,3},{1,2},{2,1},{3,0},{4,7},{5,6},{6,5},{7,4},{8,11},{9,10},{10,... | collective-permute-start | bytes 294920 | tf_op jit(solution)/shard_map/ppermute | solution.py:25
  38.4 1.7 %collective-permute-start.19 = (f32[32,768]{1,0:T(8,128)S(1)}, f32[32,768]{1,0:T(8,128)S(1)}, u32[]{:S(2)}, u32[]{:S(2)}) collective-permute-start(f32[32,768]{1,0:T(8,128)S(1)} %add.63.refs_0_), channel_id=1, source_target_pairs={{0,2},{1,3},{2,0},{3,1},{4,6},{5,7},{6,4},{7,5},{8,10},{9,11},{10,... | collective-permute-start | bytes 294920 | tf_op jit(solution)/shard_map/ppermute | solution.py:25
  40.2 0.3 collective-permute-start.23
  40.6 1.2 %collective-permute-start.24 = (f32[32,768]{1,0:T(8,128)S(1)}, f32[32,768]{1,0:T(8,128)S(1)}, u32[]{:S(2)}, u32[]{:S(2)}) collective-permute-start(f32[32,768]{1,0:T(8,128)S(1)} %add.65.refs_0_), channel_id=1, source_target_pairs={{0,3},{1,2},{2,1},{3,0},{4,7},{5,6},{6,5},{7,4},{8,11},{9,10},{10,... | collective-permute-start | bytes 294920 | tf_op jit(solution)/shard_map/ppermute | solution.py:25
  41.9 1.7 %collective-permute-start.25 = (f32[32,768]{1,0:T(8,128)S(1)}, f32[32,768]{1,0:T(8,128)S(1)}, u32[]{:S(2)}, u32[]{:S(2)}) collective-permute-start(f32[32,768]{1,0:T(8,128)S(1)} %add.65.refs_0_), channel_id=1, source_target_pairs={{0,2},{1,3},{2,0},{3,1},{4,6},{5,7},{6,4},{7,5},{8,10},{9,11},{10,... | collective-permute-start | bytes 294920 | tf_op jit(solution)/shard_map/ppermute | solution.py:25
  43.6 0.2 next_solve.6
  43.8 5.6 %collective-permute-start.20 = (f32[32,384]{1,0:T(8,128)S(1)}, f32[32,384]{1,0:T(8,128)S(1)}, u32[]{:S(2)}, u32[]{:S(2)}) collective-permute-start(f32[32,384]{1,0:T(8,128)S(1)} %next_solve.6), channel_id=1, source_target_pairs={{0,32},{32,0},{1,33},{33,1},{2,34},{34,2},{3,35},{35,3},{4,36},{36... | collective-permute-start | bytes 147464 | tf_op jit(solution)/shard_map/ppermute | solution.py:25
  49.4 0.2 next_solve.7
  49.6 3.0 %collective-permute-start.26 = (f32[32,384]{1,0:T(8,128)S(1)}, f32[32,384]{1,0:T(8,128)S(1)}, u32[]{:S(2)}, u32[]{:S(2)}) collective-permute-start(f32[32,384]{1,0:T(8,128)S(1)} %next_solve.7), channel_id=1, source_target_pairs={{0,32},{32,0},{1,33},{33,1},{2,34},{34,2},{3,35},{35,3},{4,36},{36... | collective-permute-start | bytes 147464 | tf_op jit(solution)/shard_map/ppermute | solution.py:25
  52.6 0.7 dynamic-slice_select_fusion.rhs_ref
  53.4 1.3 %collective-permute-start.21 = (f32[32,384]{1,0:T(8,128)S(1)}, f32[32,384]{1,0:T(8,128)S(1)}, u32[]{:S(2)}, u32[]{:S(2)}) collective-permute-start(f32[32,384]{1,0:T(8,128)S(1)} %add.64.one_ref), channel_id=1, source_target_pairs={{0,64},{64,0},{1,65},{65,1},{2,66},{66,2},{3,67},{67,3},{4,68},{68... | collective-permute-start | bytes 147464 | tf_op jit(solution)/shard_map/ppermute | solution.py:25
  54.7 0.4 collective-permute-start.27
  55.1 0.9 masked.1.refs_2_.factor_ref
  56.1 0.3 early_update.6.refs_0_
  56.4 0.3 early_update.7.refs_0_
  56.8 0.2 kept_update.10
  57.1 0.6 collective-permute-done.27.other_ref
  57.7 0.2 kept_update.11
  57.9 9.9 %all_to_all.10 = f32[8,8,768]{2,1,0:T(8,128)S(1)} all-to-all(f32[8,8,768]{2,1,0:T(8,128)S(1)} %bitcast.4), channel_id=1, replica_groups=mesh['grid'=2,'xl'=2,'core'=2,'zt'=4,'zl'=2,'y'=4] {'zl','y'}, dimensions={0} | all-to-all | bytes 393216 | tf_op jit(solution)/shard_map/all_to_all | solution.py:305
  67.9 2.8 %collective-permute-start.28 = (f32[8,768]{1,0:T(8,128)S(1)}, f32[8,768]{1,0:T(8,128)S(1)}, u32[]{:S(2)}, u32[]{:S(2)}) collective-permute-start(f32[8,768]{1,0:T(8,128)S(1)} %reduce_sum.9.own_ref), channel_id=1, source_target_pairs={{0,128},{8,136},{16,144},{24,152},{128,0},{136,8},{144,16},{152,24... | collective-permute-start | bytes 73736 | tf_op jit(solution)/shard_map/ppermute | solution.py:25
  70.7 3.0 %collective-permute-start.29 = (f32[8,768]{1,0:T(8,128)S(1)}, f32[8,768]{1,0:T(8,128)S(1)}, u32[]{:S(2)}, u32[]{:S(2)}) collective-permute-start(f32[8,768]{1,0:T(8,128)S(1)} %reduce_sum.9.own_ref), channel_id=1, source_target_pairs={{0,8},{8,0},{16,24},{24,16},{128,136},{136,128},{144,152},{152,144... | collective-permute-start | bytes 73736 | tf_op jit(solution)/shard_map/ppermute | solution.py:25
  73.7 0.8 stacked.1
  74.4 0.7 collective-permute-done.29.two_ref
  75.2 4.8 %collective-permute-done.30.both_ref = f32[8,768]{1,0:T(8,128)S(1)} collective-permute-done((f32[8,768]{1,0:T(8,128)S(1)}, f32[8,768]{1,0:T(8,128)S(1)}, u32[]{:S(2)}, u32[]{:S(2)}) %collective-permute-start.30) | collective-permute-done | bytes 24608 | tf_op jit(solution)/shard_map/ppermute | solution.py:25
  79.9 0.4 root_part.1
  80.3 4.1 %collective-permute-start.31 = (f32[8,1536]{1,0:T(8,128)S(1)}, f32[8,1536]{1,0:T(8,128)S(1)}, u32[]{:S(2)}, u32[]{:S(2)}) collective-permute-start(f32[8,1536]{1,0:T(8,128)S(1)} %root_part.1), channel_id=1, source_target_pairs={{0,32},{32,0},{1,33},{33,1},{2,34},{34,2},{3,35},{35,3},{4,36},{36... | collective-permute-start | bytes 147464 | tf_op jit(solution)/shard_map/ppermute | solution.py:25
  84.4 0.9 collective-permute-done.31
  85.3 2.7 %collective-permute-start.33 = (f32[8,1536]{1,0:T(8,128)S(1)}, f32[8,1536]{1,0:T(8,128)S(1)}, u32[]{:S(2)}, u32[]{:S(2)}) collective-permute-start(f32[8,1536]{1,0:T(8,128)S(1)} %add.69), channel_id=1, source_target_pairs={{0,24},{8,16},{16,8},{24,0},{64,88},{72,80},{80,72},{88,64},{1,25}... | collective-permute-start | bytes 147464 | tf_op jit(solution)/shard_map/ppermute | solution.py:25
  88.0 0.6 collective-permute-start.34
  88.6 1.5 %collective-permute-start.32 = (f32[8,1536]{1,0:T(8,128)S(1)}, f32[8,1536]{1,0:T(8,128)S(1)}, u32[]{:S(2)}, u32[]{:S(2)}) collective-permute-start(f32[8,1536]{1,0:T(8,128)S(1)} %add.69), channel_id=1, source_target_pairs={{0,64},{8,72},{16,80},{24,88},{64,0},{72,8},{80,16},{88,24},{1,65}... | collective-permute-start | bytes 147464 | tf_op jit(solution)/shard_map/ppermute | solution.py:25
  90.0 1.4 %collective-permute-done.33 = f32[8,1536]{1,0:T(8,128)S(1)} collective-permute-done((f32[8,1536]{1,0:T(8,128)S(1)}, f32[8,1536]{1,0:T(8,128)S(1)}, u32[]{:S(2)}, u32[]{:S(2)}) %collective-permute-start.33) | collective-permute-done | bytes 49184 | tf_op jit(solution)/shard_map/ppermute | solution.py:25
  91.4 2.6 %collective-permute-done.34 = f32[8,1536]{1,0:T(8,128)S(1)} collective-permute-done((f32[8,1536]{1,0:T(8,128)S(1)}, f32[8,1536]{1,0:T(8,128)S(1)}, u32[]{:S(2)}, u32[]{:S(2)}) %collective-permute-start.34) | collective-permute-done | bytes 49184 | tf_op jit(solution)/shard_map/ppermute | solution.py:25
  94.0 9.6 %all_to_all.11 = f32[8,8,1536]{2,1,0:T(8,128)S(1)} all-to-all(f32[8,8,1536]{2,1,0:T(8,128)S(1)} %broadcast_in_dim.11), channel_id=1, replica_groups=mesh['grid'=2,'xl'=2,'core'=2,'zt'=4,'zl'=2,'y'=4] {'zl','y'}, dimensions={0} | all-to-all | bytes 786432 | tf_op jit(solution)/shard_map/all_to_all | solution.py:30
  103.7 0.7 copy.11
  (54 shorter events, 1.4 us)
Async XLA Ops:
  0.6 5.9 %copy-start = (s32[3,3,24]{2,1,0:T(4,128)S(1)}, s32[3,3,24]{2,1,0:T(4,128)}, u32[]{:S(2)}) copy-start(s32[3,3,24]{2,1,0:T(4,128)} %param.13) | copy-start | bytes 2596
  2.2 4.2 %collective-permute-start = (f32[32,384]{1,0:T(8,128)S(1)}, f32[32,384]{1,0:T(8,128)S(1)}, u32[]{:S(2)}, u32[]{:S(2)}) collective-permute-start(f32[32,384]{1,0:T(8,128)S(1)} %get-tuple-element.29), channel_id=1, source_target_pairs={{0,32},{32,0},{1,33},{33,1},{2,34},{34,2},{3,35},{35,3},{4,36},{36... | collective-permute-start | bytes 147464 | tf_op jit(solution)/shard_map/ppermute | solution.py:25
  5.5 5.0 %collective-permute-start.2 = (f32[32,384]{1,0:T(8,128)S(1)}, f32[32,384]{1,0:T(8,128)S(1)}, u32[]{:S(2)}, u32[]{:S(2)}) collective-permute-start(f32[32,384]{1,0:T(8,128)S(1)} %get-tuple-element.32), channel_id=1, source_target_pairs={{0,32},{32,0},{1,33},{33,1},{2,34},{34,2},{3,35},{35,3},{4,36},{36... | collective-permute-start | bytes 147464 | tf_op jit(solution)/shard_map/ppermute | solution.py:25
  6.4 3.0 %collective-permute-start.1 = (f32[32,384]{1,0:T(8,128)S(1)}, f32[32,384]{1,0:T(8,128)S(1)}, u32[]{:S(2)}, u32[]{:S(2)}) collective-permute-start(f32[32,384]{1,0:T(8,128)S(1)} %add.55.one_ref), channel_id=1, source_target_pairs={{0,64},{64,0},{1,65},{65,1},{2,66},{66,2},{3,67},{67,3},{4,68},{68... | collective-permute-start | bytes 147464 | tf_op jit(solution)/shard_map/ppermute | solution.py:25
  9.6 5.2 %collective-permute-start.4 = (f32[32,768]{1,0:T(8,128)S(1)}, f32[32,768]{1,0:T(8,128)S(1)}, u32[]{:S(2)}, u32[]{:S(2)}) collective-permute-start(f32[32,768]{1,0:T(8,128)S(1)} %get-tuple-element.35), channel_id=1, source_target_pairs={{0,4},{4,0},{1,5},{5,1},{2,6},{6,2},{3,7},{7,3},{8,12},{12,8},{9,1... | collective-permute-start | bytes 294920 | tf_op jit(solution)/shard_map/ppermute | solution.py:25
  10.5 3.0 %collective-permute-start.3 = (f32[32,384]{1,0:T(8,128)S(1)}, f32[32,384]{1,0:T(8,128)S(1)}, u32[]{:S(2)}, u32[]{:S(2)}) collective-permute-start(f32[32,384]{1,0:T(8,128)S(1)} %add.58.one_ref), channel_id=1, source_target_pairs={{0,64},{64,0},{1,65},{65,1},{2,66},{66,2},{3,67},{67,3},{4,68},{68... | collective-permute-start | bytes 147464 | tf_op jit(solution)/shard_map/ppermute | solution.py:25
  13.8 4.4 %collective-permute-start.10 = (f32[32,768]{1,0:T(8,128)S(1)}, f32[32,768]{1,0:T(8,128)S(1)}, u32[]{:S(2)}, u32[]{:S(2)}) collective-permute-start(f32[32,768]{1,0:T(8,128)S(1)} %get-tuple-element.39), channel_id=1, source_target_pairs={{0,4},{4,0},{1,5},{5,1},{2,6},{6,2},{3,7},{7,3},{8,12},{12,8},{9,1... | collective-permute-start | bytes 294920 | tf_op jit(solution)/shard_map/ppermute | solution.py:25
  14.8 6.1 %collective-permute-start.5 = (f32[32,768]{1,0:T(8,128)S(1)}, f32[32,768]{1,0:T(8,128)S(1)}, u32[]{:S(2)}, u32[]{:S(2)}) collective-permute-start(f32[32,768]{1,0:T(8,128)S(1)} %add.59.refs_0_), channel_id=1, source_target_pairs={{0,1},{1,0},{2,3},{3,2},{4,5},{5,4},{6,7},{7,6},{8,9},{9,8},{10,11... | collective-permute-start | bytes 294920 | tf_op jit(solution)/shard_map/ppermute | solution.py:25
  15.6 6.1 %collective-permute-start.6 = (f32[32,768]{1,0:T(8,128)S(1)}, f32[32,768]{1,0:T(8,128)S(1)}, u32[]{:S(2)}, u32[]{:S(2)}) collective-permute-start(f32[32,768]{1,0:T(8,128)S(1)} %add.59.refs_0_), channel_id=1, source_target_pairs={{0,3},{1,2},{2,1},{3,0},{4,7},{5,6},{6,5},{7,4},{8,11},{9,10},{10,... | collective-permute-start | bytes 294920 | tf_op jit(solution)/shard_map/ppermute | solution.py:25
  17.5 5.9 %collective-permute-start.7 = (f32[32,768]{1,0:T(8,128)S(1)}, f32[32,768]{1,0:T(8,128)S(1)}, u32[]{:S(2)}, u32[]{:S(2)}) collective-permute-start(f32[32,768]{1,0:T(8,128)S(1)} %add.59.refs_0_), channel_id=1, source_target_pairs={{0,2},{1,3},{2,0},{3,1},{4,6},{5,7},{6,4},{7,5},{8,10},{9,11},{10,... | collective-permute-start | bytes 294920 | tf_op jit(solution)/shard_map/ppermute | solution.py:25
  18.2 10.9 %collective-permute-start.11 = (f32[32,768]{1,0:T(8,128)S(1)}, f32[32,768]{1,0:T(8,128)S(1)}, u32[]{:S(2)}, u32[]{:S(2)}) collective-permute-start(f32[32,768]{1,0:T(8,128)S(1)} %add.61.refs_0_), channel_id=1, source_target_pairs={{0,1},{1,0},{2,3},{3,2},{4,5},{5,4},{6,7},{7,6},{8,9},{9,8},{10,11... | collective-permute-start | bytes 294920 | tf_op jit(solution)/shard_map/ppermute | solution.py:25
  19.0 10.1 %collective-permute-start.12 = (f32[32,768]{1,0:T(8,128)S(1)}, f32[32,768]{1,0:T(8,128)S(1)}, u32[]{:S(2)}, u32[]{:S(2)}) collective-permute-start(f32[32,768]{1,0:T(8,128)S(1)} %add.61.refs_0_), channel_id=1, source_target_pairs={{0,3},{1,2},{2,1},{3,0},{4,7},{5,6},{6,5},{7,4},{8,11},{9,10},{10,... | collective-permute-start | bytes 294920 | tf_op jit(solution)/shard_map/ppermute | solution.py:25
  20.9 8.2 %collective-permute-start.13 = (f32[32,768]{1,0:T(8,128)S(1)}, f32[32,768]{1,0:T(8,128)S(1)}, u32[]{:S(2)}, u32[]{:S(2)}) collective-permute-start(f32[32,768]{1,0:T(8,128)S(1)} %add.61.refs_0_), channel_id=1, source_target_pairs={{0,2},{1,3},{2,0},{3,1},{4,6},{5,7},{6,4},{7,5},{8,10},{9,11},{10,... | collective-permute-start | bytes 294920 | tf_op jit(solution)/shard_map/ppermute | solution.py:25
  23.6 4.7 %collective-permute-start.8 = (f32[32,384]{1,0:T(8,128)S(1)}, f32[32,384]{1,0:T(8,128)S(1)}, u32[]{:S(2)}, u32[]{:S(2)}) collective-permute-start(f32[32,384]{1,0:T(8,128)S(1)} %next_solve.4), channel_id=1, source_target_pairs={{0,32},{32,0},{1,33},{33,1},{2,34},{34,2},{3,35},{35,3},{4,36},{36... | collective-permute-start | bytes 147464 | tf_op jit(solution)/shard_map/ppermute | solution.py:25
  28.3 3.0 %collective-permute-start.9 = (f32[32,384]{1,0:T(8,128)S(1)}, f32[32,384]{1,0:T(8,128)S(1)}, u32[]{:S(2)}, u32[]{:S(2)}) collective-permute-start(f32[32,384]{1,0:T(8,128)S(1)} %add.60.one_ref), channel_id=1, source_target_pairs={{0,64},{64,0},{1,65},{65,1},{2,66},{66,2},{3,67},{67,3},{4,68},{68... | collective-permute-start | bytes 147464 | tf_op jit(solution)/shard_map/ppermute | solution.py:25
  29.4 3.8 %collective-permute-start.14 = (f32[32,384]{1,0:T(8,128)S(1)}, f32[32,384]{1,0:T(8,128)S(1)}, u32[]{:S(2)}, u32[]{:S(2)}) collective-permute-start(f32[32,384]{1,0:T(8,128)S(1)} %next_solve.5), channel_id=1, source_target_pairs={{0,32},{32,0},{1,33},{33,1},{2,34},{34,2},{3,35},{35,3},{4,36},{36... | collective-permute-start | bytes 147464 | tf_op jit(solution)/shard_map/ppermute | solution.py:25
  31.5 5.2 %collective-permute-start.16 = (f32[32,768]{1,0:T(8,128)S(1)}, f32[32,768]{1,0:T(8,128)S(1)}, u32[]{:S(2)}, u32[]{:S(2)}) collective-permute-start(f32[32,768]{1,0:T(8,128)S(1)} %get-tuple-element.42), channel_id=1, source_target_pairs={{0,4},{4,0},{1,5},{5,1},{2,6},{6,2},{3,7},{7,3},{8,12},{12,8},{9,1... | collective-permute-start | bytes 294920 | tf_op jit(solution)/shard_map/ppermute | solution.py:25
  33.1 3.3 %collective-permute-start.15 = (f32[32,384]{1,0:T(8,128)S(1)}, f32[32,384]{1,0:T(8,128)S(1)}, u32[]{:S(2)}, u32[]{:S(2)}) collective-permute-start(f32[32,384]{1,0:T(8,128)S(1)} %add.62.one_ref), channel_id=1, source_target_pairs={{0,64},{64,0},{1,65},{65,1},{2,66},{66,2},{3,67},{67,3},{4,68},{68... | collective-permute-start | bytes 147464 | tf_op jit(solution)/shard_map/ppermute | solution.py:25
  36.7 3.6 %collective-permute-start.22 = (f32[32,768]{1,0:T(8,128)S(1)}, f32[32,768]{1,0:T(8,128)S(1)}, u32[]{:S(2)}, u32[]{:S(2)}) collective-permute-start(f32[32,768]{1,0:T(8,128)S(1)} %get-tuple-element.45), channel_id=1, source_target_pairs={{0,4},{4,0},{1,5},{5,1},{2,6},{6,2},{3,7},{7,3},{8,12},{12,8},{9,1... | collective-permute-start | bytes 294920 | tf_op jit(solution)/shard_map/ppermute | solution.py:25
  36.8 5.0 %collective-permute-start.17 = (f32[32,768]{1,0:T(8,128)S(1)}, f32[32,768]{1,0:T(8,128)S(1)}, u32[]{:S(2)}, u32[]{:S(2)}) collective-permute-start(f32[32,768]{1,0:T(8,128)S(1)} %add.63.refs_0_), channel_id=1, source_target_pairs={{0,1},{1,0},{2,3},{3,2},{4,5},{5,4},{6,7},{7,6},{8,9},{9,8},{10,11... | collective-permute-start | bytes 294920 | tf_op jit(solution)/shard_map/ppermute | solution.py:25
  37.2 6.4 %collective-permute-start.18 = (f32[32,768]{1,0:T(8,128)S(1)}, f32[32,768]{1,0:T(8,128)S(1)}, u32[]{:S(2)}, u32[]{:S(2)}) collective-permute-start(f32[32,768]{1,0:T(8,128)S(1)} %add.63.refs_0_), channel_id=1, source_target_pairs={{0,3},{1,2},{2,1},{3,0},{4,7},{5,6},{6,5},{7,4},{8,11},{9,10},{10,... | collective-permute-start | bytes 294920 | tf_op jit(solution)/shard_map/ppermute | solution.py:25
  38.4 5.2 %collective-permute-start.19 = (f32[32,768]{1,0:T(8,128)S(1)}, f32[32,768]{1,0:T(8,128)S(1)}, u32[]{:S(2)}, u32[]{:S(2)}) collective-permute-start(f32[32,768]{1,0:T(8,128)S(1)} %add.63.refs_0_), channel_id=1, source_target_pairs={{0,2},{1,3},{2,0},{3,1},{4,6},{5,7},{6,4},{7,5},{8,10},{9,11},{10,... | collective-permute-start | bytes 294920 | tf_op jit(solution)/shard_map/ppermute | solution.py:25
  40.2 9.2 %collective-permute-start.23 = (f32[32,768]{1,0:T(8,128)S(1)}, f32[32,768]{1,0:T(8,128)S(1)}, u32[]{:S(2)}, u32[]{:S(2)}) collective-permute-start(f32[32,768]{1,0:T(8,128)S(1)} %add.65.refs_0_), channel_id=1, source_target_pairs={{0,1},{1,0},{2,3},{3,2},{4,5},{5,4},{6,7},{7,6},{8,9},{9,8},{10,11... | collective-permute-start | bytes 294920 | tf_op jit(solution)/shard_map/ppermute | solution.py:25
  40.6 8.8 %collective-permute-start.24 = (f32[32,768]{1,0:T(8,128)S(1)}, f32[32,768]{1,0:T(8,128)S(1)}, u32[]{:S(2)}, u32[]{:S(2)}) collective-permute-start(f32[32,768]{1,0:T(8,128)S(1)} %add.65.refs_0_), channel_id=1, source_target_pairs={{0,3},{1,2},{2,1},{3,0},{4,7},{5,6},{6,5},{7,4},{8,11},{9,10},{10,... | collective-permute-start | bytes 294920 | tf_op jit(solution)/shard_map/ppermute | solution.py:25
  41.9 7.6 %collective-permute-start.25 = (f32[32,768]{1,0:T(8,128)S(1)}, f32[32,768]{1,0:T(8,128)S(1)}, u32[]{:S(2)}, u32[]{:S(2)}) collective-permute-start(f32[32,768]{1,0:T(8,128)S(1)} %add.65.refs_0_), channel_id=1, source_target_pairs={{0,2},{1,3},{2,0},{3,1},{4,6},{5,7},{6,4},{7,5},{8,10},{9,11},{10,... | collective-permute-start | bytes 294920 | tf_op jit(solution)/shard_map/ppermute | solution.py:25
  43.6 11.5 %copy-start.3 = (s32[3,3,24]{2,1,0:T(4,128)S(1)}, s32[3,3,24]{2,1,0:T(4,128)}, u32[]{:S(2)}) copy-start(s32[3,3,24]{2,1,0:T(4,128)} %param.15) | copy-start | bytes 2596
  43.6 11.5 %copy-start.2 = (bf16[3,384,768]{2,1,0:T(8,128)(2,1)S(1)}, bf16[3,384,768]{2,1,0:T(8,128)(2,1)}, u32[]{:S(2)}) copy-start(bf16[3,384,768]{2,1,0:T(8,128)(2,1)} %factor_ref.1) | copy-start | bytes 5308420
  43.8 9.6 %collective-permute-start.20 = (f32[32,384]{1,0:T(8,128)S(1)}, f32[32,384]{1,0:T(8,128)S(1)}, u32[]{:S(2)}, u32[]{:S(2)}) collective-permute-start(f32[32,384]{1,0:T(8,128)S(1)} %next_solve.6), channel_id=1, source_target_pairs={{0,32},{32,0},{1,33},{33,1},{2,34},{34,2},{3,35},{35,3},{4,36},{36... | collective-permute-start | bytes 147464 | tf_op jit(solution)/shard_map/ppermute | solution.py:25
  49.6 5.0 %collective-permute-start.26 = (f32[32,384]{1,0:T(8,128)S(1)}, f32[32,384]{1,0:T(8,128)S(1)}, u32[]{:S(2)}, u32[]{:S(2)}) collective-permute-start(f32[32,384]{1,0:T(8,128)S(1)} %next_solve.7), channel_id=1, source_target_pairs={{0,32},{32,0},{1,33},{33,1},{2,34},{34,2},{3,35},{35,3},{4,36},{36... | collective-permute-start | bytes 147464 | tf_op jit(solution)/shard_map/ppermute | solution.py:25
  53.4 3.4 %collective-permute-start.21 = (f32[32,384]{1,0:T(8,128)S(1)}, f32[32,384]{1,0:T(8,128)S(1)}, u32[]{:S(2)}, u32[]{:S(2)}) collective-permute-start(f32[32,384]{1,0:T(8,128)S(1)} %add.64.one_ref), channel_id=1, source_target_pairs={{0,64},{64,0},{1,65},{65,1},{2,66},{66,2},{3,67},{67,3},{4,68},{68... | collective-permute-start | bytes 147464 | tf_op jit(solution)/shard_map/ppermute | solution.py:25
  54.7 3.0 %collective-permute-start.27 = (f32[32,384]{1,0:T(8,128)S(1)}, f32[32,384]{1,0:T(8,128)S(1)}, u32[]{:S(2)}, u32[]{:S(2)}) collective-permute-start(f32[32,384]{1,0:T(8,128)S(1)} %add.66.one_ref), channel_id=1, source_target_pairs={{0,64},{64,0},{1,65},{65,1},{2,66},{66,2},{3,67},{67,3},{4,68},{68... | collective-permute-start | bytes 147464 | tf_op jit(solution)/shard_map/ppermute | solution.py:25
  57.1 22.9 %copy-start.1 = (bf16[768,1536]{1,0:T(8,128)(2,1)S(1)}, bf16[768,1536]{1,0:T(8,128)(2,1)}, u32[]{:S(2)}) copy-start(bf16[768,1536]{1,0:T(8,128)(2,1)} %inverse_ref.1) | copy-start | bytes 7077892
  67.9 6.6 %collective-permute-start.28 = (f32[8,768]{1,0:T(8,128)S(1)}, f32[8,768]{1,0:T(8,128)S(1)}, u32[]{:S(2)}, u32[]{:S(2)}) collective-permute-start(f32[8,768]{1,0:T(8,128)S(1)} %reduce_sum.9.own_ref), channel_id=1, source_target_pairs={{0,128},{8,136},{16,144},{24,152},{128,0},{136,8},{144,16},{152,24... | collective-permute-start | bytes 73736 | tf_op jit(solution)/shard_map/ppermute | solution.py:25
  70.7 4.5 %collective-permute-start.29 = (f32[8,768]{1,0:T(8,128)S(1)}, f32[8,768]{1,0:T(8,128)S(1)}, u32[]{:S(2)}, u32[]{:S(2)}) collective-permute-start(f32[8,768]{1,0:T(8,128)S(1)} %reduce_sum.9.own_ref), channel_id=1, source_target_pairs={{0,8},{8,0},{16,24},{24,16},{128,136},{136,128},{144,152},{152,144... | collective-permute-start | bytes 73736 | tf_op jit(solution)/shard_map/ppermute | solution.py:25
  73.7 6.2 %collective-permute-start.30 = (f32[8,768]{1,0:T(8,128)S(1)}, f32[8,768]{1,0:T(8,128)S(1)}, u32[]{:S(2)}, u32[]{:S(2)}) collective-permute-start(f32[8,768]{1,0:T(8,128)S(1)} %reduce_sum.9.own_ref), channel_id=1, source_target_pairs={{0,136},{8,128},{16,152},{24,144},{128,8},{136,0},{144,24},{152,16... | collective-permute-start | bytes 73736 | tf_op jit(solution)/shard_map/ppermute | solution.py:25
  80.3 4.9 %collective-permute-start.31 = (f32[8,1536]{1,0:T(8,128)S(1)}, f32[8,1536]{1,0:T(8,128)S(1)}, u32[]{:S(2)}, u32[]{:S(2)}) collective-permute-start(f32[8,1536]{1,0:T(8,128)S(1)} %root_part.1), channel_id=1, source_target_pairs={{0,32},{32,0},{1,33},{33,1},{2,34},{34,2},{3,35},{35,3},{4,36},{36... | collective-permute-start | bytes 147464 | tf_op jit(solution)/shard_map/ppermute | solution.py:25
  85.3 6.1 %collective-permute-start.33 = (f32[8,1536]{1,0:T(8,128)S(1)}, f32[8,1536]{1,0:T(8,128)S(1)}, u32[]{:S(2)}, u32[]{:S(2)}) collective-permute-start(f32[8,1536]{1,0:T(8,128)S(1)} %add.69), channel_id=1, source_target_pairs={{0,24},{8,16},{16,8},{24,0},{64,88},{72,80},{80,72},{88,64},{1,25}... | collective-permute-start | bytes 147464 | tf_op jit(solution)/shard_map/ppermute | solution.py:25
  88.0 6.0 %collective-permute-start.34 = (f32[8,1536]{1,0:T(8,128)S(1)}, f32[8,1536]{1,0:T(8,128)S(1)}, u32[]{:S(2)}, u32[]{:S(2)}) collective-permute-start(f32[8,1536]{1,0:T(8,128)S(1)} %add.69), channel_id=1, source_target_pairs={{0,88},{8,80},{16,72},{24,64},{64,24},{72,16},{80,8},{88,0},{1,89}... | collective-permute-start | bytes 147464 | tf_op jit(solution)/shard_map/ppermute | solution.py:25
  88.6 5.4 %collective-permute-start.32 = (f32[8,1536]{1,0:T(8,128)S(1)}, f32[8,1536]{1,0:T(8,128)S(1)}, u32[]{:S(2)}, u32[]{:S(2)}) collective-permute-start(f32[8,1536]{1,0:T(8,128)S(1)} %add.69), channel_id=1, source_target_pairs={{0,64},{8,72},{16,80},{24,88},{64,0},{72,8},{80,16},{88,24},{1,65}... | collective-permute-start | bytes 147464 | tf_op jit(solution)/shard_map/ppermute | solution.py:25

commit v6 on v4

--- a/solution.py
+++ b/solution.py
@@ -247,15 +247,30 @@
     return call(body, [(shape, F32)], (*kept, factor), name="early_update")[0]
 
 
-def root_part(rhs_rows, update_parts, root_inverse):
-    def body(rhs_ref, one_ref, other_ref, inverse_ref, out_ref):
-        residual = rhs_ref[...] - (one_ref[...] + other_ref[...])
-        out_ref[...] = product(residual.astype(BF16), inverse_ref[...])
+def root_part(rhs_rows, update, root_inverse):
+    def body(rhs_ref, update_ref, inverse_ref, out_ref):
+        residual = (rhs_ref[...] - update_ref[...]).astype(BF16)
+        out_ref[...] = product(residual, inverse_ref[...])
 
     shape = (rhs_rows.shape[0], root_inverse.shape[1])
-    return call(
-        body, [(shape, F32)], (rhs_rows, *update_parts, root_inverse), name="root_part"
-    )[0]
+    return call(body, [(shape, F32)], (rhs_rows, update, root_inverse), name="root_part")[0]
+
+
+def to_core1(shard):
+    return lax.ppermute(shard, "core", [(0, 1)])
+
+
+def to_core0(shard):
+    return lax.ppermute(shard, "core", [(1, 0)])
+
+
+def among_core1(shard, axis, bit=1):
+    count, cores = lax.axis_size(axis), lax.axis_size("core")
+    if axis in ("grid", "xl"):
+        axes, where = (axis, "core"), lambda i: i * cores + 1
+    else:
+        axes, where = ("core", axis), lambda i: count + i
+    return lax.ppermute(shard, axes, [(where(i), where(i ^ bit)) for i in range(count)])
 
 
 def prow_halves(partial_sum):
@@ -301,17 +316,17 @@
     own_rows = lax.all_to_all(
         root_local.reshape(owners, few, out_cols), OWN, 0, 0, tiled=True
     ).sum(axis=0)
-    sub_solution, *arrived = lax.optimization_barrier(
-        (
-            stacked(list(zip(*solved))),
-            *[partner(own_rows, TREES, bit) for bit in (4, 1, 5)],
-        )
-    )
-    total = own_rows + arrived[0] + (arrived[1] + arrived[2])
+    both = jnp.concatenate([own_rows, to_core1(own_rows)])
+    sub_solution, across = lax.optimization_barrier(
+        (stacked(list(zip(*solved))), among_core1(both, "grid"))
+    )
+    total = both + across
+    total = total + among_core1(total, "zt", 1)
+    total = total + among_core1(total, "zt", 3)
+    root_update = jnp.where(lax.axis_index("core") == 1, total[:few], to_core0(total[few:]))
     rhs_rows = lax.dynamic_slice_in_dim(root_rhs, lax.axis_index(OWN) * few, few, 0)
-    part = root_part(rhs_rows, (total, partner(total, "zt", 3)), root_inverse)
-    pair, other = prow_halves(part)
-    root_solution = to_everyone(pair + other, OWN).reshape(rhs_count, part.shape[1])
+    pair, other = prow_halves(root_part(rhs_rows, root_update, root_inverse))
+    root_solution = to_everyone(pair + other, OWN).reshape(rhs_count, pair.shape[1])
     return (sub_solution, root_solution)
 
 

time: 104 us -> 111 us (1.067)
  starting transfers between devices: 53.2 us -> 57.8 us
    ppermute x0 -> x5, starting transfers between devices: none -> 18 us  [the longest x3 15.4 us: among_core1(): lax.ppermute(shard, axes, [(where(i), where(i ^ bit)) for i in range(coun...]
    ppermute x34 -> x30, starting transfers between devices: 53.2 us -> 39.8 us  [partner(): lax.ppermute(shard, axis, [(i, i ^ bit) for i in range(lax.axis_size(axis...]
    ppermute x0 -> x5, waiting for transfers between devices: none -> 8.49 us  [the longest x3 4.4 us: among_core1(): lax.ppermute(shard, axes, [(where(i), where(i ^ bit)) for i in range(coun...]
    ppermute x34 -> x30, waiting for transfers between devices: 20.4 us -> 12.5 us  [partner(): lax.ppermute(shard, axis, [(i, i ^ bit) for i in range(lax.axis_size(axis...]
  transfers between devices with their start and end apart: 34 -> 35, of which waited for: 14 -> 16; matrix products, arithmetic and copies ran while one was open for 0% -> 0% of each run, Pallas kernels for 7% -> 6%
where the time goes in v6:
time: 111 us; the launch traced here: 110 us
  starting transfers between devices  57.8 us (52%)
  waiting for transfers between devices  21 us (19%)
  blocking collectives  19.8 us (18%)
  Pallas kernels  9.22 us (8%)
    ppermute x30, starting transfers between devices, partner(): lax.ppermute(shard, axis, [(i, i ^ bit) for i in range(lax.axis_size(axis...  39.8 us
    ppermute x3, starting transfers between devices, among_core1(): lax.ppermute(shard, axes, [(where(i), where(i ^ bit)) for i in range(coun...  15.4 us
    ppermute x30, waiting for transfers between devices, partner(): lax.ppermute(shard, axis, [(i, i ^ bit) for i in range(lax.axis_size(axis...  12.5 us
    all_to_all x1, blocking collectives, to_everyone(): lax.all_to_all(jnp.broadcast_to(shard[None], (count, *shard.shape)), axis...  10.3 us
    all_to_all x1, blocking collectives, shards(): lax.all_to_all(root_local.reshape(owners, few, out_cols), OWN, 0, 0, tile...  9.56 us
    pallas_call x18, Pallas kernels, call(): pl.pallas_call(body, out_shape=[pltpu.VMEM(shape, kind) for shape, kind i...  8.46 us
    ppermute x3, waiting for transfers between devices, among_core1(): lax.ppermute(shard, axes, [(where(i), where(i ^ bit)) for i in range(coun...  4.4 us
    ppermute x1, waiting for transfers between devices, to_core1(): return lax.ppermute(shard, 'core', [(0, 1)])  3.29 us
  transfers between devices with their start and end apart: 35, of which 16 were waited for; matrix products, arithmetic and copies ran while one was open for 0% of the time, Pallas kernels for 6%

profile of v6, /device:TPU:1, one launch (start us, length us, event | category | flops | bytes accessed | tf_op | source)
XLA Modules:
  0.0 110.0 jit_solution(15423581664247657760)
XLA Ops:
  0.7 1.6 %first_solve.1 = (f32[32,384]{1,0:T(8,128)S(1)}, f32[32,384]{1,0:T(8,128)S(1)}) custom-call(s32[1]{0:T(128)} %bitcast.tree_ref, f32[4,3,64,768]{3,2,1,0:T(8,128)} %rhs_hbm.3, bf16[3,768,384]{2,1,0:T(8,128)(2,1)} %inverse_hbm.3), custom_call_target="tpu_custom_call" | custom-call | tf_op jit(solution)/shard_map/first_solve/pallas_call | solution.py:41
  2.3 3.3 %collective-permute-start = (f32[32,384]{1,0:T(8,128)S(1)}, f32[32,384]{1,0:T(8,128)S(1)}, u32[]{:S(2)}, u32[]{:S(2)}) collective-permute-start(f32[32,384]{1,0:T(8,128)S(1)} %get-tuple-element.25), channel_id=1, source_target_pairs={{0,32},{32,0},{1,33},{33,1},{2,34},{34,2},{3,35},{35,3},{4,36},{36... | collective-permute-start | bytes 147464 | tf_op jit(solution)/shard_map/ppermute | solution.py:25
  5.7 0.8 collective-permute-done
  6.6 2.6 %stage.1 = (bf16[3,384,768]{2,1,0:T(8,128)(2,1)S(1)}, bf16[2,768,384]{2,1,0:T(8,128)(2,1)S(1)}, f32[2,64,768]{2,1,0:T(8,128)S(1)}) custom-call(s32[1]{0:T(128)} %bitcast.tree_ref, s32[3,3,6]{2,1,0:T(4,128)S(1)} %constant_dynamic-slice_fusion.2.mask_ref, f32[4,3,64,768]{3,2,1,0:T(8,128)} %rhs_hbm.3, bf16[3,768,384]{2,1,0:T(8,128)(2,1)} %inverse_hbm.3, ...), custom_call_target="tpu_custom_call" | custom-call | tf_op jit(solution)/shard_map/stage/pallas_call | solution.py:41
  9.2 0.3 collective-permute-done.1.other_ref
  9.7 0.9 collective-permute-start.4
  10.6 0.5 collective-permute-start.3
  11.0 2.6 %collective-permute-done.3.other_ref = f32[32,384]{1,0:T(8,128)S(1)} collective-permute-done((f32[32,384]{1,0:T(8,128)S(1)}, f32[32,384]{1,0:T(8,128)S(1)}, u32[]{:S(2)}, u32[]{:S(2)}) %collective-permute-start.3) | collective-permute-done | bytes 49184 | tf_op jit(solution)/shard_map/ppermute | solution.py:25
  13.8 1.0 collective-permute-start.10
  14.8 0.8 collective-permute-start.5
  15.6 1.9 %collective-permute-start.6 = (f32[32,768]{1,0:T(8,128)S(1)}, f32[32,768]{1,0:T(8,128)S(1)}, u32[]{:S(2)}, u32[]{:S(2)}) collective-permute-start(f32[32,768]{1,0:T(8,128)S(1)} %add.62.refs_0_), channel_id=1, source_target_pairs={{0,3},{1,2},{2,1},{3,0},{4,7},{5,6},{6,5},{7,4},{8,11},{9,10},{10,... | collective-permute-start | bytes 294920 | tf_op jit(solution)/shard_map/ppermute | solution.py:25
  17.5 0.7 collective-permute-start.7
  18.3 0.8 collective-permute-start.11
  19.1 1.9 %collective-permute-start.12 = (f32[32,768]{1,0:T(8,128)S(1)}, f32[32,768]{1,0:T(8,128)S(1)}, u32[]{:S(2)}, u32[]{:S(2)}) collective-permute-start(f32[32,768]{1,0:T(8,128)S(1)} %add.64.refs_0_), channel_id=1, source_target_pairs={{0,3},{1,2},{2,1},{3,0},{4,7},{5,6},{6,5},{7,4},{8,11},{9,10},{10,... | collective-permute-start | bytes 294920 | tf_op jit(solution)/shard_map/ppermute | solution.py:25
  21.0 0.7 collective-permute-start.13
  21.7 1.8 %collective-permute-done.7.refs_3_ = f32[32,768]{1,0:T(8,128)S(1)} collective-permute-done((f32[32,768]{1,0:T(8,128)S(1)}, f32[32,768]{1,0:T(8,128)S(1)}, u32[]{:S(2)}, u32[]{:S(2)}) %collective-permute-start.7) | collective-permute-done | bytes 98336 | tf_op jit(solution)/shard_map/ppermute | solution.py:25
  23.6 3.9 %collective-permute-start.8 = (f32[32,384]{1,0:T(8,128)S(1)}, f32[32,384]{1,0:T(8,128)S(1)}, u32[]{:S(2)}, u32[]{:S(2)}) collective-permute-start(f32[32,384]{1,0:T(8,128)S(1)} %next_solve.4), channel_id=1, source_target_pairs={{0,32},{32,0},{1,33},{33,1},{2,34},{34,2},{3,35},{35,3},{4,36},{36... | collective-permute-start | bytes 147464 | tf_op jit(solution)/shard_map/ppermute | solution.py:25
  27.5 0.9 collective-permute-done.8
  28.4 0.8 collective-permute-start.9
  29.2 0.2 next_solve.5
  29.4 1.5 %collective-permute-start.14 = (f32[32,384]{1,0:T(8,128)S(1)}, f32[32,384]{1,0:T(8,128)S(1)}, u32[]{:S(2)}, u32[]{:S(2)}) collective-permute-start(f32[32,384]{1,0:T(8,128)S(1)} %next_solve.5), channel_id=1, source_target_pairs={{0,32},{32,0},{1,33},{33,1},{2,34},{34,2},{3,35},{35,3},{4,36},{36... | collective-permute-start | bytes 147464 | tf_op jit(solution)/shard_map/ppermute | solution.py:25
  31.1 0.3 collective-permute-done.9.other_ref
  31.4 0.2 kept_update.8
  31.6 1.6 %collective-permute-start.16 = (f32[32,768]{1,0:T(8,128)S(1)}, f32[32,768]{1,0:T(8,128)S(1)}, u32[]{:S(2)}, u32[]{:S(2)}) collective-permute-start(f32[32,768]{1,0:T(8,128)S(1)} %get-tuple-element.38), channel_id=1, source_target_pairs={{0,4},{4,0},{1,5},{5,1},{2,6},{6,2},{3,7},{7,3},{8,12},{12,8},{9,1... | collective-permute-start | bytes 294920 | tf_op jit(solution)/shard_map/ppermute | solution.py:25
  33.2 0.8 collective-permute-start.15
  34.2 2.3 %collective-permute-done.15.other_ref = f32[32,384]{1,0:T(8,128)S(1)} collective-permute-done((f32[32,384]{1,0:T(8,128)S(1)}, f32[32,384]{1,0:T(8,128)S(1)}, u32[]{:S(2)}, u32[]{:S(2)}) %collective-permute-start.15) | collective-permute-done | bytes 49184 | tf_op jit(solution)/shard_map/ppermute | solution.py:25
  36.5 0.2 kept_update.9
  36.8 0.4 collective-permute-start.17
  37.3 1.2 %collective-permute-start.18 = (f32[32,768]{1,0:T(8,128)S(1)}, f32[32,768]{1,0:T(8,128)S(1)}, u32[]{:S(2)}, u32[]{:S(2)}) collective-permute-start(f32[32,768]{1,0:T(8,128)S(1)} %add.66.refs_0_), channel_id=1, source_target_pairs={{0,3},{1,2},{2,1},{3,0},{4,7},{5,6},{6,5},{7,4},{8,11},{9,10},{10,... | collective-permute-start | bytes 294920 | tf_op jit(solution)/shard_map/ppermute | solution.py:25
  38.4 1.7 %collective-permute-start.19 = (f32[32,768]{1,0:T(8,128)S(1)}, f32[32,768]{1,0:T(8,128)S(1)}, u32[]{:S(2)}, u32[]{:S(2)}) collective-permute-start(f32[32,768]{1,0:T(8,128)S(1)} %add.66.refs_0_), channel_id=1, source_target_pairs={{0,2},{1,3},{2,0},{3,1},{4,6},{5,7},{6,4},{7,5},{8,10},{9,11},{10,... | collective-permute-start | bytes 294920 | tf_op jit(solution)/shard_map/ppermute | solution.py:25
  40.3 0.4 collective-permute-start.23
  40.7 1.2 %collective-permute-start.24 = (f32[32,768]{1,0:T(8,128)S(1)}, f32[32,768]{1,0:T(8,128)S(1)}, u32[]{:S(2)}, u32[]{:S(2)}) collective-permute-start(f32[32,768]{1,0:T(8,128)S(1)} %add.68.refs_0_), channel_id=1, source_target_pairs={{0,3},{1,2},{2,1},{3,0},{4,7},{5,6},{6,5},{7,4},{8,11},{9,10},{10,... | collective-permute-start | bytes 294920 | tf_op jit(solution)/shard_map/ppermute | solution.py:25
  41.9 1.7 %collective-permute-start.25 = (f32[32,768]{1,0:T(8,128)S(1)}, f32[32,768]{1,0:T(8,128)S(1)}, u32[]{:S(2)}, u32[]{:S(2)}) collective-permute-start(f32[32,768]{1,0:T(8,128)S(1)} %add.68.refs_0_), channel_id=1, source_target_pairs={{0,2},{1,3},{2,0},{3,1},{4,6},{5,7},{6,4},{7,5},{8,10},{9,11},{10,... | collective-permute-start | bytes 294920 | tf_op jit(solution)/shard_map/ppermute | solution.py:25
  43.7 0.2 next_solve.6
  43.9 5.6 %collective-permute-start.20 = (f32[32,384]{1,0:T(8,128)S(1)}, f32[32,384]{1,0:T(8,128)S(1)}, u32[]{:S(2)}, u32[]{:S(2)}) collective-permute-start(f32[32,384]{1,0:T(8,128)S(1)} %next_solve.6), channel_id=1, source_target_pairs={{0,32},{32,0},{1,33},{33,1},{2,34},{34,2},{3,35},{35,3},{4,36},{36... | collective-permute-start | bytes 147464 | tf_op jit(solution)/shard_map/ppermute | solution.py:25
  49.5 0.2 next_solve.7
  49.7 3.0 %collective-permute-start.26 = (f32[32,384]{1,0:T(8,128)S(1)}, f32[32,384]{1,0:T(8,128)S(1)}, u32[]{:S(2)}, u32[]{:S(2)}) collective-permute-start(f32[32,384]{1,0:T(8,128)S(1)} %next_solve.7), channel_id=1, source_target_pairs={{0,32},{32,0},{1,33},{33,1},{2,34},{34,2},{3,35},{35,3},{4,36},{36... | collective-permute-start | bytes 147464 | tf_op jit(solution)/shard_map/ppermute | solution.py:25
  52.7 1.3 %collective-permute-start.21 = (f32[32,384]{1,0:T(8,128)S(1)}, f32[32,384]{1,0:T(8,128)S(1)}, u32[]{:S(2)}, u32[]{:S(2)}) collective-permute-start(f32[32,384]{1,0:T(8,128)S(1)} %add.67.one_ref), channel_id=1, source_target_pairs={{0,64},{64,0},{1,65},{65,1},{2,66},{66,2},{3,67},{67,3},{4,68},{68... | collective-permute-start | bytes 147464 | tf_op jit(solution)/shard_map/ppermute | solution.py:25
  54.0 0.8 collective-permute-start.27
  54.9 0.9 masked.1.refs_2_.factor_ref
  55.9 0.3 early_update.6.refs_0_
  56.2 0.3 early_update.7.refs_0_
  56.5 0.2 kept_update.10
  56.7 0.3 collective-permute-done.27.other_ref
  57.0 0.2 kept_update.11
  57.3 9.6 %all_to_all.10 = f32[8,8,768]{2,1,0:T(8,128)S(1)} all-to-all(f32[8,8,768]{2,1,0:T(8,128)S(1)} %maximum_bitcast_fusion), channel_id=1, replica_groups=mesh['grid'=2,'xl'=2,'core'=2,'zt'=4,'zl'=2,'y'=4] {'zl','y'}, dimensions={0} | all-to-all | bytes 393216 | tf_op jit(solution)/shard_map/all_to_all | solution.py:316
  66.9 1.3 %collective-permute-start.28 = (f32[8,768]{1,0:T(8,128)S(1)}, f32[8,768]{1,0:T(8,128)S(1)}, u32[]{:S(2)}, u32[]{:S(2)}) collective-permute-start(f32[8,768]{1,0:T(8,128)S(1)} %reduce_sum.9), channel_id=1, source_target_pairs={{0,32},{1,33},{2,34},{3,35},{4,36},{5,37},{6,38},{7,39},{8,40},{9,... | collective-permute-start | bytes 73736 | tf_op jit(solution)/shard_map/ppermute | solution.py:260
  68.2 3.3 %collective-permute-done.28 = f32[8,768]{1,0:T(8,128)S(1)} collective-permute-done((f32[8,768]{1,0:T(8,128)S(1)}, f32[8,768]{1,0:T(8,128)S(1)}, u32[]{:S(2)}, u32[]{:S(2)}) %collective-permute-start.28) | collective-permute-done | bytes 24608 | tf_op jit(solution)/shard_map/ppermute | solution.py:260
  71.5 4.7 %collective-permute-start.29 = (f32[16,768]{1,0:T(8,128)S(1)}, f32[16,768]{1,0:T(8,128)S(1)}, u32[]{:S(2)}, u32[]{:S(2)}) collective-permute-start(f32[16,768]{1,0:T(8,128)S(1)} %pad_maximum_fusion), channel_id=1, source_target_pairs={{32,160},{160,32},{33,161},{161,33},{34,162},{162,34},{35,163},{16... | collective-permute-start | bytes 147464 | tf_op jit(solution)/shard_map/ppermute | solution.py:273
  76.1 0.8 stacked.1
  76.9 0.9 collective-permute-done.29
  77.8 4.9 %collective-permute-start.30 = (f32[16,768]{1,0:T(8,128)S(1)}, f32[16,768]{1,0:T(8,128)S(1)}, u32[]{:S(2)}, u32[]{:S(2)}) collective-permute-start(f32[16,768]{1,0:T(8,128)S(1)} %fusion), channel_id=1, source_target_pairs={{32,40},{40,32},{48,56},{56,48},{33,41},{41,33},{49,57},{57,49},{3... | collective-permute-start | bytes 147464 | tf_op jit(solution)/shard_map/ppermute | solution.py:273
  82.7 2.0 %collective-permute-done.30 = f32[16,768]{1,0:T(8,128)S(1)} collective-permute-done((f32[16,768]{1,0:T(8,128)S(1)}, f32[16,768]{1,0:T(8,128)S(1)}, u32[]{:S(2)}, u32[]{:S(2)}) %collective-permute-start.30) | collective-permute-done | bytes 49184 | tf_op jit(solution)/shard_map/ppermute | solution.py:273
  84.7 5.9 %collective-permute-start.31 = (f32[16,768]{1,0:T(8,128)S(1)}, f32[16,768]{1,0:T(8,128)S(1)}, u32[]{:S(2)}, u32[]{:S(2)}) collective-permute-start(f32[16,768]{1,0:T(8,128)S(1)} %add.73), channel_id=1, source_target_pairs={{32,56},{40,48},{48,40},{56,32},{33,57},{41,49},{49,41},{57,33},{3... | collective-permute-start | bytes 147464 | tf_op jit(solution)/shard_map/ppermute | solution.py:273
  90.6 1.5 %collective-permute-done.31 = f32[16,768]{1,0:T(8,128)S(1)} collective-permute-done((f32[16,768]{1,0:T(8,128)S(1)}, f32[16,768]{1,0:T(8,128)S(1)}, u32[]{:S(2)}, u32[]{:S(2)}) %collective-permute-start.31) | collective-permute-done | bytes 49184 | tf_op jit(solution)/shard_map/ppermute | solution.py:273
  92.1 1.3 %collective-permute-start.32 = (f32[8,768]{1,0:T(8,128)S(1)}, f32[8,768]{1,0:T(8,128)S(1)}, u32[]{:S(2)}, u32[]{:S(2)}) collective-permute-start(f32[8,768]{1,0:T(8,128)S(1)} %slice.9), channel_id=1, source_target_pairs={{32,0},{33,1},{34,2},{35,3},{36,4},{37,5},{38,6},{39,7},{40,8},{41... | collective-permute-start | bytes 73736 | tf_op jit(solution)/shard_map/ppermute | solution.py:264
  93.4 0.8 collective-permute-done.32
  94.2 0.4 root_part.1
  94.6 0.4 collective-permute-start.33
  95.0 0.9 collective-permute-done.33
  95.9 0.7 collective-permute-start.34
  96.6 2.3 %collective-permute-done.34 = f32[8,1536]{1,0:T(8,128)S(1)} collective-permute-done((f32[8,1536]{1,0:T(8,128)S(1)}, f32[8,1536]{1,0:T(8,128)S(1)}, u32[]{:S(2)}, u32[]{:S(2)}) %collective-permute-start.34) | collective-permute-done | bytes 49184 | tf_op jit(solution)/shard_map/ppermute | solution.py:25
  99.0 10.3 %all_to_all.11 = f32[8,8,1536]{2,1,0:T(8,128)S(1)} all-to-all(f32[8,8,1536]{2,1,0:T(8,128)S(1)} %broadcast_in_dim.2), channel_id=1, replica_groups=mesh['grid'=2,'xl'=2,'core'=2,'zt'=4,'zl'=2,'y'=4] {'zl','y'}, dimensions={0} | all-to-all | bytes 786432 | tf_op jit(solution)/shard_map/all_to_all | solution.py:30
  109.2 0.7 copy.11
  (62 shorter events, 1.7 us)
Async XLA Ops:
  0.6 92.8 %copy-start = (f32[64,768]{1,0:T(8,128)S(1)}, f32[64,768]{1,0:T(8,128)}, u32[]{:S(2)}) copy-start(f32[64,768]{1,0:T(8,128)} %param.9) | copy-start | bytes 589828
  0.7 5.9 %copy-start.3 = (s32[3,3,24]{2,1,0:T(4,128)S(1)}, s32[3,3,24]{2,1,0:T(4,128)}, u32[]{:S(2)}) copy-start(s32[3,3,24]{2,1,0:T(4,128)} %param.13) | copy-start | bytes 2596
  2.3 4.2 %collective-permute-start = (f32[32,384]{1,0:T(8,128)S(1)}, f32[32,384]{1,0:T(8,128)S(1)}, u32[]{:S(2)}, u32[]{:S(2)}) collective-permute-start(f32[32,384]{1,0:T(8,128)S(1)} %get-tuple-element.25), channel_id=1, source_target_pairs={{0,32},{32,0},{1,33},{33,1},{2,34},{34,2},{3,35},{35,3},{4,36},{36... | collective-permute-start | bytes 147464 | tf_op jit(solution)/shard_map/ppermute | solution.py:25
  5.6 5.0 %collective-permute-start.2 = (f32[32,384]{1,0:T(8,128)S(1)}, f32[32,384]{1,0:T(8,128)S(1)}, u32[]{:S(2)}, u32[]{:S(2)}) collective-permute-start(f32[32,384]{1,0:T(8,128)S(1)} %get-tuple-element.28), channel_id=1, source_target_pairs={{0,32},{32,0},{1,33},{33,1},{2,34},{34,2},{3,35},{35,3},{4,36},{36... | collective-permute-start | bytes 147464 | tf_op jit(solution)/shard_map/ppermute | solution.py:25
  6.5 3.0 %collective-permute-start.1 = (f32[32,384]{1,0:T(8,128)S(1)}, f32[32,384]{1,0:T(8,128)S(1)}, u32[]{:S(2)}, u32[]{:S(2)}) collective-permute-start(f32[32,384]{1,0:T(8,128)S(1)} %add.58.one_ref), channel_id=1, source_target_pairs={{0,64},{64,0},{1,65},{65,1},{2,66},{66,2},{3,67},{67,3},{4,68},{68... | collective-permute-start | bytes 147464 | tf_op jit(solution)/shard_map/ppermute | solution.py:25
  9.7 5.2 %collective-permute-start.4 = (f32[32,768]{1,0:T(8,128)S(1)}, f32[32,768]{1,0:T(8,128)S(1)}, u32[]{:S(2)}, u32[]{:S(2)}) collective-permute-start(f32[32,768]{1,0:T(8,128)S(1)} %get-tuple-element.31), channel_id=1, source_target_pairs={{0,4},{4,0},{1,5},{5,1},{2,6},{6,2},{3,7},{7,3},{8,12},{12,8},{9,1... | collective-permute-start | bytes 294920 | tf_op jit(solution)/shard_map/ppermute | solution.py:25
  10.6 3.0 %collective-permute-start.3 = (f32[32,384]{1,0:T(8,128)S(1)}, f32[32,384]{1,0:T(8,128)S(1)}, u32[]{:S(2)}, u32[]{:S(2)}) collective-permute-start(f32[32,384]{1,0:T(8,128)S(1)} %add.61.one_ref), channel_id=1, source_target_pairs={{0,64},{64,0},{1,65},{65,1},{2,66},{66,2},{3,67},{67,3},{4,68},{68... | collective-permute-start | bytes 147464 | tf_op jit(solution)/shard_map/ppermute | solution.py:25
  13.8 4.4 %collective-permute-start.10 = (f32[32,768]{1,0:T(8,128)S(1)}, f32[32,768]{1,0:T(8,128)S(1)}, u32[]{:S(2)}, u32[]{:S(2)}) collective-permute-start(f32[32,768]{1,0:T(8,128)S(1)} %get-tuple-element.35), channel_id=1, source_target_pairs={{0,4},{4,0},{1,5},{5,1},{2,6},{6,2},{3,7},{7,3},{8,12},{12,8},{9,1... | collective-permute-start | bytes 294920 | tf_op jit(solution)/shard_map/ppermute | solution.py:25
  14.8 6.1 %collective-permute-start.5 = (f32[32,768]{1,0:T(8,128)S(1)}, f32[32,768]{1,0:T(8,128)S(1)}, u32[]{:S(2)}, u32[]{:S(2)}) collective-permute-start(f32[32,768]{1,0:T(8,128)S(1)} %add.62.refs_0_), channel_id=1, source_target_pairs={{0,1},{1,0},{2,3},{3,2},{4,5},{5,4},{6,7},{7,6},{8,9},{9,8},{10,11... | collective-permute-start | bytes 294920 | tf_op jit(solution)/shard_map/ppermute | solution.py:25
  15.6 6.1 %collective-permute-start.6 = (f32[32,768]{1,0:T(8,128)S(1)}, f32[32,768]{1,0:T(8,128)S(1)}, u32[]{:S(2)}, u32[]{:S(2)}) collective-permute-start(f32[32,768]{1,0:T(8,128)S(1)} %add.62.refs_0_), channel_id=1, source_target_pairs={{0,3},{1,2},{2,1},{3,0},{4,7},{5,6},{6,5},{7,4},{8,11},{9,10},{10,... | collective-permute-start | bytes 294920 | tf_op jit(solution)/shard_map/ppermute | solution.py:25
  17.5 5.9 %collective-permute-start.7 = (f32[32,768]{1,0:T(8,128)S(1)}, f32[32,768]{1,0:T(8,128)S(1)}, u32[]{:S(2)}, u32[]{:S(2)}) collective-permute-start(f32[32,768]{1,0:T(8,128)S(1)} %add.62.refs_0_), channel_id=1, source_target_pairs={{0,2},{1,3},{2,0},{3,1},{4,6},{5,7},{6,4},{7,5},{8,10},{9,11},{10,... | collective-permute-start | bytes 294920 | tf_op jit(solution)/shard_map/ppermute | solution.py:25
  18.3 10.9 %collective-permute-start.11 = (f32[32,768]{1,0:T(8,128)S(1)}, f32[32,768]{1,0:T(8,128)S(1)}, u32[]{:S(2)}, u32[]{:S(2)}) collective-permute-start(f32[32,768]{1,0:T(8,128)S(1)} %add.64.refs_0_), channel_id=1, source_target_pairs={{0,1},{1,0},{2,3},{3,2},{4,5},{5,4},{6,7},{7,6},{8,9},{9,8},{10,11... | collective-permute-start | bytes 294920 | tf_op jit(solution)/shard_map/ppermute | solution.py:25
  19.1 10.1 %collective-permute-start.12 = (f32[32,768]{1,0:T(8,128)S(1)}, f32[32,768]{1,0:T(8,128)S(1)}, u32[]{:S(2)}, u32[]{:S(2)}) collective-permute-start(f32[32,768]{1,0:T(8,128)S(1)} %add.64.refs_0_), channel_id=1, source_target_pairs={{0,3},{1,2},{2,1},{3,0},{4,7},{5,6},{6,5},{7,4},{8,11},{9,10},{10,... | collective-permute-start | bytes 294920 | tf_op jit(solution)/shard_map/ppermute | solution.py:25
  21.0 8.2 %collective-permute-start.13 = (f32[32,768]{1,0:T(8,128)S(1)}, f32[32,768]{1,0:T(8,128)S(1)}, u32[]{:S(2)}, u32[]{:S(2)}) collective-permute-start(f32[32,768]{1,0:T(8,128)S(1)} %add.64.refs_0_), channel_id=1, source_target_pairs={{0,2},{1,3},{2,0},{3,1},{4,6},{5,7},{6,4},{7,5},{8,10},{9,11},{10,... | collective-permute-start | bytes 294920 | tf_op jit(solution)/shard_map/ppermute | solution.py:25
  23.6 4.7 %collective-permute-start.8 = (f32[32,384]{1,0:T(8,128)S(1)}, f32[32,384]{1,0:T(8,128)S(1)}, u32[]{:S(2)}, u32[]{:S(2)}) collective-permute-start(f32[32,384]{1,0:T(8,128)S(1)} %next_solve.4), channel_id=1, source_target_pairs={{0,32},{32,0},{1,33},{33,1},{2,34},{34,2},{3,35},{35,3},{4,36},{36... | collective-permute-start | bytes 147464 | tf_op jit(solution)/shard_map/ppermute | solution.py:25
  28.4 3.0 %collective-permute-start.9 = (f32[32,384]{1,0:T(8,128)S(1)}, f32[32,384]{1,0:T(8,128)S(1)}, u32[]{:S(2)}, u32[]{:S(2)}) collective-permute-start(f32[32,384]{1,0:T(8,128)S(1)} %add.63.one_ref), channel_id=1, source_target_pairs={{0,64},{64,0},{1,65},{65,1},{2,66},{66,2},{3,67},{67,3},{4,68},{68... | collective-permute-start | bytes 147464 | tf_op jit(solution)/shard_map/ppermute | solution.py:25
  29.4 3.8 %collective-permute-start.14 = (f32[32,384]{1,0:T(8,128)S(1)}, f32[32,384]{1,0:T(8,128)S(1)}, u32[]{:S(2)}, u32[]{:S(2)}) collective-permute-start(f32[32,384]{1,0:T(8,128)S(1)} %next_solve.5), channel_id=1, source_target_pairs={{0,32},{32,0},{1,33},{33,1},{2,34},{34,2},{3,35},{35,3},{4,36},{36... | collective-permute-start | bytes 147464 | tf_op jit(solution)/shard_map/ppermute | solution.py:25
  31.6 5.2 %collective-permute-start.16 = (f32[32,768]{1,0:T(8,128)S(1)}, f32[32,768]{1,0:T(8,128)S(1)}, u32[]{:S(2)}, u32[]{:S(2)}) collective-permute-start(f32[32,768]{1,0:T(8,128)S(1)} %get-tuple-element.38), channel_id=1, source_target_pairs={{0,4},{4,0},{1,5},{5,1},{2,6},{6,2},{3,7},{7,3},{8,12},{12,8},{9,1... | collective-permute-start | bytes 294920 | tf_op jit(solution)/shard_map/ppermute | solution.py:25
  33.2 3.3 %collective-permute-start.15 = (f32[32,384]{1,0:T(8,128)S(1)}, f32[32,384]{1,0:T(8,128)S(1)}, u32[]{:S(2)}, u32[]{:S(2)}) collective-permute-start(f32[32,384]{1,0:T(8,128)S(1)} %add.65.one_ref), channel_id=1, source_target_pairs={{0,64},{64,0},{1,65},{65,1},{2,66},{66,2},{3,67},{67,3},{4,68},{68... | collective-permute-start | bytes 147464 | tf_op jit(solution)/shard_map/ppermute | solution.py:25
  36.7 3.6 %collective-permute-start.22 = (f32[32,768]{1,0:T(8,128)S(1)}, f32[32,768]{1,0:T(8,128)S(1)}, u32[]{:S(2)}, u32[]{:S(2)}) collective-permute-start(f32[32,768]{1,0:T(8,128)S(1)} %get-tuple-element.41), channel_id=1, source_target_pairs={{0,4},{4,0},{1,5},{5,1},{2,6},{6,2},{3,7},{7,3},{8,12},{12,8},{9,1... | collective-permute-start | bytes 294920 | tf_op jit(solution)/shard_map/ppermute | solution.py:25
  36.8 5.1 %collective-permute-start.17 = (f32[32,768]{1,0:T(8,128)S(1)}, f32[32,768]{1,0:T(8,128)S(1)}, u32[]{:S(2)}, u32[]{:S(2)}) collective-permute-start(f32[32,768]{1,0:T(8,128)S(1)} %add.66.refs_0_), channel_id=1, source_target_pairs={{0,1},{1,0},{2,3},{3,2},{4,5},{5,4},{6,7},{7,6},{8,9},{9,8},{10,11... | collective-permute-start | bytes 294920 | tf_op jit(solution)/shard_map/ppermute | solution.py:25
  37.3 6.4 %collective-permute-start.18 = (f32[32,768]{1,0:T(8,128)S(1)}, f32[32,768]{1,0:T(8,128)S(1)}, u32[]{:S(2)}, u32[]{:S(2)}) collective-permute-start(f32[32,768]{1,0:T(8,128)S(1)} %add.66.refs_0_), channel_id=1, source_target_pairs={{0,3},{1,2},{2,1},{3,0},{4,7},{5,6},{6,5},{7,4},{8,11},{9,10},{10,... | collective-permute-start | bytes 294920 | tf_op jit(solution)/shard_map/ppermute | solution.py:25
  38.4 5.2 %collective-permute-start.19 = (f32[32,768]{1,0:T(8,128)S(1)}, f32[32,768]{1,0:T(8,128)S(1)}, u32[]{:S(2)}, u32[]{:S(2)}) collective-permute-start(f32[32,768]{1,0:T(8,128)S(1)} %add.66.refs_0_), channel_id=1, source_target_pairs={{0,2},{1,3},{2,0},{3,1},{4,6},{5,7},{6,4},{7,5},{8,10},{9,11},{10,... | collective-permute-start | bytes 294920 | tf_op jit(solution)/shard_map/ppermute | solution.py:25
  40.3 14.6 %copy-start.4 = (s32[3,3,24]{2,1,0:T(4,128)S(1)}, s32[3,3,24]{2,1,0:T(4,128)}, u32[]{:S(2)}) copy-start(s32[3,3,24]{2,1,0:T(4,128)} %param.15) | copy-start | bytes 2596
  40.3 14.6 %copy-start.2 = (bf16[3,384,768]{2,1,0:T(8,128)(2,1)S(1)}, bf16[3,384,768]{2,1,0:T(8,128)(2,1)}, u32[]{:S(2)}) copy-start(bf16[3,384,768]{2,1,0:T(8,128)(2,1)} %factor_ref.1) | copy-start | bytes 5308420
  40.3 9.2 %collective-permute-start.23 = (f32[32,768]{1,0:T(8,128)S(1)}, f32[32,768]{1,0:T(8,128)S(1)}, u32[]{:S(2)}, u32[]{:S(2)}) collective-permute-start(f32[32,768]{1,0:T(8,128)S(1)} %add.68.refs_0_), channel_id=1, source_target_pairs={{0,1},{1,0},{2,3},{3,2},{4,5},{5,4},{6,7},{7,6},{8,9},{9,8},{10,11... | collective-permute-start | bytes 294920 | tf_op jit(solution)/shard_map/ppermute | solution.py:25
  40.7 8.8 %collective-permute-start.24 = (f32[32,768]{1,0:T(8,128)S(1)}, f32[32,768]{1,0:T(8,128)S(1)}, u32[]{:S(2)}, u32[]{:S(2)}) collective-permute-start(f32[32,768]{1,0:T(8,128)S(1)} %add.68.refs_0_), channel_id=1, source_target_pairs={{0,3},{1,2},{2,1},{3,0},{4,7},{5,6},{6,5},{7,4},{8,11},{9,10},{10,... | collective-permute-start | bytes 294920 | tf_op jit(solution)/shard_map/ppermute | solution.py:25
  41.9 7.6 %collective-permute-start.25 = (f32[32,768]{1,0:T(8,128)S(1)}, f32[32,768]{1,0:T(8,128)S(1)}, u32[]{:S(2)}, u32[]{:S(2)}) collective-permute-start(f32[32,768]{1,0:T(8,128)S(1)} %add.68.refs_0_), channel_id=1, source_target_pairs={{0,2},{1,3},{2,0},{3,1},{4,6},{5,7},{6,4},{7,5},{8,10},{9,11},{10,... | collective-permute-start | bytes 294920 | tf_op jit(solution)/shard_map/ppermute | solution.py:25
  43.9 8.9 %collective-permute-start.20 = (f32[32,384]{1,0:T(8,128)S(1)}, f32[32,384]{1,0:T(8,128)S(1)}, u32[]{:S(2)}, u32[]{:S(2)}) collective-permute-start(f32[32,384]{1,0:T(8,128)S(1)} %next_solve.6), channel_id=1, source_target_pairs={{0,32},{32,0},{1,33},{33,1},{2,34},{34,2},{3,35},{35,3},{4,36},{36... | collective-permute-start | bytes 147464 | tf_op jit(solution)/shard_map/ppermute | solution.py:25
  49.7 4.3 %collective-permute-start.26 = (f32[32,384]{1,0:T(8,128)S(1)}, f32[32,384]{1,0:T(8,128)S(1)}, u32[]{:S(2)}, u32[]{:S(2)}) collective-permute-start(f32[32,384]{1,0:T(8,128)S(1)} %next_solve.7), channel_id=1, source_target_pairs={{0,32},{32,0},{1,33},{33,1},{2,34},{34,2},{3,35},{35,3},{4,36},{36... | collective-permute-start | bytes 147464 | tf_op jit(solution)/shard_map/ppermute | solution.py:25
  52.7 3.8 %collective-permute-start.21 = (f32[32,384]{1,0:T(8,128)S(1)}, f32[32,384]{1,0:T(8,128)S(1)}, u32[]{:S(2)}, u32[]{:S(2)}) collective-permute-start(f32[32,384]{1,0:T(8,128)S(1)} %add.67.one_ref), channel_id=1, source_target_pairs={{0,64},{64,0},{1,65},{65,1},{2,66},{66,2},{3,67},{67,3},{4,68},{68... | collective-permute-start | bytes 147464 | tf_op jit(solution)/shard_map/ppermute | solution.py:25
  54.0 3.0 %collective-permute-start.27 = (f32[32,384]{1,0:T(8,128)S(1)}, f32[32,384]{1,0:T(8,128)S(1)}, u32[]{:S(2)}, u32[]{:S(2)}) collective-permute-start(f32[32,384]{1,0:T(8,128)S(1)} %add.69.one_ref), channel_id=1, source_target_pairs={{0,64},{64,0},{1,65},{65,1},{2,66},{66,2},{3,67},{67,3},{4,68},{68... | collective-permute-start | bytes 147464 | tf_op jit(solution)/shard_map/ppermute | solution.py:25
  56.7 37.5 %copy-start.1 = (bf16[768,1536]{1,0:T(8,128)(2,1)S(1)}, bf16[768,1536]{1,0:T(8,128)(2,1)}, u32[]{:S(2)}) copy-start(bf16[768,1536]{1,0:T(8,128)(2,1)} %inverse_ref.1) | copy-start | bytes 7077892
  66.9 4.6 %collective-permute-start.28 = (f32[8,768]{1,0:T(8,128)S(1)}, f32[8,768]{1,0:T(8,128)S(1)}, u32[]{:S(2)}, u32[]{:S(2)}) collective-permute-start(f32[8,768]{1,0:T(8,128)S(1)} %reduce_sum.9), channel_id=1, source_target_pairs={{0,32},{1,33},{2,34},{3,35},{4,36},{5,37},{6,38},{7,39},{8,40},{9,... | collective-permute-start | bytes 73736 | tf_op jit(solution)/shard_map/ppermute | solution.py:260
  71.5 6.3 %collective-permute-start.29 = (f32[16,768]{1,0:T(8,128)S(1)}, f32[16,768]{1,0:T(8,128)S(1)}, u32[]{:S(2)}, u32[]{:S(2)}) collective-permute-start(f32[16,768]{1,0:T(8,128)S(1)} %pad_maximum_fusion), channel_id=1, source_target_pairs={{32,160},{160,32},{33,161},{161,33},{34,162},{162,34},{35,163},{16... | collective-permute-start | bytes 147464 | tf_op jit(solution)/shard_map/ppermute | solution.py:273
  77.8 6.9 %collective-permute-start.30 = (f32[16,768]{1,0:T(8,128)S(1)}, f32[16,768]{1,0:T(8,128)S(1)}, u32[]{:S(2)}, u32[]{:S(2)}) collective-permute-start(f32[16,768]{1,0:T(8,128)S(1)} %fusion), channel_id=1, source_target_pairs={{32,40},{40,32},{48,56},{56,48},{33,41},{41,33},{49,57},{57,49},{3... | collective-permute-start | bytes 147464 | tf_op jit(solution)/shard_map/ppermute | solution.py:273
  84.7 7.4 %collective-permute-start.31 = (f32[16,768]{1,0:T(8,128)S(1)}, f32[16,768]{1,0:T(8,128)S(1)}, u32[]{:S(2)}, u32[]{:S(2)}) collective-permute-start(f32[16,768]{1,0:T(8,128)S(1)} %add.73), channel_id=1, source_target_pairs={{32,56},{40,48},{48,40},{56,32},{33,57},{41,49},{49,41},{57,33},{3... | collective-permute-start | bytes 147464 | tf_op jit(solution)/shard_map/ppermute | solution.py:273
  92.1 2.1 %collective-permute-start.32 = (f32[8,768]{1,0:T(8,128)S(1)}, f32[8,768]{1,0:T(8,128)S(1)}, u32[]{:S(2)}, u32[]{:S(2)}) collective-permute-start(f32[8,768]{1,0:T(8,128)S(1)} %slice.9), channel_id=1, source_target_pairs={{32,0},{33,1},{34,2},{35,3},{36,4},{37,5},{38,6},{39,7},{40,8},{41... | collective-permute-start | bytes 73736 | tf_op jit(solution)/shard_map/ppermute | solution.py:264
  94.6 1.2 %collective-permute-start.33 = (f32[8,1536]{1,0:T(8,128)S(1)}, f32[8,1536]{1,0:T(8,128)S(1)}, u32[]{:S(2)}, u32[]{:S(2)}) collective-permute-start(f32[8,1536]{1,0:T(8,128)S(1)} %root_part.1), channel_id=1, source_target_pairs={{0,32},{32,0},{1,33},{33,1},{2,34},{34,2},{3,35},{35,3},{4,36},{36... | collective-permute-start | bytes 147464 | tf_op jit(solution)/shard_map/ppermute | solution.py:25
  95.9 3.0 %collective-permute-start.34 = (f32[8,1536]{1,0:T(8,128)S(1)}, f32[8,1536]{1,0:T(8,128)S(1)}, u32[]{:S(2)}, u32[]{:S(2)}) collective-permute-start(f32[8,1536]{1,0:T(8,128)S(1)} %add.75), channel_id=1, source_target_pairs={{0,64},{64,0},{1,65},{65,1},{2,66},{66,2},{3,67},{67,3},{4,68},{68... | collective-permute-start | bytes 147464 | tf_op jit(solution)/shard_map/ppermute | solution.py:25

commit v7 on v4

--- a/solution.py
+++ b/solution.py
@@ -10,7 +10,7 @@
 TILE = 128
 PARTS = 2
 PROW = ("xl", "core")
-OWN = ("zl", "y")
+OWN = "own"
 TREES = ("grid", "zt")
 SCOPED_BYTES = 4 << 20
 F32 = jnp.float32
@@ -25,11 +25,14 @@
     return lax.ppermute(shard, axis, [(i, i ^ bit) for i in range(lax.axis_size(axis))])
 
 
-def to_everyone(shard, axis):
-    count = lax.axis_size(axis)
-    return lax.all_to_all(
-        jnp.broadcast_to(shard[None], (count, *shard.shape)), axis, 0, 0, tiled=True
-    )
+def swap_blocks(blocks):
+    order = list(range(lax.axis_size(OWN)))[::-1]
+    return lax.all_to_all(blocks, OWN, 0, 0, axis_index_groups=[order], tiled=True)
+
+
+def to_everyone(shard):
+    count = lax.axis_size(OWN)
+    return swap_blocks(jnp.broadcast_to(shard[None], (count, *shard.shape)))
 
 
 def call(body, outs, args, specs=None, scratch=(), name=None):
@@ -264,8 +267,8 @@
 
 
 def owner_sums(partial_sum):
-    pair = partial_sum + partner(partial_sum, "zl")
-    return [pair] + [partner(pair, "y", bit) for bit in (1, 3, 2)]
+    pair = partial_sum + partner(partial_sum, OWN, 4)
+    return [pair] + [partner(pair, OWN, bit) for bit in (2, 3, 1)]
 
 
 def shards(
@@ -298,9 +301,8 @@
 
     owners = lax.axis_size(OWN)
     few = rhs_count // owners
-    own_rows = lax.all_to_all(
-        root_local.reshape(owners, few, out_cols), OWN, 0, 0, tiled=True
-    ).sum(axis=0)
+    place = owners - 1 - lax.axis_index(OWN)
+    own_rows = swap_blocks(root_local.reshape(owners, few, out_cols)).sum(axis=0)
     sub_solution, *arrived = lax.optimization_barrier(
         (
             stacked(list(zip(*solved))),
@@ -308,24 +310,24 @@
         )
     )
     total = own_rows + arrived[0] + (arrived[1] + arrived[2])
-    rhs_rows = lax.dynamic_slice_in_dim(root_rhs, lax.axis_index(OWN) * few, few, 0)
+    rhs_rows = lax.dynamic_slice_in_dim(root_rhs, place * few, few, 0)
     part = root_part(rhs_rows, (total, partner(total, "zt", 3)), root_inverse)
     pair, other = prow_halves(part)
-    root_solution = to_everyone(pair + other, OWN).reshape(rhs_count, part.shape[1])
+    root_solution = to_everyone(pair + other).reshape(rhs_count, part.shape[1])
     return (sub_solution, root_solution)
 
 
 def solution(mesh):
     prow, pcol = mesh.shape["prow"], mesh.shape["pcol"]
-    cores, y = 2, 4
+    cores = 2
     trees = 8 // mesh.shape["grid"]
     fine = Mesh(
         mesh.devices.reshape(
-            mesh.shape["grid"], prow // cores, cores, trees, pcol // (trees * y), y
+            mesh.shape["grid"], prow // cores, cores, trees, pcol // trees
         ),
-        ("grid", "xl", "core", "zt", "zl", "y"),
-    )
-    columns = ("grid", "zt", "zl", "y")
+        ("grid", "xl", "core", "zt", "own"),
+    )
+    columns = ("grid", "zt", "own")
     return jax.shard_map(
         shards,
         mesh=fine,

time: 104 us -> 103 us (level)
  waiting for transfers between devices: 20.4 us -> 17.5 us
  starting transfers between devices: 53.2 us -> 55 us
    ppermute x34, waiting for transfers between devices: 20.4 us -> 17.5 us  [partner(): lax.ppermute(shard, axis, [(i, i ^ bit) for i in range(lax.axis_size(axis...]
    ppermute x34, starting transfers between devices: 53.2 us -> 55 us  [partner(): lax.ppermute(shard, axis, [(i, i ^ bit) for i in range(lax.axis_size(axis...]
  transfers between devices with their start and end apart: 34 -> 34, of which waited for: 14 -> 13; matrix products, arithmetic and copies ran while one was open for 0% -> 0% of each run, Pallas kernels for 7% -> 7%
where the time goes in v7:
time: 103 us; the launch traced here: 102 us
  starting transfers between devices  55 us (53%)
  blocking collectives  18.6 us (18%)
  waiting for transfers between devices  17.5 us (17%)
  Pallas kernels  9.21 us (9%)
    ppermute x34, starting transfers between devices, partner(): lax.ppermute(shard, axis, [(i, i ^ bit) for i in range(lax.axis_size(axis...  55 us
    all_to_all x2, blocking collectives, swap_blocks(): lax.all_to_all(blocks, OWN, 0, 0, axis_index_groups=[order], tiled=True)  18.6 us
    ppermute x34, waiting for transfers between devices, partner(): lax.ppermute(shard, axis, [(i, i ^ bit) for i in range(lax.axis_size(axis...  17.5 us
    pallas_call x18, Pallas kernels, call(): pl.pallas_call(body, out_shape=[pltpu.VMEM(shape, kind) for shape, kind i...  8.46 us
  transfers between devices with their start and end apart: 34, of which 13 were waited for; matrix products, arithmetic and copies ran while one was open for 0% of the time, Pallas kernels for 7%

profile of v7, /device:TPU:1, one launch (start us, length us, event | category | flops | bytes accessed | tf_op | source)
XLA Modules:
  0.0 102.3 jit_solution(13229208014618132296)
XLA Ops:
  0.7 1.6 %first_solve.1 = (f32[32,384]{1,0:T(8,128)S(1)}, f32[32,384]{1,0:T(8,128)S(1)}) custom-call(s32[1]{0:T(128)} %bitcast.tree_ref, f32[4,3,64,768]{3,2,1,0:T(8,128)} %rhs_hbm.3, bf16[3,768,384]{2,1,0:T(8,128)(2,1)} %inverse_hbm.3), custom_call_target="tpu_custom_call" | custom-call | tf_op jit(solution)/shard_map/first_solve/pallas_call | solution.py:44
  2.3 3.3 %collective-permute-start = (f32[32,384]{1,0:T(8,128)S(1)}, f32[32,384]{1,0:T(8,128)S(1)}, u32[]{:S(2)}, u32[]{:S(2)}) collective-permute-start(f32[32,384]{1,0:T(8,128)S(1)} %get-tuple-element.27), channel_id=1, source_target_pairs={{0,32},{32,0},{1,33},{33,1},{2,34},{34,2},{3,35},{35,3},{4,36},{36... | collective-permute-start | bytes 147464 | tf_op jit(solution)/shard_map/ppermute | solution.py:25
  5.7 0.8 collective-permute-done
  6.6 2.6 %stage.1 = (bf16[3,384,768]{2,1,0:T(8,128)(2,1)S(1)}, bf16[2,768,384]{2,1,0:T(8,128)(2,1)S(1)}, f32[2,64,768]{2,1,0:T(8,128)S(1)}) custom-call(s32[1]{0:T(128)} %bitcast.tree_ref, s32[3,3,6]{2,1,0:T(4,128)S(1)} %constant_dynamic-slice_fusion.2.mask_ref, f32[4,3,64,768]{3,2,1,0:T(8,128)} %rhs_hbm.3, bf16[3,768,384]{2,1,0:T(8,128)(2,1)} %inverse_hbm.3, ...), custom_call_target="tpu_custom_call" | custom-call | tf_op jit(solution)/shard_map/stage/pallas_call | solution.py:44
  9.2 0.3 collective-permute-done.1.other_ref
  9.5 0.2 kept_update.6
  9.7 0.9 collective-permute-start.4
  10.6 0.5 collective-permute-start.3
  11.0 2.6 %collective-permute-done.3.other_ref = f32[32,384]{1,0:T(8,128)S(1)} collective-permute-done((f32[32,384]{1,0:T(8,128)S(1)}, f32[32,384]{1,0:T(8,128)S(1)}, u32[]{:S(2)}, u32[]{:S(2)}) %collective-permute-start.3) | collective-permute-done | bytes 49184 | tf_op jit(solution)/shard_map/ppermute | solution.py:25
  13.6 0.2 kept_update.7
  13.8 1.0 collective-permute-start.10
  14.8 2.4 %collective-permute-start.5 = (f32[32,768]{1,0:T(8,128)S(1)}, f32[32,768]{1,0:T(8,128)S(1)}, u32[]{:S(2)}, u32[]{:S(2)}) collective-permute-start(f32[32,768]{1,0:T(8,128)S(1)} %add.59.refs_0_), channel_id=1, source_target_pairs={{0,2},{1,3},{2,0},{3,1},{4,6},{5,7},{6,4},{7,5},{8,10},{9,11},{10,... | collective-permute-start | bytes 294920 | tf_op jit(solution)/shard_map/ppermute | solution.py:25
  17.2 0.8 collective-permute-start.6
  18.0 3.2 %collective-permute-start.11 = (f32[32,768]{1,0:T(8,128)S(1)}, f32[32,768]{1,0:T(8,128)S(1)}, u32[]{:S(2)}, u32[]{:S(2)}) collective-permute-start(f32[32,768]{1,0:T(8,128)S(1)} %add.61.refs_0_), channel_id=1, source_target_pairs={{0,2},{1,3},{2,0},{3,1},{4,6},{5,7},{6,4},{7,5},{8,10},{9,11},{10,... | collective-permute-start | bytes 294920 | tf_op jit(solution)/shard_map/ppermute | solution.py:25
  21.2 0.8 collective-permute-start.12
  22.0 0.1 collective-permute-done.7.refs_3_
  22.1 0.2 next_solve.4
  22.3 5.7 %collective-permute-start.8 = (f32[32,384]{1,0:T(8,128)S(1)}, f32[32,384]{1,0:T(8,128)S(1)}, u32[]{:S(2)}, u32[]{:S(2)}) collective-permute-start(f32[32,384]{1,0:T(8,128)S(1)} %next_solve.4), channel_id=1, source_target_pairs={{0,32},{32,0},{1,33},{33,1},{2,34},{34,2},{3,35},{35,3},{4,36},{36... | collective-permute-start | bytes 147464 | tf_op jit(solution)/shard_map/ppermute | solution.py:25
  28.0 0.9 collective-permute-done.8
  28.8 0.6 collective-permute-start.9
  29.5 0.2 next_solve.5
  29.7 0.8 collective-permute-start.14
  30.4 0.2 early_update.4.refs_0_
  30.6 1.2 %collective-permute-done.9.other_ref = f32[32,384]{1,0:T(8,128)S(1)} collective-permute-done((f32[32,384]{1,0:T(8,128)S(1)}, f32[32,384]{1,0:T(8,128)S(1)}, u32[]{:S(2)}, u32[]{:S(2)}) %collective-permute-start.9) | collective-permute-done | bytes 49184 | tf_op jit(solution)/shard_map/ppermute | solution.py:25
  31.8 0.2 kept_update.8
  32.0 0.4 collective-permute-start.16
  32.5 1.4 %collective-permute-start.15 = (f32[32,384]{1,0:T(8,128)S(1)}, f32[32,384]{1,0:T(8,128)S(1)}, u32[]{:S(2)}, u32[]{:S(2)}) collective-permute-start(f32[32,384]{1,0:T(8,128)S(1)} %add.62.one_ref), channel_id=1, source_target_pairs={{0,64},{64,0},{1,65},{65,1},{2,66},{66,2},{3,67},{67,3},{4,68},{68... | collective-permute-start | bytes 147464 | tf_op jit(solution)/shard_map/ppermute | solution.py:25
  33.9 0.2 early_update.5.refs_0_
  34.1 1.4 %collective-permute-done.15.other_ref = f32[32,384]{1,0:T(8,128)S(1)} collective-permute-done((f32[32,384]{1,0:T(8,128)S(1)}, f32[32,384]{1,0:T(8,128)S(1)}, u32[]{:S(2)}, u32[]{:S(2)}) %collective-permute-start.15) | collective-permute-done | bytes 49184 | tf_op jit(solution)/shard_map/ppermute | solution.py:25
  35.5 0.2 kept_update.9
  35.7 1.5 %collective-permute-start.22 = (f32[32,768]{1,0:T(8,128)S(1)}, f32[32,768]{1,0:T(8,128)S(1)}, u32[]{:S(2)}, u32[]{:S(2)}) collective-permute-start(f32[32,768]{1,0:T(8,128)S(1)} %get-tuple-element.43), channel_id=1, source_target_pairs={{0,4},{1,5},{2,6},{3,7},{4,0},{5,1},{6,2},{7,3},{8,12},{9,13},{10,... | collective-permute-start | bytes 294920 | tf_op jit(solution)/shard_map/ppermute | solution.py:25
  37.2 1.3 %collective-permute-start.17 = (f32[32,768]{1,0:T(8,128)S(1)}, f32[32,768]{1,0:T(8,128)S(1)}, u32[]{:S(2)}, u32[]{:S(2)}) collective-permute-start(f32[32,768]{1,0:T(8,128)S(1)} %add.63.refs_0_), channel_id=1, source_target_pairs={{0,2},{1,3},{2,0},{3,1},{4,6},{5,7},{6,4},{7,5},{8,10},{9,11},{10,... | collective-permute-start | bytes 294920 | tf_op jit(solution)/shard_map/ppermute | solution.py:25
  38.5 0.8 collective-permute-start.18
  39.3 0.7 collective-permute-start.19
  40.0 2.5 %collective-permute-start.23 = (f32[32,768]{1,0:T(8,128)S(1)}, f32[32,768]{1,0:T(8,128)S(1)}, u32[]{:S(2)}, u32[]{:S(2)}) collective-permute-start(f32[32,768]{1,0:T(8,128)S(1)} %add.65.refs_0_), channel_id=1, source_target_pairs={{0,2},{1,3},{2,0},{3,1},{4,6},{5,7},{6,4},{7,5},{8,10},{9,11},{10,... | collective-permute-start | bytes 294920 | tf_op jit(solution)/shard_map/ppermute | solution.py:25
  42.5 0.8 collective-permute-start.24
  43.3 0.2 next_solve.6
  43.5 6.0 %collective-permute-start.20 = (f32[32,384]{1,0:T(8,128)S(1)}, f32[32,384]{1,0:T(8,128)S(1)}, u32[]{:S(2)}, u32[]{:S(2)}) collective-permute-start(f32[32,384]{1,0:T(8,128)S(1)} %next_solve.6), channel_id=1, source_target_pairs={{0,32},{32,0},{1,33},{33,1},{2,34},{34,2},{3,35},{35,3},{4,36},{36... | collective-permute-start | bytes 147464 | tf_op jit(solution)/shard_map/ppermute | solution.py:25
  49.5 0.2 next_solve.7
  49.7 2.8 %collective-permute-start.26 = (f32[32,384]{1,0:T(8,128)S(1)}, f32[32,384]{1,0:T(8,128)S(1)}, u32[]{:S(2)}, u32[]{:S(2)}) collective-permute-start(f32[32,384]{1,0:T(8,128)S(1)} %next_solve.7), channel_id=1, source_target_pairs={{0,32},{32,0},{1,33},{33,1},{2,34},{34,2},{3,35},{35,3},{4,36},{36... | collective-permute-start | bytes 147464 | tf_op jit(solution)/shard_map/ppermute | solution.py:25
  52.5 1.2 %collective-permute-start.21 = (f32[32,384]{1,0:T(8,128)S(1)}, f32[32,384]{1,0:T(8,128)S(1)}, u32[]{:S(2)}, u32[]{:S(2)}) collective-permute-start(f32[32,384]{1,0:T(8,128)S(1)} %add.64.one_ref), channel_id=1, source_target_pairs={{0,64},{64,0},{1,65},{65,1},{2,66},{66,2},{3,67},{67,3},{4,68},{68... | collective-permute-start | bytes 147464 | tf_op jit(solution)/shard_map/ppermute | solution.py:25
  53.8 0.8 collective-permute-start.27
  54.7 0.9 masked.1.refs_2_.factor_ref
  55.6 0.3 early_update.6.refs_0_
  55.9 0.3 early_update.7.refs_0_
  56.2 0.2 kept_update.10
  56.5 0.3 collective-permute-done.27.other_ref
  56.8 0.2 kept_update.11
  57.0 9.1 %all_to_all.10 = f32[8,8,768]{2,1,0:T(8,128)S(1)} all-to-all(f32[8,8,768]{2,1,0:T(8,128)S(1)} %maximum_bitcast_fusion), channel_id=1, replica_groups={{7,6,5,4,3,2,1,0},{15,14,13,12,11,10,9,8},{23,22,21,20,19,18,17,16},{31..., dimensions={0} | all-to-all | bytes 393216 | tf_op jit(solution)/shard_map/all_to_all | solution.py:30
  66.1 2.6 %collective-permute-start.28 = (f32[8,768]{1,0:T(8,128)S(1)}, f32[8,768]{1,0:T(8,128)S(1)}, u32[]{:S(2)}, u32[]{:S(2)}) collective-permute-start(f32[8,768]{1,0:T(8,128)S(1)} %reduce_sum.9), channel_id=1, source_target_pairs={{0,128},{8,136},{16,144},{24,152},{128,0},{136,8},{144,16},{152,24... | collective-permute-start | bytes 73736 | tf_op jit(solution)/shard_map/ppermute | solution.py:25
  68.7 3.0 %collective-permute-start.29 = (f32[8,768]{1,0:T(8,128)S(1)}, f32[8,768]{1,0:T(8,128)S(1)}, u32[]{:S(2)}, u32[]{:S(2)}) collective-permute-start(f32[8,768]{1,0:T(8,128)S(1)} %reduce_sum.9), channel_id=1, source_target_pairs={{0,8},{8,0},{16,24},{24,16},{128,136},{136,128},{144,152},{152,144... | collective-permute-start | bytes 73736 | tf_op jit(solution)/shard_map/ppermute | solution.py:25
  71.7 0.2 collective-permute-start.30
  71.9 0.8 stacked.1
  72.6 0.5 collective-permute-done.29
  73.2 4.5 %collective-permute-done.30 = f32[8,768]{1,0:T(8,128)S(1)} collective-permute-done((f32[8,768]{1,0:T(8,128)S(1)}, f32[8,768]{1,0:T(8,128)S(1)}, u32[]{:S(2)}, u32[]{:S(2)}) %collective-permute-start.30) | collective-permute-done | bytes 24608 | tf_op jit(solution)/shard_map/ppermute | solution.py:25
  77.6 3.7 %collective-permute-start.31 = (f32[8,768]{1,0:T(8,128)S(1)}, f32[8,768]{1,0:T(8,128)S(1)}, u32[]{:S(2)}, u32[]{:S(2)}) collective-permute-start(f32[8,768]{1,0:T(8,128)S(1)} %add_add_fusion.one_ref), channel_id=1, source_target_pairs={{0,24},{8,16},{16,8},{24,0},{1,25},{9,17},{17,9},{25,1},{2,26},{10... | collective-permute-start | bytes 73736 | tf_op jit(solution)/shard_map/ppermute | solution.py:25
  81.4 1.2 %collective-permute-done.31.other_ref = f32[8,768]{1,0:T(8,128)S(1)} collective-permute-done((f32[8,768]{1,0:T(8,128)S(1)}, f32[8,768]{1,0:T(8,128)S(1)}, u32[]{:S(2)}, u32[]{:S(2)}) %collective-permute-start.31) | collective-permute-done | bytes 24608 | tf_op jit(solution)/shard_map/ppermute | solution.py:25
  82.6 0.4 root_part.1
  83.0 5.2 %collective-permute-start.32 = (f32[8,1536]{1,0:T(8,128)S(1)}, f32[8,1536]{1,0:T(8,128)S(1)}, u32[]{:S(2)}, u32[]{:S(2)}) collective-permute-start(f32[8,1536]{1,0:T(8,128)S(1)} %root_part.1), channel_id=1, source_target_pairs={{0,32},{32,0},{1,33},{33,1},{2,34},{34,2},{3,35},{35,3},{4,36},{36... | collective-permute-start | bytes 147464 | tf_op jit(solution)/shard_map/ppermute | solution.py:25
  88.2 0.9 collective-permute-done.32
  89.1 0.2 collective-permute-start.33
  89.3 2.7 %collective-permute-done.33 = f32[8,1536]{1,0:T(8,128)S(1)} collective-permute-done((f32[8,1536]{1,0:T(8,128)S(1)}, f32[8,1536]{1,0:T(8,128)S(1)}, u32[]{:S(2)}, u32[]{:S(2)}) %collective-permute-start.33) | collective-permute-done | bytes 49184 | tf_op jit(solution)/shard_map/ppermute | solution.py:25
  92.1 9.5 %all_to_all.11 = f32[8,8,1536]{2,1,0:T(8,128)S(1)} all-to-all(f32[8,8,1536]{2,1,0:T(8,128)S(1)} %broadcast_in_dim.2), channel_id=1, replica_groups={{7,6,5,4,3,2,1,0},{15,14,13,12,11,10,9,8},{23,22,21,20,19,18,17,16},{31..., dimensions={0} | all-to-all | bytes 786432 | tf_op jit(solution)/shard_map/all_to_all | solution.py:30
  101.6 0.7 copy.11
  (55 shorter events, 0.6 us)
Async XLA Ops:
  0.6 80.7 %copy-start = (f32[64,768]{1,0:T(8,128)S(1)}, f32[64,768]{1,0:T(8,128)}, u32[]{:S(2)}) copy-start(f32[64,768]{1,0:T(8,128)} %param.9) | copy-start | bytes 589828
  0.7 5.9 %copy-start.3 = (s32[3,3,24]{2,1,0:T(4,128)S(1)}, s32[3,3,24]{2,1,0:T(4,128)}, u32[]{:S(2)}) copy-start(s32[3,3,24]{2,1,0:T(4,128)} %param.13) | copy-start | bytes 2596
  2.3 4.2 %collective-permute-start = (f32[32,384]{1,0:T(8,128)S(1)}, f32[32,384]{1,0:T(8,128)S(1)}, u32[]{:S(2)}, u32[]{:S(2)}) collective-permute-start(f32[32,384]{1,0:T(8,128)S(1)} %get-tuple-element.27), channel_id=1, source_target_pairs={{0,32},{32,0},{1,33},{33,1},{2,34},{34,2},{3,35},{35,3},{4,36},{36... | collective-permute-start | bytes 147464 | tf_op jit(solution)/shard_map/ppermute | solution.py:25
  5.6 5.0 %collective-permute-start.2 = (f32[32,384]{1,0:T(8,128)S(1)}, f32[32,384]{1,0:T(8,128)S(1)}, u32[]{:S(2)}, u32[]{:S(2)}) collective-permute-start(f32[32,384]{1,0:T(8,128)S(1)} %get-tuple-element.30), channel_id=1, source_target_pairs={{0,32},{32,0},{1,33},{33,1},{2,34},{34,2},{3,35},{35,3},{4,36},{36... | collective-permute-start | bytes 147464 | tf_op jit(solution)/shard_map/ppermute | solution.py:25
  6.5 3.0 %collective-permute-start.1 = (f32[32,384]{1,0:T(8,128)S(1)}, f32[32,384]{1,0:T(8,128)S(1)}, u32[]{:S(2)}, u32[]{:S(2)}) collective-permute-start(f32[32,384]{1,0:T(8,128)S(1)} %add.55.one_ref), channel_id=1, source_target_pairs={{0,64},{64,0},{1,65},{65,1},{2,66},{66,2},{3,67},{67,3},{4,68},{68... | collective-permute-start | bytes 147464 | tf_op jit(solution)/shard_map/ppermute | solution.py:25
  9.7 5.2 %collective-permute-start.4 = (f32[32,768]{1,0:T(8,128)S(1)}, f32[32,768]{1,0:T(8,128)S(1)}, u32[]{:S(2)}, u32[]{:S(2)}) collective-permute-start(f32[32,768]{1,0:T(8,128)S(1)} %get-tuple-element.33), channel_id=1, source_target_pairs={{0,4},{1,5},{2,6},{3,7},{4,0},{5,1},{6,2},{7,3},{8,12},{9,13},{10,... | collective-permute-start | bytes 294920 | tf_op jit(solution)/shard_map/ppermute | solution.py:25
  10.6 3.0 %collective-permute-start.3 = (f32[32,384]{1,0:T(8,128)S(1)}, f32[32,384]{1,0:T(8,128)S(1)}, u32[]{:S(2)}, u32[]{:S(2)}) collective-permute-start(f32[32,384]{1,0:T(8,128)S(1)} %add.58.one_ref), channel_id=1, source_target_pairs={{0,64},{64,0},{1,65},{65,1},{2,66},{66,2},{3,67},{67,3},{4,68},{68... | collective-permute-start | bytes 147464 | tf_op jit(solution)/shard_map/ppermute | solution.py:25
  13.8 4.2 %collective-permute-start.10 = (f32[32,768]{1,0:T(8,128)S(1)}, f32[32,768]{1,0:T(8,128)S(1)}, u32[]{:S(2)}, u32[]{:S(2)}) collective-permute-start(f32[32,768]{1,0:T(8,128)S(1)} %get-tuple-element.37), channel_id=1, source_target_pairs={{0,4},{1,5},{2,6},{3,7},{4,0},{5,1},{6,2},{7,3},{8,12},{9,13},{10,... | collective-permute-start | bytes 294920 | tf_op jit(solution)/shard_map/ppermute | solution.py:25
  14.8 7.1 %collective-permute-start.5 = (f32[32,768]{1,0:T(8,128)S(1)}, f32[32,768]{1,0:T(8,128)S(1)}, u32[]{:S(2)}, u32[]{:S(2)}) collective-permute-start(f32[32,768]{1,0:T(8,128)S(1)} %add.59.refs_0_), channel_id=1, source_target_pairs={{0,2},{1,3},{2,0},{3,1},{4,6},{5,7},{6,4},{7,5},{8,10},{9,11},{10,... | collective-permute-start | bytes 294920 | tf_op jit(solution)/shard_map/ppermute | solution.py:25
  17.2 4.8 %collective-permute-start.6 = (f32[32,768]{1,0:T(8,128)S(1)}, f32[32,768]{1,0:T(8,128)S(1)}, u32[]{:S(2)}, u32[]{:S(2)}) collective-permute-start(f32[32,768]{1,0:T(8,128)S(1)} %add.59.refs_0_), channel_id=1, source_target_pairs={{0,3},{1,2},{2,1},{3,0},{4,7},{5,6},{6,5},{7,4},{8,11},{9,10},{10,... | collective-permute-start | bytes 294920 | tf_op jit(solution)/shard_map/ppermute | solution.py:25
  18.0 4.1 %collective-permute-start.7 = (f32[32,768]{1,0:T(8,128)S(1)}, f32[32,768]{1,0:T(8,128)S(1)}, u32[]{:S(2)}, u32[]{:S(2)}) collective-permute-start(f32[32,768]{1,0:T(8,128)S(1)} %add.59.refs_0_), channel_id=1, source_target_pairs={{0,1},{1,0},{2,3},{3,2},{4,5},{5,4},{6,7},{7,6},{8,9},{9,8},{10,11... | collective-permute-start | bytes 294920 | tf_op jit(solution)/shard_map/ppermute | solution.py:25
  18.0 11.4 %collective-permute-start.11 = (f32[32,768]{1,0:T(8,128)S(1)}, f32[32,768]{1,0:T(8,128)S(1)}, u32[]{:S(2)}, u32[]{:S(2)}) collective-permute-start(f32[32,768]{1,0:T(8,128)S(1)} %add.61.refs_0_), channel_id=1, source_target_pairs={{0,2},{1,3},{2,0},{3,1},{4,6},{5,7},{6,4},{7,5},{8,10},{9,11},{10,... | collective-permute-start | bytes 294920 | tf_op jit(solution)/shard_map/ppermute | solution.py:25
  21.2 8.3 %collective-permute-start.12 = (f32[32,768]{1,0:T(8,128)S(1)}, f32[32,768]{1,0:T(8,128)S(1)}, u32[]{:S(2)}, u32[]{:S(2)}) collective-permute-start(f32[32,768]{1,0:T(8,128)S(1)} %add.61.refs_0_), channel_id=1, source_target_pairs={{0,3},{1,2},{2,1},{3,0},{4,7},{5,6},{6,5},{7,4},{8,11},{9,10},{10,... | collective-permute-start | bytes 294920 | tf_op jit(solution)/shard_map/ppermute | solution.py:25
  22.0 7.5 %collective-permute-start.13 = (f32[32,768]{1,0:T(8,128)S(1)}, f32[32,768]{1,0:T(8,128)S(1)}, u32[]{:S(2)}, u32[]{:S(2)}) collective-permute-start(f32[32,768]{1,0:T(8,128)S(1)} %add.61.refs_0_), channel_id=1, source_target_pairs={{0,1},{1,0},{2,3},{3,2},{4,5},{5,4},{6,7},{7,6},{8,9},{9,8},{10,11... | collective-permute-start | bytes 294920 | tf_op jit(solution)/shard_map/ppermute | solution.py:25
  22.3 6.5 %collective-permute-start.8 = (f32[32,384]{1,0:T(8,128)S(1)}, f32[32,384]{1,0:T(8,128)S(1)}, u32[]{:S(2)}, u32[]{:S(2)}) collective-permute-start(f32[32,384]{1,0:T(8,128)S(1)} %next_solve.4), channel_id=1, source_target_pairs={{0,32},{32,0},{1,33},{33,1},{2,34},{34,2},{3,35},{35,3},{4,36},{36... | collective-permute-start | bytes 147464 | tf_op jit(solution)/shard_map/ppermute | solution.py:25
  28.8 3.0 %collective-permute-start.9 = (f32[32,384]{1,0:T(8,128)S(1)}, f32[32,384]{1,0:T(8,128)S(1)}, u32[]{:S(2)}, u32[]{:S(2)}) collective-permute-start(f32[32,384]{1,0:T(8,128)S(1)} %add.60.one_ref), channel_id=1, source_target_pairs={{0,64},{64,0},{1,65},{65,1},{2,66},{66,2},{3,67},{67,3},{4,68},{68... | collective-permute-start | bytes 147464 | tf_op jit(solution)/shard_map/ppermute | solution.py:25
  29.7 2.8 %collective-permute-start.14 = (f32[32,384]{1,0:T(8,128)S(1)}, f32[32,384]{1,0:T(8,128)S(1)}, u32[]{:S(2)}, u32[]{:S(2)}) collective-permute-start(f32[32,384]{1,0:T(8,128)S(1)} %next_solve.5), channel_id=1, source_target_pairs={{0,32},{32,0},{1,33},{33,1},{2,34},{34,2},{3,35},{35,3},{4,36},{36... | collective-permute-start | bytes 147464 | tf_op jit(solution)/shard_map/ppermute | solution.py:25
  32.0 5.2 %collective-permute-start.16 = (f32[32,768]{1,0:T(8,128)S(1)}, f32[32,768]{1,0:T(8,128)S(1)}, u32[]{:S(2)}, u32[]{:S(2)}) collective-permute-start(f32[32,768]{1,0:T(8,128)S(1)} %get-tuple-element.40), channel_id=1, source_target_pairs={{0,4},{1,5},{2,6},{3,7},{4,0},{5,1},{6,2},{7,3},{8,12},{9,13},{10,... | collective-permute-start | bytes 294920 | tf_op jit(solution)/shard_map/ppermute | solution.py:25
  32.5 3.0 %collective-permute-start.15 = (f32[32,384]{1,0:T(8,128)S(1)}, f32[32,384]{1,0:T(8,128)S(1)}, u32[]{:S(2)}, u32[]{:S(2)}) collective-permute-start(f32[32,384]{1,0:T(8,128)S(1)} %add.62.one_ref), channel_id=1, source_target_pairs={{0,64},{64,0},{1,65},{65,1},{2,66},{66,2},{3,67},{67,3},{4,68},{68... | collective-permute-start | bytes 147464 | tf_op jit(solution)/shard_map/ppermute | solution.py:25
  35.7 4.3 %collective-permute-start.22 = (f32[32,768]{1,0:T(8,128)S(1)}, f32[32,768]{1,0:T(8,128)S(1)}, u32[]{:S(2)}, u32[]{:S(2)}) collective-permute-start(f32[32,768]{1,0:T(8,128)S(1)} %get-tuple-element.43), channel_id=1, source_target_pairs={{0,4},{1,5},{2,6},{3,7},{4,0},{5,1},{6,2},{7,3},{8,12},{9,13},{10,... | collective-permute-start | bytes 294920 | tf_op jit(solution)/shard_map/ppermute | solution.py:25
  37.2 6.1 %collective-permute-start.17 = (f32[32,768]{1,0:T(8,128)S(1)}, f32[32,768]{1,0:T(8,128)S(1)}, u32[]{:S(2)}, u32[]{:S(2)}) collective-permute-start(f32[32,768]{1,0:T(8,128)S(1)} %add.63.refs_0_), channel_id=1, source_target_pairs={{0,2},{1,3},{2,0},{3,1},{4,6},{5,7},{6,4},{7,5},{8,10},{9,11},{10,... | collective-permute-start | bytes 294920 | tf_op jit(solution)/shard_map/ppermute | solution.py:25
  38.5 4.9 %collective-permute-start.18 = (f32[32,768]{1,0:T(8,128)S(1)}, f32[32,768]{1,0:T(8,128)S(1)}, u32[]{:S(2)}, u32[]{:S(2)}) collective-permute-start(f32[32,768]{1,0:T(8,128)S(1)} %add.63.refs_0_), channel_id=1, source_target_pairs={{0,3},{1,2},{2,1},{3,0},{4,7},{5,6},{6,5},{7,4},{8,11},{9,10},{10,... | collective-permute-start | bytes 294920 | tf_op jit(solution)/shard_map/ppermute | solution.py:25
  39.3 4.0 %collective-permute-start.19 = (f32[32,768]{1,0:T(8,128)S(1)}, f32[32,768]{1,0:T(8,128)S(1)}, u32[]{:S(2)}, u32[]{:S(2)}) collective-permute-start(f32[32,768]{1,0:T(8,128)S(1)} %add.63.refs_0_), channel_id=1, source_target_pairs={{0,1},{1,0},{2,3},{3,2},{4,5},{5,4},{6,7},{7,6},{8,9},{9,8},{10,11... | collective-permute-start | bytes 294920 | tf_op jit(solution)/shard_map/ppermute | solution.py:25
  40.0 14.6 %copy-start.4 = (s32[3,3,24]{2,1,0:T(4,128)S(1)}, s32[3,3,24]{2,1,0:T(4,128)}, u32[]{:S(2)}) copy-start(s32[3,3,24]{2,1,0:T(4,128)} %param.15) | copy-start | bytes 2596
  40.0 14.7 %copy-start.2 = (bf16[3,384,768]{2,1,0:T(8,128)(2,1)S(1)}, bf16[3,384,768]{2,1,0:T(8,128)(2,1)}, u32[]{:S(2)}) copy-start(bf16[3,384,768]{2,1,0:T(8,128)(2,1)} %factor_ref.1) | copy-start | bytes 5308420
  40.0 9.5 %collective-permute-start.23 = (f32[32,768]{1,0:T(8,128)S(1)}, f32[32,768]{1,0:T(8,128)S(1)}, u32[]{:S(2)}, u32[]{:S(2)}) collective-permute-start(f32[32,768]{1,0:T(8,128)S(1)} %add.65.refs_0_), channel_id=1, source_target_pairs={{0,2},{1,3},{2,0},{3,1},{4,6},{5,7},{6,4},{7,5},{8,10},{9,11},{10,... | collective-permute-start | bytes 294920 | tf_op jit(solution)/shard_map/ppermute | solution.py:25
  42.5 7.0 %collective-permute-start.24 = (f32[32,768]{1,0:T(8,128)S(1)}, f32[32,768]{1,0:T(8,128)S(1)}, u32[]{:S(2)}, u32[]{:S(2)}) collective-permute-start(f32[32,768]{1,0:T(8,128)S(1)} %add.65.refs_0_), channel_id=1, source_target_pairs={{0,3},{1,2},{2,1},{3,0},{4,7},{5,6},{6,5},{7,4},{8,11},{9,10},{10,... | collective-permute-start | bytes 294920 | tf_op jit(solution)/shard_map/ppermute | solution.py:25
  43.3 6.2 %collective-permute-start.25 = (f32[32,768]{1,0:T(8,128)S(1)}, f32[32,768]{1,0:T(8,128)S(1)}, u32[]{:S(2)}, u32[]{:S(2)}) collective-permute-start(f32[32,768]{1,0:T(8,128)S(1)} %add.65.refs_0_), channel_id=1, source_target_pairs={{0,1},{1,0},{2,3},{3,2},{4,5},{5,4},{6,7},{7,6},{8,9},{9,8},{10,11... | collective-permute-start | bytes 294920 | tf_op jit(solution)/shard_map/ppermute | solution.py:25
  43.5 9.0 %collective-permute-start.20 = (f32[32,384]{1,0:T(8,128)S(1)}, f32[32,384]{1,0:T(8,128)S(1)}, u32[]{:S(2)}, u32[]{:S(2)}) collective-permute-start(f32[32,384]{1,0:T(8,128)S(1)} %next_solve.6), channel_id=1, source_target_pairs={{0,32},{32,0},{1,33},{33,1},{2,34},{34,2},{3,35},{35,3},{4,36},{36... | collective-permute-start | bytes 147464 | tf_op jit(solution)/shard_map/ppermute | solution.py:25
  49.7 4.0 %collective-permute-start.26 = (f32[32,384]{1,0:T(8,128)S(1)}, f32[32,384]{1,0:T(8,128)S(1)}, u32[]{:S(2)}, u32[]{:S(2)}) collective-permute-start(f32[32,384]{1,0:T(8,128)S(1)} %next_solve.7), channel_id=1, source_target_pairs={{0,32},{32,0},{1,33},{33,1},{2,34},{34,2},{3,35},{35,3},{4,36},{36... | collective-permute-start | bytes 147464 | tf_op jit(solution)/shard_map/ppermute | solution.py:25
  52.5 3.7 %collective-permute-start.21 = (f32[32,384]{1,0:T(8,128)S(1)}, f32[32,384]{1,0:T(8,128)S(1)}, u32[]{:S(2)}, u32[]{:S(2)}) collective-permute-start(f32[32,384]{1,0:T(8,128)S(1)} %add.64.one_ref), channel_id=1, source_target_pairs={{0,64},{64,0},{1,65},{65,1},{2,66},{66,2},{3,67},{67,3},{4,68},{68... | collective-permute-start | bytes 147464 | tf_op jit(solution)/shard_map/ppermute | solution.py:25
  53.8 3.0 %collective-permute-start.27 = (f32[32,384]{1,0:T(8,128)S(1)}, f32[32,384]{1,0:T(8,128)S(1)}, u32[]{:S(2)}, u32[]{:S(2)}) collective-permute-start(f32[32,384]{1,0:T(8,128)S(1)} %add.66.one_ref), channel_id=1, source_target_pairs={{0,64},{64,0},{1,65},{65,1},{2,66},{66,2},{3,67},{67,3},{4,68},{68... | collective-permute-start | bytes 147464 | tf_op jit(solution)/shard_map/ppermute | solution.py:25
  56.5 26.1 %copy-start.1 = (bf16[768,1536]{1,0:T(8,128)(2,1)S(1)}, bf16[768,1536]{1,0:T(8,128)(2,1)}, u32[]{:S(2)}) copy-start(bf16[768,1536]{1,0:T(8,128)(2,1)} %inverse_ref.1) | copy-start | bytes 7077892
  66.1 6.5 %collective-permute-start.28 = (f32[8,768]{1,0:T(8,128)S(1)}, f32[8,768]{1,0:T(8,128)S(1)}, u32[]{:S(2)}, u32[]{:S(2)}) collective-permute-start(f32[8,768]{1,0:T(8,128)S(1)} %reduce_sum.9), channel_id=1, source_target_pairs={{0,128},{8,136},{16,144},{24,152},{128,0},{136,8},{144,16},{152,24... | collective-permute-start | bytes 73736 | tf_op jit(solution)/shard_map/ppermute | solution.py:25
  68.7 4.5 %collective-permute-start.29 = (f32[8,768]{1,0:T(8,128)S(1)}, f32[8,768]{1,0:T(8,128)S(1)}, u32[]{:S(2)}, u32[]{:S(2)}) collective-permute-start(f32[8,768]{1,0:T(8,128)S(1)} %reduce_sum.9), channel_id=1, source_target_pairs={{0,8},{8,0},{16,24},{24,16},{128,136},{136,128},{144,152},{152,144... | collective-permute-start | bytes 73736 | tf_op jit(solution)/shard_map/ppermute | solution.py:25
  71.7 6.0 %collective-permute-start.30 = (f32[8,768]{1,0:T(8,128)S(1)}, f32[8,768]{1,0:T(8,128)S(1)}, u32[]{:S(2)}, u32[]{:S(2)}) collective-permute-start(f32[8,768]{1,0:T(8,128)S(1)} %reduce_sum.9), channel_id=1, source_target_pairs={{0,136},{8,128},{16,152},{24,144},{128,8},{136,0},{144,24},{152,16... | collective-permute-start | bytes 73736 | tf_op jit(solution)/shard_map/ppermute | solution.py:25
  77.6 4.9 %collective-permute-start.31 = (f32[8,768]{1,0:T(8,128)S(1)}, f32[8,768]{1,0:T(8,128)S(1)}, u32[]{:S(2)}, u32[]{:S(2)}) collective-permute-start(f32[8,768]{1,0:T(8,128)S(1)} %add_add_fusion.one_ref), channel_id=1, source_target_pairs={{0,24},{8,16},{16,8},{24,0},{1,25},{9,17},{17,9},{25,1},{2,26},{10... | collective-permute-start | bytes 73736 | tf_op jit(solution)/shard_map/ppermute | solution.py:25
  83.0 6.1 %collective-permute-start.32 = (f32[8,1536]{1,0:T(8,128)S(1)}, f32[8,1536]{1,0:T(8,128)S(1)}, u32[]{:S(2)}, u32[]{:S(2)}) collective-permute-start(f32[8,1536]{1,0:T(8,128)S(1)} %root_part.1), channel_id=1, source_target_pairs={{0,32},{32,0},{1,33},{33,1},{2,34},{34,2},{3,35},{35,3},{4,36},{36... | collective-permute-start | bytes 147464 | tf_op jit(solution)/shard_map/ppermute | solution.py:25
  89.1 2.9 %collective-permute-start.33 = (f32[8,1536]{1,0:T(8,128)S(1)}, f32[8,1536]{1,0:T(8,128)S(1)}, u32[]{:S(2)}, u32[]{:S(2)}) collective-permute-start(f32[8,1536]{1,0:T(8,128)S(1)} %add.71), channel_id=1, source_target_pairs={{0,64},{64,0},{1,65},{65,1},{2,66},{66,2},{3,67},{67,3},{4,68},{68... | collective-permute-start | bytes 147464 | tf_op jit(solution)/shard_map/ppermute | solution.py:25

commit v8 on v7

--- a/solution.py
+++ b/solution.py
@@ -11,7 +11,6 @@
 PARTS = 2
 PROW = ("xl", "core")
 OWN = "own"
-TREES = ("grid", "zt")
 SCOPED_BYTES = 4 << 20
 F32 = jnp.float32
 BF16 = jnp.bfloat16
@@ -56,16 +55,13 @@
     return jnp.dot(left, right, preferred_element_type=F32)
 
 
-def first_solve(tree, sub_rhs, diag_inverse, parts):
+def first_solve(tree, sub_rhs, diag_inverse):
     rhs_count, depth = sub_rhs.shape[2:]
     cols = diag_inverse.shape[2]
     pieces = 3
     step = depth // pieces
 
-    few = rhs_count // parts
-
-    def body(tree_ref, rhs_hbm, inverse_hbm, *refs):
-        *out_refs, rhs, inverse, rhs_sem, inverse_sem = refs
+    def body(tree_ref, rhs_hbm, inverse_hbm, out_ref, rhs, inverse, rhs_sem, inverse_sem):
         rhs_copy = pltpu.make_async_copy(rhs_hbm.at[tree_ref[0], 0], rhs, rhs_sem)
         rhs_copy.start()
         copies = []
@@ -83,12 +79,11 @@
             copies[piece].wait()
             part = slice(piece * step, (piece + 1) * step)
             total = total + product(rhs[:, part].astype(BF16), inverse[part, :])
-        for k, ref in enumerate(out_refs):
-            ref[...] = total[k * few : (k + 1) * few]
+        out_ref[...] = total
 
     return call(
         body,
-        [((few, cols), F32)] * parts,
+        [((rhs_count, cols), F32)],
         (tree, sub_rhs, diag_inverse),
         [SCALARS, IN_PLACE, IN_PLACE],
         [
@@ -98,7 +93,7 @@
             pltpu.SemaphoreType.DMA((pieces,)),
         ],
         "first_solve",
-    )
+    )[0]
 
 
 def next_solve(place, part, rhs, sums, diag_inverse):
@@ -214,28 +209,26 @@
     )(*args)
 
 
-def kept_update(halves, factor, block, before, last=False):
+def kept_update(halves, factor, block, before, parts=1, last=False):
     rows, cols = halves[0].shape
     out_cols = factor.shape[2]
+    few = rows // parts
+    places = [slice(k * few, (k + 1) * few) for k in range(parts)]
 
     def body(one_ref, other_ref, factor_ref, *refs):
-        before_ref, (out_ref, solved_ref, *kept_ref) = refs[: len(before)], refs[len(before) :]
+        before_refs, outs = refs[: len(before)], refs[len(before) :]
         solved = one_ref[...] + other_ref[...]
         kept = solved.astype(BF16)
-        solved_ref[...] = solved
-        for ref in kept_ref:
-            ref[...] = kept
         update = product(kept, factor_ref[block])
-        for ref in before_ref:
+        for ref in before_refs:
             update = update + ref[...]
-        out_ref[...] = update
-
-    return call(
-        body,
-        [((rows, out_cols), F32), ((rows, cols), F32), ((rows, cols), BF16)][: 2 if last else 3],
-        (*halves, factor, *before),
-        name="kept_update",
-    )
+        for k, whole in enumerate((update, solved, kept)):
+            for ref, place in zip(outs[k * parts : (k + 1) * parts], places):
+                ref[...] = whole[place]
+
+    kinds = [((few, out_cols), F32), ((few, cols), F32), ((few, cols), BF16)]
+    outs = [kind for kind in kinds[: 2 if last else 3] for _ in range(parts)]
+    return call(body, outs, (*halves, factor, *before), name="kept_update")
 
 
 def early_update(kept, factor, blocks):
@@ -283,12 +276,13 @@
     root_tiles = lax.dynamic_slice_in_dim(root_mask, first_tile, tiles, 2)
     tree = tree.reshape(1)
 
-    firsts = first_solve(tree, sub_rhs, diag_inverse, PARTS)
+    halves = prow_halves(first_solve(tree, sub_rhs, diag_inverse))
     inner, inverse, rhs = stage(tree, inner_tiles, sub_rhs, diag_inverse, inner_factor)
     root = masked(root_tiles, root_factor)
     solved, locals_ = [], []
-    for part, first in enumerate(firsts):
-        update, solved0, kept0 = kept_update(prow_halves(first), inner, 0, ())
+    outs = kept_update(halves, inner, 0, (), PARTS)
+    for part in range(PARTS):
+        update, solved0, kept0 = outs[part::PARTS]
         halves = prow_halves(next_solve(0, part, rhs, owner_sums(update), inverse))
         early = early_update((kept0,), inner, (1,))
         update, solved1, kept1 = kept_update(halves, inner, 2, (early,))
@@ -303,13 +297,11 @@
     few = rhs_count // owners
     place = owners - 1 - lax.axis_index(OWN)
     own_rows = swap_blocks(root_local.reshape(owners, few, out_cols)).sum(axis=0)
-    sub_solution, *arrived = lax.optimization_barrier(
-        (
-            stacked(list(zip(*solved))),
-            *[partner(own_rows, TREES, bit) for bit in (4, 1, 5)],
-        )
+    sub_solution, across = lax.optimization_barrier(
+        (stacked(list(zip(*solved))), partner(own_rows, "grid"))
     )
-    total = own_rows + arrived[0] + (arrived[1] + arrived[2])
+    total = own_rows + across
+    total = total + partner(total, "zt", 1)
     rhs_rows = lax.dynamic_slice_in_dim(root_rhs, place * few, few, 0)
     part = root_part(rhs_rows, (total, partner(total, "zt", 3)), root_inverse)
     pair, other = prow_halves(part)

time: 103 us -> 102 us (level)
  waiting for transfers between devices: 17.5 us -> 15.4 us
    ppermute x34 -> x31, waiting for transfers between devices: 17.5 us -> 15.4 us  [partner(): lax.ppermute(shard, axis, [(i, i ^ bit) for i in range(lax.axis_size(axis...]
    ppermute x34 -> x31, starting transfers between devices: 55 us -> 55.9 us  [partner(): lax.ppermute(shard, axis, [(i, i ^ bit) for i in range(lax.axis_size(axis...]
    pallas_call x18 -> x17, Pallas kernels: 8.46 us -> 8.3 us  [call(): pl.pallas_call(body, out_shape=[pltpu.VMEM(shape, kind) for shape, kind i...]
  transfers between devices with their start and end apart: 34 -> 31, of which waited for: 13 -> 13; matrix products, arithmetic and copies ran while one was open for 0% -> 0% of each run, Pallas kernels for 7% -> 7%
where the time goes in v8:
time: 102 us; the launch traced here: 101 us
  starting transfers between devices  55.9 us (55%)
  blocking collectives  18.1 us (18%)
  waiting for transfers between devices  15.4 us (15%)
  Pallas kernels  9.05 us (9%)
    ppermute x31, starting transfers between devices, partner(): lax.ppermute(shard, axis, [(i, i ^ bit) for i in range(lax.axis_size(axis...  55.9 us
    all_to_all x2, blocking collectives, swap_blocks(): lax.all_to_all(blocks, OWN, 0, 0, axis_index_groups=[order], tiled=True)  18.1 us
    ppermute x31, waiting for transfers between devices, partner(): lax.ppermute(shard, axis, [(i, i ^ bit) for i in range(lax.axis_size(axis...  15.4 us
    pallas_call x17, Pallas kernels, call(): pl.pallas_call(body, out_shape=[pltpu.VMEM(shape, kind) for shape, kind i...  8.3 us
  transfers between devices with their start and end apart: 31, of which 13 were waited for; matrix products, arithmetic and copies ran while one was open for 0% of the time, Pallas kernels for 7%

profile of v8, /device:TPU:1, one launch (start us, length us, event | category | flops | bytes accessed | tf_op | source)
XLA Modules:
  0.0 100.5 jit_solution(3440933440460165536)
XLA Ops:
  0.7 1.6 %first_solve.1 = f32[64,384]{1,0:T(8,128)S(1)} custom-call(s32[1]{0:T(128)} %bitcast.tree_ref, f32[4,3,64,768]{3,2,1,0:T(8,128)} %rhs_hbm.3, bf16[3,768,384]{2,1,0:T(8,128)(2,1)} %inverse_hbm.3), custom_call_target="tpu_custom_call" | custom-call | tf_op jit(solution)/shard_map/first_solve/pallas_call | solution.py:43
  2.3 3.3 %collective-permute-start = (f32[64,384]{1,0:T(8,128)S(1)}, f32[64,384]{1,0:T(8,128)S(1)}, u32[]{:S(2)}, u32[]{:S(2)}) collective-permute-start(f32[64,384]{1,0:T(8,128)S(1)} %first_solve.1), channel_id=1, source_target_pairs={{0,32},{32,0},{1,33},{33,1},{2,34},{34,2},{3,35},{35,3},{4,36},{36... | collective-permute-start | bytes 294920 | tf_op jit(solution)/shard_map/ppermute | solution.py:24
  5.6 0.9 collective-permute-done
  6.5 0.1 collective-permute-start.1
  6.7 0.1 constant_dynamic-slice_fusion.2.mask_ref
  6.7 2.6 %stage.1 = (bf16[3,384,768]{2,1,0:T(8,128)(2,1)S(1)}, bf16[2,768,384]{2,1,0:T(8,128)(2,1)S(1)}, f32[2,64,768]{2,1,0:T(8,128)S(1)}) custom-call(s32[1]{0:T(128)} %bitcast.tree_ref, s32[3,3,6]{2,1,0:T(4,128)S(1)} %constant_dynamic-slice_fusion.2.mask_ref, f32[4,3,64,768]{3,2,1,0:T(8,128)} %rhs_hbm.3, bf16[3,768,384]{2,1,0:T(8,128)(2,1)} %inverse_hbm.3, ...), custom_call_target="tpu_custom_call" | custom-call | tf_op jit(solution)/shard_map/stage/pallas_call | solution.py:43
  9.3 1.4 %collective-permute-done.1.other_ref = f32[64,384]{1,0:T(8,128)S(1)} collective-permute-done((f32[64,384]{1,0:T(8,128)S(1)}, f32[64,384]{1,0:T(8,128)S(1)}, u32[]{:S(2)}, u32[]{:S(2)}) %collective-permute-start.1) | collective-permute-done | bytes 98336 | tf_op jit(solution)/shard_map/ppermute | solution.py:24
  10.7 0.2 kept_update.5
  10.9 0.1 collective-permute-start.2
  11.0 1.5 %collective-permute-start.8 = (f32[32,768]{1,0:T(8,128)S(1)}, f32[32,768]{1,0:T(8,128)S(1)}, u32[]{:S(2)}, u32[]{:S(2)}) collective-permute-start(f32[32,768]{1,0:T(8,128)S(1)} %get-tuple-element.31), channel_id=1, source_target_pairs={{0,4},{1,5},{2,6},{3,7},{4,0},{5,1},{6,2},{7,3},{8,12},{9,13},{10,... | collective-permute-start | bytes 294920 | tf_op jit(solution)/shard_map/ppermute | solution.py:24
  12.4 2.0 %collective-permute-done.2 = f32[32,768]{1,0:T(8,128)S(1)} collective-permute-done((f32[32,768]{1,0:T(8,128)S(1)}, f32[32,768]{1,0:T(8,128)S(1)}, u32[]{:S(2)}, u32[]{:S(2)}) %collective-permute-start.2) | collective-permute-done | bytes 98336 | tf_op jit(solution)/shard_map/ppermute | solution.py:24
  14.4 1.4 %collective-permute-start.3 = (f32[32,768]{1,0:T(8,128)S(1)}, f32[32,768]{1,0:T(8,128)S(1)}, u32[]{:S(2)}, u32[]{:S(2)}) collective-permute-start(f32[32,768]{1,0:T(8,128)S(1)} %add.52.refs_0_), channel_id=1, source_target_pairs={{0,2},{1,3},{2,0},{3,1},{4,6},{5,7},{6,4},{7,5},{8,10},{9,11},{10,... | collective-permute-start | bytes 294920 | tf_op jit(solution)/shard_map/ppermute | solution.py:24
  15.9 0.8 collective-permute-start.4
  16.7 0.5 collective-permute-start.5
  17.2 2.7 %collective-permute-start.9 = (f32[32,768]{1,0:T(8,128)S(1)}, f32[32,768]{1,0:T(8,128)S(1)}, u32[]{:S(2)}, u32[]{:S(2)}) collective-permute-start(f32[32,768]{1,0:T(8,128)S(1)} %add.54.refs_0_), channel_id=1, source_target_pairs={{0,2},{1,3},{2,0},{3,1},{4,6},{5,7},{6,4},{7,5},{8,10},{9,11},{10,... | collective-permute-start | bytes 294920 | tf_op jit(solution)/shard_map/ppermute | solution.py:24
  19.9 0.8 collective-permute-start.10
  20.6 0.2 next_solve.4
  20.8 6.1 %collective-permute-start.6 = (f32[32,384]{1,0:T(8,128)S(1)}, f32[32,384]{1,0:T(8,128)S(1)}, u32[]{:S(2)}, u32[]{:S(2)}) collective-permute-start(f32[32,384]{1,0:T(8,128)S(1)} %next_solve.4), channel_id=1, source_target_pairs={{0,32},{32,0},{1,33},{33,1},{2,34},{34,2},{3,35},{35,3},{4,36},{36... | collective-permute-start | bytes 147464 | tf_op jit(solution)/shard_map/ppermute | solution.py:24
  26.9 0.9 collective-permute-done.6
  27.8 1.3 %collective-permute-start.7 = (f32[32,384]{1,0:T(8,128)S(1)}, f32[32,384]{1,0:T(8,128)S(1)}, u32[]{:S(2)}, u32[]{:S(2)}) collective-permute-start(f32[32,384]{1,0:T(8,128)S(1)} %add.53.one_ref), channel_id=1, source_target_pairs={{0,64},{64,0},{1,65},{65,1},{2,66},{66,2},{3,67},{67,3},{4,68},{68... | collective-permute-start | bytes 147464 | tf_op jit(solution)/shard_map/ppermute | solution.py:24
  29.1 0.2 next_solve.5
  29.3 1.0 collective-permute-start.12
  30.3 0.2 early_update.4.refs_0_
  30.5 0.3 collective-permute-done.7.other_ref
  30.8 0.2 kept_update.6
  31.0 1.5 %collective-permute-start.14 = (f32[32,768]{1,0:T(8,128)S(1)}, f32[32,768]{1,0:T(8,128)S(1)}, u32[]{:S(2)}, u32[]{:S(2)}) collective-permute-start(f32[32,768]{1,0:T(8,128)S(1)} %get-tuple-element.34), channel_id=1, source_target_pairs={{0,4},{1,5},{2,6},{3,7},{4,0},{5,1},{6,2},{7,3},{8,12},{9,13},{10,... | collective-permute-start | bytes 294920 | tf_op jit(solution)/shard_map/ppermute | solution.py:24
  32.5 0.7 collective-permute-start.13
  33.2 0.2 early_update.5.refs_0_
  33.4 2.5 %collective-permute-done.13.other_ref = f32[32,384]{1,0:T(8,128)S(1)} collective-permute-done((f32[32,384]{1,0:T(8,128)S(1)}, f32[32,384]{1,0:T(8,128)S(1)}, u32[]{:S(2)}, u32[]{:S(2)}) %collective-permute-start.13) | collective-permute-done | bytes 49184 | tf_op jit(solution)/shard_map/ppermute | solution.py:24
  35.8 0.2 kept_update.7
  36.0 0.1 collective-permute-start.20
  36.2 1.8 %collective-permute-start.15 = (f32[32,768]{1,0:T(8,128)S(1)}, f32[32,768]{1,0:T(8,128)S(1)}, u32[]{:S(2)}, u32[]{:S(2)}) collective-permute-start(f32[32,768]{1,0:T(8,128)S(1)} %add.56.refs_0_), channel_id=1, source_target_pairs={{0,2},{1,3},{2,0},{3,1},{4,6},{5,7},{6,4},{7,5},{8,10},{9,11},{10,... | collective-permute-start | bytes 294920 | tf_op jit(solution)/shard_map/ppermute | solution.py:24
  38.0 0.8 collective-permute-start.16
  38.7 0.2 collective-permute-start.17
  38.9 0.7 collective-permute-done.20
  39.6 2.5 %collective-permute-start.21 = (f32[32,768]{1,0:T(8,128)S(1)}, f32[32,768]{1,0:T(8,128)S(1)}, u32[]{:S(2)}, u32[]{:S(2)}) collective-permute-start(f32[32,768]{1,0:T(8,128)S(1)} %add.58.refs_0_), channel_id=1, source_target_pairs={{0,2},{1,3},{2,0},{3,1},{4,6},{5,7},{6,4},{7,5},{8,10},{9,11},{10,... | collective-permute-start | bytes 294920 | tf_op jit(solution)/shard_map/ppermute | solution.py:24
  42.1 0.8 collective-permute-start.22
  42.9 0.2 next_solve.6
  43.1 5.9 %collective-permute-start.18 = (f32[32,384]{1,0:T(8,128)S(1)}, f32[32,384]{1,0:T(8,128)S(1)}, u32[]{:S(2)}, u32[]{:S(2)}) collective-permute-start(f32[32,384]{1,0:T(8,128)S(1)} %next_solve.6), channel_id=1, source_target_pairs={{0,32},{32,0},{1,33},{33,1},{2,34},{34,2},{3,35},{35,3},{4,36},{36... | collective-permute-start | bytes 147464 | tf_op jit(solution)/shard_map/ppermute | solution.py:24
  49.0 0.2 next_solve.7
  49.2 3.4 %collective-permute-start.24 = (f32[32,384]{1,0:T(8,128)S(1)}, f32[32,384]{1,0:T(8,128)S(1)}, u32[]{:S(2)}, u32[]{:S(2)}) collective-permute-start(f32[32,384]{1,0:T(8,128)S(1)} %next_solve.7), channel_id=1, source_target_pairs={{0,32},{32,0},{1,33},{33,1},{2,34},{34,2},{3,35},{35,3},{4,36},{36... | collective-permute-start | bytes 147464 | tf_op jit(solution)/shard_map/ppermute | solution.py:24
  52.7 1.3 %collective-permute-start.19 = (f32[32,384]{1,0:T(8,128)S(1)}, f32[32,384]{1,0:T(8,128)S(1)}, u32[]{:S(2)}, u32[]{:S(2)}) collective-permute-start(f32[32,384]{1,0:T(8,128)S(1)} %add.57.one_ref), channel_id=1, source_target_pairs={{0,64},{64,0},{1,65},{65,1},{2,66},{66,2},{3,67},{67,3},{4,68},{68... | collective-permute-start | bytes 147464 | tf_op jit(solution)/shard_map/ppermute | solution.py:24
  54.0 0.8 collective-permute-start.25
  54.9 0.9 masked.1.refs_2_.factor_ref
  55.8 0.3 early_update.6.refs_0_
  56.1 0.3 early_update.7.refs_0_
  56.4 0.2 kept_update.8
  56.7 0.3 collective-permute-done.25.other_ref
  57.0 0.2 kept_update.9
  57.2 8.5 %all_to_all.10 = f32[8,8,768]{2,1,0:T(8,128)S(1)} all-to-all(f32[8,8,768]{2,1,0:T(8,128)S(1)} %maximum_bitcast_fusion), channel_id=1, replica_groups={{7,6,5,4,3,2,1,0},{15,14,13,12,11,10,9,8},{23,22,21,20,19,18,17,16},{31..., dimensions={0} | all-to-all | bytes 393216 | tf_op jit(solution)/shard_map/all_to_all | solution.py:29
  65.7 2.6 %collective-permute-start.26 = (f32[8,768]{1,0:T(8,128)S(1)}, f32[8,768]{1,0:T(8,128)S(1)}, u32[]{:S(2)}, u32[]{:S(2)}) collective-permute-start(f32[8,768]{1,0:T(8,128)S(1)} %reduce_sum.9), channel_id=1, source_target_pairs={{0,128},{128,0},{1,129},{129,1},{2,130},{130,2},{3,131},{131,3},{4... | collective-permute-start | bytes 73736 | tf_op jit(solution)/shard_map/ppermute | solution.py:24
  68.3 0.8 stacked.1
  69.0 0.9 collective-permute-done.26
  70.0 3.0 %collective-permute-start.27 = (f32[8,768]{1,0:T(8,128)S(1)}, f32[8,768]{1,0:T(8,128)S(1)}, u32[]{:S(2)}, u32[]{:S(2)}) collective-permute-start(f32[8,768]{1,0:T(8,128)S(1)} %add.61), channel_id=1, source_target_pairs={{0,8},{8,0},{16,24},{24,16},{1,9},{9,1},{17,25},{25,17},{2,10},{10... | collective-permute-start | bytes 73736 | tf_op jit(solution)/shard_map/ppermute | solution.py:24
  73.0 1.2 %collective-permute-done.27 = f32[8,768]{1,0:T(8,128)S(1)} collective-permute-done((f32[8,768]{1,0:T(8,128)S(1)}, f32[8,768]{1,0:T(8,128)S(1)}, u32[]{:S(2)}, u32[]{:S(2)}) %collective-permute-start.27) | collective-permute-done | bytes 24608 | tf_op jit(solution)/shard_map/ppermute | solution.py:24
  74.2 4.6 %collective-permute-start.28 = (f32[8,768]{1,0:T(8,128)S(1)}, f32[8,768]{1,0:T(8,128)S(1)}, u32[]{:S(2)}, u32[]{:S(2)}) collective-permute-start(f32[8,768]{1,0:T(8,128)S(1)} %add.62.one_ref), channel_id=1, source_target_pairs={{0,24},{8,16},{16,8},{24,0},{1,25},{9,17},{17,9},{25,1},{2,26},{10... | collective-permute-start | bytes 73736 | tf_op jit(solution)/shard_map/ppermute | solution.py:24
  78.8 1.2 %collective-permute-done.28.other_ref = f32[8,768]{1,0:T(8,128)S(1)} collective-permute-done((f32[8,768]{1,0:T(8,128)S(1)}, f32[8,768]{1,0:T(8,128)S(1)}, u32[]{:S(2)}, u32[]{:S(2)}) %collective-permute-start.28) | collective-permute-done | bytes 24608 | tf_op jit(solution)/shard_map/ppermute | solution.py:24
  80.0 0.4 root_part.1
  80.4 5.8 %collective-permute-start.29 = (f32[8,1536]{1,0:T(8,128)S(1)}, f32[8,1536]{1,0:T(8,128)S(1)}, u32[]{:S(2)}, u32[]{:S(2)}) collective-permute-start(f32[8,1536]{1,0:T(8,128)S(1)} %root_part.1), channel_id=1, source_target_pairs={{0,32},{32,0},{1,33},{33,1},{2,34},{34,2},{3,35},{35,3},{4,36},{36... | collective-permute-start | bytes 147464 | tf_op jit(solution)/shard_map/ppermute | solution.py:24
  86.3 0.9 collective-permute-done.29
  87.2 0.8 collective-permute-start.30
  88.0 2.1 %collective-permute-done.30 = f32[8,1536]{1,0:T(8,128)S(1)} collective-permute-done((f32[8,1536]{1,0:T(8,128)S(1)}, f32[8,1536]{1,0:T(8,128)S(1)}, u32[]{:S(2)}, u32[]{:S(2)}) %collective-permute-start.30) | collective-permute-done | bytes 49184 | tf_op jit(solution)/shard_map/ppermute | solution.py:24
  90.1 9.6 %all_to_all.11 = f32[8,8,1536]{2,1,0:T(8,128)S(1)} all-to-all(f32[8,8,1536]{2,1,0:T(8,128)S(1)} %broadcast_in_dim.2), channel_id=1, replica_groups={{7,6,5,4,3,2,1,0},{15,14,13,12,11,10,9,8},{23,22,21,20,19,18,17,16},{31..., dimensions={0} | all-to-all | bytes 786432 | tf_op jit(solution)/shard_map/all_to_all | solution.py:29
  99.8 0.7 copy.11
  (48 shorter events, 0.3 us)
Async XLA Ops:
  0.6 78.2 %copy-start = (f32[64,768]{1,0:T(8,128)S(1)}, f32[64,768]{1,0:T(8,128)}, u32[]{:S(2)}) copy-start(f32[64,768]{1,0:T(8,128)} %param.9) | copy-start | bytes 589828
  0.7 6.0 %copy-start.3 = (s32[3,3,24]{2,1,0:T(4,128)S(1)}, s32[3,3,24]{2,1,0:T(4,128)}, u32[]{:S(2)}) copy-start(s32[3,3,24]{2,1,0:T(4,128)} %param.13) | copy-start | bytes 2596
  2.3 4.3 %collective-permute-start = (f32[64,384]{1,0:T(8,128)S(1)}, f32[64,384]{1,0:T(8,128)S(1)}, u32[]{:S(2)}, u32[]{:S(2)}) collective-permute-start(f32[64,384]{1,0:T(8,128)S(1)} %first_solve.1), channel_id=1, source_target_pairs={{0,32},{32,0},{1,33},{33,1},{2,34},{34,2},{3,35},{35,3},{4,36},{36... | collective-permute-start | bytes 294920 | tf_op jit(solution)/shard_map/ppermute | solution.py:24
  6.5 4.1 %collective-permute-start.1 = (f32[64,384]{1,0:T(8,128)S(1)}, f32[64,384]{1,0:T(8,128)S(1)}, u32[]{:S(2)}, u32[]{:S(2)}) collective-permute-start(f32[64,384]{1,0:T(8,128)S(1)} %add.49.one_ref), channel_id=1, source_target_pairs={{0,64},{64,0},{1,65},{65,1},{2,66},{66,2},{3,67},{67,3},{4,68},{68... | collective-permute-start | bytes 294920 | tf_op jit(solution)/shard_map/ppermute | solution.py:24
  10.9 3.6 %collective-permute-start.2 = (f32[32,768]{1,0:T(8,128)S(1)}, f32[32,768]{1,0:T(8,128)S(1)}, u32[]{:S(2)}, u32[]{:S(2)}) collective-permute-start(f32[32,768]{1,0:T(8,128)S(1)} %get-tuple-element.27), channel_id=1, source_target_pairs={{0,4},{1,5},{2,6},{3,7},{4,0},{5,1},{6,2},{7,3},{8,12},{9,13},{10,... | collective-permute-start | bytes 294920 | tf_op jit(solution)/shard_map/ppermute | solution.py:24
  11.0 6.2 %collective-permute-start.8 = (f32[32,768]{1,0:T(8,128)S(1)}, f32[32,768]{1,0:T(8,128)S(1)}, u32[]{:S(2)}, u32[]{:S(2)}) collective-permute-start(f32[32,768]{1,0:T(8,128)S(1)} %get-tuple-element.31), channel_id=1, source_target_pairs={{0,4},{1,5},{2,6},{3,7},{4,0},{5,1},{6,2},{7,3},{8,12},{9,13},{10,... | collective-permute-start | bytes 294920 | tf_op jit(solution)/shard_map/ppermute | solution.py:24
  14.4 6.2 %collective-permute-start.3 = (f32[32,768]{1,0:T(8,128)S(1)}, f32[32,768]{1,0:T(8,128)S(1)}, u32[]{:S(2)}, u32[]{:S(2)}) collective-permute-start(f32[32,768]{1,0:T(8,128)S(1)} %add.52.refs_0_), channel_id=1, source_target_pairs={{0,2},{1,3},{2,0},{3,1},{4,6},{5,7},{6,4},{7,5},{8,10},{9,11},{10,... | collective-permute-start | bytes 294920 | tf_op jit(solution)/shard_map/ppermute | solution.py:24
  15.9 4.8 %collective-permute-start.4 = (f32[32,768]{1,0:T(8,128)S(1)}, f32[32,768]{1,0:T(8,128)S(1)}, u32[]{:S(2)}, u32[]{:S(2)}) collective-permute-start(f32[32,768]{1,0:T(8,128)S(1)} %add.52.refs_0_), channel_id=1, source_target_pairs={{0,3},{1,2},{2,1},{3,0},{4,7},{5,6},{6,5},{7,4},{8,11},{9,10},{10,... | collective-permute-start | bytes 294920 | tf_op jit(solution)/shard_map/ppermute | solution.py:24
  16.7 4.0 %collective-permute-start.5 = (f32[32,768]{1,0:T(8,128)S(1)}, f32[32,768]{1,0:T(8,128)S(1)}, u32[]{:S(2)}, u32[]{:S(2)}) collective-permute-start(f32[32,768]{1,0:T(8,128)S(1)} %add.52.refs_0_), channel_id=1, source_target_pairs={{0,1},{1,0},{2,3},{3,2},{4,5},{5,4},{6,7},{7,6},{8,9},{9,8},{10,11... | collective-permute-start | bytes 294920 | tf_op jit(solution)/shard_map/ppermute | solution.py:24
  17.2 11.9 %collective-permute-start.9 = (f32[32,768]{1,0:T(8,128)S(1)}, f32[32,768]{1,0:T(8,128)S(1)}, u32[]{:S(2)}, u32[]{:S(2)}) collective-permute-start(f32[32,768]{1,0:T(8,128)S(1)} %add.54.refs_0_), channel_id=1, source_target_pairs={{0,2},{1,3},{2,0},{3,1},{4,6},{5,7},{6,4},{7,5},{8,10},{9,11},{10,... | collective-permute-start | bytes 294920 | tf_op jit(solution)/shard_map/ppermute | solution.py:24
  19.9 9.2 %collective-permute-start.10 = (f32[32,768]{1,0:T(8,128)S(1)}, f32[32,768]{1,0:T(8,128)S(1)}, u32[]{:S(2)}, u32[]{:S(2)}) collective-permute-start(f32[32,768]{1,0:T(8,128)S(1)} %add.54.refs_0_), channel_id=1, source_target_pairs={{0,3},{1,2},{2,1},{3,0},{4,7},{5,6},{6,5},{7,4},{8,11},{9,10},{10,... | collective-permute-start | bytes 294920 | tf_op jit(solution)/shard_map/ppermute | solution.py:24
  20.6 8.5 %collective-permute-start.11 = (f32[32,768]{1,0:T(8,128)S(1)}, f32[32,768]{1,0:T(8,128)S(1)}, u32[]{:S(2)}, u32[]{:S(2)}) collective-permute-start(f32[32,768]{1,0:T(8,128)S(1)} %add.54.refs_0_), channel_id=1, source_target_pairs={{0,1},{1,0},{2,3},{3,2},{4,5},{5,4},{6,7},{7,6},{8,9},{9,8},{10,11... | collective-permute-start | bytes 294920 | tf_op jit(solution)/shard_map/ppermute | solution.py:24
  20.8 7.0 %collective-permute-start.6 = (f32[32,384]{1,0:T(8,128)S(1)}, f32[32,384]{1,0:T(8,128)S(1)}, u32[]{:S(2)}, u32[]{:S(2)}) collective-permute-start(f32[32,384]{1,0:T(8,128)S(1)} %next_solve.4), channel_id=1, source_target_pairs={{0,32},{32,0},{1,33},{33,1},{2,34},{34,2},{3,35},{35,3},{4,36},{36... | collective-permute-start | bytes 147464 | tf_op jit(solution)/shard_map/ppermute | solution.py:24
  27.8 3.0 %collective-permute-start.7 = (f32[32,384]{1,0:T(8,128)S(1)}, f32[32,384]{1,0:T(8,128)S(1)}, u32[]{:S(2)}, u32[]{:S(2)}) collective-permute-start(f32[32,384]{1,0:T(8,128)S(1)} %add.53.one_ref), channel_id=1, source_target_pairs={{0,64},{64,0},{1,65},{65,1},{2,66},{66,2},{3,67},{67,3},{4,68},{68... | collective-permute-start | bytes 147464 | tf_op jit(solution)/shard_map/ppermute | solution.py:24
  29.3 3.2 %collective-permute-start.12 = (f32[32,384]{1,0:T(8,128)S(1)}, f32[32,384]{1,0:T(8,128)S(1)}, u32[]{:S(2)}, u32[]{:S(2)}) collective-permute-start(f32[32,384]{1,0:T(8,128)S(1)} %next_solve.5), channel_id=1, source_target_pairs={{0,32},{32,0},{1,33},{33,1},{2,34},{34,2},{3,35},{35,3},{4,36},{36... | collective-permute-start | bytes 147464 | tf_op jit(solution)/shard_map/ppermute | solution.py:24
  31.0 5.1 %collective-permute-start.14 = (f32[32,768]{1,0:T(8,128)S(1)}, f32[32,768]{1,0:T(8,128)S(1)}, u32[]{:S(2)}, u32[]{:S(2)}) collective-permute-start(f32[32,768]{1,0:T(8,128)S(1)} %get-tuple-element.34), channel_id=1, source_target_pairs={{0,4},{1,5},{2,6},{3,7},{4,0},{5,1},{6,2},{7,3},{8,12},{9,13},{10,... | collective-permute-start | bytes 294920 | tf_op jit(solution)/shard_map/ppermute | solution.py:24
  32.5 3.3 %collective-permute-start.13 = (f32[32,384]{1,0:T(8,128)S(1)}, f32[32,384]{1,0:T(8,128)S(1)}, u32[]{:S(2)}, u32[]{:S(2)}) collective-permute-start(f32[32,384]{1,0:T(8,128)S(1)} %add.55.one_ref), channel_id=1, source_target_pairs={{0,64},{64,0},{1,65},{65,1},{2,66},{66,2},{3,67},{67,3},{4,68},{68... | collective-permute-start | bytes 147464 | tf_op jit(solution)/shard_map/ppermute | solution.py:24
  36.0 3.6 %collective-permute-start.20 = (f32[32,768]{1,0:T(8,128)S(1)}, f32[32,768]{1,0:T(8,128)S(1)}, u32[]{:S(2)}, u32[]{:S(2)}) collective-permute-start(f32[32,768]{1,0:T(8,128)S(1)} %get-tuple-element.37), channel_id=1, source_target_pairs={{0,4},{1,5},{2,6},{3,7},{4,0},{5,1},{6,2},{7,3},{8,12},{9,13},{10,... | collective-permute-start | bytes 294920 | tf_op jit(solution)/shard_map/ppermute | solution.py:24
  36.2 6.7 %collective-permute-start.15 = (f32[32,768]{1,0:T(8,128)S(1)}, f32[32,768]{1,0:T(8,128)S(1)}, u32[]{:S(2)}, u32[]{:S(2)}) collective-permute-start(f32[32,768]{1,0:T(8,128)S(1)} %add.56.refs_0_), channel_id=1, source_target_pairs={{0,2},{1,3},{2,0},{3,1},{4,6},{5,7},{6,4},{7,5},{8,10},{9,11},{10,... | collective-permute-start | bytes 294920 | tf_op jit(solution)/shard_map/ppermute | solution.py:24
  38.0 5.0 %collective-permute-start.16 = (f32[32,768]{1,0:T(8,128)S(1)}, f32[32,768]{1,0:T(8,128)S(1)}, u32[]{:S(2)}, u32[]{:S(2)}) collective-permute-start(f32[32,768]{1,0:T(8,128)S(1)} %add.56.refs_0_), channel_id=1, source_target_pairs={{0,3},{1,2},{2,1},{3,0},{4,7},{5,6},{6,5},{7,4},{8,11},{9,10},{10,... | collective-permute-start | bytes 294920 | tf_op jit(solution)/shard_map/ppermute | solution.py:24
  38.7 4.2 %collective-permute-start.17 = (f32[32,768]{1,0:T(8,128)S(1)}, f32[32,768]{1,0:T(8,128)S(1)}, u32[]{:S(2)}, u32[]{:S(2)}) collective-permute-start(f32[32,768]{1,0:T(8,128)S(1)} %add.56.refs_0_), channel_id=1, source_target_pairs={{0,1},{1,0},{2,3},{3,2},{4,5},{5,4},{6,7},{7,6},{8,9},{9,8},{10,11... | collective-permute-start | bytes 294920 | tf_op jit(solution)/shard_map/ppermute | solution.py:24
  39.6 15.2 %copy-start.4 = (s32[3,3,24]{2,1,0:T(4,128)S(1)}, s32[3,3,24]{2,1,0:T(4,128)}, u32[]{:S(2)}) copy-start(s32[3,3,24]{2,1,0:T(4,128)} %param.15) | copy-start | bytes 2596
  39.6 15.3 %copy-start.2 = (bf16[3,384,768]{2,1,0:T(8,128)(2,1)S(1)}, bf16[3,384,768]{2,1,0:T(8,128)(2,1)}, u32[]{:S(2)}) copy-start(bf16[3,384,768]{2,1,0:T(8,128)(2,1)} %factor_ref.1) | copy-start | bytes 5308420
  39.6 9.4 %collective-permute-start.21 = (f32[32,768]{1,0:T(8,128)S(1)}, f32[32,768]{1,0:T(8,128)S(1)}, u32[]{:S(2)}, u32[]{:S(2)}) collective-permute-start(f32[32,768]{1,0:T(8,128)S(1)} %add.58.refs_0_), channel_id=1, source_target_pairs={{0,2},{1,3},{2,0},{3,1},{4,6},{5,7},{6,4},{7,5},{8,10},{9,11},{10,... | collective-permute-start | bytes 294920 | tf_op jit(solution)/shard_map/ppermute | solution.py:24
  42.1 6.9 %collective-permute-start.22 = (f32[32,768]{1,0:T(8,128)S(1)}, f32[32,768]{1,0:T(8,128)S(1)}, u32[]{:S(2)}, u32[]{:S(2)}) collective-permute-start(f32[32,768]{1,0:T(8,128)S(1)} %add.58.refs_0_), channel_id=1, source_target_pairs={{0,3},{1,2},{2,1},{3,0},{4,7},{5,6},{6,5},{7,4},{8,11},{9,10},{10,... | collective-permute-start | bytes 294920 | tf_op jit(solution)/shard_map/ppermute | solution.py:24
  42.9 6.1 %collective-permute-start.23 = (f32[32,768]{1,0:T(8,128)S(1)}, f32[32,768]{1,0:T(8,128)S(1)}, u32[]{:S(2)}, u32[]{:S(2)}) collective-permute-start(f32[32,768]{1,0:T(8,128)S(1)} %add.58.refs_0_), channel_id=1, source_target_pairs={{0,1},{1,0},{2,3},{3,2},{4,5},{5,4},{6,7},{7,6},{8,9},{9,8},{10,11... | collective-permute-start | bytes 294920 | tf_op jit(solution)/shard_map/ppermute | solution.py:24
  43.1 9.5 %collective-permute-start.18 = (f32[32,384]{1,0:T(8,128)S(1)}, f32[32,384]{1,0:T(8,128)S(1)}, u32[]{:S(2)}, u32[]{:S(2)}) collective-permute-start(f32[32,384]{1,0:T(8,128)S(1)} %next_solve.6), channel_id=1, source_target_pairs={{0,32},{32,0},{1,33},{33,1},{2,34},{34,2},{3,35},{35,3},{4,36},{36... | collective-permute-start | bytes 147464 | tf_op jit(solution)/shard_map/ppermute | solution.py:24
  49.2 4.7 %collective-permute-start.24 = (f32[32,384]{1,0:T(8,128)S(1)}, f32[32,384]{1,0:T(8,128)S(1)}, u32[]{:S(2)}, u32[]{:S(2)}) collective-permute-start(f32[32,384]{1,0:T(8,128)S(1)} %next_solve.7), channel_id=1, source_target_pairs={{0,32},{32,0},{1,33},{33,1},{2,34},{34,2},{3,35},{35,3},{4,36},{36... | collective-permute-start | bytes 147464 | tf_op jit(solution)/shard_map/ppermute | solution.py:24
  52.7 3.8 %collective-permute-start.19 = (f32[32,384]{1,0:T(8,128)S(1)}, f32[32,384]{1,0:T(8,128)S(1)}, u32[]{:S(2)}, u32[]{:S(2)}) collective-permute-start(f32[32,384]{1,0:T(8,128)S(1)} %add.57.one_ref), channel_id=1, source_target_pairs={{0,64},{64,0},{1,65},{65,1},{2,66},{66,2},{3,67},{67,3},{4,68},{68... | collective-permute-start | bytes 147464 | tf_op jit(solution)/shard_map/ppermute | solution.py:24
  54.0 3.0 %collective-permute-start.25 = (f32[32,384]{1,0:T(8,128)S(1)}, f32[32,384]{1,0:T(8,128)S(1)}, u32[]{:S(2)}, u32[]{:S(2)}) collective-permute-start(f32[32,384]{1,0:T(8,128)S(1)} %add.59.one_ref), channel_id=1, source_target_pairs={{0,64},{64,0},{1,65},{65,1},{2,66},{66,2},{3,67},{67,3},{4,68},{68... | collective-permute-start | bytes 147464 | tf_op jit(solution)/shard_map/ppermute | solution.py:24
  56.7 23.4 %copy-start.1 = (bf16[768,1536]{1,0:T(8,128)(2,1)S(1)}, bf16[768,1536]{1,0:T(8,128)(2,1)}, u32[]{:S(2)}) copy-start(bf16[768,1536]{1,0:T(8,128)(2,1)} %inverse_ref.1) | copy-start | bytes 7077892
  65.7 4.3 %collective-permute-start.26 = (f32[8,768]{1,0:T(8,128)S(1)}, f32[8,768]{1,0:T(8,128)S(1)}, u32[]{:S(2)}, u32[]{:S(2)}) collective-permute-start(f32[8,768]{1,0:T(8,128)S(1)} %reduce_sum.9), channel_id=1, source_target_pairs={{0,128},{128,0},{1,129},{129,1},{2,130},{130,2},{3,131},{131,3},{4... | collective-permute-start | bytes 73736 | tf_op jit(solution)/shard_map/ppermute | solution.py:24
  70.0 4.2 %collective-permute-start.27 = (f32[8,768]{1,0:T(8,128)S(1)}, f32[8,768]{1,0:T(8,128)S(1)}, u32[]{:S(2)}, u32[]{:S(2)}) collective-permute-start(f32[8,768]{1,0:T(8,128)S(1)} %add.61), channel_id=1, source_target_pairs={{0,8},{8,0},{16,24},{24,16},{1,9},{9,1},{17,25},{25,17},{2,10},{10... | collective-permute-start | bytes 73736 | tf_op jit(solution)/shard_map/ppermute | solution.py:24
  74.2 5.8 %collective-permute-start.28 = (f32[8,768]{1,0:T(8,128)S(1)}, f32[8,768]{1,0:T(8,128)S(1)}, u32[]{:S(2)}, u32[]{:S(2)}) collective-permute-start(f32[8,768]{1,0:T(8,128)S(1)} %add.62.one_ref), channel_id=1, source_target_pairs={{0,24},{8,16},{16,8},{24,0},{1,25},{9,17},{17,9},{25,1},{2,26},{10... | collective-permute-start | bytes 73736 | tf_op jit(solution)/shard_map/ppermute | solution.py:24
  80.4 6.7 %collective-permute-start.29 = (f32[8,1536]{1,0:T(8,128)S(1)}, f32[8,1536]{1,0:T(8,128)S(1)}, u32[]{:S(2)}, u32[]{:S(2)}) collective-permute-start(f32[8,1536]{1,0:T(8,128)S(1)} %root_part.1), channel_id=1, source_target_pairs={{0,32},{32,0},{1,33},{33,1},{2,34},{34,2},{3,35},{35,3},{4,36},{36... | collective-permute-start | bytes 147464 | tf_op jit(solution)/shard_map/ppermute | solution.py:24
  87.2 2.9 %collective-permute-start.30 = (f32[8,1536]{1,0:T(8,128)S(1)}, f32[8,1536]{1,0:T(8,128)S(1)}, u32[]{:S(2)}, u32[]{:S(2)}) collective-permute-start(f32[8,1536]{1,0:T(8,128)S(1)} %add.63), channel_id=1, source_target_pairs={{0,64},{64,0},{1,65},{65,1},{2,66},{66,2},{3,67},{67,3},{4,68},{68... | collective-permute-start | bytes 147464 | tf_op jit(solution)/shard_map/ppermute | solution.py:24

commit v9 on v8

--- a/solution.py
+++ b/solution.py
@@ -10,7 +10,8 @@
 TILE = 128
 PARTS = 2
 PROW = ("xl", "core")
-OWN = "own"
+PCOL = "pcol"
+SUBTREES = 8
 SCOPED_BYTES = 4 << 20
 F32 = jnp.float32
 BF16 = jnp.bfloat16
@@ -24,14 +25,11 @@
     return lax.ppermute(shard, axis, [(i, i ^ bit) for i in range(lax.axis_size(axis))])
 
 
-def swap_blocks(blocks):
-    order = list(range(lax.axis_size(OWN)))[::-1]
-    return lax.all_to_all(blocks, OWN, 0, 0, axis_index_groups=[order], tiled=True)
-
-
-def to_everyone(shard):
-    count = lax.axis_size(OWN)
-    return swap_blocks(jnp.broadcast_to(shard[None], (count, *shard.shape)))
+def to_everyone(shard, axis):
+    count = lax.axis_size(axis)
+    return lax.all_to_all(
+        jnp.broadcast_to(shard[None], (count, *shard.shape)), axis, 0, 0, tiled=True
+    )
 
 
 def call(body, outs, args, specs=None, scratch=(), name=None):
@@ -260,8 +258,8 @@
 
 
 def owner_sums(partial_sum):
-    pair = partial_sum + partner(partial_sum, OWN, 4)
-    return [pair] + [partner(pair, OWN, bit) for bit in (2, 3, 1)]
+    pair = partial_sum + partner(partial_sum, PCOL, 4)
+    return [pair] + [partner(pair, PCOL, bit) for bit in (2, 3, 1)]
 
 
 def shards(
@@ -270,7 +268,8 @@
     out_cols = inner_factor.shape[2]
     rhs_count = root_rhs.shape[0]
     tiles = out_cols // TILE
-    tree = lax.axis_index("zt")
+    owners = lax.axis_size(PCOL) * lax.axis_size("grid") // SUBTREES
+    tree = lax.axis_index(PCOL) // owners
     first_tile = lax.axis_index(PROW) * tiles
     inner_tiles = lax.dynamic_slice_in_dim(inner_mask, first_tile, tiles, 2)
     root_tiles = lax.dynamic_slice_in_dim(root_mask, first_tile, tiles, 2)
@@ -293,33 +292,41 @@
         locals_.append(root_local)
     root_local = jnp.concatenate(locals_)
 
-    owners = lax.axis_size(OWN)
-    few = rhs_count // owners
-    place = owners - 1 - lax.axis_index(OWN)
-    own_rows = swap_blocks(root_local.reshape(owners, few, out_cols)).sum(axis=0)
-    sub_solution, across = lax.optimization_barrier(
-        (stacked(list(zip(*solved))), partner(own_rows, "grid"))
-    )
-    total = own_rows + across
-    total = total + partner(total, "zt", 1)
-    rhs_rows = lax.dynamic_slice_in_dim(root_rhs, place * few, few, 0)
-    part = root_part(rhs_rows, (total, partner(total, "zt", 3)), root_inverse)
-    pair, other = prow_halves(part)
-    root_solution = to_everyone(pair + other).reshape(rhs_count, part.shape[1])
+    few = rhs_count // lax.axis_size(PCOL)
+    first_row, first, root_local = lax.optimization_barrier(
+        (lax.axis_index(PCOL) * few, lax.axis_index("core") == 0, root_local)
+    )
+    own_rows = lax.all_to_all(
+        root_local.reshape(-1, few, out_cols), PCOL, 0, 0, tiled=True
+    ).sum(axis=0)
+    rhs_rows = lax.dynamic_slice(
+        root_rhs, (first_row, 0), (few, out_cols), allow_negative_indices=False
+    )
+    sub_solution, across, rhs_rows = lax.optimization_barrier(
+        (stacked(list(zip(*solved))), partner(own_rows, "grid"), rhs_rows)
+    )
+    part = root_part(rhs_rows, (own_rows, across), root_inverse)
+    half = part.shape[1] // 2
+    low, high = part[:, :half], part[:, half:]
+    mine = jnp.where(first, low, high) + partner(jnp.where(first, high, low), "core")
+    mine = mine + partner(mine, "xl")
+    columns = to_everyone(mine, PCOL).reshape(rhs_count, half)
+    others = partner(columns, "core")
+    root_solution = jnp.concatenate(
+        [jnp.where(first, columns, others), jnp.where(first, others, columns)], axis=1
+    )
     return (sub_solution, root_solution)
 
 
 def solution(mesh):
-    prow, pcol = mesh.shape["prow"], mesh.shape["pcol"]
     cores = 2
-    trees = 8 // mesh.shape["grid"]
     fine = Mesh(
         mesh.devices.reshape(
-            mesh.shape["grid"], prow // cores, cores, trees, pcol // trees
+            mesh.shape["grid"], mesh.shape["prow"] // cores, cores, mesh.shape["pcol"]
         ),
-        ("grid", "xl", "core", "zt", "own"),
-    )
-    columns = ("grid", "zt", "own")
+        ("grid", "xl", "core", PCOL),
+    )
+    columns = ("grid", PCOL)
     return jax.shard_map(
         shards,
         mesh=fine,

time: 102 us -> 107 us (1.049); the launches traced: 101 us -> 107 us
  blocking collectives: 18.1 us -> 32.1 us
  starting transfers between devices: 55.9 us -> 49.9 us
  waiting for transfers between devices: 15.4 us -> 13.4 us
    all_to_all x2, blocking collectives: 18.1 us -> 32.1 us  [the longest x1 19.3 us: shards(): lax.all_to_all(root_local.reshape(-1, few, out_cols), PCOL, 0, 0, tiled=T...]
    ppermute x31 -> x30, starting transfers between devices: 55.9 us -> 49.9 us  [partner(): lax.ppermute(shard, axis, [(i, i ^ bit) for i in range(lax.axis_size(axis...]
    ppermute x31 -> x30, waiting for transfers between devices: 15.4 us -> 13.4 us  [partner(): lax.ppermute(shard, axis, [(i, i ^ bit) for i in range(lax.axis_size(axis...]
  transfers between devices with their start and end apart: 31 -> 30, of which waited for: 13 -> 12; matrix products, arithmetic and copies ran while one was open for 0% -> 0% of each run, Pallas kernels for 7% -> 6%
where the time goes in v9:
time: 107 us
  starting transfers between devices  49.9 us (47%)
  blocking collectives  32.1 us (30%)
  waiting for transfers between devices  13.4 us (13%)
  Pallas kernels  9.04 us (8%)
    ppermute x30, starting transfers between devices, partner(): lax.ppermute(shard, axis, [(i, i ^ bit) for i in range(lax.axis_size(axis...  49.9 us
    all_to_all x1, blocking collectives, shards(): lax.all_to_all(root_local.reshape(-1, few, out_cols), PCOL, 0, 0, tiled=T...  19.3 us
    ppermute x30, waiting for transfers between devices, partner(): lax.ppermute(shard, axis, [(i, i ^ bit) for i in range(lax.axis_size(axis...  13.4 us
    all_to_all x1, blocking collectives, to_everyone(): lax.all_to_all(jnp.broadcast_to(shard[None], (count, *shard.shape)), axis...  12.9 us
    pallas_call x17, Pallas kernels, call(): pl.pallas_call(body, out_shape=[pltpu.VMEM(shape, kind) for shape, kind i...  8.28 us
  transfers between devices with their start and end apart: 30, of which 12 were waited for; matrix products, arithmetic and copies ran while one was open for 0% of the time, Pallas kernels for 6%

profile of v9, /device:TPU:1, one launch (start us, length us, event | category | flops | bytes accessed | tf_op | source)
XLA Modules:
  0.0 106.9 jit_solution(8579984606982976112)
XLA Ops:
  0.7 1.6 %first_solve.1 = f32[64,384]{1,0:T(8,128)S(1)} custom-call(s32[1]{0:T(128)} %bitcast.tree_ref, f32[4,3,64,768]{3,2,1,0:T(8,128)} %rhs_hbm.3, bf16[3,768,384]{2,1,0:T(8,128)(2,1)} %inverse_hbm.3), custom_call_target="tpu_custom_call" | custom-call | tf_op jit(solution)/shard_map/first_solve/pallas_call | solution.py:41
  2.3 3.3 %collective-permute-start = (f32[64,384]{1,0:T(8,128)S(1)}, f32[64,384]{1,0:T(8,128)S(1)}, u32[]{:S(2)}, u32[]{:S(2)}) collective-permute-start(f32[64,384]{1,0:T(8,128)S(1)} %first_solve.1), channel_id=1, source_target_pairs={{0,32},{32,0},{1,33},{33,1},{2,34},{34,2},{3,35},{35,3},{4,36},{36... | collective-permute-start | bytes 294920 | tf_op jit(solution)/shard_map/ppermute | solution.py:25
  5.6 0.9 collective-permute-done
  6.6 0.1 collective-permute-start.1
  6.7 2.6 %stage.1 = (bf16[3,384,768]{2,1,0:T(8,128)(2,1)S(1)}, bf16[2,768,384]{2,1,0:T(8,128)(2,1)S(1)}, f32[2,64,768]{2,1,0:T(8,128)S(1)}) custom-call(s32[1]{0:T(128)} %bitcast.tree_ref, s32[3,3,6]{2,1,0:T(4,128)S(1)} %constant_dynamic-slice_fusion.2.mask_ref, f32[4,3,64,768]{3,2,1,0:T(8,128)} %rhs_hbm.3, bf16[3,768,384]{2,1,0:T(8,128)(2,1)} %inverse_hbm.3, ...), custom_call_target="tpu_custom_call" | custom-call | tf_op jit(solution)/shard_map/stage/pallas_call | solution.py:41
  9.3 1.4 %collective-permute-done.1.other_ref = f32[64,384]{1,0:T(8,128)S(1)} collective-permute-done((f32[64,384]{1,0:T(8,128)S(1)}, f32[64,384]{1,0:T(8,128)S(1)}, u32[]{:S(2)}, u32[]{:S(2)}) %collective-permute-start.1) | collective-permute-done | bytes 98336 | tf_op jit(solution)/shard_map/ppermute | solution.py:25
  10.7 0.2 kept_update.5
  10.9 0.1 collective-permute-start.2
  11.0 1.5 %collective-permute-start.8 = (f32[32,768]{1,0:T(8,128)S(1)}, f32[32,768]{1,0:T(8,128)S(1)}, u32[]{:S(2)}, u32[]{:S(2)}) collective-permute-start(f32[32,768]{1,0:T(8,128)S(1)} %get-tuple-element.35), channel_id=1, source_target_pairs={{0,4},{1,5},{2,6},{3,7},{4,0},{5,1},{6,2},{7,3},{8,12},{9,13},{10,... | collective-permute-start | bytes 294920 | tf_op jit(solution)/shard_map/ppermute | solution.py:25
  12.4 2.0 %collective-permute-done.2 = f32[32,768]{1,0:T(8,128)S(1)} collective-permute-done((f32[32,768]{1,0:T(8,128)S(1)}, f32[32,768]{1,0:T(8,128)S(1)}, u32[]{:S(2)}, u32[]{:S(2)}) %collective-permute-start.2) | collective-permute-done | bytes 98336 | tf_op jit(solution)/shard_map/ppermute | solution.py:25
  14.5 1.4 %collective-permute-start.3 = (f32[32,768]{1,0:T(8,128)S(1)}, f32[32,768]{1,0:T(8,128)S(1)}, u32[]{:S(2)}, u32[]{:S(2)}) collective-permute-start(f32[32,768]{1,0:T(8,128)S(1)} %add.44.refs_0_), channel_id=1, source_target_pairs={{0,2},{1,3},{2,0},{3,1},{4,6},{5,7},{6,4},{7,5},{8,10},{9,11},{10,... | collective-permute-start | bytes 294920 | tf_op jit(solution)/shard_map/ppermute | solution.py:25
  15.9 0.8 collective-permute-start.4
  16.7 0.5 collective-permute-start.5
  17.2 2.7 %collective-permute-start.9 = (f32[32,768]{1,0:T(8,128)S(1)}, f32[32,768]{1,0:T(8,128)S(1)}, u32[]{:S(2)}, u32[]{:S(2)}) collective-permute-start(f32[32,768]{1,0:T(8,128)S(1)} %add.46.refs_0_), channel_id=1, source_target_pairs={{0,2},{1,3},{2,0},{3,1},{4,6},{5,7},{6,4},{7,5},{8,10},{9,11},{10,... | collective-permute-start | bytes 294920 | tf_op jit(solution)/shard_map/ppermute | solution.py:25
  19.9 0.8 collective-permute-start.10
  20.7 0.2 next_solve.4
  20.9 6.1 %collective-permute-start.6 = (f32[32,384]{1,0:T(8,128)S(1)}, f32[32,384]{1,0:T(8,128)S(1)}, u32[]{:S(2)}, u32[]{:S(2)}) collective-permute-start(f32[32,384]{1,0:T(8,128)S(1)} %next_solve.4), channel_id=1, source_target_pairs={{0,32},{32,0},{1,33},{33,1},{2,34},{34,2},{3,35},{35,3},{4,36},{36... | collective-permute-start | bytes 147464 | tf_op jit(solution)/shard_map/ppermute | solution.py:25
  26.9 0.9 collective-permute-done.6
  27.8 1.3 %collective-permute-start.7 = (f32[32,384]{1,0:T(8,128)S(1)}, f32[32,384]{1,0:T(8,128)S(1)}, u32[]{:S(2)}, u32[]{:S(2)}) collective-permute-start(f32[32,384]{1,0:T(8,128)S(1)} %add.45.one_ref), channel_id=1, source_target_pairs={{0,64},{64,0},{1,65},{65,1},{2,66},{66,2},{3,67},{67,3},{4,68},{68... | collective-permute-start | bytes 147464 | tf_op jit(solution)/shard_map/ppermute | solution.py:25
  29.1 0.2 next_solve.5
  29.3 1.0 collective-permute-start.12
  30.3 0.2 early_update.4.refs_0_
  30.5 0.3 collective-permute-done.7.other_ref
  30.8 0.2 kept_update.6
  31.0 1.5 %collective-permute-start.14 = (f32[32,768]{1,0:T(8,128)S(1)}, f32[32,768]{1,0:T(8,128)S(1)}, u32[]{:S(2)}, u32[]{:S(2)}) collective-permute-start(f32[32,768]{1,0:T(8,128)S(1)} %get-tuple-element.38), channel_id=1, source_target_pairs={{0,4},{1,5},{2,6},{3,7},{4,0},{5,1},{6,2},{7,3},{8,12},{9,13},{10,... | collective-permute-start | bytes 294920 | tf_op jit(solution)/shard_map/ppermute | solution.py:25
  32.5 0.7 collective-permute-start.13
  33.2 0.2 early_update.5.refs_0_
  33.4 2.5 %collective-permute-done.13.other_ref = f32[32,384]{1,0:T(8,128)S(1)} collective-permute-done((f32[32,384]{1,0:T(8,128)S(1)}, f32[32,384]{1,0:T(8,128)S(1)}, u32[]{:S(2)}, u32[]{:S(2)}) %collective-permute-start.13) | collective-permute-done | bytes 49184 | tf_op jit(solution)/shard_map/ppermute | solution.py:25
  35.8 0.2 kept_update.7
  36.0 0.1 collective-permute-start.20
  36.2 1.8 %collective-permute-start.15 = (f32[32,768]{1,0:T(8,128)S(1)}, f32[32,768]{1,0:T(8,128)S(1)}, u32[]{:S(2)}, u32[]{:S(2)}) collective-permute-start(f32[32,768]{1,0:T(8,128)S(1)} %add.48.refs_0_), channel_id=1, source_target_pairs={{0,2},{1,3},{2,0},{3,1},{4,6},{5,7},{6,4},{7,5},{8,10},{9,11},{10,... | collective-permute-start | bytes 294920 | tf_op jit(solution)/shard_map/ppermute | solution.py:25
  38.0 0.8 collective-permute-start.16
  38.7 0.2 collective-permute-start.17
  38.9 0.7 collective-permute-done.20
  39.6 2.5 %collective-permute-start.21 = (f32[32,768]{1,0:T(8,128)S(1)}, f32[32,768]{1,0:T(8,128)S(1)}, u32[]{:S(2)}, u32[]{:S(2)}) collective-permute-start(f32[32,768]{1,0:T(8,128)S(1)} %add.50.refs_0_), channel_id=1, source_target_pairs={{0,2},{1,3},{2,0},{3,1},{4,6},{5,7},{6,4},{7,5},{8,10},{9,11},{10,... | collective-permute-start | bytes 294920 | tf_op jit(solution)/shard_map/ppermute | solution.py:25
  42.1 0.8 collective-permute-start.22
  42.9 0.2 next_solve.6
  43.1 5.9 %collective-permute-start.18 = (f32[32,384]{1,0:T(8,128)S(1)}, f32[32,384]{1,0:T(8,128)S(1)}, u32[]{:S(2)}, u32[]{:S(2)}) collective-permute-start(f32[32,384]{1,0:T(8,128)S(1)} %next_solve.6), channel_id=1, source_target_pairs={{0,32},{32,0},{1,33},{33,1},{2,34},{34,2},{3,35},{35,3},{4,36},{36... | collective-permute-start | bytes 147464 | tf_op jit(solution)/shard_map/ppermute | solution.py:25
  49.0 0.2 next_solve.7
  49.2 3.4 %collective-permute-start.24 = (f32[32,384]{1,0:T(8,128)S(1)}, f32[32,384]{1,0:T(8,128)S(1)}, u32[]{:S(2)}, u32[]{:S(2)}) collective-permute-start(f32[32,384]{1,0:T(8,128)S(1)} %next_solve.7), channel_id=1, source_target_pairs={{0,32},{32,0},{1,33},{33,1},{2,34},{34,2},{3,35},{35,3},{4,36},{36... | collective-permute-start | bytes 147464 | tf_op jit(solution)/shard_map/ppermute | solution.py:25
  52.6 1.3 %collective-permute-start.19 = (f32[32,384]{1,0:T(8,128)S(1)}, f32[32,384]{1,0:T(8,128)S(1)}, u32[]{:S(2)}, u32[]{:S(2)}) collective-permute-start(f32[32,384]{1,0:T(8,128)S(1)} %add.49.one_ref), channel_id=1, source_target_pairs={{0,64},{64,0},{1,65},{65,1},{2,66},{66,2},{3,67},{67,3},{4,68},{68... | collective-permute-start | bytes 147464 | tf_op jit(solution)/shard_map/ppermute | solution.py:25
  54.0 0.8 collective-permute-start.25
  54.9 0.9 masked.1.refs_2_.factor_ref
  55.8 0.3 early_update.6.refs_0_
  56.1 0.3 early_update.7.refs_0_
  56.4 0.2 kept_update.8
  56.7 0.3 collective-permute-done.25.other_ref
  57.0 0.2 kept_update.9
  57.2 0.1 reshape.15
  57.3 19.3 %all_to_all.10 = f32[32,2,768]{2,1,0:T(2,128)S(1)} all-to-all(f32[32,2,768]{2,1,0:T(2,128)S(1)} %reshape.15), channel_id=1, replica_groups=mesh['grid'=2,'xl'=2,'core'=2,'pcol'=32] {'pcol'}, dimensions={0} | all-to-all | bytes 393216 | tf_op jit(solution)/shard_map/all_to_all | solution.py:299
  76.6 0.1 reduce_sum.9.one_ref
  76.7 2.5 %collective-permute-start.26 = (f32[2,768]{1,0:T(2,128)S(1)}, f32[2,768]{1,0:T(2,128)S(1)}, u32[]{:S(2)}, u32[]{:S(2)}) collective-permute-start(f32[2,768]{1,0:T(2,128)S(1)} %reduce_sum.9.one_ref), channel_id=1, source_target_pairs={{0,128},{128,0},{1,129},{129,1},{2,130},{130,2},{3,131},{131,3},{4... | collective-permute-start | bytes 18440 | tf_op jit(solution)/shard_map/ppermute | solution.py:25
  79.2 0.8 stacked.1
  79.9 0.8 collective-permute-done.26.other_ref
  80.7 0.4 root_part.1
  81.2 4.2 %collective-permute-start.27 = (f32[2,768]{1,0:T(2,128)S(1)}, f32[2,768]{1,0:T(2,128)S(1)}, u32[]{:S(2)}, u32[]{:S(2)}) collective-permute-start(f32[2,768]{1,0:T(2,128)S(1)} %broadcast_select_fusion.2), channel_id=1, source_target_pairs={{0,32},{32,0},{1,33},{33,1},{2,34},{34,2},{3,35},{35,3},{4,36},{36... | collective-permute-start | bytes 18440 | tf_op jit(solution)/shard_map/ppermute | solution.py:25
  85.4 0.8 collective-permute-done.27
  86.2 0.8 collective-permute-start.28
  87.0 1.7 %collective-permute-done.28 = f32[2,768]{1,0:T(2,128)S(1)} collective-permute-done((f32[2,768]{1,0:T(2,128)S(1)}, f32[2,768]{1,0:T(2,128)S(1)}, u32[]{:S(2)}, u32[]{:S(2)}) %collective-permute-start.28) | collective-permute-done | bytes 6176 | tf_op jit(solution)/shard_map/ppermute | solution.py:25
  88.7 12.9 %all_to_all.11 = f32[32,2,768]{2,1,0:T(2,128)S(1)} all-to-all(f32[32,2,768]{2,1,0:T(2,128)S(1)} %broadcast_in_dim.2), channel_id=1, replica_groups=mesh['grid'=2,'xl'=2,'core'=2,'pcol'=32] {'pcol'}, dimensions={0} | all-to-all | bytes 393216 | tf_op jit(solution)/shard_map/all_to_all | solution.py:30
  101.6 0.1 reshape.16
  101.7 3.2 %collective-permute-start.29 = (f32[64,768]{1,0:T(8,128)S(1)}, f32[64,768]{1,0:T(8,128)S(1)}, u32[]{:S(2)}, u32[]{:S(2)}) collective-permute-start(f32[64,768]{1,0:T(8,128)S(1)} %reshape.16), channel_id=1, source_target_pairs={{0,32},{32,0},{1,33},{33,1},{2,34},{34,2},{3,35},{35,3},{4,36},{36... | collective-permute-start | bytes 589832 | tf_op jit(solution)/shard_map/ppermute | solution.py:25
  105.0 1.1 %collective-permute-done.29 = f32[64,768]{1,0:T(8,128)S(1)} collective-permute-done((f32[64,768]{1,0:T(8,128)S(1)}, f32[64,768]{1,0:T(8,128)S(1)}, u32[]{:S(2)}, u32[]{:S(2)}) %collective-permute-start.29) | collective-permute-done | bytes 196640 | tf_op jit(solution)/shard_map/ppermute | solution.py:25
  106.1 0.8 pad_maximum_fusion
  (48 shorter events, 0.5 us)
Async XLA Ops:
  0.6 78.5 %copy-start = (f32[64,768]{1,0:T(8,128)S(1)}, f32[64,768]{1,0:T(8,128)}, u32[]{:S(2)}) copy-start(f32[64,768]{1,0:T(8,128)} %param.9) | copy-start | bytes 589828
  0.7 6.0 %copy-start.3 = (s32[3,3,24]{2,1,0:T(4,128)S(1)}, s32[3,3,24]{2,1,0:T(4,128)}, u32[]{:S(2)}) copy-start(s32[3,3,24]{2,1,0:T(4,128)} %param.13) | copy-start | bytes 2596
  2.3 4.3 %collective-permute-start = (f32[64,384]{1,0:T(8,128)S(1)}, f32[64,384]{1,0:T(8,128)S(1)}, u32[]{:S(2)}, u32[]{:S(2)}) collective-permute-start(f32[64,384]{1,0:T(8,128)S(1)} %first_solve.1), channel_id=1, source_target_pairs={{0,32},{32,0},{1,33},{33,1},{2,34},{34,2},{3,35},{35,3},{4,36},{36... | collective-permute-start | bytes 294920 | tf_op jit(solution)/shard_map/ppermute | solution.py:25
  6.6 4.1 %collective-permute-start.1 = (f32[64,384]{1,0:T(8,128)S(1)}, f32[64,384]{1,0:T(8,128)S(1)}, u32[]{:S(2)}, u32[]{:S(2)}) collective-permute-start(f32[64,384]{1,0:T(8,128)S(1)} %add.41.one_ref), channel_id=1, source_target_pairs={{0,64},{64,0},{1,65},{65,1},{2,66},{66,2},{3,67},{67,3},{4,68},{68... | collective-permute-start | bytes 294920 | tf_op jit(solution)/shard_map/ppermute | solution.py:25
  10.9 3.6 %collective-permute-start.2 = (f32[32,768]{1,0:T(8,128)S(1)}, f32[32,768]{1,0:T(8,128)S(1)}, u32[]{:S(2)}, u32[]{:S(2)}) collective-permute-start(f32[32,768]{1,0:T(8,128)S(1)} %get-tuple-element.31), channel_id=1, source_target_pairs={{0,4},{1,5},{2,6},{3,7},{4,0},{5,1},{6,2},{7,3},{8,12},{9,13},{10,... | collective-permute-start | bytes 294920 | tf_op jit(solution)/shard_map/ppermute | solution.py:25
  11.0 6.2 %collective-permute-start.8 = (f32[32,768]{1,0:T(8,128)S(1)}, f32[32,768]{1,0:T(8,128)S(1)}, u32[]{:S(2)}, u32[]{:S(2)}) collective-permute-start(f32[32,768]{1,0:T(8,128)S(1)} %get-tuple-element.35), channel_id=1, source_target_pairs={{0,4},{1,5},{2,6},{3,7},{4,0},{5,1},{6,2},{7,3},{8,12},{9,13},{10,... | collective-permute-start | bytes 294920 | tf_op jit(solution)/shard_map/ppermute | solution.py:25
  14.5 6.2 %collective-permute-start.3 = (f32[32,768]{1,0:T(8,128)S(1)}, f32[32,768]{1,0:T(8,128)S(1)}, u32[]{:S(2)}, u32[]{:S(2)}) collective-permute-start(f32[32,768]{1,0:T(8,128)S(1)} %add.44.refs_0_), channel_id=1, source_target_pairs={{0,2},{1,3},{2,0},{3,1},{4,6},{5,7},{6,4},{7,5},{8,10},{9,11},{10,... | collective-permute-start | bytes 294920 | tf_op jit(solution)/shard_map/ppermute | solution.py:25
  15.9 4.8 %collective-permute-start.4 = (f32[32,768]{1,0:T(8,128)S(1)}, f32[32,768]{1,0:T(8,128)S(1)}, u32[]{:S(2)}, u32[]{:S(2)}) collective-permute-start(f32[32,768]{1,0:T(8,128)S(1)} %add.44.refs_0_), channel_id=1, source_target_pairs={{0,3},{1,2},{2,1},{3,0},{4,7},{5,6},{6,5},{7,4},{8,11},{9,10},{10,... | collective-permute-start | bytes 294920 | tf_op jit(solution)/shard_map/ppermute | solution.py:25
  16.7 4.0 %collective-permute-start.5 = (f32[32,768]{1,0:T(8,128)S(1)}, f32[32,768]{1,0:T(8,128)S(1)}, u32[]{:S(2)}, u32[]{:S(2)}) collective-permute-start(f32[32,768]{1,0:T(8,128)S(1)} %add.44.refs_0_), channel_id=1, source_target_pairs={{0,1},{1,0},{2,3},{3,2},{4,5},{5,4},{6,7},{7,6},{8,9},{9,8},{10,11... | collective-permute-start | bytes 294920 | tf_op jit(solution)/shard_map/ppermute | solution.py:25
  17.2 11.9 %collective-permute-start.9 = (f32[32,768]{1,0:T(8,128)S(1)}, f32[32,768]{1,0:T(8,128)S(1)}, u32[]{:S(2)}, u32[]{:S(2)}) collective-permute-start(f32[32,768]{1,0:T(8,128)S(1)} %add.46.refs_0_), channel_id=1, source_target_pairs={{0,2},{1,3},{2,0},{3,1},{4,6},{5,7},{6,4},{7,5},{8,10},{9,11},{10,... | collective-permute-start | bytes 294920 | tf_op jit(solution)/shard_map/ppermute | solution.py:25
  19.9 9.2 %collective-permute-start.10 = (f32[32,768]{1,0:T(8,128)S(1)}, f32[32,768]{1,0:T(8,128)S(1)}, u32[]{:S(2)}, u32[]{:S(2)}) collective-permute-start(f32[32,768]{1,0:T(8,128)S(1)} %add.46.refs_0_), channel_id=1, source_target_pairs={{0,3},{1,2},{2,1},{3,0},{4,7},{5,6},{6,5},{7,4},{8,11},{9,10},{10,... | collective-permute-start | bytes 294920 | tf_op jit(solution)/shard_map/ppermute | solution.py:25
  20.6 8.5 %collective-permute-start.11 = (f32[32,768]{1,0:T(8,128)S(1)}, f32[32,768]{1,0:T(8,128)S(1)}, u32[]{:S(2)}, u32[]{:S(2)}) collective-permute-start(f32[32,768]{1,0:T(8,128)S(1)} %add.46.refs_0_), channel_id=1, source_target_pairs={{0,1},{1,0},{2,3},{3,2},{4,5},{5,4},{6,7},{7,6},{8,9},{9,8},{10,11... | collective-permute-start | bytes 294920 | tf_op jit(solution)/shard_map/ppermute | solution.py:25
  20.9 7.0 %collective-permute-start.6 = (f32[32,384]{1,0:T(8,128)S(1)}, f32[32,384]{1,0:T(8,128)S(1)}, u32[]{:S(2)}, u32[]{:S(2)}) collective-permute-start(f32[32,384]{1,0:T(8,128)S(1)} %next_solve.4), channel_id=1, source_target_pairs={{0,32},{32,0},{1,33},{33,1},{2,34},{34,2},{3,35},{35,3},{4,36},{36... | collective-permute-start | bytes 147464 | tf_op jit(solution)/shard_map/ppermute | solution.py:25
  27.8 3.0 %collective-permute-start.7 = (f32[32,384]{1,0:T(8,128)S(1)}, f32[32,384]{1,0:T(8,128)S(1)}, u32[]{:S(2)}, u32[]{:S(2)}) collective-permute-start(f32[32,384]{1,0:T(8,128)S(1)} %add.45.one_ref), channel_id=1, source_target_pairs={{0,64},{64,0},{1,65},{65,1},{2,66},{66,2},{3,67},{67,3},{4,68},{68... | collective-permute-start | bytes 147464 | tf_op jit(solution)/shard_map/ppermute | solution.py:25
  29.3 3.2 %collective-permute-start.12 = (f32[32,384]{1,0:T(8,128)S(1)}, f32[32,384]{1,0:T(8,128)S(1)}, u32[]{:S(2)}, u32[]{:S(2)}) collective-permute-start(f32[32,384]{1,0:T(8,128)S(1)} %next_solve.5), channel_id=1, source_target_pairs={{0,32},{32,0},{1,33},{33,1},{2,34},{34,2},{3,35},{35,3},{4,36},{36... | collective-permute-start | bytes 147464 | tf_op jit(solution)/shard_map/ppermute | solution.py:25
  31.0 5.1 %collective-permute-start.14 = (f32[32,768]{1,0:T(8,128)S(1)}, f32[32,768]{1,0:T(8,128)S(1)}, u32[]{:S(2)}, u32[]{:S(2)}) collective-permute-start(f32[32,768]{1,0:T(8,128)S(1)} %get-tuple-element.38), channel_id=1, source_target_pairs={{0,4},{1,5},{2,6},{3,7},{4,0},{5,1},{6,2},{7,3},{8,12},{9,13},{10,... | collective-permute-start | bytes 294920 | tf_op jit(solution)/shard_map/ppermute | solution.py:25
  32.5 3.3 %collective-permute-start.13 = (f32[32,384]{1,0:T(8,128)S(1)}, f32[32,384]{1,0:T(8,128)S(1)}, u32[]{:S(2)}, u32[]{:S(2)}) collective-permute-start(f32[32,384]{1,0:T(8,128)S(1)} %add.47.one_ref), channel_id=1, source_target_pairs={{0,64},{64,0},{1,65},{65,1},{2,66},{66,2},{3,67},{67,3},{4,68},{68... | collective-permute-start | bytes 147464 | tf_op jit(solution)/shard_map/ppermute | solution.py:25
  36.0 3.6 %collective-permute-start.20 = (f32[32,768]{1,0:T(8,128)S(1)}, f32[32,768]{1,0:T(8,128)S(1)}, u32[]{:S(2)}, u32[]{:S(2)}) collective-permute-start(f32[32,768]{1,0:T(8,128)S(1)} %get-tuple-element.41), channel_id=1, source_target_pairs={{0,4},{1,5},{2,6},{3,7},{4,0},{5,1},{6,2},{7,3},{8,12},{9,13},{10,... | collective-permute-start | bytes 294920 | tf_op jit(solution)/shard_map/ppermute | solution.py:25
  36.2 6.7 %collective-permute-start.15 = (f32[32,768]{1,0:T(8,128)S(1)}, f32[32,768]{1,0:T(8,128)S(1)}, u32[]{:S(2)}, u32[]{:S(2)}) collective-permute-start(f32[32,768]{1,0:T(8,128)S(1)} %add.48.refs_0_), channel_id=1, source_target_pairs={{0,2},{1,3},{2,0},{3,1},{4,6},{5,7},{6,4},{7,5},{8,10},{9,11},{10,... | collective-permute-start | bytes 294920 | tf_op jit(solution)/shard_map/ppermute | solution.py:25
  38.0 5.0 %collective-permute-start.16 = (f32[32,768]{1,0:T(8,128)S(1)}, f32[32,768]{1,0:T(8,128)S(1)}, u32[]{:S(2)}, u32[]{:S(2)}) collective-permute-start(f32[32,768]{1,0:T(8,128)S(1)} %add.48.refs_0_), channel_id=1, source_target_pairs={{0,3},{1,2},{2,1},{3,0},{4,7},{5,6},{6,5},{7,4},{8,11},{9,10},{10,... | collective-permute-start | bytes 294920 | tf_op jit(solution)/shard_map/ppermute | solution.py:25
  38.7 4.2 %collective-permute-start.17 = (f32[32,768]{1,0:T(8,128)S(1)}, f32[32,768]{1,0:T(8,128)S(1)}, u32[]{:S(2)}, u32[]{:S(2)}) collective-permute-start(f32[32,768]{1,0:T(8,128)S(1)} %add.48.refs_0_), channel_id=1, source_target_pairs={{0,1},{1,0},{2,3},{3,2},{4,5},{5,4},{6,7},{7,6},{8,9},{9,8},{10,11... | collective-permute-start | bytes 294920 | tf_op jit(solution)/shard_map/ppermute | solution.py:25
  39.6 15.2 %copy-start.4 = (s32[3,3,24]{2,1,0:T(4,128)S(1)}, s32[3,3,24]{2,1,0:T(4,128)}, u32[]{:S(2)}) copy-start(s32[3,3,24]{2,1,0:T(4,128)} %param.15) | copy-start | bytes 2596
  39.6 15.2 %copy-start.2 = (bf16[3,384,768]{2,1,0:T(8,128)(2,1)S(1)}, bf16[3,384,768]{2,1,0:T(8,128)(2,1)}, u32[]{:S(2)}) copy-start(bf16[3,384,768]{2,1,0:T(8,128)(2,1)} %factor_ref.1) | copy-start | bytes 5308420
  39.6 9.4 %collective-permute-start.21 = (f32[32,768]{1,0:T(8,128)S(1)}, f32[32,768]{1,0:T(8,128)S(1)}, u32[]{:S(2)}, u32[]{:S(2)}) collective-permute-start(f32[32,768]{1,0:T(8,128)S(1)} %add.50.refs_0_), channel_id=1, source_target_pairs={{0,2},{1,3},{2,0},{3,1},{4,6},{5,7},{6,4},{7,5},{8,10},{9,11},{10,... | collective-permute-start | bytes 294920 | tf_op jit(solution)/shard_map/ppermute | solution.py:25
  42.1 6.9 %collective-permute-start.22 = (f32[32,768]{1,0:T(8,128)S(1)}, f32[32,768]{1,0:T(8,128)S(1)}, u32[]{:S(2)}, u32[]{:S(2)}) collective-permute-start(f32[32,768]{1,0:T(8,128)S(1)} %add.50.refs_0_), channel_id=1, source_target_pairs={{0,3},{1,2},{2,1},{3,0},{4,7},{5,6},{6,5},{7,4},{8,11},{9,10},{10,... | collective-permute-start | bytes 294920 | tf_op jit(solution)/shard_map/ppermute | solution.py:25
  42.9 6.1 %collective-permute-start.23 = (f32[32,768]{1,0:T(8,128)S(1)}, f32[32,768]{1,0:T(8,128)S(1)}, u32[]{:S(2)}, u32[]{:S(2)}) collective-permute-start(f32[32,768]{1,0:T(8,128)S(1)} %add.50.refs_0_), channel_id=1, source_target_pairs={{0,1},{1,0},{2,3},{3,2},{4,5},{5,4},{6,7},{7,6},{8,9},{9,8},{10,11... | collective-permute-start | bytes 294920 | tf_op jit(solution)/shard_map/ppermute | solution.py:25
  43.1 9.5 %collective-permute-start.18 = (f32[32,384]{1,0:T(8,128)S(1)}, f32[32,384]{1,0:T(8,128)S(1)}, u32[]{:S(2)}, u32[]{:S(2)}) collective-permute-start(f32[32,384]{1,0:T(8,128)S(1)} %next_solve.6), channel_id=1, source_target_pairs={{0,32},{32,0},{1,33},{33,1},{2,34},{34,2},{3,35},{35,3},{4,36},{36... | collective-permute-start | bytes 147464 | tf_op jit(solution)/shard_map/ppermute | solution.py:25
  49.2 4.7 %collective-permute-start.24 = (f32[32,384]{1,0:T(8,128)S(1)}, f32[32,384]{1,0:T(8,128)S(1)}, u32[]{:S(2)}, u32[]{:S(2)}) collective-permute-start(f32[32,384]{1,0:T(8,128)S(1)} %next_solve.7), channel_id=1, source_target_pairs={{0,32},{32,0},{1,33},{33,1},{2,34},{34,2},{3,35},{35,3},{4,36},{36... | collective-permute-start | bytes 147464 | tf_op jit(solution)/shard_map/ppermute | solution.py:25
  52.6 3.8 %collective-permute-start.19 = (f32[32,384]{1,0:T(8,128)S(1)}, f32[32,384]{1,0:T(8,128)S(1)}, u32[]{:S(2)}, u32[]{:S(2)}) collective-permute-start(f32[32,384]{1,0:T(8,128)S(1)} %add.49.one_ref), channel_id=1, source_target_pairs={{0,64},{64,0},{1,65},{65,1},{2,66},{66,2},{3,67},{67,3},{4,68},{68... | collective-permute-start | bytes 147464 | tf_op jit(solution)/shard_map/ppermute | solution.py:25
  54.0 3.0 %collective-permute-start.25 = (f32[32,384]{1,0:T(8,128)S(1)}, f32[32,384]{1,0:T(8,128)S(1)}, u32[]{:S(2)}, u32[]{:S(2)}) collective-permute-start(f32[32,384]{1,0:T(8,128)S(1)} %add.51.one_ref), channel_id=1, source_target_pairs={{0,64},{64,0},{1,65},{65,1},{2,66},{66,2},{3,67},{67,3},{4,68},{68... | collective-permute-start | bytes 147464 | tf_op jit(solution)/shard_map/ppermute | solution.py:25
  56.7 24.1 %copy-start.1 = (bf16[768,1536]{1,0:T(8,128)(2,1)S(1)}, bf16[768,1536]{1,0:T(8,128)(2,1)}, u32[]{:S(2)}) copy-start(bf16[768,1536]{1,0:T(8,128)(2,1)} %inverse_ref.1) | copy-start | bytes 7077892
  76.7 4.1 %collective-permute-start.26 = (f32[2,768]{1,0:T(2,128)S(1)}, f32[2,768]{1,0:T(2,128)S(1)}, u32[]{:S(2)}, u32[]{:S(2)}) collective-permute-start(f32[2,768]{1,0:T(2,128)S(1)} %reduce_sum.9.one_ref), channel_id=1, source_target_pairs={{0,128},{128,0},{1,129},{129,1},{2,130},{130,2},{3,131},{131,3},{4... | collective-permute-start | bytes 18440 | tf_op jit(solution)/shard_map/ppermute | solution.py:25
  81.2 5.0 %collective-permute-start.27 = (f32[2,768]{1,0:T(2,128)S(1)}, f32[2,768]{1,0:T(2,128)S(1)}, u32[]{:S(2)}, u32[]{:S(2)}) collective-permute-start(f32[2,768]{1,0:T(2,128)S(1)} %broadcast_select_fusion.2), channel_id=1, source_target_pairs={{0,32},{32,0},{1,33},{33,1},{2,34},{34,2},{3,35},{35,3},{4,36},{36... | collective-permute-start | bytes 18440 | tf_op jit(solution)/shard_map/ppermute | solution.py:25
  86.2 2.5 %collective-permute-start.28 = (f32[2,768]{1,0:T(2,128)S(1)}, f32[2,768]{1,0:T(2,128)S(1)}, u32[]{:S(2)}, u32[]{:S(2)}) collective-permute-start(f32[2,768]{1,0:T(2,128)S(1)} %select_add_fusion), channel_id=1, source_target_pairs={{0,64},{64,0},{1,65},{65,1},{2,66},{66,2},{3,67},{67,3},{4,68},{68... | collective-permute-start | bytes 18440 | tf_op jit(solution)/shard_map/ppermute | solution.py:25
  101.7 4.3 %collective-permute-start.29 = (f32[64,768]{1,0:T(8,128)S(1)}, f32[64,768]{1,0:T(8,128)S(1)}, u32[]{:S(2)}, u32[]{:S(2)}) collective-permute-start(f32[64,768]{1,0:T(8,128)S(1)} %reshape.16), channel_id=1, source_target_pairs={{0,32},{32,0},{1,33},{33,1},{2,34},{34,2},{3,35},{35,3},{4,36},{36... | collective-permute-start | bytes 589832 | tf_op jit(solution)/shard_map/ppermute | solution.py:25

commit v10 on v8

--- a/solution.py
+++ b/solution.py
@@ -260,8 +260,9 @@
 
 
 def owner_sums(partial_sum):
-    pair = partial_sum + partner(partial_sum, OWN, 4)
-    return [pair] + [partner(pair, OWN, bit) for bit in (2, 3, 1)]
+    far, back, near = [partner(partial_sum, OWN, bit) for bit in (2, 3, 1)]
+    line = (partial_sum + near) + (far + back)
+    return [line, partner(line, OWN, 4)]
 
 
 def shards(

time: 102 us -> 104 us (1.020)
  waiting for transfers between devices: 15.4 us -> 19.3 us
  starting transfers between devices: 55.9 us -> 54.2 us
    ppermute x31, waiting for transfers between devices: 15.4 us -> 19.3 us  [partner(): lax.ppermute(shard, axis, [(i, i ^ bit) for i in range(lax.axis_size(axis...]
    ppermute x31, starting transfers between devices: 55.9 us -> 54.2 us  [partner(): lax.ppermute(shard, axis, [(i, i ^ bit) for i in range(lax.axis_size(axis...]
  transfers between devices with their start and end apart: 31 -> 31, of which waited for: 13 -> 15; matrix products, arithmetic and copies ran while one was open for 0% -> 0% of each run, Pallas kernels for 7% -> 6%
where the time goes in v10:
time: 104 us; the launch traced here: 103 us
  starting transfers between devices  54.2 us (52%)
  waiting for transfers between devices  19.3 us (19%)
  blocking collectives  18.5 us (18%)
  Pallas kernels  9.05 us (9%)
    ppermute x31, starting transfers between devices, partner(): lax.ppermute(shard, axis, [(i, i ^ bit) for i in range(lax.axis_size(axis...  54.2 us
    ppermute x31, waiting for transfers between devices, partner(): lax.ppermute(shard, axis, [(i, i ^ bit) for i in range(lax.axis_size(axis...  19.3 us
    all_to_all x2, blocking collectives, swap_blocks(): lax.all_to_all(blocks, OWN, 0, 0, axis_index_groups=[order], tiled=True)  18.5 us
    pallas_call x17, Pallas kernels, call(): pl.pallas_call(body, out_shape=[pltpu.VMEM(shape, kind) for shape, kind i...  8.3 us
  transfers between devices with their start and end apart: 31, of which 15 were waited for; matrix products, arithmetic and copies ran while one was open for 0% of the time, Pallas kernels for 6%

profile of v10, /device:TPU:1, one launch (start us, length us, event | category | flops | bytes accessed | tf_op | source)
XLA Modules:
  0.0 103.1 jit_solution(17105076515715577881)
XLA Ops:
  0.7 1.6 %first_solve.1 = f32[64,384]{1,0:T(8,128)S(1)} custom-call(s32[1]{0:T(128)} %bitcast.tree_ref, f32[4,3,64,768]{3,2,1,0:T(8,128)} %rhs_hbm.3, bf16[3,768,384]{2,1,0:T(8,128)(2,1)} %inverse_hbm.3), custom_call_target="tpu_custom_call" | custom-call | tf_op jit(solution)/shard_map/first_solve/pallas_call | solution.py:43
  2.3 3.3 %collective-permute-start = (f32[64,384]{1,0:T(8,128)S(1)}, f32[64,384]{1,0:T(8,128)S(1)}, u32[]{:S(2)}, u32[]{:S(2)}) collective-permute-start(f32[64,384]{1,0:T(8,128)S(1)} %first_solve.1), channel_id=1, source_target_pairs={{0,32},{32,0},{1,33},{33,1},{2,34},{34,2},{3,35},{35,3},{4,36},{36... | collective-permute-start | bytes 294920 | tf_op jit(solution)/shard_map/ppermute | solution.py:24
  5.6 0.9 collective-permute-done
  6.5 0.1 collective-permute-start.1
  6.7 2.6 %stage.1 = (bf16[3,384,768]{2,1,0:T(8,128)(2,1)S(1)}, bf16[2,768,384]{2,1,0:T(8,128)(2,1)S(1)}, f32[2,64,768]{2,1,0:T(8,128)S(1)}) custom-call(s32[1]{0:T(128)} %bitcast.tree_ref, s32[3,3,6]{2,1,0:T(4,128)S(1)} %constant_dynamic-slice_fusion.2.mask_ref, f32[4,3,64,768]{3,2,1,0:T(8,128)} %rhs_hbm.3, bf16[3,768,384]{2,1,0:T(8,128)(2,1)} %inverse_hbm.3, ...), custom_call_target="tpu_custom_call" | custom-call | tf_op jit(solution)/shard_map/stage/pallas_call | solution.py:43
  9.3 1.4 %collective-permute-done.1.other_ref = f32[64,384]{1,0:T(8,128)S(1)} collective-permute-done((f32[64,384]{1,0:T(8,128)S(1)}, f32[64,384]{1,0:T(8,128)S(1)}, u32[]{:S(2)}, u32[]{:S(2)}) %collective-permute-start.1) | collective-permute-done | bytes 98336 | tf_op jit(solution)/shard_map/ppermute | solution.py:24
  10.7 0.2 kept_update.5
  10.9 1.3 %collective-permute-start.3 = (f32[32,768]{1,0:T(8,128)S(1)}, f32[32,768]{1,0:T(8,128)S(1)}, u32[]{:S(2)}, u32[]{:S(2)}) collective-permute-start(f32[32,768]{1,0:T(8,128)S(1)} %get-tuple-element.27), channel_id=1, source_target_pairs={{0,2},{1,3},{2,0},{3,1},{4,6},{5,7},{6,4},{7,5},{8,10},{9,11},{10,... | collective-permute-start | bytes 294920 | tf_op jit(solution)/shard_map/ppermute | solution.py:24
  12.1 0.8 collective-permute-start.4
  12.9 0.7 collective-permute-start.2
  13.6 2.4 %collective-permute-start.9 = (f32[32,768]{1,0:T(8,128)S(1)}, f32[32,768]{1,0:T(8,128)S(1)}, u32[]{:S(2)}, u32[]{:S(2)}) collective-permute-start(f32[32,768]{1,0:T(8,128)S(1)} %get-tuple-element.31), channel_id=1, source_target_pairs={{0,2},{1,3},{2,0},{3,1},{4,6},{5,7},{6,4},{7,5},{8,10},{9,11},{10,... | collective-permute-start | bytes 294920 | tf_op jit(solution)/shard_map/ppermute | solution.py:24
  16.0 0.8 collective-permute-start.10
  16.8 1.3 %collective-permute-done.4 = f32[32,768]{1,0:T(8,128)S(1)} collective-permute-done((f32[32,768]{1,0:T(8,128)S(1)}, f32[32,768]{1,0:T(8,128)S(1)}, u32[]{:S(2)}, u32[]{:S(2)}) %collective-permute-start.4) | collective-permute-done | bytes 98336 | tf_op jit(solution)/shard_map/ppermute | solution.py:24
  18.1 0.9 collective-permute-start.5
  19.0 1.2 %collective-permute-done.9 = f32[32,768]{1,0:T(8,128)S(1)} collective-permute-done((f32[32,768]{1,0:T(8,128)S(1)}, f32[32,768]{1,0:T(8,128)S(1)}, u32[]{:S(2)}, u32[]{:S(2)}) %collective-permute-start.9) | collective-permute-done | bytes 98336 | tf_op jit(solution)/shard_map/ppermute | solution.py:24
  20.1 1.9 %collective-permute-done.10 = f32[32,768]{1,0:T(8,128)S(1)} collective-permute-done((f32[32,768]{1,0:T(8,128)S(1)}, f32[32,768]{1,0:T(8,128)S(1)}, u32[]{:S(2)}, u32[]{:S(2)}) %collective-permute-start.10) | collective-permute-done | bytes 98336 | tf_op jit(solution)/shard_map/ppermute | solution.py:24
  22.1 1.6 %collective-permute-start.11 = (f32[32,768]{1,0:T(8,128)S(1)}, f32[32,768]{1,0:T(8,128)S(1)}, u32[]{:S(2)}, u32[]{:S(2)}) collective-permute-start(f32[32,768]{1,0:T(8,128)S(1)} %add_add_fusion.2.refs_0_), channel_id=1, source_target_pairs={{0,4},{1,5},{2,6},{3,7},{4,0},{5,1},{6,2},{7,3},{8,12},{9,13},{10,... | collective-permute-start | bytes 294920 | tf_op jit(solution)/shard_map/ppermute | solution.py:24
  23.7 0.2 next_solve.4
  23.9 2.6 %collective-permute-start.6 = (f32[32,384]{1,0:T(8,128)S(1)}, f32[32,384]{1,0:T(8,128)S(1)}, u32[]{:S(2)}, u32[]{:S(2)}) collective-permute-start(f32[32,384]{1,0:T(8,128)S(1)} %next_solve.4), channel_id=1, source_target_pairs={{0,32},{32,0},{1,33},{33,1},{2,34},{34,2},{3,35},{35,3},{4,36},{36... | collective-permute-start | bytes 147464 | tf_op jit(solution)/shard_map/ppermute | solution.py:24
  26.5 0.9 collective-permute-done.6
  27.4 1.2 %collective-permute-start.7 = (f32[32,384]{1,0:T(8,128)S(1)}, f32[32,384]{1,0:T(8,128)S(1)}, u32[]{:S(2)}, u32[]{:S(2)}) collective-permute-start(f32[32,384]{1,0:T(8,128)S(1)} %add.79.one_ref), channel_id=1, source_target_pairs={{0,64},{64,0},{1,65},{65,1},{2,66},{66,2},{3,67},{67,3},{4,68},{68... | collective-permute-start | bytes 147464 | tf_op jit(solution)/shard_map/ppermute | solution.py:24
  28.6 0.2 next_solve.5
  28.8 0.8 collective-permute-start.12
  29.6 0.2 early_update.4.refs_0_
  29.8 0.6 collective-permute-done.7.other_ref
  30.4 0.2 kept_update.6
  30.6 2.3 %collective-permute-start.15 = (f32[32,768]{1,0:T(8,128)S(1)}, f32[32,768]{1,0:T(8,128)S(1)}, u32[]{:S(2)}, u32[]{:S(2)}) collective-permute-start(f32[32,768]{1,0:T(8,128)S(1)} %get-tuple-element.34), channel_id=1, source_target_pairs={{0,2},{1,3},{2,0},{3,1},{4,6},{5,7},{6,4},{7,5},{8,10},{9,11},{10,... | collective-permute-start | bytes 294920 | tf_op jit(solution)/shard_map/ppermute | solution.py:24
  32.9 0.6 collective-permute-start.16
  33.5 1.5 %collective-permute-start.13 = (f32[32,384]{1,0:T(8,128)S(1)}, f32[32,384]{1,0:T(8,128)S(1)}, u32[]{:S(2)}, u32[]{:S(2)}) collective-permute-start(f32[32,384]{1,0:T(8,128)S(1)} %add.83.one_ref), channel_id=1, source_target_pairs={{0,64},{64,0},{1,65},{65,1},{2,66},{66,2},{3,67},{67,3},{4,68},{68... | collective-permute-start | bytes 147464 | tf_op jit(solution)/shard_map/ppermute | solution.py:24
  35.1 0.2 early_update.5.refs_0_
  35.3 1.3 %collective-permute-done.13.other_ref = f32[32,384]{1,0:T(8,128)S(1)} collective-permute-done((f32[32,384]{1,0:T(8,128)S(1)}, f32[32,384]{1,0:T(8,128)S(1)}, u32[]{:S(2)}, u32[]{:S(2)}) %collective-permute-start.13) | collective-permute-done | bytes 49184 | tf_op jit(solution)/shard_map/ppermute | solution.py:24
  36.6 0.2 kept_update.7
  36.8 3.6 %collective-permute-start.21 = (f32[32,768]{1,0:T(8,128)S(1)}, f32[32,768]{1,0:T(8,128)S(1)}, u32[]{:S(2)}, u32[]{:S(2)}) collective-permute-start(f32[32,768]{1,0:T(8,128)S(1)} %get-tuple-element.37), channel_id=1, source_target_pairs={{0,2},{1,3},{2,0},{3,1},{4,6},{5,7},{6,4},{7,5},{8,10},{9,11},{10,... | collective-permute-start | bytes 294920 | tf_op jit(solution)/shard_map/ppermute | solution.py:24
  40.4 0.6 collective-permute-start.22
  41.1 1.9 %collective-permute-start.17 = (f32[32,768]{1,0:T(8,128)S(1)}, f32[32,768]{1,0:T(8,128)S(1)}, u32[]{:S(2)}, u32[]{:S(2)}) collective-permute-start(f32[32,768]{1,0:T(8,128)S(1)} %add_add_fusion.1.refs_0_), channel_id=1, source_target_pairs={{0,4},{1,5},{2,6},{3,7},{4,0},{5,1},{6,2},{7,3},{8,12},{9,13},{10,... | collective-permute-start | bytes 294920 | tf_op jit(solution)/shard_map/ppermute | solution.py:24
  42.9 3.1 %collective-permute-done.22 = f32[32,768]{1,0:T(8,128)S(1)} collective-permute-done((f32[32,768]{1,0:T(8,128)S(1)}, f32[32,768]{1,0:T(8,128)S(1)}, u32[]{:S(2)}, u32[]{:S(2)}) %collective-permute-start.22) | collective-permute-done | bytes 98336 | tf_op jit(solution)/shard_map/ppermute | solution.py:24
  46.1 1.5 %collective-permute-start.23 = (f32[32,768]{1,0:T(8,128)S(1)}, f32[32,768]{1,0:T(8,128)S(1)}, u32[]{:S(2)}, u32[]{:S(2)}) collective-permute-start(f32[32,768]{1,0:T(8,128)S(1)} %add_add_fusion.refs_0_), channel_id=1, source_target_pairs={{0,4},{1,5},{2,6},{3,7},{4,0},{5,1},{6,2},{7,3},{8,12},{9,13},{10,... | collective-permute-start | bytes 294920 | tf_op jit(solution)/shard_map/ppermute | solution.py:24
  47.6 0.2 next_solve.6
  47.8 4.2 %collective-permute-start.18 = (f32[32,384]{1,0:T(8,128)S(1)}, f32[32,384]{1,0:T(8,128)S(1)}, u32[]{:S(2)}, u32[]{:S(2)}) collective-permute-start(f32[32,384]{1,0:T(8,128)S(1)} %next_solve.6), channel_id=1, source_target_pairs={{0,32},{32,0},{1,33},{33,1},{2,34},{34,2},{3,35},{35,3},{4,36},{36... | collective-permute-start | bytes 147464 | tf_op jit(solution)/shard_map/ppermute | solution.py:24
  51.9 0.2 next_solve.7
  52.1 2.7 %collective-permute-start.24 = (f32[32,384]{1,0:T(8,128)S(1)}, f32[32,384]{1,0:T(8,128)S(1)}, u32[]{:S(2)}, u32[]{:S(2)}) collective-permute-start(f32[32,384]{1,0:T(8,128)S(1)} %next_solve.7), channel_id=1, source_target_pairs={{0,32},{32,0},{1,33},{33,1},{2,34},{34,2},{3,35},{35,3},{4,36},{36... | collective-permute-start | bytes 147464 | tf_op jit(solution)/shard_map/ppermute | solution.py:24
  54.8 1.3 %collective-permute-start.19 = (f32[32,384]{1,0:T(8,128)S(1)}, f32[32,384]{1,0:T(8,128)S(1)}, u32[]{:S(2)}, u32[]{:S(2)}) collective-permute-start(f32[32,384]{1,0:T(8,128)S(1)} %add.87.one_ref), channel_id=1, source_target_pairs={{0,64},{64,0},{1,65},{65,1},{2,66},{66,2},{3,67},{67,3},{4,68},{68... | collective-permute-start | bytes 147464 | tf_op jit(solution)/shard_map/ppermute | solution.py:24
  56.1 0.8 collective-permute-start.25
  57.0 0.9 masked.1.refs_2_.factor_ref
  58.0 0.3 early_update.6.refs_0_
  58.3 0.3 early_update.7.refs_0_
  58.6 0.2 kept_update.8
  58.8 0.3 collective-permute-done.25.other_ref
  59.2 0.2 kept_update.9
  59.4 8.9 %all_to_all.10 = f32[8,8,768]{2,1,0:T(8,128)S(1)} all-to-all(f32[8,8,768]{2,1,0:T(8,128)S(1)} %maximum_bitcast_fusion), channel_id=1, replica_groups={{7,6,5,4,3,2,1,0},{15,14,13,12,11,10,9,8},{23,22,21,20,19,18,17,16},{31..., dimensions={0} | all-to-all | bytes 393216 | tf_op jit(solution)/shard_map/all_to_all | solution.py:29
  68.3 2.6 %collective-permute-start.26 = (f32[8,768]{1,0:T(8,128)S(1)}, f32[8,768]{1,0:T(8,128)S(1)}, u32[]{:S(2)}, u32[]{:S(2)}) collective-permute-start(f32[8,768]{1,0:T(8,128)S(1)} %reduce_sum.9), channel_id=1, source_target_pairs={{0,128},{128,0},{1,129},{129,1},{2,130},{130,2},{3,131},{131,3},{4... | collective-permute-start | bytes 73736 | tf_op jit(solution)/shard_map/ppermute | solution.py:24
  70.9 0.8 stacked.1
  71.6 0.9 collective-permute-done.26
  72.6 3.0 %collective-permute-start.27 = (f32[8,768]{1,0:T(8,128)S(1)}, f32[8,768]{1,0:T(8,128)S(1)}, u32[]{:S(2)}, u32[]{:S(2)}) collective-permute-start(f32[8,768]{1,0:T(8,128)S(1)} %add.93), channel_id=1, source_target_pairs={{0,8},{8,0},{16,24},{24,16},{1,9},{9,1},{17,25},{25,17},{2,10},{10... | collective-permute-start | bytes 73736 | tf_op jit(solution)/shard_map/ppermute | solution.py:24
  75.5 1.2 %collective-permute-done.27 = f32[8,768]{1,0:T(8,128)S(1)} collective-permute-done((f32[8,768]{1,0:T(8,128)S(1)}, f32[8,768]{1,0:T(8,128)S(1)}, u32[]{:S(2)}, u32[]{:S(2)}) %collective-permute-start.27) | collective-permute-done | bytes 24608 | tf_op jit(solution)/shard_map/ppermute | solution.py:24
  76.8 4.6 %collective-permute-start.28 = (f32[8,768]{1,0:T(8,128)S(1)}, f32[8,768]{1,0:T(8,128)S(1)}, u32[]{:S(2)}, u32[]{:S(2)}) collective-permute-start(f32[8,768]{1,0:T(8,128)S(1)} %add.94.one_ref), channel_id=1, source_target_pairs={{0,24},{8,16},{16,8},{24,0},{1,25},{9,17},{17,9},{25,1},{2,26},{10... | collective-permute-start | bytes 73736 | tf_op jit(solution)/shard_map/ppermute | solution.py:24
  81.4 1.2 %collective-permute-done.28.other_ref = f32[8,768]{1,0:T(8,128)S(1)} collective-permute-done((f32[8,768]{1,0:T(8,128)S(1)}, f32[8,768]{1,0:T(8,128)S(1)}, u32[]{:S(2)}, u32[]{:S(2)}) %collective-permute-start.28) | collective-permute-done | bytes 24608 | tf_op jit(solution)/shard_map/ppermute | solution.py:24
  82.6 0.4 root_part.1
  83.0 5.8 %collective-permute-start.29 = (f32[8,1536]{1,0:T(8,128)S(1)}, f32[8,1536]{1,0:T(8,128)S(1)}, u32[]{:S(2)}, u32[]{:S(2)}) collective-permute-start(f32[8,1536]{1,0:T(8,128)S(1)} %root_part.1), channel_id=1, source_target_pairs={{0,32},{32,0},{1,33},{33,1},{2,34},{34,2},{3,35},{35,3},{4,36},{36... | collective-permute-start | bytes 147464 | tf_op jit(solution)/shard_map/ppermute | solution.py:24
  88.8 0.9 collective-permute-done.29
  89.7 0.8 collective-permute-start.30
  90.6 2.1 %collective-permute-done.30 = f32[8,1536]{1,0:T(8,128)S(1)} collective-permute-done((f32[8,1536]{1,0:T(8,128)S(1)}, f32[8,1536]{1,0:T(8,128)S(1)}, u32[]{:S(2)}, u32[]{:S(2)}) %collective-permute-start.30) | collective-permute-done | bytes 49184 | tf_op jit(solution)/shard_map/ppermute | solution.py:24
  92.7 9.6 %all_to_all.11 = f32[8,8,1536]{2,1,0:T(8,128)S(1)} all-to-all(f32[8,8,1536]{2,1,0:T(8,128)S(1)} %broadcast_in_dim.2), channel_id=1, replica_groups={{7,6,5,4,3,2,1,0},{15,14,13,12,11,10,9,8},{23,22,21,20,19,18,17,16},{31..., dimensions={0} | all-to-all | bytes 786432 | tf_op jit(solution)/shard_map/all_to_all | solution.py:29
  102.3 0.7 copy.11
  (48 shorter events, 0.5 us)
Async XLA Ops:
  0.6 80.8 %copy-start = (f32[64,768]{1,0:T(8,128)S(1)}, f32[64,768]{1,0:T(8,128)}, u32[]{:S(2)}) copy-start(f32[64,768]{1,0:T(8,128)} %param.9) | copy-start | bytes 589828
  0.7 6.0 %copy-start.3 = (s32[3,3,24]{2,1,0:T(4,128)S(1)}, s32[3,3,24]{2,1,0:T(4,128)}, u32[]{:S(2)}) copy-start(s32[3,3,24]{2,1,0:T(4,128)} %param.13) | copy-start | bytes 2596
  2.3 4.3 %collective-permute-start = (f32[64,384]{1,0:T(8,128)S(1)}, f32[64,384]{1,0:T(8,128)S(1)}, u32[]{:S(2)}, u32[]{:S(2)}) collective-permute-start(f32[64,384]{1,0:T(8,128)S(1)} %first_solve.1), channel_id=1, source_target_pairs={{0,32},{32,0},{1,33},{33,1},{2,34},{34,2},{3,35},{35,3},{4,36},{36... | collective-permute-start | bytes 294920 | tf_op jit(solution)/shard_map/ppermute | solution.py:24
  6.5 4.1 %collective-permute-start.1 = (f32[64,384]{1,0:T(8,128)S(1)}, f32[64,384]{1,0:T(8,128)S(1)}, u32[]{:S(2)}, u32[]{:S(2)}) collective-permute-start(f32[64,384]{1,0:T(8,128)S(1)} %add.73.one_ref), channel_id=1, source_target_pairs={{0,64},{64,0},{1,65},{65,1},{2,66},{66,2},{3,67},{67,3},{4,68},{68... | collective-permute-start | bytes 294920 | tf_op jit(solution)/shard_map/ppermute | solution.py:24
  10.9 5.9 %collective-permute-start.3 = (f32[32,768]{1,0:T(8,128)S(1)}, f32[32,768]{1,0:T(8,128)S(1)}, u32[]{:S(2)}, u32[]{:S(2)}) collective-permute-start(f32[32,768]{1,0:T(8,128)S(1)} %get-tuple-element.27), channel_id=1, source_target_pairs={{0,2},{1,3},{2,0},{3,1},{4,6},{5,7},{6,4},{7,5},{8,10},{9,11},{10,... | collective-permute-start | bytes 294920 | tf_op jit(solution)/shard_map/ppermute | solution.py:24
  12.1 5.9 %collective-permute-start.4 = (f32[32,768]{1,0:T(8,128)S(1)}, f32[32,768]{1,0:T(8,128)S(1)}, u32[]{:S(2)}, u32[]{:S(2)}) collective-permute-start(f32[32,768]{1,0:T(8,128)S(1)} %get-tuple-element.27), channel_id=1, source_target_pairs={{0,3},{1,2},{2,1},{3,0},{4,7},{5,6},{6,5},{7,4},{8,11},{9,10},{10,... | collective-permute-start | bytes 294920 | tf_op jit(solution)/shard_map/ppermute | solution.py:24
  12.9 5.2 %collective-permute-start.2 = (f32[32,768]{1,0:T(8,128)S(1)}, f32[32,768]{1,0:T(8,128)S(1)}, u32[]{:S(2)}, u32[]{:S(2)}) collective-permute-start(f32[32,768]{1,0:T(8,128)S(1)} %get-tuple-element.27), channel_id=1, source_target_pairs={{0,1},{1,0},{2,3},{3,2},{4,5},{5,4},{6,7},{7,6},{8,9},{9,8},{10,11... | collective-permute-start | bytes 294920 | tf_op jit(solution)/shard_map/ppermute | solution.py:24
  13.6 6.5 %collective-permute-start.9 = (f32[32,768]{1,0:T(8,128)S(1)}, f32[32,768]{1,0:T(8,128)S(1)}, u32[]{:S(2)}, u32[]{:S(2)}) collective-permute-start(f32[32,768]{1,0:T(8,128)S(1)} %get-tuple-element.31), channel_id=1, source_target_pairs={{0,2},{1,3},{2,0},{3,1},{4,6},{5,7},{6,4},{7,5},{8,10},{9,11},{10,... | collective-permute-start | bytes 294920 | tf_op jit(solution)/shard_map/ppermute | solution.py:24
  16.0 6.1 %collective-permute-start.10 = (f32[32,768]{1,0:T(8,128)S(1)}, f32[32,768]{1,0:T(8,128)S(1)}, u32[]{:S(2)}, u32[]{:S(2)}) collective-permute-start(f32[32,768]{1,0:T(8,128)S(1)} %get-tuple-element.31), channel_id=1, source_target_pairs={{0,3},{1,2},{2,1},{3,0},{4,7},{5,6},{6,5},{7,4},{8,11},{9,10},{10,... | collective-permute-start | bytes 294920 | tf_op jit(solution)/shard_map/ppermute | solution.py:24
  16.8 5.3 %collective-permute-start.8 = (f32[32,768]{1,0:T(8,128)S(1)}, f32[32,768]{1,0:T(8,128)S(1)}, u32[]{:S(2)}, u32[]{:S(2)}) collective-permute-start(f32[32,768]{1,0:T(8,128)S(1)} %get-tuple-element.31), channel_id=1, source_target_pairs={{0,1},{1,0},{2,3},{3,2},{4,5},{5,4},{6,7},{7,6},{8,9},{9,8},{10,11... | collective-permute-start | bytes 294920 | tf_op jit(solution)/shard_map/ppermute | solution.py:24
  18.1 5.6 %collective-permute-start.5 = (f32[32,768]{1,0:T(8,128)S(1)}, f32[32,768]{1,0:T(8,128)S(1)}, u32[]{:S(2)}, u32[]{:S(2)}) collective-permute-start(f32[32,768]{1,0:T(8,128)S(1)} %add_add_fusion.3.refs_0_), channel_id=1, source_target_pairs={{0,4},{1,5},{2,6},{3,7},{4,0},{5,1},{6,2},{7,3},{8,12},{9,13},{10,... | collective-permute-start | bytes 294920 | tf_op jit(solution)/shard_map/ppermute | solution.py:24
  22.1 6.5 %collective-permute-start.11 = (f32[32,768]{1,0:T(8,128)S(1)}, f32[32,768]{1,0:T(8,128)S(1)}, u32[]{:S(2)}, u32[]{:S(2)}) collective-permute-start(f32[32,768]{1,0:T(8,128)S(1)} %add_add_fusion.2.refs_0_), channel_id=1, source_target_pairs={{0,4},{1,5},{2,6},{3,7},{4,0},{5,1},{6,2},{7,3},{8,12},{9,13},{10,... | collective-permute-start | bytes 294920 | tf_op jit(solution)/shard_map/ppermute | solution.py:24
  23.9 3.5 %collective-permute-start.6 = (f32[32,384]{1,0:T(8,128)S(1)}, f32[32,384]{1,0:T(8,128)S(1)}, u32[]{:S(2)}, u32[]{:S(2)}) collective-permute-start(f32[32,384]{1,0:T(8,128)S(1)} %next_solve.4), channel_id=1, source_target_pairs={{0,32},{32,0},{1,33},{33,1},{2,34},{34,2},{3,35},{35,3},{4,36},{36... | collective-permute-start | bytes 147464 | tf_op jit(solution)/shard_map/ppermute | solution.py:24
  27.4 3.0 %collective-permute-start.7 = (f32[32,384]{1,0:T(8,128)S(1)}, f32[32,384]{1,0:T(8,128)S(1)}, u32[]{:S(2)}, u32[]{:S(2)}) collective-permute-start(f32[32,384]{1,0:T(8,128)S(1)} %add.79.one_ref), channel_id=1, source_target_pairs={{0,64},{64,0},{1,65},{65,1},{2,66},{66,2},{3,67},{67,3},{4,68},{68... | collective-permute-start | bytes 147464 | tf_op jit(solution)/shard_map/ppermute | solution.py:24
  28.8 4.7 %collective-permute-start.12 = (f32[32,384]{1,0:T(8,128)S(1)}, f32[32,384]{1,0:T(8,128)S(1)}, u32[]{:S(2)}, u32[]{:S(2)}) collective-permute-start(f32[32,384]{1,0:T(8,128)S(1)} %next_solve.5), channel_id=1, source_target_pairs={{0,32},{32,0},{1,33},{33,1},{2,34},{34,2},{3,35},{35,3},{4,36},{36... | collective-permute-start | bytes 147464 | tf_op jit(solution)/shard_map/ppermute | solution.py:24
  30.6 10.4 %collective-permute-start.15 = (f32[32,768]{1,0:T(8,128)S(1)}, f32[32,768]{1,0:T(8,128)S(1)}, u32[]{:S(2)}, u32[]{:S(2)}) collective-permute-start(f32[32,768]{1,0:T(8,128)S(1)} %get-tuple-element.34), channel_id=1, source_target_pairs={{0,2},{1,3},{2,0},{3,1},{4,6},{5,7},{6,4},{7,5},{8,10},{9,11},{10,... | collective-permute-start | bytes 294920 | tf_op jit(solution)/shard_map/ppermute | solution.py:24
  32.9 8.1 %collective-permute-start.16 = (f32[32,768]{1,0:T(8,128)S(1)}, f32[32,768]{1,0:T(8,128)S(1)}, u32[]{:S(2)}, u32[]{:S(2)}) collective-permute-start(f32[32,768]{1,0:T(8,128)S(1)} %get-tuple-element.34), channel_id=1, source_target_pairs={{0,3},{1,2},{2,1},{3,0},{4,7},{5,6},{6,5},{7,4},{8,11},{9,10},{10,... | collective-permute-start | bytes 294920 | tf_op jit(solution)/shard_map/ppermute | solution.py:24
  33.5 7.5 %collective-permute-start.14 = (f32[32,768]{1,0:T(8,128)S(1)}, f32[32,768]{1,0:T(8,128)S(1)}, u32[]{:S(2)}, u32[]{:S(2)}) collective-permute-start(f32[32,768]{1,0:T(8,128)S(1)} %get-tuple-element.34), channel_id=1, source_target_pairs={{0,1},{1,0},{2,3},{3,2},{4,5},{5,4},{6,7},{7,6},{8,9},{9,8},{10,11... | collective-permute-start | bytes 294920 | tf_op jit(solution)/shard_map/ppermute | solution.py:24
  33.5 3.0 %collective-permute-start.13 = (f32[32,384]{1,0:T(8,128)S(1)}, f32[32,384]{1,0:T(8,128)S(1)}, u32[]{:S(2)}, u32[]{:S(2)}) collective-permute-start(f32[32,384]{1,0:T(8,128)S(1)} %add.83.one_ref), channel_id=1, source_target_pairs={{0,64},{64,0},{1,65},{65,1},{2,66},{66,2},{3,67},{67,3},{4,68},{68... | collective-permute-start | bytes 147464 | tf_op jit(solution)/shard_map/ppermute | solution.py:24
  36.8 6.2 %collective-permute-start.21 = (f32[32,768]{1,0:T(8,128)S(1)}, f32[32,768]{1,0:T(8,128)S(1)}, u32[]{:S(2)}, u32[]{:S(2)}) collective-permute-start(f32[32,768]{1,0:T(8,128)S(1)} %get-tuple-element.37), channel_id=1, source_target_pairs={{0,2},{1,3},{2,0},{3,1},{4,6},{5,7},{6,4},{7,5},{8,10},{9,11},{10,... | collective-permute-start | bytes 294920 | tf_op jit(solution)/shard_map/ppermute | solution.py:24
  40.4 5.6 %collective-permute-start.22 = (f32[32,768]{1,0:T(8,128)S(1)}, f32[32,768]{1,0:T(8,128)S(1)}, u32[]{:S(2)}, u32[]{:S(2)}) collective-permute-start(f32[32,768]{1,0:T(8,128)S(1)} %get-tuple-element.37), channel_id=1, source_target_pairs={{0,3},{1,2},{2,1},{3,0},{4,7},{5,6},{6,5},{7,4},{8,11},{9,10},{10,... | collective-permute-start | bytes 294920 | tf_op jit(solution)/shard_map/ppermute | solution.py:24
  41.0 5.0 %collective-permute-start.20 = (f32[32,768]{1,0:T(8,128)S(1)}, f32[32,768]{1,0:T(8,128)S(1)}, u32[]{:S(2)}, u32[]{:S(2)}) collective-permute-start(f32[32,768]{1,0:T(8,128)S(1)} %get-tuple-element.37), channel_id=1, source_target_pairs={{0,1},{1,0},{2,3},{3,2},{4,5},{5,4},{6,7},{7,6},{8,9},{9,8},{10,11... | collective-permute-start | bytes 294920 | tf_op jit(solution)/shard_map/ppermute | solution.py:24
  41.1 6.5 %collective-permute-start.17 = (f32[32,768]{1,0:T(8,128)S(1)}, f32[32,768]{1,0:T(8,128)S(1)}, u32[]{:S(2)}, u32[]{:S(2)}) collective-permute-start(f32[32,768]{1,0:T(8,128)S(1)} %add_add_fusion.1.refs_0_), channel_id=1, source_target_pairs={{0,4},{1,5},{2,6},{3,7},{4,0},{5,1},{6,2},{7,3},{8,12},{9,13},{10,... | collective-permute-start | bytes 294920 | tf_op jit(solution)/shard_map/ppermute | solution.py:24
  46.1 10.9 %copy-start.4 = (s32[3,3,24]{2,1,0:T(4,128)S(1)}, s32[3,3,24]{2,1,0:T(4,128)}, u32[]{:S(2)}) copy-start(s32[3,3,24]{2,1,0:T(4,128)} %param.15) | copy-start | bytes 2596
  46.1 11.0 %copy-start.2 = (bf16[3,384,768]{2,1,0:T(8,128)(2,1)S(1)}, bf16[3,384,768]{2,1,0:T(8,128)(2,1)}, u32[]{:S(2)}) copy-start(bf16[3,384,768]{2,1,0:T(8,128)(2,1)} %factor_ref.1) | copy-start | bytes 5308420
  46.1 5.8 %collective-permute-start.23 = (f32[32,768]{1,0:T(8,128)S(1)}, f32[32,768]{1,0:T(8,128)S(1)}, u32[]{:S(2)}, u32[]{:S(2)}) collective-permute-start(f32[32,768]{1,0:T(8,128)S(1)} %add_add_fusion.refs_0_), channel_id=1, source_target_pairs={{0,4},{1,5},{2,6},{3,7},{4,0},{5,1},{6,2},{7,3},{8,12},{9,13},{10,... | collective-permute-start | bytes 294920 | tf_op jit(solution)/shard_map/ppermute | solution.py:24
  47.8 7.0 %collective-permute-start.18 = (f32[32,384]{1,0:T(8,128)S(1)}, f32[32,384]{1,0:T(8,128)S(1)}, u32[]{:S(2)}, u32[]{:S(2)}) collective-permute-start(f32[32,384]{1,0:T(8,128)S(1)} %next_solve.6), channel_id=1, source_target_pairs={{0,32},{32,0},{1,33},{33,1},{2,34},{34,2},{3,35},{35,3},{4,36},{36... | collective-permute-start | bytes 147464 | tf_op jit(solution)/shard_map/ppermute | solution.py:24
  52.1 4.0 %collective-permute-start.24 = (f32[32,384]{1,0:T(8,128)S(1)}, f32[32,384]{1,0:T(8,128)S(1)}, u32[]{:S(2)}, u32[]{:S(2)}) collective-permute-start(f32[32,384]{1,0:T(8,128)S(1)} %next_solve.7), channel_id=1, source_target_pairs={{0,32},{32,0},{1,33},{33,1},{2,34},{34,2},{3,35},{35,3},{4,36},{36... | collective-permute-start | bytes 147464 | tf_op jit(solution)/shard_map/ppermute | solution.py:24
  54.8 3.8 %collective-permute-start.19 = (f32[32,384]{1,0:T(8,128)S(1)}, f32[32,384]{1,0:T(8,128)S(1)}, u32[]{:S(2)}, u32[]{:S(2)}) collective-permute-start(f32[32,384]{1,0:T(8,128)S(1)} %add.87.one_ref), channel_id=1, source_target_pairs={{0,64},{64,0},{1,65},{65,1},{2,66},{66,2},{3,67},{67,3},{4,68},{68... | collective-permute-start | bytes 147464 | tf_op jit(solution)/shard_map/ppermute | solution.py:24
  56.1 3.0 %collective-permute-start.25 = (f32[32,384]{1,0:T(8,128)S(1)}, f32[32,384]{1,0:T(8,128)S(1)}, u32[]{:S(2)}, u32[]{:S(2)}) collective-permute-start(f32[32,384]{1,0:T(8,128)S(1)} %add.91.one_ref), channel_id=1, source_target_pairs={{0,64},{64,0},{1,65},{65,1},{2,66},{66,2},{3,67},{67,3},{4,68},{68... | collective-permute-start | bytes 147464 | tf_op jit(solution)/shard_map/ppermute | solution.py:24
  58.8 23.8 %copy-start.1 = (bf16[768,1536]{1,0:T(8,128)(2,1)S(1)}, bf16[768,1536]{1,0:T(8,128)(2,1)}, u32[]{:S(2)}) copy-start(bf16[768,1536]{1,0:T(8,128)(2,1)} %inverse_ref.1) | copy-start | bytes 7077892
  68.3 4.3 %collective-permute-start.26 = (f32[8,768]{1,0:T(8,128)S(1)}, f32[8,768]{1,0:T(8,128)S(1)}, u32[]{:S(2)}, u32[]{:S(2)}) collective-permute-start(f32[8,768]{1,0:T(8,128)S(1)} %reduce_sum.9), channel_id=1, source_target_pairs={{0,128},{128,0},{1,129},{129,1},{2,130},{130,2},{3,131},{131,3},{4... | collective-permute-start | bytes 73736 | tf_op jit(solution)/shard_map/ppermute | solution.py:24
  72.6 4.2 %collective-permute-start.27 = (f32[8,768]{1,0:T(8,128)S(1)}, f32[8,768]{1,0:T(8,128)S(1)}, u32[]{:S(2)}, u32[]{:S(2)}) collective-permute-start(f32[8,768]{1,0:T(8,128)S(1)} %add.93), channel_id=1, source_target_pairs={{0,8},{8,0},{16,24},{24,16},{1,9},{9,1},{17,25},{25,17},{2,10},{10... | collective-permute-start | bytes 73736 | tf_op jit(solution)/shard_map/ppermute | solution.py:24
  76.8 5.8 %collective-permute-start.28 = (f32[8,768]{1,0:T(8,128)S(1)}, f32[8,768]{1,0:T(8,128)S(1)}, u32[]{:S(2)}, u32[]{:S(2)}) collective-permute-start(f32[8,768]{1,0:T(8,128)S(1)} %add.94.one_ref), channel_id=1, source_target_pairs={{0,24},{8,16},{16,8},{24,0},{1,25},{9,17},{17,9},{25,1},{2,26},{10... | collective-permute-start | bytes 73736 | tf_op jit(solution)/shard_map/ppermute | solution.py:24
  83.0 6.7 %collective-permute-start.29 = (f32[8,1536]{1,0:T(8,128)S(1)}, f32[8,1536]{1,0:T(8,128)S(1)}, u32[]{:S(2)}, u32[]{:S(2)}) collective-permute-start(f32[8,1536]{1,0:T(8,128)S(1)} %root_part.1), channel_id=1, source_target_pairs={{0,32},{32,0},{1,33},{33,1},{2,34},{34,2},{3,35},{35,3},{4,36},{36... | collective-permute-start | bytes 147464 | tf_op jit(solution)/shard_map/ppermute | solution.py:24
  89.7 2.9 %collective-permute-start.30 = (f32[8,1536]{1,0:T(8,128)S(1)}, f32[8,1536]{1,0:T(8,128)S(1)}, u32[]{:S(2)}, u32[]{:S(2)}) collective-permute-start(f32[8,1536]{1,0:T(8,128)S(1)} %add.95), channel_id=1, source_target_pairs={{0,64},{64,0},{1,65},{65,1},{2,66},{66,2},{3,67},{67,3},{4,68},{68... | collective-permute-start | bytes 147464 | tf_op jit(solution)/shard_map/ppermute | solution.py:24

commit v11 on v10

--- a/solution.py
+++ b/solution.py
@@ -259,7 +259,10 @@
     return pair, partner(pair, "xl")
 
 
-def owner_sums(partial_sum):
+def owner_sums(partial_sum, part):
+    if part % 2 == 0:
+        pair = partial_sum + partner(partial_sum, OWN, 4)
+        return [pair] + [partner(pair, OWN, bit) for bit in (2, 3, 1)]
     far, back, near = [partner(partial_sum, OWN, bit) for bit in (2, 3, 1)]
     line = (partial_sum + near) + (far + back)
     return [line, partner(line, OWN, 4)]
@@ -284,10 +287,10 @@
     outs = kept_update(halves, inner, 0, (), PARTS)
     for part in range(PARTS):
         update, solved0, kept0 = outs[part::PARTS]
-        halves = prow_halves(next_solve(0, part, rhs, owner_sums(update), inverse))
+        halves = prow_halves(next_solve(0, part, rhs, owner_sums(update, part), inverse))
         early = early_update((kept0,), inner, (1,))
         update, solved1, kept1 = kept_update(halves, inner, 2, (early,))
-        halves = prow_halves(next_solve(1, part, rhs, owner_sums(update), inverse))
+        halves = prow_halves(next_solve(1, part, rhs, owner_sums(update, part), inverse))
         early = early_update((kept0, kept1), root, (0, 1))
         root_local, solved2 = kept_update(halves, root, 2, (early,), last=True)
         solved.append((solved0, solved1, solved2))

time: 104 us -> 97.2 us (0.935)
  starting transfers between devices: 54.2 us -> 46.6 us
  waiting for transfers between devices: 19.3 us -> 20.4 us
    ppermute x31, starting transfers between devices: 54.2 us -> 46.6 us  [partner(): lax.ppermute(shard, axis, [(i, i ^ bit) for i in range(lax.axis_size(axis...]
    ppermute x31, waiting for transfers between devices: 19.3 us -> 20.4 us  [partner(): lax.ppermute(shard, axis, [(i, i ^ bit) for i in range(lax.axis_size(axis...]
  transfers between devices with their start and end apart: 31 -> 31, of which waited for: 15 -> 18; matrix products, arithmetic and copies ran while one was open for 0% -> 0% of each run, Pallas kernels for 6% -> 7%
where the time goes in v11:
time: 97.2 us; the launch traced here: 96.1 us
  starting transfers between devices  46.6 us (48%)
  waiting for transfers between devices  20.4 us (21%)
  blocking collectives  18 us (19%)
  Pallas kernels  9.04 us (9%)
    ppermute x31, starting transfers between devices, partner(): lax.ppermute(shard, axis, [(i, i ^ bit) for i in range(lax.axis_size(axis...  46.6 us
    ppermute x31, waiting for transfers between devices, partner(): lax.ppermute(shard, axis, [(i, i ^ bit) for i in range(lax.axis_size(axis...  20.4 us
    all_to_all x2, blocking collectives, swap_blocks(): lax.all_to_all(blocks, OWN, 0, 0, axis_index_groups=[order], tiled=True)  18 us
    pallas_call x17, Pallas kernels, call(): pl.pallas_call(body, out_shape=[pltpu.VMEM(shape, kind) for shape, kind i...  8.28 us
  transfers between devices with their start and end apart: 31, of which 18 were waited for; matrix products, arithmetic and copies ran while one was open for 0% of the time, Pallas kernels for 7%

profile of v11, /device:TPU:1, one launch (start us, length us, event | category | flops | bytes accessed | tf_op | source)
XLA Modules:
  0.0 96.1 jit_solution(1042644015122410468)
XLA Ops:
  0.7 1.6 %first_solve.1 = f32[64,384]{1,0:T(8,128)S(1)} custom-call(s32[1]{0:T(128)} %bitcast.tree_ref, f32[4,3,64,768]{3,2,1,0:T(8,128)} %rhs_hbm.3, bf16[3,768,384]{2,1,0:T(8,128)(2,1)} %inverse_hbm.3), custom_call_target="tpu_custom_call" | custom-call | tf_op jit(solution)/shard_map/first_solve/pallas_call | solution.py:43
  2.3 3.3 %collective-permute-start = (f32[64,384]{1,0:T(8,128)S(1)}, f32[64,384]{1,0:T(8,128)S(1)}, u32[]{:S(2)}, u32[]{:S(2)}) collective-permute-start(f32[64,384]{1,0:T(8,128)S(1)} %first_solve.1), channel_id=1, source_target_pairs={{0,32},{32,0},{1,33},{33,1},{2,34},{34,2},{3,35},{35,3},{4,36},{36... | collective-permute-start | bytes 294920 | tf_op jit(solution)/shard_map/ppermute | solution.py:24
  5.6 0.9 collective-permute-done
  6.7 2.6 %stage.1 = (bf16[3,384,768]{2,1,0:T(8,128)(2,1)S(1)}, bf16[2,768,384]{2,1,0:T(8,128)(2,1)S(1)}, f32[2,64,768]{2,1,0:T(8,128)S(1)}) custom-call(s32[1]{0:T(128)} %bitcast.tree_ref, s32[3,3,6]{2,1,0:T(4,128)S(1)} %constant_dynamic-slice_fusion.2.mask_ref, f32[4,3,64,768]{3,2,1,0:T(8,128)} %rhs_hbm.3, bf16[3,768,384]{2,1,0:T(8,128)(2,1)} %inverse_hbm.3, ...), custom_call_target="tpu_custom_call" | custom-call | tf_op jit(solution)/shard_map/stage/pallas_call | solution.py:43
  9.3 1.4 %collective-permute-done.1.other_ref = f32[64,384]{1,0:T(8,128)S(1)} collective-permute-done((f32[64,384]{1,0:T(8,128)S(1)}, f32[64,384]{1,0:T(8,128)S(1)}, u32[]{:S(2)}, u32[]{:S(2)}) %collective-permute-start.1) | collective-permute-done | bytes 98336 | tf_op jit(solution)/shard_map/ppermute | solution.py:24
  10.7 0.2 kept_update.5
  10.9 0.1 collective-permute-start.2
  11.0 2.8 %collective-permute-start.9 = (f32[32,768]{1,0:T(8,128)S(1)}, f32[32,768]{1,0:T(8,128)S(1)}, u32[]{:S(2)}, u32[]{:S(2)}) collective-permute-start(f32[32,768]{1,0:T(8,128)S(1)} %get-tuple-element.31), channel_id=1, source_target_pairs={{0,2},{1,3},{2,0},{3,1},{4,6},{5,7},{6,4},{7,5},{8,10},{9,11},{10,... | collective-permute-start | bytes 294920 | tf_op jit(solution)/shard_map/ppermute | solution.py:24
  13.8 0.8 collective-permute-start.10
  14.6 3.2 %collective-permute-start.3 = (f32[32,768]{1,0:T(8,128)S(1)}, f32[32,768]{1,0:T(8,128)S(1)}, u32[]{:S(2)}, u32[]{:S(2)}) collective-permute-start(f32[32,768]{1,0:T(8,128)S(1)} %add.64.refs_0_), channel_id=1, source_target_pairs={{0,2},{1,3},{2,0},{3,1},{4,6},{5,7},{6,4},{7,5},{8,10},{9,11},{10,... | collective-permute-start | bytes 294920 | tf_op jit(solution)/shard_map/ppermute | solution.py:24
  17.7 0.8 collective-permute-start.4
  18.5 0.3 collective-permute-done.10
  18.8 0.2 collective-permute-done.8
  19.0 0.6 collective-permute-start.11
  19.6 1.2 %collective-permute-done.3.refs_1_ = f32[32,768]{1,0:T(8,128)S(1)} collective-permute-done((f32[32,768]{1,0:T(8,128)S(1)}, f32[32,768]{1,0:T(8,128)S(1)}, u32[]{:S(2)}, u32[]{:S(2)}) %collective-permute-start.3) | collective-permute-done | bytes 98336 | tf_op jit(solution)/shard_map/ppermute | solution.py:24
  20.8 3.2 %collective-permute-done.4.refs_2_ = f32[32,768]{1,0:T(8,128)S(1)} collective-permute-done((f32[32,768]{1,0:T(8,128)S(1)}, f32[32,768]{1,0:T(8,128)S(1)}, u32[]{:S(2)}, u32[]{:S(2)}) %collective-permute-start.4) | collective-permute-done | bytes 98336 | tf_op jit(solution)/shard_map/ppermute | solution.py:24
  24.0 0.2 next_solve.4
  24.2 2.2 %collective-permute-start.6 = (f32[32,384]{1,0:T(8,128)S(1)}, f32[32,384]{1,0:T(8,128)S(1)}, u32[]{:S(2)}, u32[]{:S(2)}) collective-permute-start(f32[32,384]{1,0:T(8,128)S(1)} %next_solve.4), channel_id=1, source_target_pairs={{0,32},{32,0},{1,33},{33,1},{2,34},{34,2},{3,35},{35,3},{4,36},{36... | collective-permute-start | bytes 147464 | tf_op jit(solution)/shard_map/ppermute | solution.py:24
  26.4 0.2 next_solve.5
  26.7 1.1 %collective-permute-start.12 = (f32[32,384]{1,0:T(8,128)S(1)}, f32[32,384]{1,0:T(8,128)S(1)}, u32[]{:S(2)}, u32[]{:S(2)}) collective-permute-start(f32[32,384]{1,0:T(8,128)S(1)} %next_solve.5), channel_id=1, source_target_pairs={{0,32},{32,0},{1,33},{33,1},{2,34},{34,2},{3,35},{35,3},{4,36},{36... | collective-permute-start | bytes 147464 | tf_op jit(solution)/shard_map/ppermute | solution.py:24
  27.7 1.3 %collective-permute-start.7 = (f32[32,384]{1,0:T(8,128)S(1)}, f32[32,384]{1,0:T(8,128)S(1)}, u32[]{:S(2)}, u32[]{:S(2)}) collective-permute-start(f32[32,384]{1,0:T(8,128)S(1)} %add.65.one_ref), channel_id=1, source_target_pairs={{0,64},{64,0},{1,65},{65,1},{2,66},{66,2},{3,67},{67,3},{4,68},{68... | collective-permute-start | bytes 147464 | tf_op jit(solution)/shard_map/ppermute | solution.py:24
  29.0 0.8 collective-permute-start.13
  29.9 0.2 early_update.4.refs_0_
  30.0 0.2 early_update.5.refs_0_
  30.3 0.9 collective-permute-done.7.other_ref
  31.2 0.2 kept_update.6
  31.4 0.1 collective-permute-start.14
  31.5 0.6 collective-permute-done.13.other_ref
  32.1 0.2 kept_update.7
  32.3 2.2 %collective-permute-start.21 = (f32[32,768]{1,0:T(8,128)S(1)}, f32[32,768]{1,0:T(8,128)S(1)}, u32[]{:S(2)}, u32[]{:S(2)}) collective-permute-start(f32[32,768]{1,0:T(8,128)S(1)} %get-tuple-element.37), channel_id=1, source_target_pairs={{0,2},{1,3},{2,0},{3,1},{4,6},{5,7},{6,4},{7,5},{8,10},{9,11},{10,... | collective-permute-start | bytes 294920 | tf_op jit(solution)/shard_map/ppermute | solution.py:24
  34.4 0.8 collective-permute-start.22
  35.2 3.2 %collective-permute-start.15 = (f32[32,768]{1,0:T(8,128)S(1)}, f32[32,768]{1,0:T(8,128)S(1)}, u32[]{:S(2)}, u32[]{:S(2)}) collective-permute-start(f32[32,768]{1,0:T(8,128)S(1)} %add.70.refs_0_), channel_id=1, source_target_pairs={{0,2},{1,3},{2,0},{3,1},{4,6},{5,7},{6,4},{7,5},{8,10},{9,11},{10,... | collective-permute-start | bytes 294920 | tf_op jit(solution)/shard_map/ppermute | solution.py:24
  38.4 0.8 collective-permute-start.16
  39.2 1.0 %collective-permute-done.22 = f32[32,768]{1,0:T(8,128)S(1)} collective-permute-done((f32[32,768]{1,0:T(8,128)S(1)}, f32[32,768]{1,0:T(8,128)S(1)}, u32[]{:S(2)}, u32[]{:S(2)}) %collective-permute-start.22) | collective-permute-done | bytes 98336 | tf_op jit(solution)/shard_map/ppermute | solution.py:24
  40.2 0.7 collective-permute-start.23
  40.9 0.5 collective-permute-done.15.refs_1_
  41.4 3.2 %collective-permute-done.16.refs_2_ = f32[32,768]{1,0:T(8,128)S(1)} collective-permute-done((f32[32,768]{1,0:T(8,128)S(1)}, f32[32,768]{1,0:T(8,128)S(1)}, u32[]{:S(2)}, u32[]{:S(2)}) %collective-permute-start.16) | collective-permute-done | bytes 98336 | tf_op jit(solution)/shard_map/ppermute | solution.py:24
  44.7 0.2 next_solve.6
  44.9 2.2 %collective-permute-start.18 = (f32[32,384]{1,0:T(8,128)S(1)}, f32[32,384]{1,0:T(8,128)S(1)}, u32[]{:S(2)}, u32[]{:S(2)}) collective-permute-start(f32[32,384]{1,0:T(8,128)S(1)} %next_solve.6), channel_id=1, source_target_pairs={{0,32},{32,0},{1,33},{33,1},{2,34},{34,2},{3,35},{35,3},{4,36},{36... | collective-permute-start | bytes 147464 | tf_op jit(solution)/shard_map/ppermute | solution.py:24
  47.1 0.2 next_solve.7
  47.3 1.1 %collective-permute-start.24 = (f32[32,384]{1,0:T(8,128)S(1)}, f32[32,384]{1,0:T(8,128)S(1)}, u32[]{:S(2)}, u32[]{:S(2)}) collective-permute-start(f32[32,384]{1,0:T(8,128)S(1)} %next_solve.7), channel_id=1, source_target_pairs={{0,32},{32,0},{1,33},{33,1},{2,34},{34,2},{3,35},{35,3},{4,36},{36... | collective-permute-start | bytes 147464 | tf_op jit(solution)/shard_map/ppermute | solution.py:24
  48.4 0.9 collective-permute-start.19
  49.3 0.8 collective-permute-start.25
  50.2 0.9 masked.1.refs_2_.factor_ref
  51.1 0.3 early_update.6.refs_0_
  51.4 0.3 early_update.7.refs_0_
  51.8 0.2 kept_update.8
  52.0 0.4 collective-permute-done.25.other_ref
  52.5 0.2 kept_update.9
  52.7 8.4 %all_to_all.10 = f32[8,8,768]{2,1,0:T(8,128)S(1)} all-to-all(f32[8,8,768]{2,1,0:T(8,128)S(1)} %maximum_bitcast_fusion), channel_id=1, replica_groups={{7,6,5,4,3,2,1,0},{15,14,13,12,11,10,9,8},{23,22,21,20,19,18,17,16},{31..., dimensions={0} | all-to-all | bytes 393216 | tf_op jit(solution)/shard_map/all_to_all | solution.py:29
  61.1 2.5 %collective-permute-start.26 = (f32[8,768]{1,0:T(8,128)S(1)}, f32[8,768]{1,0:T(8,128)S(1)}, u32[]{:S(2)}, u32[]{:S(2)}) collective-permute-start(f32[8,768]{1,0:T(8,128)S(1)} %reduce_sum.9), channel_id=1, source_target_pairs={{0,128},{128,0},{1,129},{129,1},{2,130},{130,2},{3,131},{131,3},{4... | collective-permute-start | bytes 73736 | tf_op jit(solution)/shard_map/ppermute | solution.py:24
  63.6 0.8 stacked.1
  64.4 1.0 %collective-permute-done.26 = f32[8,768]{1,0:T(8,128)S(1)} collective-permute-done((f32[8,768]{1,0:T(8,128)S(1)}, f32[8,768]{1,0:T(8,128)S(1)}, u32[]{:S(2)}, u32[]{:S(2)}) %collective-permute-start.26) | collective-permute-done | bytes 24608 | tf_op jit(solution)/shard_map/ppermute | solution.py:24
  65.4 3.0 %collective-permute-start.27 = (f32[8,768]{1,0:T(8,128)S(1)}, f32[8,768]{1,0:T(8,128)S(1)}, u32[]{:S(2)}, u32[]{:S(2)}) collective-permute-start(f32[8,768]{1,0:T(8,128)S(1)} %add.77), channel_id=1, source_target_pairs={{0,8},{8,0},{16,24},{24,16},{1,9},{9,1},{17,25},{25,17},{2,10},{10... | collective-permute-start | bytes 73736 | tf_op jit(solution)/shard_map/ppermute | solution.py:24
  68.4 1.2 %collective-permute-done.27 = f32[8,768]{1,0:T(8,128)S(1)} collective-permute-done((f32[8,768]{1,0:T(8,128)S(1)}, f32[8,768]{1,0:T(8,128)S(1)}, u32[]{:S(2)}, u32[]{:S(2)}) %collective-permute-start.27) | collective-permute-done | bytes 24608 | tf_op jit(solution)/shard_map/ppermute | solution.py:24
  69.6 4.8 %collective-permute-start.28 = (f32[8,768]{1,0:T(8,128)S(1)}, f32[8,768]{1,0:T(8,128)S(1)}, u32[]{:S(2)}, u32[]{:S(2)}) collective-permute-start(f32[8,768]{1,0:T(8,128)S(1)} %add.78.one_ref), channel_id=1, source_target_pairs={{0,24},{8,16},{16,8},{24,0},{1,25},{9,17},{17,9},{25,1},{2,26},{10... | collective-permute-start | bytes 73736 | tf_op jit(solution)/shard_map/ppermute | solution.py:24
  74.4 1.2 %collective-permute-done.28.other_ref = f32[8,768]{1,0:T(8,128)S(1)} collective-permute-done((f32[8,768]{1,0:T(8,128)S(1)}, f32[8,768]{1,0:T(8,128)S(1)}, u32[]{:S(2)}, u32[]{:S(2)}) %collective-permute-start.28) | collective-permute-done | bytes 24608 | tf_op jit(solution)/shard_map/ppermute | solution.py:24
  75.6 0.4 root_part.1
  76.0 5.8 %collective-permute-start.29 = (f32[8,1536]{1,0:T(8,128)S(1)}, f32[8,1536]{1,0:T(8,128)S(1)}, u32[]{:S(2)}, u32[]{:S(2)}) collective-permute-start(f32[8,1536]{1,0:T(8,128)S(1)} %root_part.1), channel_id=1, source_target_pairs={{0,32},{32,0},{1,33},{33,1},{2,34},{34,2},{3,35},{35,3},{4,36},{36... | collective-permute-start | bytes 147464 | tf_op jit(solution)/shard_map/ppermute | solution.py:24
  81.8 0.9 collective-permute-done.29
  82.7 0.8 collective-permute-start.30
  83.5 2.1 %collective-permute-done.30 = f32[8,1536]{1,0:T(8,128)S(1)} collective-permute-done((f32[8,1536]{1,0:T(8,128)S(1)}, f32[8,1536]{1,0:T(8,128)S(1)}, u32[]{:S(2)}, u32[]{:S(2)}) %collective-permute-start.30) | collective-permute-done | bytes 49184 | tf_op jit(solution)/shard_map/ppermute | solution.py:24
  85.7 9.6 %all_to_all.11 = f32[8,8,1536]{2,1,0:T(8,128)S(1)} all-to-all(f32[8,8,1536]{2,1,0:T(8,128)S(1)} %broadcast_in_dim.2), channel_id=1, replica_groups={{7,6,5,4,3,2,1,0},{15,14,13,12,11,10,9,8},{23,22,21,20,19,18,17,16},{31..., dimensions={0} | all-to-all | bytes 786432 | tf_op jit(solution)/shard_map/all_to_all | solution.py:29
  95.3 0.7 copy.11
  (48 shorter events, 0.6 us)
Async XLA Ops:
  0.6 73.7 %copy-start = (f32[64,768]{1,0:T(8,128)S(1)}, f32[64,768]{1,0:T(8,128)}, u32[]{:S(2)}) copy-start(f32[64,768]{1,0:T(8,128)} %param.9) | copy-start | bytes 589828
  0.7 6.0 %copy-start.3 = (s32[3,3,24]{2,1,0:T(4,128)S(1)}, s32[3,3,24]{2,1,0:T(4,128)}, u32[]{:S(2)}) copy-start(s32[3,3,24]{2,1,0:T(4,128)} %param.13) | copy-start | bytes 2596
  2.3 4.3 %collective-permute-start = (f32[64,384]{1,0:T(8,128)S(1)}, f32[64,384]{1,0:T(8,128)S(1)}, u32[]{:S(2)}, u32[]{:S(2)}) collective-permute-start(f32[64,384]{1,0:T(8,128)S(1)} %first_solve.1), channel_id=1, source_target_pairs={{0,32},{32,0},{1,33},{33,1},{2,34},{34,2},{3,35},{35,3},{4,36},{36... | collective-permute-start | bytes 294920 | tf_op jit(solution)/shard_map/ppermute | solution.py:24
  6.5 4.1 %collective-permute-start.1 = (f32[64,384]{1,0:T(8,128)S(1)}, f32[64,384]{1,0:T(8,128)S(1)}, u32[]{:S(2)}, u32[]{:S(2)}) collective-permute-start(f32[64,384]{1,0:T(8,128)S(1)} %add.61.one_ref), channel_id=1, source_target_pairs={{0,64},{64,0},{1,65},{65,1},{2,66},{66,2},{3,67},{67,3},{4,68},{68... | collective-permute-start | bytes 294920 | tf_op jit(solution)/shard_map/ppermute | solution.py:24
  10.9 3.7 %collective-permute-start.2 = (f32[32,768]{1,0:T(8,128)S(1)}, f32[32,768]{1,0:T(8,128)S(1)}, u32[]{:S(2)}, u32[]{:S(2)}) collective-permute-start(f32[32,768]{1,0:T(8,128)S(1)} %get-tuple-element.27), channel_id=1, source_target_pairs={{0,4},{1,5},{2,6},{3,7},{4,0},{5,1},{6,2},{7,3},{8,12},{9,13},{10,... | collective-permute-start | bytes 294920 | tf_op jit(solution)/shard_map/ppermute | solution.py:24
  11.0 7.5 %collective-permute-start.9 = (f32[32,768]{1,0:T(8,128)S(1)}, f32[32,768]{1,0:T(8,128)S(1)}, u32[]{:S(2)}, u32[]{:S(2)}) collective-permute-start(f32[32,768]{1,0:T(8,128)S(1)} %get-tuple-element.31), channel_id=1, source_target_pairs={{0,2},{1,3},{2,0},{3,1},{4,6},{5,7},{6,4},{7,5},{8,10},{9,11},{10,... | collective-permute-start | bytes 294920 | tf_op jit(solution)/shard_map/ppermute | solution.py:24
  13.8 5.0 %collective-permute-start.10 = (f32[32,768]{1,0:T(8,128)S(1)}, f32[32,768]{1,0:T(8,128)S(1)}, u32[]{:S(2)}, u32[]{:S(2)}) collective-permute-start(f32[32,768]{1,0:T(8,128)S(1)} %get-tuple-element.31), channel_id=1, source_target_pairs={{0,3},{1,2},{2,1},{3,0},{4,7},{5,6},{6,5},{7,4},{8,11},{9,10},{10,... | collective-permute-start | bytes 294920 | tf_op jit(solution)/shard_map/ppermute | solution.py:24
  14.5 4.4 %collective-permute-start.8 = (f32[32,768]{1,0:T(8,128)S(1)}, f32[32,768]{1,0:T(8,128)S(1)}, u32[]{:S(2)}, u32[]{:S(2)}) collective-permute-start(f32[32,768]{1,0:T(8,128)S(1)} %get-tuple-element.31), channel_id=1, source_target_pairs={{0,1},{1,0},{2,3},{3,2},{4,5},{5,4},{6,7},{7,6},{8,9},{9,8},{10,11... | collective-permute-start | bytes 294920 | tf_op jit(solution)/shard_map/ppermute | solution.py:24
  14.6 6.2 %collective-permute-start.3 = (f32[32,768]{1,0:T(8,128)S(1)}, f32[32,768]{1,0:T(8,128)S(1)}, u32[]{:S(2)}, u32[]{:S(2)}) collective-permute-start(f32[32,768]{1,0:T(8,128)S(1)} %add.64.refs_0_), channel_id=1, source_target_pairs={{0,2},{1,3},{2,0},{3,1},{4,6},{5,7},{6,4},{7,5},{8,10},{9,11},{10,... | collective-permute-start | bytes 294920 | tf_op jit(solution)/shard_map/ppermute | solution.py:24
  17.7 6.3 %collective-permute-start.4 = (f32[32,768]{1,0:T(8,128)S(1)}, f32[32,768]{1,0:T(8,128)S(1)}, u32[]{:S(2)}, u32[]{:S(2)}) collective-permute-start(f32[32,768]{1,0:T(8,128)S(1)} %add.64.refs_0_), channel_id=1, source_target_pairs={{0,3},{1,2},{2,1},{3,0},{4,7},{5,6},{6,5},{7,4},{8,11},{9,10},{10,... | collective-permute-start | bytes 294920 | tf_op jit(solution)/shard_map/ppermute | solution.py:24
  18.5 5.5 %collective-permute-start.5 = (f32[32,768]{1,0:T(8,128)S(1)}, f32[32,768]{1,0:T(8,128)S(1)}, u32[]{:S(2)}, u32[]{:S(2)}) collective-permute-start(f32[32,768]{1,0:T(8,128)S(1)} %add.64.refs_0_), channel_id=1, source_target_pairs={{0,1},{1,0},{2,3},{3,2},{4,5},{5,4},{6,7},{7,6},{8,9},{9,8},{10,11... | collective-permute-start | bytes 294920 | tf_op jit(solution)/shard_map/ppermute | solution.py:24
  19.0 7.4 %collective-permute-start.11 = (f32[32,768]{1,0:T(8,128)S(1)}, f32[32,768]{1,0:T(8,128)S(1)}, u32[]{:S(2)}, u32[]{:S(2)}) collective-permute-start(f32[32,768]{1,0:T(8,128)S(1)} %add_add_fusion.1.refs_0_), channel_id=1, source_target_pairs={{0,4},{1,5},{2,6},{3,7},{4,0},{5,1},{6,2},{7,3},{8,12},{9,13},{10,... | collective-permute-start | bytes 294920 | tf_op jit(solution)/shard_map/ppermute | solution.py:24
  24.2 3.5 %collective-permute-start.6 = (f32[32,384]{1,0:T(8,128)S(1)}, f32[32,384]{1,0:T(8,128)S(1)}, u32[]{:S(2)}, u32[]{:S(2)}) collective-permute-start(f32[32,384]{1,0:T(8,128)S(1)} %next_solve.4), channel_id=1, source_target_pairs={{0,32},{32,0},{1,33},{33,1},{2,34},{34,2},{3,35},{35,3},{4,36},{36... | collective-permute-start | bytes 147464 | tf_op jit(solution)/shard_map/ppermute | solution.py:24
  26.7 2.4 %collective-permute-start.12 = (f32[32,384]{1,0:T(8,128)S(1)}, f32[32,384]{1,0:T(8,128)S(1)}, u32[]{:S(2)}, u32[]{:S(2)}) collective-permute-start(f32[32,384]{1,0:T(8,128)S(1)} %next_solve.5), channel_id=1, source_target_pairs={{0,32},{32,0},{1,33},{33,1},{2,34},{34,2},{3,35},{35,3},{4,36},{36... | collective-permute-start | bytes 147464 | tf_op jit(solution)/shard_map/ppermute | solution.py:24
  27.7 3.4 %collective-permute-start.7 = (f32[32,384]{1,0:T(8,128)S(1)}, f32[32,384]{1,0:T(8,128)S(1)}, u32[]{:S(2)}, u32[]{:S(2)}) collective-permute-start(f32[32,384]{1,0:T(8,128)S(1)} %add.65.one_ref), channel_id=1, source_target_pairs={{0,64},{64,0},{1,65},{65,1},{2,66},{66,2},{3,67},{67,3},{4,68},{68... | collective-permute-start | bytes 147464 | tf_op jit(solution)/shard_map/ppermute | solution.py:24
  29.0 3.0 %collective-permute-start.13 = (f32[32,384]{1,0:T(8,128)S(1)}, f32[32,384]{1,0:T(8,128)S(1)}, u32[]{:S(2)}, u32[]{:S(2)}) collective-permute-start(f32[32,384]{1,0:T(8,128)S(1)} %add.69.one_ref), channel_id=1, source_target_pairs={{0,64},{64,0},{1,65},{65,1},{2,66},{66,2},{3,67},{67,3},{4,68},{68... | collective-permute-start | bytes 147464 | tf_op jit(solution)/shard_map/ppermute | solution.py:24
  31.4 3.9 %collective-permute-start.14 = (f32[32,768]{1,0:T(8,128)S(1)}, f32[32,768]{1,0:T(8,128)S(1)}, u32[]{:S(2)}, u32[]{:S(2)}) collective-permute-start(f32[32,768]{1,0:T(8,128)S(1)} %get-tuple-element.34), channel_id=1, source_target_pairs={{0,4},{1,5},{2,6},{3,7},{4,0},{5,1},{6,2},{7,3},{8,12},{9,13},{10,... | collective-permute-start | bytes 294920 | tf_op jit(solution)/shard_map/ppermute | solution.py:24
  32.3 6.9 %collective-permute-start.21 = (f32[32,768]{1,0:T(8,128)S(1)}, f32[32,768]{1,0:T(8,128)S(1)}, u32[]{:S(2)}, u32[]{:S(2)}) collective-permute-start(f32[32,768]{1,0:T(8,128)S(1)} %get-tuple-element.37), channel_id=1, source_target_pairs={{0,2},{1,3},{2,0},{3,1},{4,6},{5,7},{6,4},{7,5},{8,10},{9,11},{10,... | collective-permute-start | bytes 294920 | tf_op jit(solution)/shard_map/ppermute | solution.py:24
  34.4 5.7 %collective-permute-start.22 = (f32[32,768]{1,0:T(8,128)S(1)}, f32[32,768]{1,0:T(8,128)S(1)}, u32[]{:S(2)}, u32[]{:S(2)}) collective-permute-start(f32[32,768]{1,0:T(8,128)S(1)} %get-tuple-element.37), channel_id=1, source_target_pairs={{0,3},{1,2},{2,1},{3,0},{4,7},{5,6},{6,5},{7,4},{8,11},{9,10},{10,... | collective-permute-start | bytes 294920 | tf_op jit(solution)/shard_map/ppermute | solution.py:24
  35.2 5.0 %collective-permute-start.20 = (f32[32,768]{1,0:T(8,128)S(1)}, f32[32,768]{1,0:T(8,128)S(1)}, u32[]{:S(2)}, u32[]{:S(2)}) collective-permute-start(f32[32,768]{1,0:T(8,128)S(1)} %get-tuple-element.37), channel_id=1, source_target_pairs={{0,1},{1,0},{2,3},{3,2},{4,5},{5,4},{6,7},{7,6},{8,9},{9,8},{10,11... | collective-permute-start | bytes 294920 | tf_op jit(solution)/shard_map/ppermute | solution.py:24
  35.2 6.2 %collective-permute-start.15 = (f32[32,768]{1,0:T(8,128)S(1)}, f32[32,768]{1,0:T(8,128)S(1)}, u32[]{:S(2)}, u32[]{:S(2)}) collective-permute-start(f32[32,768]{1,0:T(8,128)S(1)} %add.70.refs_0_), channel_id=1, source_target_pairs={{0,2},{1,3},{2,0},{3,1},{4,6},{5,7},{6,4},{7,5},{8,10},{9,11},{10,... | collective-permute-start | bytes 294920 | tf_op jit(solution)/shard_map/ppermute | solution.py:24
  38.4 6.3 %collective-permute-start.16 = (f32[32,768]{1,0:T(8,128)S(1)}, f32[32,768]{1,0:T(8,128)S(1)}, u32[]{:S(2)}, u32[]{:S(2)}) collective-permute-start(f32[32,768]{1,0:T(8,128)S(1)} %add.70.refs_0_), channel_id=1, source_target_pairs={{0,3},{1,2},{2,1},{3,0},{4,7},{5,6},{6,5},{7,4},{8,11},{9,10},{10,... | collective-permute-start | bytes 294920 | tf_op jit(solution)/shard_map/ppermute | solution.py:24
  39.2 5.5 %collective-permute-start.17 = (f32[32,768]{1,0:T(8,128)S(1)}, f32[32,768]{1,0:T(8,128)S(1)}, u32[]{:S(2)}, u32[]{:S(2)}) collective-permute-start(f32[32,768]{1,0:T(8,128)S(1)} %add.70.refs_0_), channel_id=1, source_target_pairs={{0,1},{1,0},{2,3},{3,2},{4,5},{5,4},{6,7},{7,6},{8,9},{9,8},{10,11... | collective-permute-start | bytes 294920 | tf_op jit(solution)/shard_map/ppermute | solution.py:24
  40.2 9.9 %copy-start.4 = (s32[3,3,24]{2,1,0:T(4,128)S(1)}, s32[3,3,24]{2,1,0:T(4,128)}, u32[]{:S(2)}) copy-start(s32[3,3,24]{2,1,0:T(4,128)} %param.15) | copy-start | bytes 2596
  40.2 10.0 %copy-start.2 = (bf16[3,384,768]{2,1,0:T(8,128)(2,1)S(1)}, bf16[3,384,768]{2,1,0:T(8,128)(2,1)}, u32[]{:S(2)}) copy-start(bf16[3,384,768]{2,1,0:T(8,128)(2,1)} %factor_ref.1) | copy-start | bytes 5308420
  40.2 6.9 %collective-permute-start.23 = (f32[32,768]{1,0:T(8,128)S(1)}, f32[32,768]{1,0:T(8,128)S(1)}, u32[]{:S(2)}, u32[]{:S(2)}) collective-permute-start(f32[32,768]{1,0:T(8,128)S(1)} %add_add_fusion.refs_0_), channel_id=1, source_target_pairs={{0,4},{1,5},{2,6},{3,7},{4,0},{5,1},{6,2},{7,3},{8,12},{9,13},{10,... | collective-permute-start | bytes 294920 | tf_op jit(solution)/shard_map/ppermute | solution.py:24
  44.9 3.5 %collective-permute-start.18 = (f32[32,384]{1,0:T(8,128)S(1)}, f32[32,384]{1,0:T(8,128)S(1)}, u32[]{:S(2)}, u32[]{:S(2)}) collective-permute-start(f32[32,384]{1,0:T(8,128)S(1)} %next_solve.6), channel_id=1, source_target_pairs={{0,32},{32,0},{1,33},{33,1},{2,34},{34,2},{3,35},{35,3},{4,36},{36... | collective-permute-start | bytes 147464 | tf_op jit(solution)/shard_map/ppermute | solution.py:24
  47.3 1.9 %collective-permute-start.24 = (f32[32,384]{1,0:T(8,128)S(1)}, f32[32,384]{1,0:T(8,128)S(1)}, u32[]{:S(2)}, u32[]{:S(2)}) collective-permute-start(f32[32,384]{1,0:T(8,128)S(1)} %next_solve.7), channel_id=1, source_target_pairs={{0,32},{32,0},{1,33},{33,1},{2,34},{34,2},{3,35},{35,3},{4,36},{36... | collective-permute-start | bytes 147464 | tf_op jit(solution)/shard_map/ppermute | solution.py:24
  48.4 3.4 %collective-permute-start.19 = (f32[32,384]{1,0:T(8,128)S(1)}, f32[32,384]{1,0:T(8,128)S(1)}, u32[]{:S(2)}, u32[]{:S(2)}) collective-permute-start(f32[32,384]{1,0:T(8,128)S(1)} %add.71.one_ref), channel_id=1, source_target_pairs={{0,64},{64,0},{1,65},{65,1},{2,66},{66,2},{3,67},{67,3},{4,68},{68... | collective-permute-start | bytes 147464 | tf_op jit(solution)/shard_map/ppermute | solution.py:24
  49.3 3.2 %collective-permute-start.25 = (f32[32,384]{1,0:T(8,128)S(1)}, f32[32,384]{1,0:T(8,128)S(1)}, u32[]{:S(2)}, u32[]{:S(2)}) collective-permute-start(f32[32,384]{1,0:T(8,128)S(1)} %add.75.one_ref), channel_id=1, source_target_pairs={{0,64},{64,0},{1,65},{65,1},{2,66},{66,2},{3,67},{67,3},{4,68},{68... | collective-permute-start | bytes 147464 | tf_op jit(solution)/shard_map/ppermute | solution.py:24
  52.0 23.6 %copy-start.1 = (bf16[768,1536]{1,0:T(8,128)(2,1)S(1)}, bf16[768,1536]{1,0:T(8,128)(2,1)}, u32[]{:S(2)}) copy-start(bf16[768,1536]{1,0:T(8,128)(2,1)} %inverse_ref.1) | copy-start | bytes 7077892
  61.1 4.3 %collective-permute-start.26 = (f32[8,768]{1,0:T(8,128)S(1)}, f32[8,768]{1,0:T(8,128)S(1)}, u32[]{:S(2)}, u32[]{:S(2)}) collective-permute-start(f32[8,768]{1,0:T(8,128)S(1)} %reduce_sum.9), channel_id=1, source_target_pairs={{0,128},{128,0},{1,129},{129,1},{2,130},{130,2},{3,131},{131,3},{4... | collective-permute-start | bytes 73736 | tf_op jit(solution)/shard_map/ppermute | solution.py:24
  65.4 4.2 %collective-permute-start.27 = (f32[8,768]{1,0:T(8,128)S(1)}, f32[8,768]{1,0:T(8,128)S(1)}, u32[]{:S(2)}, u32[]{:S(2)}) collective-permute-start(f32[8,768]{1,0:T(8,128)S(1)} %add.77), channel_id=1, source_target_pairs={{0,8},{8,0},{16,24},{24,16},{1,9},{9,1},{17,25},{25,17},{2,10},{10... | collective-permute-start | bytes 73736 | tf_op jit(solution)/shard_map/ppermute | solution.py:24
  69.6 6.0 %collective-permute-start.28 = (f32[8,768]{1,0:T(8,128)S(1)}, f32[8,768]{1,0:T(8,128)S(1)}, u32[]{:S(2)}, u32[]{:S(2)}) collective-permute-start(f32[8,768]{1,0:T(8,128)S(1)} %add.78.one_ref), channel_id=1, source_target_pairs={{0,24},{8,16},{16,8},{24,0},{1,25},{9,17},{17,9},{25,1},{2,26},{10... | collective-permute-start | bytes 73736 | tf_op jit(solution)/shard_map/ppermute | solution.py:24
  76.0 6.7 %collective-permute-start.29 = (f32[8,1536]{1,0:T(8,128)S(1)}, f32[8,1536]{1,0:T(8,128)S(1)}, u32[]{:S(2)}, u32[]{:S(2)}) collective-permute-start(f32[8,1536]{1,0:T(8,128)S(1)} %root_part.1), channel_id=1, source_target_pairs={{0,32},{32,0},{1,33},{33,1},{2,34},{34,2},{3,35},{35,3},{4,36},{36... | collective-permute-start | bytes 147464 | tf_op jit(solution)/shard_map/ppermute | solution.py:24
  82.7 2.9 %collective-permute-start.30 = (f32[8,1536]{1,0:T(8,128)S(1)}, f32[8,1536]{1,0:T(8,128)S(1)}, u32[]{:S(2)}, u32[]{:S(2)}) collective-permute-start(f32[8,1536]{1,0:T(8,128)S(1)} %add.79), channel_id=1, source_target_pairs={{0,64},{64,0},{1,65},{65,1},{2,66},{66,2},{3,67},{67,3},{4,68},{68... | collective-permute-start | bytes 147464 | tf_op jit(solution)/shard_map/ppermute | solution.py:24

commit v12 on v11

--- a/solution.py
+++ b/solution.py
@@ -8,10 +8,10 @@
 
 LEVELS = 3
 TILE = 128
-PARTS = 2
+SPLIT = (5, 3)
 PROW = ("xl", "core")
 OWN = "own"
-SCOPED_BYTES = 4 << 20
+SCOPED_BYTES = 8 << 20
 F32 = jnp.float32
 BF16 = jnp.bfloat16
 
@@ -49,6 +49,11 @@
         compiler_params=pltpu.CompilerParams(vmem_limit_bytes=SCOPED_BYTES),
         name=name,
     )(*args)
+
+
+def places(rows):
+    ends = [rows * sum(SPLIT[:k]) // sum(SPLIT) for k in range(len(SPLIT) + 1)]
+    return [slice(*pair) for pair in zip(ends[:-1], ends[1:])]
 
 
 def product(left, right):
@@ -98,7 +103,7 @@
 
 def next_solve(place, part, rhs, sums, diag_inverse):
     few = sums[0].shape[0]
-    rows = slice(part * few, (part + 1) * few)
+    rows = places(rhs.shape[1])[part]
 
     def body(rhs_ref, *refs):
         *sum_refs, inverse_ref, out_ref = refs
@@ -182,13 +187,15 @@
 
 def stacked(parts):
     levels, count = len(parts), len(parts[0])
-    rows, cols = parts[0][0].shape
+    rows = sum(part.shape[0] for part in parts[0])
+    cols = parts[0][0].shape[1]
+    pieces = places(rows)
 
     def body(*refs):
         *part_refs, out_hbm, sems = refs
         copies = [
             pltpu.make_async_copy(
-                ref, out_hbm.at[k // count, pl.ds(k % count * rows, rows)], sems.at[k]
+                ref, out_hbm.at[k // count, pieces[k % count]], sems.at[k]
             )
             for k, ref in enumerate(part_refs)
         ]
@@ -200,7 +207,7 @@
     args = [pltpu.with_memory_space_constraint(part, pltpu.VMEM) for one in parts for part in one]
     return pl.pallas_call(
         body,
-        out_shape=jax.ShapeDtypeStruct((levels, count * rows, cols), F32),
+        out_shape=jax.ShapeDtypeStruct((levels, rows, cols), F32),
         in_specs=[ON_CHIP] * len(args),
         out_specs=IN_PLACE,
         scratch_shapes=[pltpu.SemaphoreType.DMA((len(args),))],
@@ -209,11 +216,11 @@
     )(*args)
 
 
-def kept_update(halves, factor, block, before, parts=1, last=False):
+def kept_update(halves, factor, block, before, split=False, last=False):
     rows, cols = halves[0].shape
     out_cols = factor.shape[2]
-    few = rows // parts
-    places = [slice(k * few, (k + 1) * few) for k in range(parts)]
+    pieces = places(rows) if split else [slice(0, rows)]
+    parts = len(pieces)
 
     def body(one_ref, other_ref, factor_ref, *refs):
         before_refs, outs = refs[: len(before)], refs[len(before) :]
@@ -223,11 +230,13 @@
         for ref in before_refs:
             update = update + ref[...]
         for k, whole in enumerate((update, solved, kept)):
-            for ref, place in zip(outs[k * parts : (k + 1) * parts], places):
+            for ref, place in zip(outs[k * parts : (k + 1) * parts], pieces):
                 ref[...] = whole[place]
 
-    kinds = [((few, out_cols), F32), ((few, cols), F32), ((few, cols), BF16)]
-    outs = [kind for kind in kinds[: 2 if last else 3] for _ in range(parts)]
+    kinds = [(out_cols, F32), (cols, F32), (cols, BF16)][: 2 if last else 3]
+    outs = [
+        ((piece.stop - piece.start, width), kind) for width, kind in kinds for piece in pieces
+    ]
     return call(body, outs, (*halves, factor, *before), name="kept_update")
 
 
@@ -284,9 +293,9 @@
     inner, inverse, rhs = stage(tree, inner_tiles, sub_rhs, diag_inverse, inner_factor)
     root = masked(root_tiles, root_factor)
     solved, locals_ = [], []
-    outs = kept_update(halves, inner, 0, (), PARTS)
-    for part in range(PARTS):
-        update, solved0, kept0 = outs[part::PARTS]
+    outs = kept_update(halves, inner, 0, (), split=True)
+    for part in range(len(SPLIT)):
+        update, solved0, kept0 = outs[part :: len(SPLIT)]
         halves = prow_halves(next_solve(0, part, rhs, owner_sums(update, part), inverse))
         early = early_update((kept0,), inner, (1,))
         update, solved1, kept1 = kept_update(halves, inner, 2, (early,))

time: 97.2 us -> 105 us (1.080)
  starting transfers between devices: 46.6 us -> 52 us
  waiting for transfers between devices: 20.4 us -> 22.6 us
    ppermute x31, starting transfers between devices: 46.6 us -> 52 us  [partner(): lax.ppermute(shard, axis, [(i, i ^ bit) for i in range(lax.axis_size(axis...]
    ppermute x31, waiting for transfers between devices: 20.4 us -> 22.6 us  [partner(): lax.ppermute(shard, axis, [(i, i ^ bit) for i in range(lax.axis_size(axis...]
  transfers between devices with their start and end apart: 31 -> 31, of which waited for: 18 -> 16; matrix products, arithmetic and copies ran while one was open for 0% -> 0% of each run, Pallas kernels for 7% -> 6%
where the time goes in v12:
time: 105 us; the launch traced here: 104 us
  starting transfers between devices  52 us (50%)
  waiting for transfers between devices  22.6 us (22%)
  blocking collectives  18.2 us (17%)
  Pallas kernels  9.17 us (9%)
    ppermute x31, starting transfers between devices, partner(): lax.ppermute(shard, axis, [(i, i ^ bit) for i in range(lax.axis_size(axis...  52 us
    ppermute x31, waiting for transfers between devices, partner(): lax.ppermute(shard, axis, [(i, i ^ bit) for i in range(lax.axis_size(axis...  22.6 us
    all_to_all x2, blocking collectives, swap_blocks(): lax.all_to_all(blocks, OWN, 0, 0, axis_index_groups=[order], tiled=True)  18.2 us
    pallas_call x17, Pallas kernels, call(): pl.pallas_call(body, out_shape=[pltpu.VMEM(shape, kind) for shape, kind i...  8.42 us
  transfers between devices with their start and end apart: 31, of which 16 were waited for; matrix products, arithmetic and copies ran while one was open for 0% of the time, Pallas kernels for 6%

profile of v12, /device:TPU:1, one launch (start us, length us, event | category | flops | bytes accessed | tf_op | source)
XLA Modules:
  0.0 104.0 jit_solution(14865594918463203868)
XLA Ops:
  0.7 1.6 %first_solve.1 = f32[64,384]{1,0:T(8,128)S(1)} custom-call(s32[1]{0:T(128)} %bitcast.tree_ref, f32[4,3,64,768]{3,2,1,0:T(8,128)} %rhs_hbm.3, bf16[3,768,384]{2,1,0:T(8,128)(2,1)} %inverse_hbm.3), custom_call_target="tpu_custom_call" | custom-call | tf_op jit(solution)/shard_map/first_solve/pallas_call | solution.py:43
  2.3 3.3 %collective-permute-start = (f32[64,384]{1,0:T(8,128)S(1)}, f32[64,384]{1,0:T(8,128)S(1)}, u32[]{:S(2)}, u32[]{:S(2)}) collective-permute-start(f32[64,384]{1,0:T(8,128)S(1)} %first_solve.1), channel_id=1, source_target_pairs={{0,32},{32,0},{1,33},{33,1},{2,34},{34,2},{3,35},{35,3},{4,36},{36... | collective-permute-start | bytes 294920 | tf_op jit(solution)/shard_map/ppermute | solution.py:24
  5.6 0.9 collective-permute-done
  6.7 2.6 %stage.1 = (bf16[3,384,768]{2,1,0:T(8,128)(2,1)S(1)}, bf16[2,768,384]{2,1,0:T(8,128)(2,1)S(1)}, f32[2,64,768]{2,1,0:T(8,128)S(1)}) custom-call(s32[1]{0:T(128)} %bitcast.tree_ref, s32[3,3,6]{2,1,0:T(4,128)S(1)} %constant_dynamic-slice_fusion.2.mask_ref, f32[4,3,64,768]{3,2,1,0:T(8,128)} %rhs_hbm.3, bf16[3,768,384]{2,1,0:T(8,128)(2,1)} %inverse_hbm.3, ...), custom_call_target="tpu_custom_call" | custom-call | tf_op jit(solution)/shard_map/stage/pallas_call | solution.py:43
  9.3 1.4 %collective-permute-done.1.other_ref = f32[64,384]{1,0:T(8,128)S(1)} collective-permute-done((f32[64,384]{1,0:T(8,128)S(1)}, f32[64,384]{1,0:T(8,128)S(1)}, u32[]{:S(2)}, u32[]{:S(2)}) %collective-permute-start.1) | collective-permute-done | bytes 98336 | tf_op jit(solution)/shard_map/ppermute | solution.py:24
  10.7 0.2 kept_update.5
  10.9 0.1 collective-permute-start.2
  11.0 3.7 %collective-permute-done.2 = f32[40,768]{1,0:T(8,128)S(1)} collective-permute-done((f32[40,768]{1,0:T(8,128)S(1)}, f32[40,768]{1,0:T(8,128)S(1)}, u32[]{:S(2)}, u32[]{:S(2)}) %collective-permute-start.2) | collective-permute-done | bytes 122912 | tf_op jit(solution)/shard_map/ppermute | solution.py:24
  14.7 1.4 %collective-permute-start.3 = (f32[40,768]{1,0:T(8,128)S(1)}, f32[40,768]{1,0:T(8,128)S(1)}, u32[]{:S(2)}, u32[]{:S(2)}) collective-permute-start(f32[40,768]{1,0:T(8,128)S(1)} %add.64.refs_0_), channel_id=1, source_target_pairs={{0,2},{1,3},{2,0},{3,1},{4,6},{5,7},{6,4},{7,5},{8,10},{9,11},{10,... | collective-permute-start | bytes 368648 | tf_op jit(solution)/shard_map/ppermute | solution.py:24
  16.2 0.8 collective-permute-start.4
  16.9 0.5 collective-permute-start.5
  17.4 2.6 %collective-permute-start.9 = (f32[24,768]{1,0:T(8,128)S(1)}, f32[24,768]{1,0:T(8,128)S(1)}, u32[]{:S(2)}, u32[]{:S(2)}) collective-permute-start(f32[24,768]{1,0:T(8,128)S(1)} %get-tuple-element.31), channel_id=1, source_target_pairs={{0,2},{1,3},{2,0},{3,1},{4,6},{5,7},{6,4},{7,5},{8,10},{9,11},{10,... | collective-permute-start | bytes 221192 | tf_op jit(solution)/shard_map/ppermute | solution.py:24
  20.0 0.8 collective-permute-start.10
  20.8 0.6 collective-permute-done.4.refs_2_
  21.4 0.2 next_solve.4
  21.6 5.7 %collective-permute-start.6 = (f32[40,384]{1,0:T(8,128)S(1)}, f32[40,384]{1,0:T(8,128)S(1)}, u32[]{:S(2)}, u32[]{:S(2)}) collective-permute-start(f32[40,384]{1,0:T(8,128)S(1)} %next_solve.4), channel_id=1, source_target_pairs={{0,32},{32,0},{1,33},{33,1},{2,34},{34,2},{3,35},{35,3},{4,36},{36... | collective-permute-start | bytes 184328 | tf_op jit(solution)/shard_map/ppermute | solution.py:24
  27.3 0.8 collective-permute-start.11
  28.2 1.2 %collective-permute-start.7 = (f32[40,384]{1,0:T(8,128)S(1)}, f32[40,384]{1,0:T(8,128)S(1)}, u32[]{:S(2)}, u32[]{:S(2)}) collective-permute-start(f32[40,384]{1,0:T(8,128)S(1)} %add.65.one_ref), channel_id=1, source_target_pairs={{0,64},{64,0},{1,65},{65,1},{2,66},{66,2},{3,67},{67,3},{4,68},{68... | collective-permute-start | bytes 184328 | tf_op jit(solution)/shard_map/ppermute | solution.py:24
  29.4 1.2 %collective-permute-done.11.refs_1_ = f32[24,768]{1,0:T(8,128)S(1)} collective-permute-done((f32[24,768]{1,0:T(8,128)S(1)}, f32[24,768]{1,0:T(8,128)S(1)}, u32[]{:S(2)}, u32[]{:S(2)}) %collective-permute-start.11) | collective-permute-done | bytes 73760 | tf_op jit(solution)/shard_map/ppermute | solution.py:24
  30.6 0.2 next_solve.5
  30.8 3.1 %collective-permute-start.12 = (f32[24,384]{1,0:T(8,128)S(1)}, f32[24,384]{1,0:T(8,128)S(1)}, u32[]{:S(2)}, u32[]{:S(2)}) collective-permute-start(f32[24,384]{1,0:T(8,128)S(1)} %next_solve.5), channel_id=1, source_target_pairs={{0,32},{32,0},{1,33},{33,1},{2,34},{34,2},{3,35},{35,3},{4,36},{36... | collective-permute-start | bytes 110600 | tf_op jit(solution)/shard_map/ppermute | solution.py:24
  34.0 0.2 early_update.4.refs_0_
  34.2 0.2 kept_update.6
  34.4 1.4 %collective-permute-start.14 = (f32[40,768]{1,0:T(8,128)S(1)}, f32[40,768]{1,0:T(8,128)S(1)}, u32[]{:S(2)}, u32[]{:S(2)}) collective-permute-start(f32[40,768]{1,0:T(8,128)S(1)} %get-tuple-element.34), channel_id=1, source_target_pairs={{0,4},{1,5},{2,6},{3,7},{4,0},{5,1},{6,2},{7,3},{8,12},{9,13},{10,... | collective-permute-start | bytes 368648 | tf_op jit(solution)/shard_map/ppermute | solution.py:24
  35.8 1.3 %collective-permute-start.13 = (f32[24,384]{1,0:T(8,128)S(1)}, f32[24,384]{1,0:T(8,128)S(1)}, u32[]{:S(2)}, u32[]{:S(2)}) collective-permute-start(f32[24,384]{1,0:T(8,128)S(1)} %add.69.one_ref), channel_id=1, source_target_pairs={{0,64},{64,0},{1,65},{65,1},{2,66},{66,2},{3,67},{67,3},{4,68},{68... | collective-permute-start | bytes 110600 | tf_op jit(solution)/shard_map/ppermute | solution.py:24
  37.1 0.2 early_update.5.refs_0_
  37.3 1.7 %collective-permute-done.13.other_ref = f32[24,384]{1,0:T(8,128)S(1)} collective-permute-done((f32[24,384]{1,0:T(8,128)S(1)}, f32[24,384]{1,0:T(8,128)S(1)}, u32[]{:S(2)}, u32[]{:S(2)}) %collective-permute-start.13) | collective-permute-done | bytes 36896 | tf_op jit(solution)/shard_map/ppermute | solution.py:24
  39.0 0.2 kept_update.7
  39.2 1.3 %collective-permute-start.21 = (f32[24,768]{1,0:T(8,128)S(1)}, f32[24,768]{1,0:T(8,128)S(1)}, u32[]{:S(2)}, u32[]{:S(2)}) collective-permute-start(f32[24,768]{1,0:T(8,128)S(1)} %get-tuple-element.37), channel_id=1, source_target_pairs={{0,2},{1,3},{2,0},{3,1},{4,6},{5,7},{6,4},{7,5},{8,10},{9,11},{10,... | collective-permute-start | bytes 221192 | tf_op jit(solution)/shard_map/ppermute | solution.py:24
  40.5 1.0 collective-permute-start.22
  41.4 0.5 collective-permute-start.20
  41.9 2.5 %collective-permute-start.15 = (f32[40,768]{1,0:T(8,128)S(1)}, f32[40,768]{1,0:T(8,128)S(1)}, u32[]{:S(2)}, u32[]{:S(2)}) collective-permute-start(f32[40,768]{1,0:T(8,128)S(1)} %add.70.refs_0_), channel_id=1, source_target_pairs={{0,2},{1,3},{2,0},{3,1},{4,6},{5,7},{6,4},{7,5},{8,10},{9,11},{10,... | collective-permute-start | bytes 368648 | tf_op jit(solution)/shard_map/ppermute | solution.py:24
  44.4 1.0 collective-permute-start.16
  45.5 0.3 collective-permute-start.23
  45.8 2.1 %collective-permute-done.15.refs_1_ = f32[40,768]{1,0:T(8,128)S(1)} collective-permute-done((f32[40,768]{1,0:T(8,128)S(1)}, f32[40,768]{1,0:T(8,128)S(1)}, u32[]{:S(2)}, u32[]{:S(2)}) %collective-permute-start.15) | collective-permute-done | bytes 122912 | tf_op jit(solution)/shard_map/ppermute | solution.py:24
  47.9 2.8 %collective-permute-done.16.refs_2_ = f32[40,768]{1,0:T(8,128)S(1)} collective-permute-done((f32[40,768]{1,0:T(8,128)S(1)}, f32[40,768]{1,0:T(8,128)S(1)}, u32[]{:S(2)}, u32[]{:S(2)}) %collective-permute-start.16) | collective-permute-done | bytes 122912 | tf_op jit(solution)/shard_map/ppermute | solution.py:24
  50.7 0.2 next_solve.6
  51.0 2.2 %collective-permute-start.18 = (f32[40,384]{1,0:T(8,128)S(1)}, f32[40,384]{1,0:T(8,128)S(1)}, u32[]{:S(2)}, u32[]{:S(2)}) collective-permute-start(f32[40,384]{1,0:T(8,128)S(1)} %next_solve.6), channel_id=1, source_target_pairs={{0,32},{32,0},{1,33},{33,1},{2,34},{34,2},{3,35},{35,3},{4,36},{36... | collective-permute-start | bytes 184328 | tf_op jit(solution)/shard_map/ppermute | solution.py:24
  53.2 0.2 next_solve.7
  53.4 0.6 collective-permute-start.24
  53.9 0.9 collective-permute-done.24
  54.8 1.2 %collective-permute-start.25 = (f32[24,384]{1,0:T(8,128)S(1)}, f32[24,384]{1,0:T(8,128)S(1)}, u32[]{:S(2)}, u32[]{:S(2)}) collective-permute-start(f32[24,384]{1,0:T(8,128)S(1)} %add.75.one_ref), channel_id=1, source_target_pairs={{0,64},{64,0},{1,65},{65,1},{2,66},{66,2},{3,67},{67,3},{4,68},{68... | collective-permute-start | bytes 110600 | tf_op jit(solution)/shard_map/ppermute | solution.py:24
  56.0 0.3 collective-permute-start.19
  56.5 0.9 masked.1.refs_2_.factor_ref
  57.4 0.3 early_update.7.refs_0_
  57.7 0.3 early_update.6.refs_0_
  58.1 0.2 kept_update.9
  58.3 0.9 collective-permute-done.19.other_ref
  59.2 0.2 kept_update.8
  59.4 8.6 %all_to_all.10 = f32[8,8,768]{2,1,0:T(8,128)S(1)} all-to-all(f32[8,8,768]{2,1,0:T(8,128)S(1)} %maximum_bitcast_fusion), channel_id=1, replica_groups={{7,6,5,4,3,2,1,0},{15,14,13,12,11,10,9,8},{23,22,21,20,19,18,17,16},{31..., dimensions={0} | all-to-all | bytes 393216 | tf_op jit(solution)/shard_map/all_to_all | solution.py:29
  68.1 3.0 %collective-permute-start.26 = (f32[8,768]{1,0:T(8,128)S(1)}, f32[8,768]{1,0:T(8,128)S(1)}, u32[]{:S(2)}, u32[]{:S(2)}) collective-permute-start(f32[8,768]{1,0:T(8,128)S(1)} %reduce_sum.9), channel_id=1, source_target_pairs={{0,128},{128,0},{1,129},{129,1},{2,130},{130,2},{3,131},{131,3},{4... | collective-permute-start | bytes 73736 | tf_op jit(solution)/shard_map/ppermute | solution.py:24
  71.1 0.8 stacked.1
  71.8 0.5 collective-permute-done.26
  72.3 3.0 %collective-permute-start.27 = (f32[8,768]{1,0:T(8,128)S(1)}, f32[8,768]{1,0:T(8,128)S(1)}, u32[]{:S(2)}, u32[]{:S(2)}) collective-permute-start(f32[8,768]{1,0:T(8,128)S(1)} %add.77), channel_id=1, source_target_pairs={{0,8},{8,0},{16,24},{24,16},{1,9},{9,1},{17,25},{25,17},{2,10},{10... | collective-permute-start | bytes 73736 | tf_op jit(solution)/shard_map/ppermute | solution.py:24
  75.3 1.2 %collective-permute-done.27 = f32[8,768]{1,0:T(8,128)S(1)} collective-permute-done((f32[8,768]{1,0:T(8,128)S(1)}, f32[8,768]{1,0:T(8,128)S(1)}, u32[]{:S(2)}, u32[]{:S(2)}) %collective-permute-start.27) | collective-permute-done | bytes 24608 | tf_op jit(solution)/shard_map/ppermute | solution.py:24
  76.5 5.5 %collective-permute-start.28 = (f32[8,768]{1,0:T(8,128)S(1)}, f32[8,768]{1,0:T(8,128)S(1)}, u32[]{:S(2)}, u32[]{:S(2)}) collective-permute-start(f32[8,768]{1,0:T(8,128)S(1)} %add.78.one_ref), channel_id=1, source_target_pairs={{0,24},{8,16},{16,8},{24,0},{1,25},{9,17},{17,9},{25,1},{2,26},{10... | collective-permute-start | bytes 73736 | tf_op jit(solution)/shard_map/ppermute | solution.py:24
  82.0 1.2 %collective-permute-done.28.other_ref = f32[8,768]{1,0:T(8,128)S(1)} collective-permute-done((f32[8,768]{1,0:T(8,128)S(1)}, f32[8,768]{1,0:T(8,128)S(1)}, u32[]{:S(2)}, u32[]{:S(2)}) %collective-permute-start.28) | collective-permute-done | bytes 24608 | tf_op jit(solution)/shard_map/ppermute | solution.py:24
  83.2 0.4 root_part.1
  83.6 6.1 %collective-permute-start.29 = (f32[8,1536]{1,0:T(8,128)S(1)}, f32[8,1536]{1,0:T(8,128)S(1)}, u32[]{:S(2)}, u32[]{:S(2)}) collective-permute-start(f32[8,1536]{1,0:T(8,128)S(1)} %root_part.1), channel_id=1, source_target_pairs={{0,32},{32,0},{1,33},{33,1},{2,34},{34,2},{3,35},{35,3},{4,36},{36... | collective-permute-start | bytes 147464 | tf_op jit(solution)/shard_map/ppermute | solution.py:24
  89.7 0.9 collective-permute-done.29
  90.6 0.4 collective-permute-start.30
  91.0 2.6 %collective-permute-done.30 = f32[8,1536]{1,0:T(8,128)S(1)} collective-permute-done((f32[8,1536]{1,0:T(8,128)S(1)}, f32[8,1536]{1,0:T(8,128)S(1)}, u32[]{:S(2)}, u32[]{:S(2)}) %collective-permute-start.30) | collective-permute-done | bytes 49184 | tf_op jit(solution)/shard_map/ppermute | solution.py:24
  93.6 9.6 %all_to_all.11 = f32[8,8,1536]{2,1,0:T(8,128)S(1)} all-to-all(f32[8,8,1536]{2,1,0:T(8,128)S(1)} %broadcast_in_dim.2), channel_id=1, replica_groups={{7,6,5,4,3,2,1,0},{15,14,13,12,11,10,9,8},{23,22,21,20,19,18,17,16},{31..., dimensions={0} | all-to-all | bytes 786432 | tf_op jit(solution)/shard_map/all_to_all | solution.py:29
  103.2 0.7 copy.11
  (48 shorter events, 0.6 us)
Async XLA Ops:
  0.6 81.4 %copy-start = (f32[64,768]{1,0:T(8,128)S(1)}, f32[64,768]{1,0:T(8,128)}, u32[]{:S(2)}) copy-start(f32[64,768]{1,0:T(8,128)} %param.9) | copy-start | bytes 589828
  0.7 6.0 %copy-start.3 = (s32[3,3,24]{2,1,0:T(4,128)S(1)}, s32[3,3,24]{2,1,0:T(4,128)}, u32[]{:S(2)}) copy-start(s32[3,3,24]{2,1,0:T(4,128)} %param.13) | copy-start | bytes 2596
  2.3 4.3 %collective-permute-start = (f32[64,384]{1,0:T(8,128)S(1)}, f32[64,384]{1,0:T(8,128)S(1)}, u32[]{:S(2)}, u32[]{:S(2)}) collective-permute-start(f32[64,384]{1,0:T(8,128)S(1)} %first_solve.1), channel_id=1, source_target_pairs={{0,32},{32,0},{1,33},{33,1},{2,34},{34,2},{3,35},{35,3},{4,36},{36... | collective-permute-start | bytes 294920 | tf_op jit(solution)/shard_map/ppermute | solution.py:24
  6.5 4.1 %collective-permute-start.1 = (f32[64,384]{1,0:T(8,128)S(1)}, f32[64,384]{1,0:T(8,128)S(1)}, u32[]{:S(2)}, u32[]{:S(2)}) collective-permute-start(f32[64,384]{1,0:T(8,128)S(1)} %add.61.one_ref), channel_id=1, source_target_pairs={{0,64},{64,0},{1,65},{65,1},{2,66},{66,2},{3,67},{67,3},{4,68},{68... | collective-permute-start | bytes 294920 | tf_op jit(solution)/shard_map/ppermute | solution.py:24
  10.9 3.8 %collective-permute-start.2 = (f32[40,768]{1,0:T(8,128)S(1)}, f32[40,768]{1,0:T(8,128)S(1)}, u32[]{:S(2)}, u32[]{:S(2)}) collective-permute-start(f32[40,768]{1,0:T(8,128)S(1)} %get-tuple-element.27), channel_id=1, source_target_pairs={{0,4},{1,5},{2,6},{3,7},{4,0},{5,1},{6,2},{7,3},{8,12},{9,13},{10,... | collective-permute-start | bytes 368648 | tf_op jit(solution)/shard_map/ppermute | solution.py:24
  14.7 6.1 %collective-permute-start.3 = (f32[40,768]{1,0:T(8,128)S(1)}, f32[40,768]{1,0:T(8,128)S(1)}, u32[]{:S(2)}, u32[]{:S(2)}) collective-permute-start(f32[40,768]{1,0:T(8,128)S(1)} %add.64.refs_0_), channel_id=1, source_target_pairs={{0,2},{1,3},{2,0},{3,1},{4,6},{5,7},{6,4},{7,5},{8,10},{9,11},{10,... | collective-permute-start | bytes 368648 | tf_op jit(solution)/shard_map/ppermute | solution.py:24
  16.2 5.2 %collective-permute-start.4 = (f32[40,768]{1,0:T(8,128)S(1)}, f32[40,768]{1,0:T(8,128)S(1)}, u32[]{:S(2)}, u32[]{:S(2)}) collective-permute-start(f32[40,768]{1,0:T(8,128)S(1)} %add.64.refs_0_), channel_id=1, source_target_pairs={{0,3},{1,2},{2,1},{3,0},{4,7},{5,6},{6,5},{7,4},{8,11},{9,10},{10,... | collective-permute-start | bytes 368648 | tf_op jit(solution)/shard_map/ppermute | solution.py:24
  16.9 4.4 %collective-permute-start.5 = (f32[40,768]{1,0:T(8,128)S(1)}, f32[40,768]{1,0:T(8,128)S(1)}, u32[]{:S(2)}, u32[]{:S(2)}) collective-permute-start(f32[40,768]{1,0:T(8,128)S(1)} %add.64.refs_0_), channel_id=1, source_target_pairs={{0,1},{1,0},{2,3},{3,2},{4,5},{5,4},{6,7},{7,6},{8,9},{9,8},{10,11... | collective-permute-start | bytes 368648 | tf_op jit(solution)/shard_map/ppermute | solution.py:24
  17.4 9.9 %collective-permute-start.9 = (f32[24,768]{1,0:T(8,128)S(1)}, f32[24,768]{1,0:T(8,128)S(1)}, u32[]{:S(2)}, u32[]{:S(2)}) collective-permute-start(f32[24,768]{1,0:T(8,128)S(1)} %get-tuple-element.31), channel_id=1, source_target_pairs={{0,2},{1,3},{2,0},{3,1},{4,6},{5,7},{6,4},{7,5},{8,10},{9,11},{10,... | collective-permute-start | bytes 221192 | tf_op jit(solution)/shard_map/ppermute | solution.py:24
  20.0 7.3 %collective-permute-start.10 = (f32[24,768]{1,0:T(8,128)S(1)}, f32[24,768]{1,0:T(8,128)S(1)}, u32[]{:S(2)}, u32[]{:S(2)}) collective-permute-start(f32[24,768]{1,0:T(8,128)S(1)} %get-tuple-element.31), channel_id=1, source_target_pairs={{0,3},{1,2},{2,1},{3,0},{4,7},{5,6},{6,5},{7,4},{8,11},{9,10},{10,... | collective-permute-start | bytes 221192 | tf_op jit(solution)/shard_map/ppermute | solution.py:24
  20.8 6.5 %collective-permute-start.8 = (f32[24,768]{1,0:T(8,128)S(1)}, f32[24,768]{1,0:T(8,128)S(1)}, u32[]{:S(2)}, u32[]{:S(2)}) collective-permute-start(f32[24,768]{1,0:T(8,128)S(1)} %get-tuple-element.31), channel_id=1, source_target_pairs={{0,1},{1,0},{2,3},{3,2},{4,5},{5,4},{6,7},{7,6},{8,9},{9,8},{10,11... | collective-permute-start | bytes 221192 | tf_op jit(solution)/shard_map/ppermute | solution.py:24
  21.6 6.6 %collective-permute-start.6 = (f32[40,384]{1,0:T(8,128)S(1)}, f32[40,384]{1,0:T(8,128)S(1)}, u32[]{:S(2)}, u32[]{:S(2)}) collective-permute-start(f32[40,384]{1,0:T(8,128)S(1)} %next_solve.4), channel_id=1, source_target_pairs={{0,32},{32,0},{1,33},{33,1},{2,34},{34,2},{3,35},{35,3},{4,36},{36... | collective-permute-start | bytes 184328 | tf_op jit(solution)/shard_map/ppermute | solution.py:24
  27.3 3.3 %collective-permute-start.11 = (f32[24,768]{1,0:T(8,128)S(1)}, f32[24,768]{1,0:T(8,128)S(1)}, u32[]{:S(2)}, u32[]{:S(2)}) collective-permute-start(f32[24,768]{1,0:T(8,128)S(1)} %add_add_fusion.1.refs_0_), channel_id=1, source_target_pairs={{0,4},{1,5},{2,6},{3,7},{4,0},{5,1},{6,2},{7,3},{8,12},{9,13},{10,... | collective-permute-start | bytes 221192 | tf_op jit(solution)/shard_map/ppermute | solution.py:24
  28.2 6.0 %collective-permute-start.7 = (f32[40,384]{1,0:T(8,128)S(1)}, f32[40,384]{1,0:T(8,128)S(1)}, u32[]{:S(2)}, u32[]{:S(2)}) collective-permute-start(f32[40,384]{1,0:T(8,128)S(1)} %add.65.one_ref), channel_id=1, source_target_pairs={{0,64},{64,0},{1,65},{65,1},{2,66},{66,2},{3,67},{67,3},{4,68},{68... | collective-permute-start | bytes 184328 | tf_op jit(solution)/shard_map/ppermute | solution.py:24
  30.8 4.9 %collective-permute-start.12 = (f32[24,384]{1,0:T(8,128)S(1)}, f32[24,384]{1,0:T(8,128)S(1)}, u32[]{:S(2)}, u32[]{:S(2)}) collective-permute-start(f32[24,384]{1,0:T(8,128)S(1)} %next_solve.5), channel_id=1, source_target_pairs={{0,32},{32,0},{1,33},{33,1},{2,34},{34,2},{3,35},{35,3},{4,36},{36... | collective-permute-start | bytes 110600 | tf_op jit(solution)/shard_map/ppermute | solution.py:24
  34.4 7.5 %collective-permute-start.14 = (f32[40,768]{1,0:T(8,128)S(1)}, f32[40,768]{1,0:T(8,128)S(1)}, u32[]{:S(2)}, u32[]{:S(2)}) collective-permute-start(f32[40,768]{1,0:T(8,128)S(1)} %get-tuple-element.34), channel_id=1, source_target_pairs={{0,4},{1,5},{2,6},{3,7},{4,0},{5,1},{6,2},{7,3},{8,12},{9,13},{10,... | collective-permute-start | bytes 368648 | tf_op jit(solution)/shard_map/ppermute | solution.py:24
  35.8 3.2 %collective-permute-start.13 = (f32[24,384]{1,0:T(8,128)S(1)}, f32[24,384]{1,0:T(8,128)S(1)}, u32[]{:S(2)}, u32[]{:S(2)}) collective-permute-start(f32[24,384]{1,0:T(8,128)S(1)} %add.69.one_ref), channel_id=1, source_target_pairs={{0,64},{64,0},{1,65},{65,1},{2,66},{66,2},{3,67},{67,3},{4,68},{68... | collective-permute-start | bytes 110600 | tf_op jit(solution)/shard_map/ppermute | solution.py:24
  39.2 6.2 %collective-permute-start.21 = (f32[24,768]{1,0:T(8,128)S(1)}, f32[24,768]{1,0:T(8,128)S(1)}, u32[]{:S(2)}, u32[]{:S(2)}) collective-permute-start(f32[24,768]{1,0:T(8,128)S(1)} %get-tuple-element.37), channel_id=1, source_target_pairs={{0,2},{1,3},{2,0},{3,1},{4,6},{5,7},{6,4},{7,5},{8,10},{9,11},{10,... | collective-permute-start | bytes 221192 | tf_op jit(solution)/shard_map/ppermute | solution.py:24
  40.5 5.0 %collective-permute-start.22 = (f32[24,768]{1,0:T(8,128)S(1)}, f32[24,768]{1,0:T(8,128)S(1)}, u32[]{:S(2)}, u32[]{:S(2)}) collective-permute-start(f32[24,768]{1,0:T(8,128)S(1)} %get-tuple-element.37), channel_id=1, source_target_pairs={{0,3},{1,2},{2,1},{3,0},{4,7},{5,6},{6,5},{7,4},{8,11},{9,10},{10,... | collective-permute-start | bytes 221192 | tf_op jit(solution)/shard_map/ppermute | solution.py:24
  41.4 4.0 %collective-permute-start.20 = (f32[24,768]{1,0:T(8,128)S(1)}, f32[24,768]{1,0:T(8,128)S(1)}, u32[]{:S(2)}, u32[]{:S(2)}) collective-permute-start(f32[24,768]{1,0:T(8,128)S(1)} %get-tuple-element.37), channel_id=1, source_target_pairs={{0,1},{1,0},{2,3},{3,2},{4,5},{5,4},{6,7},{7,6},{8,9},{9,8},{10,11... | collective-permute-start | bytes 221192 | tf_op jit(solution)/shard_map/ppermute | solution.py:24
  41.9 5.9 %collective-permute-start.15 = (f32[40,768]{1,0:T(8,128)S(1)}, f32[40,768]{1,0:T(8,128)S(1)}, u32[]{:S(2)}, u32[]{:S(2)}) collective-permute-start(f32[40,768]{1,0:T(8,128)S(1)} %add.70.refs_0_), channel_id=1, source_target_pairs={{0,2},{1,3},{2,0},{3,1},{4,6},{5,7},{6,4},{7,5},{8,10},{9,11},{10,... | collective-permute-start | bytes 368648 | tf_op jit(solution)/shard_map/ppermute | solution.py:24
  44.4 6.3 %collective-permute-start.16 = (f32[40,768]{1,0:T(8,128)S(1)}, f32[40,768]{1,0:T(8,128)S(1)}, u32[]{:S(2)}, u32[]{:S(2)}) collective-permute-start(f32[40,768]{1,0:T(8,128)S(1)} %add.70.refs_0_), channel_id=1, source_target_pairs={{0,3},{1,2},{2,1},{3,0},{4,7},{5,6},{6,5},{7,4},{8,11},{9,10},{10,... | collective-permute-start | bytes 368648 | tf_op jit(solution)/shard_map/ppermute | solution.py:24
  45.4 5.3 %collective-permute-start.17 = (f32[40,768]{1,0:T(8,128)S(1)}, f32[40,768]{1,0:T(8,128)S(1)}, u32[]{:S(2)}, u32[]{:S(2)}) collective-permute-start(f32[40,768]{1,0:T(8,128)S(1)} %add.70.refs_0_), channel_id=1, source_target_pairs={{0,1},{1,0},{2,3},{3,2},{4,5},{5,4},{6,7},{7,6},{8,9},{9,8},{10,11... | collective-permute-start | bytes 368648 | tf_op jit(solution)/shard_map/ppermute | solution.py:24
  45.4 10.9 %copy-start.4 = (s32[3,3,24]{2,1,0:T(4,128)S(1)}, s32[3,3,24]{2,1,0:T(4,128)}, u32[]{:S(2)}) copy-start(s32[3,3,24]{2,1,0:T(4,128)} %param.15) | copy-start | bytes 2596
  45.5 11.0 %copy-start.2 = (bf16[3,384,768]{2,1,0:T(8,128)(2,1)S(1)}, bf16[3,384,768]{2,1,0:T(8,128)(2,1)}, u32[]{:S(2)}) copy-start(bf16[3,384,768]{2,1,0:T(8,128)(2,1)} %factor_ref.1) | copy-start | bytes 5308420
  45.5 7.7 %collective-permute-start.23 = (f32[24,768]{1,0:T(8,128)S(1)}, f32[24,768]{1,0:T(8,128)S(1)}, u32[]{:S(2)}, u32[]{:S(2)}) collective-permute-start(f32[24,768]{1,0:T(8,128)S(1)} %add_add_fusion.refs_0_), channel_id=1, source_target_pairs={{0,4},{1,5},{2,6},{3,7},{4,0},{5,1},{6,2},{7,3},{8,12},{9,13},{10,... | collective-permute-start | bytes 221192 | tf_op jit(solution)/shard_map/ppermute | solution.py:24
  51.0 5.1 %collective-permute-start.18 = (f32[40,384]{1,0:T(8,128)S(1)}, f32[40,384]{1,0:T(8,128)S(1)}, u32[]{:S(2)}, u32[]{:S(2)}) collective-permute-start(f32[40,384]{1,0:T(8,128)S(1)} %next_solve.6), channel_id=1, source_target_pairs={{0,32},{32,0},{1,33},{33,1},{2,34},{34,2},{3,35},{35,3},{4,36},{36... | collective-permute-start | bytes 184328 | tf_op jit(solution)/shard_map/ppermute | solution.py:24
  53.4 1.4 %collective-permute-start.24 = (f32[24,384]{1,0:T(8,128)S(1)}, f32[24,384]{1,0:T(8,128)S(1)}, u32[]{:S(2)}, u32[]{:S(2)}) collective-permute-start(f32[24,384]{1,0:T(8,128)S(1)} %next_solve.7), channel_id=1, source_target_pairs={{0,32},{32,0},{1,33},{33,1},{2,34},{34,2},{3,35},{35,3},{4,36},{36... | collective-permute-start | bytes 110600 | tf_op jit(solution)/shard_map/ppermute | solution.py:24
  54.8 3.2 %collective-permute-start.25 = (f32[24,384]{1,0:T(8,128)S(1)}, f32[24,384]{1,0:T(8,128)S(1)}, u32[]{:S(2)}, u32[]{:S(2)}) collective-permute-start(f32[24,384]{1,0:T(8,128)S(1)} %add.75.one_ref), channel_id=1, source_target_pairs={{0,64},{64,0},{1,65},{65,1},{2,66},{66,2},{3,67},{67,3},{4,68},{68... | collective-permute-start | bytes 110600 | tf_op jit(solution)/shard_map/ppermute | solution.py:24
  56.0 3.2 %collective-permute-start.19 = (f32[40,384]{1,0:T(8,128)S(1)}, f32[40,384]{1,0:T(8,128)S(1)}, u32[]{:S(2)}, u32[]{:S(2)}) collective-permute-start(f32[40,384]{1,0:T(8,128)S(1)} %add.71.one_ref), channel_id=1, source_target_pairs={{0,64},{64,0},{1,65},{65,1},{2,66},{66,2},{3,67},{67,3},{4,68},{68... | collective-permute-start | bytes 184328 | tf_op jit(solution)/shard_map/ppermute | solution.py:24
  58.3 25.0 %copy-start.1 = (bf16[768,1536]{1,0:T(8,128)(2,1)S(1)}, bf16[768,1536]{1,0:T(8,128)(2,1)}, u32[]{:S(2)}) copy-start(bf16[768,1536]{1,0:T(8,128)(2,1)} %inverse_ref.1) | copy-start | bytes 7077892
  68.1 4.3 %collective-permute-start.26 = (f32[8,768]{1,0:T(8,128)S(1)}, f32[8,768]{1,0:T(8,128)S(1)}, u32[]{:S(2)}, u32[]{:S(2)}) collective-permute-start(f32[8,768]{1,0:T(8,128)S(1)} %reduce_sum.9), channel_id=1, source_target_pairs={{0,128},{128,0},{1,129},{129,1},{2,130},{130,2},{3,131},{131,3},{4... | collective-permute-start | bytes 73736 | tf_op jit(solution)/shard_map/ppermute | solution.py:24
  72.3 4.2 %collective-permute-start.27 = (f32[8,768]{1,0:T(8,128)S(1)}, f32[8,768]{1,0:T(8,128)S(1)}, u32[]{:S(2)}, u32[]{:S(2)}) collective-permute-start(f32[8,768]{1,0:T(8,128)S(1)} %add.77), channel_id=1, source_target_pairs={{0,8},{8,0},{16,24},{24,16},{1,9},{9,1},{17,25},{25,17},{2,10},{10... | collective-permute-start | bytes 73736 | tf_op jit(solution)/shard_map/ppermute | solution.py:24
  76.5 6.7 %collective-permute-start.28 = (f32[8,768]{1,0:T(8,128)S(1)}, f32[8,768]{1,0:T(8,128)S(1)}, u32[]{:S(2)}, u32[]{:S(2)}) collective-permute-start(f32[8,768]{1,0:T(8,128)S(1)} %add.78.one_ref), channel_id=1, source_target_pairs={{0,24},{8,16},{16,8},{24,0},{1,25},{9,17},{17,9},{25,1},{2,26},{10... | collective-permute-start | bytes 73736 | tf_op jit(solution)/shard_map/ppermute | solution.py:24
  83.6 7.0 %collective-permute-start.29 = (f32[8,1536]{1,0:T(8,128)S(1)}, f32[8,1536]{1,0:T(8,128)S(1)}, u32[]{:S(2)}, u32[]{:S(2)}) collective-permute-start(f32[8,1536]{1,0:T(8,128)S(1)} %root_part.1), channel_id=1, source_target_pairs={{0,32},{32,0},{1,33},{33,1},{2,34},{34,2},{3,35},{35,3},{4,36},{36... | collective-permute-start | bytes 147464 | tf_op jit(solution)/shard_map/ppermute | solution.py:24
  90.6 2.9 %collective-permute-start.30 = (f32[8,1536]{1,0:T(8,128)S(1)}, f32[8,1536]{1,0:T(8,128)S(1)}, u32[]{:S(2)}, u32[]{:S(2)}) collective-permute-start(f32[8,1536]{1,0:T(8,128)S(1)} %add.79), channel_id=1, source_target_pairs={{0,64},{64,0},{1,65},{65,1},{2,66},{66,2},{3,67},{67,3},{4,68},{68... | collective-permute-start | bytes 147464 | tf_op jit(solution)/shard_map/ppermute | solution.py:24

commit v13 on v11

--- a/solution.py
+++ b/solution.py
@@ -254,9 +254,10 @@
     )[0]
 
 
-def prow_halves(partial_sum):
-    pair = partial_sum + partner(partial_sum, "core")
-    return pair, partner(pair, "xl")
+def prow_halves(partial_sum, part=0):
+    near, far = ("core", "xl") if part % 2 == 0 else ("xl", "core")
+    pair = partial_sum + partner(partial_sum, near)
+    return pair, partner(pair, far)
 
 
 def owner_sums(partial_sum, part):
@@ -287,11 +288,12 @@
     outs = kept_update(halves, inner, 0, (), PARTS)
     for part in range(PARTS):
         update, solved0, kept0 = outs[part::PARTS]
-        halves = prow_halves(next_solve(0, part, rhs, owner_sums(update, part), inverse))
+        halves = prow_halves(next_solve(0, part, rhs, owner_sums(update, part), inverse), part)
         early = early_update((kept0,), inner, (1,))
         update, solved1, kept1 = kept_update(halves, inner, 2, (early,))
-        halves = prow_halves(next_solve(1, part, rhs, owner_sums(update, part), inverse))
         early = early_update((kept0, kept1), root, (0, 1))
+        *sums, early = lax.optimization_barrier((*owner_sums(update, part), early))
+        halves = prow_halves(next_solve(1, part, rhs, sums, inverse), part)
         root_local, solved2 = kept_update(halves, root, 2, (early,), last=True)
         solved.append((solved0, solved1, solved2))
         locals_.append(root_local)

time: 97.2 us -> 98.7 us (1.015)
  starting transfers between devices: 46.6 us -> 49.1 us
  waiting for transfers between devices: 20.4 us -> 18.5 us
    ppermute x31, starting transfers between devices: 46.6 us -> 49.1 us  [partner(): lax.ppermute(shard, axis, [(i, i ^ bit) for i in range(lax.axis_size(axis...]
    ppermute x31, waiting for transfers between devices: 20.4 us -> 18.5 us  [partner(): lax.ppermute(shard, axis, [(i, i ^ bit) for i in range(lax.axis_size(axis...]
where the time goes in v13:
time: 98.7 us; the launch traced here: 97 us
  starting transfers between devices  49.1 us (50%)
  waiting for transfers between devices  18.5 us (19%)
  blocking collectives  18.4 us (19%)
  Pallas kernels  9.03 us (9%)
    ppermute x31, starting transfers between devices, partner(): lax.ppermute(shard, axis, [(i, i ^ bit) for i in range(lax.axis_size(axis...  49.1 us
    ppermute x31, waiting for transfers between devices, partner(): lax.ppermute(shard, axis, [(i, i ^ bit) for i in range(lax.axis_size(axis...  18.5 us
    all_to_all x2, blocking collectives, swap_blocks(): lax.all_to_all(blocks, OWN, 0, 0, axis_index_groups=[order], tiled=True)  18.4 us
    pallas_call x17, Pallas kernels, call(): pl.pallas_call(body, out_shape=[pltpu.VMEM(shape, kind) for shape, kind i...  8.27 us
  transfers between devices with their start and end apart: 31, of which 18 were waited for; matrix products, arithmetic and copies ran while one was open for 0% of the time, Pallas kernels for 7%

profile of v13, /device:TPU:1, one launch (start us, length us, event | category | flops | bytes accessed | tf_op | source)
XLA Modules:
  0.0 97.0 jit_solution(391202880515150532)
XLA Ops:
  0.7 1.6 %first_solve.1 = f32[64,384]{1,0:T(8,128)S(1)} custom-call(s32[1]{0:T(128)} %bitcast.tree_ref, f32[4,3,64,768]{3,2,1,0:T(8,128)} %rhs_hbm.3, bf16[3,768,384]{2,1,0:T(8,128)(2,1)} %inverse_hbm.3), custom_call_target="tpu_custom_call" | custom-call | tf_op jit(solution)/shard_map/first_solve/pallas_call | solution.py:43
  2.3 3.3 %collective-permute-start = (f32[64,384]{1,0:T(8,128)S(1)}, f32[64,384]{1,0:T(8,128)S(1)}, u32[]{:S(2)}, u32[]{:S(2)}) collective-permute-start(f32[64,384]{1,0:T(8,128)S(1)} %first_solve.1), channel_id=1, source_target_pairs={{0,32},{32,0},{1,33},{33,1},{2,34},{34,2},{3,35},{35,3},{4,36},{36... | collective-permute-start | bytes 294920 | tf_op jit(solution)/shard_map/ppermute | solution.py:24
  5.6 0.9 collective-permute-done
  6.7 2.6 %stage.1 = (bf16[3,384,768]{2,1,0:T(8,128)(2,1)S(1)}, bf16[2,768,384]{2,1,0:T(8,128)(2,1)S(1)}, f32[2,64,768]{2,1,0:T(8,128)S(1)}) custom-call(s32[1]{0:T(128)} %bitcast.tree_ref, s32[3,3,6]{2,1,0:T(4,128)S(1)} %constant_dynamic-slice_fusion.2.mask_ref, f32[4,3,64,768]{3,2,1,0:T(8,128)} %rhs_hbm.3, bf16[3,768,384]{2,1,0:T(8,128)(2,1)} %inverse_hbm.3, ...), custom_call_target="tpu_custom_call" | custom-call | tf_op jit(solution)/shard_map/stage/pallas_call | solution.py:43
  9.3 1.4 %collective-permute-done.1.other_ref = f32[64,384]{1,0:T(8,128)S(1)} collective-permute-done((f32[64,384]{1,0:T(8,128)S(1)}, f32[64,384]{1,0:T(8,128)S(1)}, u32[]{:S(2)}, u32[]{:S(2)}) %collective-permute-start.1) | collective-permute-done | bytes 98336 | tf_op jit(solution)/shard_map/ppermute | solution.py:24
  10.7 0.2 kept_update.5
  11.0 2.8 %collective-permute-start.9 = (f32[32,768]{1,0:T(8,128)S(1)}, f32[32,768]{1,0:T(8,128)S(1)}, u32[]{:S(2)}, u32[]{:S(2)}) collective-permute-start(f32[32,768]{1,0:T(8,128)S(1)} %get-tuple-element.39), channel_id=1, source_target_pairs={{0,2},{1,3},{2,0},{3,1},{4,6},{5,7},{6,4},{7,5},{8,10},{9,11},{10,... | collective-permute-start | bytes 294920 | tf_op jit(solution)/shard_map/ppermute | solution.py:24
  13.8 0.8 collective-permute-start.10
  14.6 3.2 %collective-permute-start.3 = (f32[32,768]{1,0:T(8,128)S(1)}, f32[32,768]{1,0:T(8,128)S(1)}, u32[]{:S(2)}, u32[]{:S(2)}) collective-permute-start(f32[32,768]{1,0:T(8,128)S(1)} %add.64.refs_0_), channel_id=1, source_target_pairs={{0,2},{1,3},{2,0},{3,1},{4,6},{5,7},{6,4},{7,5},{8,10},{9,11},{10,... | collective-permute-start | bytes 294920 | tf_op jit(solution)/shard_map/ppermute | solution.py:24
  17.7 0.8 collective-permute-start.4
  18.5 0.3 collective-permute-done.10
  18.8 0.2 collective-permute-done.8
  19.0 0.6 collective-permute-start.11
  19.6 1.2 %collective-permute-done.3.refs_1_ = f32[32,768]{1,0:T(8,128)S(1)} collective-permute-done((f32[32,768]{1,0:T(8,128)S(1)}, f32[32,768]{1,0:T(8,128)S(1)}, u32[]{:S(2)}, u32[]{:S(2)}) %collective-permute-start.3) | collective-permute-done | bytes 98336 | tf_op jit(solution)/shard_map/ppermute | solution.py:24
  20.8 3.2 %collective-permute-done.4.refs_2_ = f32[32,768]{1,0:T(8,128)S(1)} collective-permute-done((f32[32,768]{1,0:T(8,128)S(1)}, f32[32,768]{1,0:T(8,128)S(1)}, u32[]{:S(2)}, u32[]{:S(2)}) %collective-permute-start.4) | collective-permute-done | bytes 98336 | tf_op jit(solution)/shard_map/ppermute | solution.py:24
  24.0 0.2 next_solve.4
  24.2 2.2 %collective-permute-start.6 = (f32[32,384]{1,0:T(8,128)S(1)}, f32[32,384]{1,0:T(8,128)S(1)}, u32[]{:S(2)}, u32[]{:S(2)}) collective-permute-start(f32[32,384]{1,0:T(8,128)S(1)} %next_solve.4), channel_id=1, source_target_pairs={{0,32},{32,0},{1,33},{33,1},{2,34},{34,2},{3,35},{35,3},{4,36},{36... | collective-permute-start | bytes 147464 | tf_op jit(solution)/shard_map/ppermute | solution.py:24
  26.4 0.2 next_solve.5
  26.7 1.3 %collective-permute-start.12 = (f32[32,384]{1,0:T(8,128)S(1)}, f32[32,384]{1,0:T(8,128)S(1)}, u32[]{:S(2)}, u32[]{:S(2)}) collective-permute-start(f32[32,384]{1,0:T(8,128)S(1)} %next_solve.5), channel_id=1, source_target_pairs={{0,64},{64,0},{1,65},{65,1},{2,66},{66,2},{3,67},{67,3},{4,68},{68... | collective-permute-start | bytes 147464 | tf_op jit(solution)/shard_map/ppermute | solution.py:24
  28.0 0.6 collective-permute-start.7
  28.6 1.1 %collective-permute-done.12 = f32[32,384]{1,0:T(8,128)S(1)} collective-permute-done((f32[32,384]{1,0:T(8,128)S(1)}, f32[32,384]{1,0:T(8,128)S(1)}, u32[]{:S(2)}, u32[]{:S(2)}) %collective-permute-start.12) | collective-permute-done | bytes 49184 | tf_op jit(solution)/shard_map/ppermute | solution.py:24
  29.7 2.6 %collective-permute-start.13 = (f32[32,384]{1,0:T(8,128)S(1)}, f32[32,384]{1,0:T(8,128)S(1)}, u32[]{:S(2)}, u32[]{:S(2)}) collective-permute-start(f32[32,384]{1,0:T(8,128)S(1)} %add.69.one_ref), channel_id=1, source_target_pairs={{0,32},{32,0},{1,33},{33,1},{2,34},{34,2},{3,35},{35,3},{4,36},{36... | collective-permute-start | bytes 147464 | tf_op jit(solution)/shard_map/ppermute | solution.py:24
  32.3 0.2 early_update.4.refs_0_
  32.5 0.2 early_update.5.refs_0_
  32.7 0.2 kept_update.6
  33.1 0.1 collective-permute-done.13.other_ref
  33.2 0.2 kept_update.7
  33.4 1.7 %collective-permute-start.21 = (f32[32,768]{1,0:T(8,128)S(1)}, f32[32,768]{1,0:T(8,128)S(1)}, u32[]{:S(2)}, u32[]{:S(2)}) collective-permute-start(f32[32,768]{1,0:T(8,128)S(1)} %get-tuple-element.50), channel_id=1, source_target_pairs={{0,2},{1,3},{2,0},{3,1},{4,6},{5,7},{6,4},{7,5},{8,10},{9,11},{10,... | collective-permute-start | bytes 294920 | tf_op jit(solution)/shard_map/ppermute | solution.py:24
  35.1 0.8 collective-permute-start.22
  35.9 0.2 collective-permute-start.20
  36.1 0.4 collective-permute-done.14
  36.5 2.6 %collective-permute-start.15 = (f32[32,768]{1,0:T(8,128)S(1)}, f32[32,768]{1,0:T(8,128)S(1)}, u32[]{:S(2)}, u32[]{:S(2)}) collective-permute-start(f32[32,768]{1,0:T(8,128)S(1)} %add.70.refs_0_), channel_id=1, source_target_pairs={{0,2},{1,3},{2,0},{3,1},{4,6},{5,7},{6,4},{7,5},{8,10},{9,11},{10,... | collective-permute-start | bytes 294920 | tf_op jit(solution)/shard_map/ppermute | solution.py:24
  39.1 0.8 collective-permute-start.16
  39.9 0.7 collective-permute-done.22
  40.6 1.7 %collective-permute-start.23 = (f32[32,768]{1,0:T(8,128)S(1)}, f32[32,768]{1,0:T(8,128)S(1)}, u32[]{:S(2)}, u32[]{:S(2)}) collective-permute-start(f32[32,768]{1,0:T(8,128)S(1)} %add_add_fusion.refs_0_), channel_id=1, source_target_pairs={{0,4},{1,5},{2,6},{3,7},{4,0},{5,1},{6,2},{7,3},{8,12},{9,13},{10,... | collective-permute-start | bytes 294920 | tf_op jit(solution)/shard_map/ppermute | solution.py:24
  42.4 0.9 masked.1.refs_2_.factor_ref
  43.3 0.3 early_update.6.refs_0_
  43.6 0.3 early_update.7.refs_0_
  44.0 0.9 collective-permute-done.16.refs_2_
  44.8 0.2 next_solve.6
  45.0 2.5 %collective-permute-start.18 = (f32[32,384]{1,0:T(8,128)S(1)}, f32[32,384]{1,0:T(8,128)S(1)}, u32[]{:S(2)}, u32[]{:S(2)}) collective-permute-start(f32[32,384]{1,0:T(8,128)S(1)} %next_solve.6), channel_id=1, source_target_pairs={{0,32},{32,0},{1,33},{33,1},{2,34},{34,2},{3,35},{35,3},{4,36},{36... | collective-permute-start | bytes 147464 | tf_op jit(solution)/shard_map/ppermute | solution.py:24
  47.5 0.2 next_solve.7
  47.7 0.6 collective-permute-start.24
  48.4 1.0 %collective-permute-start.19 = (f32[32,384]{1,0:T(8,128)S(1)}, f32[32,384]{1,0:T(8,128)S(1)}, u32[]{:S(2)}, u32[]{:S(2)}) collective-permute-start(f32[32,384]{1,0:T(8,128)S(1)} %add.71.one_ref), channel_id=1, source_target_pairs={{0,64},{64,0},{1,65},{65,1},{2,66},{66,2},{3,67},{67,3},{4,68},{68... | collective-permute-start | bytes 147464 | tf_op jit(solution)/shard_map/ppermute | solution.py:24
  49.4 1.4 %collective-permute-done.24 = f32[32,384]{1,0:T(8,128)S(1)} collective-permute-done((f32[32,384]{1,0:T(8,128)S(1)}, f32[32,384]{1,0:T(8,128)S(1)}, u32[]{:S(2)}, u32[]{:S(2)}) %collective-permute-start.24) | collective-permute-done | bytes 49184 | tf_op jit(solution)/shard_map/ppermute | solution.py:24
  50.8 2.0 %collective-permute-start.25 = (f32[32,384]{1,0:T(8,128)S(1)}, f32[32,384]{1,0:T(8,128)S(1)}, u32[]{:S(2)}, u32[]{:S(2)}) collective-permute-start(f32[32,384]{1,0:T(8,128)S(1)} %add.75.one_ref), channel_id=1, source_target_pairs={{0,32},{32,0},{1,33},{33,1},{2,34},{34,2},{3,35},{35,3},{4,36},{36... | collective-permute-start | bytes 147464 | tf_op jit(solution)/shard_map/ppermute | solution.py:24
  52.8 0.2 kept_update.8
  53.0 0.7 collective-permute-done.25.other_ref
  53.6 0.2 kept_update.9
  53.9 8.8 %all_to_all.10 = f32[8,8,768]{2,1,0:T(8,128)S(1)} all-to-all(f32[8,8,768]{2,1,0:T(8,128)S(1)} %maximum_bitcast_fusion), channel_id=1, replica_groups={{7,6,5,4,3,2,1,0},{15,14,13,12,11,10,9,8},{23,22,21,20,19,18,17,16},{31..., dimensions={0} | all-to-all | bytes 393216 | tf_op jit(solution)/shard_map/all_to_all | solution.py:29
  62.6 4.4 %collective-permute-start.26 = (f32[8,768]{1,0:T(8,128)S(1)}, f32[8,768]{1,0:T(8,128)S(1)}, u32[]{:S(2)}, u32[]{:S(2)}) collective-permute-start(f32[8,768]{1,0:T(8,128)S(1)} %reduce_sum.9), channel_id=1, source_target_pairs={{0,128},{128,0},{1,129},{129,1},{2,130},{130,2},{3,131},{131,3},{4... | collective-permute-start | bytes 73736 | tf_op jit(solution)/shard_map/ppermute | solution.py:24
  67.1 0.8 stacked.1
  67.8 0.5 collective-permute-done.26
  68.3 3.0 %collective-permute-start.27 = (f32[8,768]{1,0:T(8,128)S(1)}, f32[8,768]{1,0:T(8,128)S(1)}, u32[]{:S(2)}, u32[]{:S(2)}) collective-permute-start(f32[8,768]{1,0:T(8,128)S(1)} %add.77), channel_id=1, source_target_pairs={{0,8},{8,0},{16,24},{24,16},{1,9},{9,1},{17,25},{25,17},{2,10},{10... | collective-permute-start | bytes 73736 | tf_op jit(solution)/shard_map/ppermute | solution.py:24
  71.3 1.2 %collective-permute-done.27 = f32[8,768]{1,0:T(8,128)S(1)} collective-permute-done((f32[8,768]{1,0:T(8,128)S(1)}, f32[8,768]{1,0:T(8,128)S(1)}, u32[]{:S(2)}, u32[]{:S(2)}) %collective-permute-start.27) | collective-permute-done | bytes 24608 | tf_op jit(solution)/shard_map/ppermute | solution.py:24
  72.5 4.5 %collective-permute-start.28 = (f32[8,768]{1,0:T(8,128)S(1)}, f32[8,768]{1,0:T(8,128)S(1)}, u32[]{:S(2)}, u32[]{:S(2)}) collective-permute-start(f32[8,768]{1,0:T(8,128)S(1)} %add.78.one_ref), channel_id=1, source_target_pairs={{0,24},{8,16},{16,8},{24,0},{1,25},{9,17},{17,9},{25,1},{2,26},{10... | collective-permute-start | bytes 73736 | tf_op jit(solution)/shard_map/ppermute | solution.py:24
  77.0 1.2 %collective-permute-done.28.other_ref = f32[8,768]{1,0:T(8,128)S(1)} collective-permute-done((f32[8,768]{1,0:T(8,128)S(1)}, f32[8,768]{1,0:T(8,128)S(1)}, u32[]{:S(2)}, u32[]{:S(2)}) %collective-permute-start.28) | collective-permute-done | bytes 24608 | tf_op jit(solution)/shard_map/ppermute | solution.py:24
  78.2 0.4 root_part.1
  78.6 4.2 %collective-permute-start.29 = (f32[8,1536]{1,0:T(8,128)S(1)}, f32[8,1536]{1,0:T(8,128)S(1)}, u32[]{:S(2)}, u32[]{:S(2)}) collective-permute-start(f32[8,1536]{1,0:T(8,128)S(1)} %root_part.1), channel_id=1, source_target_pairs={{0,32},{32,0},{1,33},{33,1},{2,34},{34,2},{3,35},{35,3},{4,36},{36... | collective-permute-start | bytes 147464 | tf_op jit(solution)/shard_map/ppermute | solution.py:24
  82.8 0.9 collective-permute-done.29
  83.6 0.7 collective-permute-start.30
  84.4 2.2 %collective-permute-done.30 = f32[8,1536]{1,0:T(8,128)S(1)} collective-permute-done((f32[8,1536]{1,0:T(8,128)S(1)}, f32[8,1536]{1,0:T(8,128)S(1)}, u32[]{:S(2)}, u32[]{:S(2)}) %collective-permute-start.30) | collective-permute-done | bytes 49184 | tf_op jit(solution)/shard_map/ppermute | solution.py:24
  86.6 9.6 %all_to_all.11 = f32[8,8,1536]{2,1,0:T(8,128)S(1)} all-to-all(f32[8,8,1536]{2,1,0:T(8,128)S(1)} %broadcast_in_dim.2), channel_id=1, replica_groups={{7,6,5,4,3,2,1,0},{15,14,13,12,11,10,9,8},{23,22,21,20,19,18,17,16},{31..., dimensions={0} | all-to-all | bytes 786432 | tf_op jit(solution)/shard_map/all_to_all | solution.py:29
  96.3 0.7 copy.11
  (48 shorter events, 0.7 us)
Async XLA Ops:
  0.6 76.4 %copy-start = (f32[64,768]{1,0:T(8,128)S(1)}, f32[64,768]{1,0:T(8,128)}, u32[]{:S(2)}) copy-start(f32[64,768]{1,0:T(8,128)} %param.9) | copy-start | bytes 589828
  0.7 6.0 %copy-start.3 = (s32[3,3,24]{2,1,0:T(4,128)S(1)}, s32[3,3,24]{2,1,0:T(4,128)}, u32[]{:S(2)}) copy-start(s32[3,3,24]{2,1,0:T(4,128)} %param.13) | copy-start | bytes 2596
  2.3 4.3 %collective-permute-start = (f32[64,384]{1,0:T(8,128)S(1)}, f32[64,384]{1,0:T(8,128)S(1)}, u32[]{:S(2)}, u32[]{:S(2)}) collective-permute-start(f32[64,384]{1,0:T(8,128)S(1)} %first_solve.1), channel_id=1, source_target_pairs={{0,32},{32,0},{1,33},{33,1},{2,34},{34,2},{3,35},{35,3},{4,36},{36... | collective-permute-start | bytes 294920 | tf_op jit(solution)/shard_map/ppermute | solution.py:24
  6.5 4.1 %collective-permute-start.1 = (f32[64,384]{1,0:T(8,128)S(1)}, f32[64,384]{1,0:T(8,128)S(1)}, u32[]{:S(2)}, u32[]{:S(2)}) collective-permute-start(f32[64,384]{1,0:T(8,128)S(1)} %add.61.one_ref), channel_id=1, source_target_pairs={{0,64},{64,0},{1,65},{65,1},{2,66},{66,2},{3,67},{67,3},{4,68},{68... | collective-permute-start | bytes 294920 | tf_op jit(solution)/shard_map/ppermute | solution.py:24
  10.9 3.7 %collective-permute-start.2 = (f32[32,768]{1,0:T(8,128)S(1)}, f32[32,768]{1,0:T(8,128)S(1)}, u32[]{:S(2)}, u32[]{:S(2)}) collective-permute-start(f32[32,768]{1,0:T(8,128)S(1)} %get-tuple-element.35), channel_id=1, source_target_pairs={{0,4},{1,5},{2,6},{3,7},{4,0},{5,1},{6,2},{7,3},{8,12},{9,13},{10,... | collective-permute-start | bytes 294920 | tf_op jit(solution)/shard_map/ppermute | solution.py:24
  11.0 7.5 %collective-permute-start.9 = (f32[32,768]{1,0:T(8,128)S(1)}, f32[32,768]{1,0:T(8,128)S(1)}, u32[]{:S(2)}, u32[]{:S(2)}) collective-permute-start(f32[32,768]{1,0:T(8,128)S(1)} %get-tuple-element.39), channel_id=1, source_target_pairs={{0,2},{1,3},{2,0},{3,1},{4,6},{5,7},{6,4},{7,5},{8,10},{9,11},{10,... | collective-permute-start | bytes 294920 | tf_op jit(solution)/shard_map/ppermute | solution.py:24
  13.8 5.0 %collective-permute-start.10 = (f32[32,768]{1,0:T(8,128)S(1)}, f32[32,768]{1,0:T(8,128)S(1)}, u32[]{:S(2)}, u32[]{:S(2)}) collective-permute-start(f32[32,768]{1,0:T(8,128)S(1)} %get-tuple-element.39), channel_id=1, source_target_pairs={{0,3},{1,2},{2,1},{3,0},{4,7},{5,6},{6,5},{7,4},{8,11},{9,10},{10,... | collective-permute-start | bytes 294920 | tf_op jit(solution)/shard_map/ppermute | solution.py:24
  14.5 4.4 %collective-permute-start.8 = (f32[32,768]{1,0:T(8,128)S(1)}, f32[32,768]{1,0:T(8,128)S(1)}, u32[]{:S(2)}, u32[]{:S(2)}) collective-permute-start(f32[32,768]{1,0:T(8,128)S(1)} %get-tuple-element.39), channel_id=1, source_target_pairs={{0,1},{1,0},{2,3},{3,2},{4,5},{5,4},{6,7},{7,6},{8,9},{9,8},{10,11... | collective-permute-start | bytes 294920 | tf_op jit(solution)/shard_map/ppermute | solution.py:24
  14.6 6.2 %collective-permute-start.3 = (f32[32,768]{1,0:T(8,128)S(1)}, f32[32,768]{1,0:T(8,128)S(1)}, u32[]{:S(2)}, u32[]{:S(2)}) collective-permute-start(f32[32,768]{1,0:T(8,128)S(1)} %add.64.refs_0_), channel_id=1, source_target_pairs={{0,2},{1,3},{2,0},{3,1},{4,6},{5,7},{6,4},{7,5},{8,10},{9,11},{10,... | collective-permute-start | bytes 294920 | tf_op jit(solution)/shard_map/ppermute | solution.py:24
  17.7 6.3 %collective-permute-start.4 = (f32[32,768]{1,0:T(8,128)S(1)}, f32[32,768]{1,0:T(8,128)S(1)}, u32[]{:S(2)}, u32[]{:S(2)}) collective-permute-start(f32[32,768]{1,0:T(8,128)S(1)} %add.64.refs_0_), channel_id=1, source_target_pairs={{0,3},{1,2},{2,1},{3,0},{4,7},{5,6},{6,5},{7,4},{8,11},{9,10},{10,... | collective-permute-start | bytes 294920 | tf_op jit(solution)/shard_map/ppermute | solution.py:24
  18.5 5.5 %collective-permute-start.5 = (f32[32,768]{1,0:T(8,128)S(1)}, f32[32,768]{1,0:T(8,128)S(1)}, u32[]{:S(2)}, u32[]{:S(2)}) collective-permute-start(f32[32,768]{1,0:T(8,128)S(1)} %add.64.refs_0_), channel_id=1, source_target_pairs={{0,1},{1,0},{2,3},{3,2},{4,5},{5,4},{6,7},{7,6},{8,9},{9,8},{10,11... | collective-permute-start | bytes 294920 | tf_op jit(solution)/shard_map/ppermute | solution.py:24
  19.0 7.4 %collective-permute-start.11 = (f32[32,768]{1,0:T(8,128)S(1)}, f32[32,768]{1,0:T(8,128)S(1)}, u32[]{:S(2)}, u32[]{:S(2)}) collective-permute-start(f32[32,768]{1,0:T(8,128)S(1)} %add_add_fusion.1.refs_0_), channel_id=1, source_target_pairs={{0,4},{1,5},{2,6},{3,7},{4,0},{5,1},{6,2},{7,3},{8,12},{9,13},{10,... | collective-permute-start | bytes 294920 | tf_op jit(solution)/shard_map/ppermute | solution.py:24
  24.2 3.7 %collective-permute-start.6 = (f32[32,384]{1,0:T(8,128)S(1)}, f32[32,384]{1,0:T(8,128)S(1)}, u32[]{:S(2)}, u32[]{:S(2)}) collective-permute-start(f32[32,384]{1,0:T(8,128)S(1)} %next_solve.4), channel_id=1, source_target_pairs={{0,32},{32,0},{1,33},{33,1},{2,34},{34,2},{3,35},{35,3},{4,36},{36... | collective-permute-start | bytes 147464 | tf_op jit(solution)/shard_map/ppermute | solution.py:24
  26.7 3.0 %collective-permute-start.12 = (f32[32,384]{1,0:T(8,128)S(1)}, f32[32,384]{1,0:T(8,128)S(1)}, u32[]{:S(2)}, u32[]{:S(2)}) collective-permute-start(f32[32,384]{1,0:T(8,128)S(1)} %next_solve.5), channel_id=1, source_target_pairs={{0,64},{64,0},{1,65},{65,1},{2,66},{66,2},{3,67},{67,3},{4,68},{68... | collective-permute-start | bytes 147464 | tf_op jit(solution)/shard_map/ppermute | solution.py:24
  28.0 4.7 %collective-permute-start.7 = (f32[32,384]{1,0:T(8,128)S(1)}, f32[32,384]{1,0:T(8,128)S(1)}, u32[]{:S(2)}, u32[]{:S(2)}) collective-permute-start(f32[32,384]{1,0:T(8,128)S(1)} %add.65.one_ref), channel_id=1, source_target_pairs={{0,64},{64,0},{1,65},{65,1},{2,66},{66,2},{3,67},{67,3},{4,68},{68... | collective-permute-start | bytes 147464 | tf_op jit(solution)/shard_map/ppermute | solution.py:24
  29.7 3.5 %collective-permute-start.13 = (f32[32,384]{1,0:T(8,128)S(1)}, f32[32,384]{1,0:T(8,128)S(1)}, u32[]{:S(2)}, u32[]{:S(2)}) collective-permute-start(f32[32,384]{1,0:T(8,128)S(1)} %add.69.one_ref), channel_id=1, source_target_pairs={{0,32},{32,0},{1,33},{33,1},{2,34},{34,2},{3,35},{35,3},{4,36},{36... | collective-permute-start | bytes 147464 | tf_op jit(solution)/shard_map/ppermute | solution.py:24
  32.9 9.4 %copy-start.4 = (s32[3,3,24]{2,1,0:T(4,128)S(1)}, s32[3,3,24]{2,1,0:T(4,128)}, u32[]{:S(2)}) copy-start(s32[3,3,24]{2,1,0:T(4,128)} %param.15) | copy-start | bytes 2596
  32.9 9.4 %copy-start.2 = (bf16[3,384,768]{2,1,0:T(8,128)(2,1)S(1)}, bf16[3,384,768]{2,1,0:T(8,128)(2,1)}, u32[]{:S(2)}) copy-start(bf16[3,384,768]{2,1,0:T(8,128)(2,1)} %factor_ref.1) | copy-start | bytes 5308420
  33.0 3.6 %collective-permute-start.14 = (f32[32,768]{1,0:T(8,128)S(1)}, f32[32,768]{1,0:T(8,128)S(1)}, u32[]{:S(2)}, u32[]{:S(2)}) collective-permute-start(f32[32,768]{1,0:T(8,128)S(1)} %get-tuple-element.42), channel_id=1, source_target_pairs={{0,4},{1,5},{2,6},{3,7},{4,0},{5,1},{6,2},{7,3},{8,12},{9,13},{10,... | collective-permute-start | bytes 294920 | tf_op jit(solution)/shard_map/ppermute | solution.py:24
  33.4 6.5 %collective-permute-start.21 = (f32[32,768]{1,0:T(8,128)S(1)}, f32[32,768]{1,0:T(8,128)S(1)}, u32[]{:S(2)}, u32[]{:S(2)}) collective-permute-start(f32[32,768]{1,0:T(8,128)S(1)} %get-tuple-element.50), channel_id=1, source_target_pairs={{0,2},{1,3},{2,0},{3,1},{4,6},{5,7},{6,4},{7,5},{8,10},{9,11},{10,... | collective-permute-start | bytes 294920 | tf_op jit(solution)/shard_map/ppermute | solution.py:24
  35.1 5.4 %collective-permute-start.22 = (f32[32,768]{1,0:T(8,128)S(1)}, f32[32,768]{1,0:T(8,128)S(1)}, u32[]{:S(2)}, u32[]{:S(2)}) collective-permute-start(f32[32,768]{1,0:T(8,128)S(1)} %get-tuple-element.50), channel_id=1, source_target_pairs={{0,3},{1,2},{2,1},{3,0},{4,7},{5,6},{6,5},{7,4},{8,11},{9,10},{10,... | collective-permute-start | bytes 294920 | tf_op jit(solution)/shard_map/ppermute | solution.py:24
  35.9 4.6 %collective-permute-start.20 = (f32[32,768]{1,0:T(8,128)S(1)}, f32[32,768]{1,0:T(8,128)S(1)}, u32[]{:S(2)}, u32[]{:S(2)}) collective-permute-start(f32[32,768]{1,0:T(8,128)S(1)} %get-tuple-element.50), channel_id=1, source_target_pairs={{0,1},{1,0},{2,3},{3,2},{4,5},{5,4},{6,7},{7,6},{8,9},{9,8},{10,11... | collective-permute-start | bytes 294920 | tf_op jit(solution)/shard_map/ppermute | solution.py:24
  36.5 7.4 %collective-permute-start.15 = (f32[32,768]{1,0:T(8,128)S(1)}, f32[32,768]{1,0:T(8,128)S(1)}, u32[]{:S(2)}, u32[]{:S(2)}) collective-permute-start(f32[32,768]{1,0:T(8,128)S(1)} %add.70.refs_0_), channel_id=1, source_target_pairs={{0,2},{1,3},{2,0},{3,1},{4,6},{5,7},{6,4},{7,5},{8,10},{9,11},{10,... | collective-permute-start | bytes 294920 | tf_op jit(solution)/shard_map/ppermute | solution.py:24
  39.1 5.7 %collective-permute-start.16 = (f32[32,768]{1,0:T(8,128)S(1)}, f32[32,768]{1,0:T(8,128)S(1)}, u32[]{:S(2)}, u32[]{:S(2)}) collective-permute-start(f32[32,768]{1,0:T(8,128)S(1)} %add.70.refs_0_), channel_id=1, source_target_pairs={{0,3},{1,2},{2,1},{3,0},{4,7},{5,6},{6,5},{7,4},{8,11},{9,10},{10,... | collective-permute-start | bytes 294920 | tf_op jit(solution)/shard_map/ppermute | solution.py:24
  39.9 5.0 %collective-permute-start.17 = (f32[32,768]{1,0:T(8,128)S(1)}, f32[32,768]{1,0:T(8,128)S(1)}, u32[]{:S(2)}, u32[]{:S(2)}) collective-permute-start(f32[32,768]{1,0:T(8,128)S(1)} %add.70.refs_0_), channel_id=1, source_target_pairs={{0,1},{1,0},{2,3},{3,2},{4,5},{5,4},{6,7},{7,6},{8,9},{9,8},{10,11... | collective-permute-start | bytes 294920 | tf_op jit(solution)/shard_map/ppermute | solution.py:24
  40.6 6.9 %collective-permute-start.23 = (f32[32,768]{1,0:T(8,128)S(1)}, f32[32,768]{1,0:T(8,128)S(1)}, u32[]{:S(2)}, u32[]{:S(2)}) collective-permute-start(f32[32,768]{1,0:T(8,128)S(1)} %add_add_fusion.refs_0_), channel_id=1, source_target_pairs={{0,4},{1,5},{2,6},{3,7},{4,0},{5,1},{6,2},{7,3},{8,12},{9,13},{10,... | collective-permute-start | bytes 294920 | tf_op jit(solution)/shard_map/ppermute | solution.py:24
  45.0 3.4 %collective-permute-start.18 = (f32[32,384]{1,0:T(8,128)S(1)}, f32[32,384]{1,0:T(8,128)S(1)}, u32[]{:S(2)}, u32[]{:S(2)}) collective-permute-start(f32[32,384]{1,0:T(8,128)S(1)} %next_solve.6), channel_id=1, source_target_pairs={{0,32},{32,0},{1,33},{33,1},{2,34},{34,2},{3,35},{35,3},{4,36},{36... | collective-permute-start | bytes 147464 | tf_op jit(solution)/shard_map/ppermute | solution.py:24
  47.7 3.0 %collective-permute-start.24 = (f32[32,384]{1,0:T(8,128)S(1)}, f32[32,384]{1,0:T(8,128)S(1)}, u32[]{:S(2)}, u32[]{:S(2)}) collective-permute-start(f32[32,384]{1,0:T(8,128)S(1)} %next_solve.7), channel_id=1, source_target_pairs={{0,64},{64,0},{1,65},{65,1},{2,66},{66,2},{3,67},{67,3},{4,68},{68... | collective-permute-start | bytes 147464 | tf_op jit(solution)/shard_map/ppermute | solution.py:24
  48.4 4.3 %collective-permute-start.19 = (f32[32,384]{1,0:T(8,128)S(1)}, f32[32,384]{1,0:T(8,128)S(1)}, u32[]{:S(2)}, u32[]{:S(2)}) collective-permute-start(f32[32,384]{1,0:T(8,128)S(1)} %add.71.one_ref), channel_id=1, source_target_pairs={{0,64},{64,0},{1,65},{65,1},{2,66},{66,2},{3,67},{67,3},{4,68},{68... | collective-permute-start | bytes 147464 | tf_op jit(solution)/shard_map/ppermute | solution.py:24
  50.8 2.9 %collective-permute-start.25 = (f32[32,384]{1,0:T(8,128)S(1)}, f32[32,384]{1,0:T(8,128)S(1)}, u32[]{:S(2)}, u32[]{:S(2)}) collective-permute-start(f32[32,384]{1,0:T(8,128)S(1)} %add.75.one_ref), channel_id=1, source_target_pairs={{0,32},{32,0},{1,33},{33,1},{2,34},{34,2},{3,35},{35,3},{4,36},{36... | collective-permute-start | bytes 147464 | tf_op jit(solution)/shard_map/ppermute | solution.py:24
  53.0 25.2 %copy-start.1 = (bf16[768,1536]{1,0:T(8,128)(2,1)S(1)}, bf16[768,1536]{1,0:T(8,128)(2,1)}, u32[]{:S(2)}) copy-start(bf16[768,1536]{1,0:T(8,128)(2,1)} %inverse_ref.1) | copy-start | bytes 7077892
  62.6 5.6 %collective-permute-start.26 = (f32[8,768]{1,0:T(8,128)S(1)}, f32[8,768]{1,0:T(8,128)S(1)}, u32[]{:S(2)}, u32[]{:S(2)}) collective-permute-start(f32[8,768]{1,0:T(8,128)S(1)} %reduce_sum.9), channel_id=1, source_target_pairs={{0,128},{128,0},{1,129},{129,1},{2,130},{130,2},{3,131},{131,3},{4... | collective-permute-start | bytes 73736 | tf_op jit(solution)/shard_map/ppermute | solution.py:24
  68.3 4.2 %collective-permute-start.27 = (f32[8,768]{1,0:T(8,128)S(1)}, f32[8,768]{1,0:T(8,128)S(1)}, u32[]{:S(2)}, u32[]{:S(2)}) collective-permute-start(f32[8,768]{1,0:T(8,128)S(1)} %add.77), channel_id=1, source_target_pairs={{0,8},{8,0},{16,24},{24,16},{1,9},{9,1},{17,25},{25,17},{2,10},{10... | collective-permute-start | bytes 73736 | tf_op jit(solution)/shard_map/ppermute | solution.py:24
  72.5 5.7 %collective-permute-start.28 = (f32[8,768]{1,0:T(8,128)S(1)}, f32[8,768]{1,0:T(8,128)S(1)}, u32[]{:S(2)}, u32[]{:S(2)}) collective-permute-start(f32[8,768]{1,0:T(8,128)S(1)} %add.78.one_ref), channel_id=1, source_target_pairs={{0,24},{8,16},{16,8},{24,0},{1,25},{9,17},{17,9},{25,1},{2,26},{10... | collective-permute-start | bytes 73736 | tf_op jit(solution)/shard_map/ppermute | solution.py:24
  78.6 5.0 %collective-permute-start.29 = (f32[8,1536]{1,0:T(8,128)S(1)}, f32[8,1536]{1,0:T(8,128)S(1)}, u32[]{:S(2)}, u32[]{:S(2)}) collective-permute-start(f32[8,1536]{1,0:T(8,128)S(1)} %root_part.1), channel_id=1, source_target_pairs={{0,32},{32,0},{1,33},{33,1},{2,34},{34,2},{3,35},{35,3},{4,36},{36... | collective-permute-start | bytes 147464 | tf_op jit(solution)/shard_map/ppermute | solution.py:24
  83.6 2.9 %collective-permute-start.30 = (f32[8,1536]{1,0:T(8,128)S(1)}, f32[8,1536]{1,0:T(8,128)S(1)}, u32[]{:S(2)}, u32[]{:S(2)}) collective-permute-start(f32[8,1536]{1,0:T(8,128)S(1)} %add.79), channel_id=1, source_target_pairs={{0,64},{64,0},{1,65},{65,1},{2,66},{66,2},{3,67},{67,3},{4,68},{68... | collective-permute-start | bytes 147464 | tf_op jit(solution)/shard_map/ppermute | solution.py:24

commit v14 on v11

--- a/solution.py
+++ b/solution.py
@@ -290,8 +290,9 @@
         halves = prow_halves(next_solve(0, part, rhs, owner_sums(update, part), inverse))
         early = early_update((kept0,), inner, (1,))
         update, solved1, kept1 = kept_update(halves, inner, 2, (early,))
-        halves = prow_halves(next_solve(1, part, rhs, owner_sums(update, part), inverse))
         early = early_update((kept0, kept1), root, (0, 1))
+        *sums, early = lax.optimization_barrier((*owner_sums(update, part), early))
+        halves = prow_halves(next_solve(1, part, rhs, sums, inverse))
         root_local, solved2 = kept_update(halves, root, 2, (early,), last=True)
         solved.append((solved0, solved1, solved2))
         locals_.append(root_local)

time: 97.2 us -> 97.2 us (level)
  transfers between devices with their start and end apart: 31 -> 31, of which waited for: 18 -> 17; matrix products, arithmetic and copies ran while one was open for 0% -> 0% of each run, Pallas kernels for 7% -> 7%
where the time goes in v14:
time: 97.2 us; the launch traced here: 96.1 us
  starting transfers between devices  46.6 us (48%)
  waiting for transfers between devices  20.4 us (21%)
  blocking collectives  18 us (19%)
  Pallas kernels  9.03 us (9%)
    ppermute x31, starting transfers between devices, partner(): lax.ppermute(shard, axis, [(i, i ^ bit) for i in range(lax.axis_size(axis...  46.6 us
    ppermute x31, waiting for transfers between devices, partner(): lax.ppermute(shard, axis, [(i, i ^ bit) for i in range(lax.axis_size(axis...  20.4 us
    all_to_all x2, blocking collectives, swap_blocks(): lax.all_to_all(blocks, OWN, 0, 0, axis_index_groups=[order], tiled=True)  18 us
    pallas_call x17, Pallas kernels, call(): pl.pallas_call(body, out_shape=[pltpu.VMEM(shape, kind) for shape, kind i...  8.27 us
  transfers between devices with their start and end apart: 31, of which 17 were waited for; matrix products, arithmetic and copies ran while one was open for 0% of the time, Pallas kernels for 7%

profile of v14, /device:TPU:1, one launch (start us, length us, event | category | flops | bytes accessed | tf_op | source)
XLA Modules:
  0.0 96.1 jit_solution(16800563309239425799)
XLA Ops:
  0.7 1.6 %first_solve.1 = f32[64,384]{1,0:T(8,128)S(1)} custom-call(s32[1]{0:T(128)} %bitcast.tree_ref, f32[4,3,64,768]{3,2,1,0:T(8,128)} %rhs_hbm.3, bf16[3,768,384]{2,1,0:T(8,128)(2,1)} %inverse_hbm.3), custom_call_target="tpu_custom_call" | custom-call | tf_op jit(solution)/shard_map/first_solve/pallas_call | solution.py:43
  2.3 3.3 %collective-permute-start = (f32[64,384]{1,0:T(8,128)S(1)}, f32[64,384]{1,0:T(8,128)S(1)}, u32[]{:S(2)}, u32[]{:S(2)}) collective-permute-start(f32[64,384]{1,0:T(8,128)S(1)} %first_solve.1), channel_id=1, source_target_pairs={{0,32},{32,0},{1,33},{33,1},{2,34},{34,2},{3,35},{35,3},{4,36},{36... | collective-permute-start | bytes 294920 | tf_op jit(solution)/shard_map/ppermute | solution.py:24
  5.6 0.9 collective-permute-done
  6.7 2.6 %stage.1 = (bf16[3,384,768]{2,1,0:T(8,128)(2,1)S(1)}, bf16[2,768,384]{2,1,0:T(8,128)(2,1)S(1)}, f32[2,64,768]{2,1,0:T(8,128)S(1)}) custom-call(s32[1]{0:T(128)} %bitcast.tree_ref, s32[3,3,6]{2,1,0:T(4,128)S(1)} %constant_dynamic-slice_fusion.2.mask_ref, f32[4,3,64,768]{3,2,1,0:T(8,128)} %rhs_hbm.3, bf16[3,768,384]{2,1,0:T(8,128)(2,1)} %inverse_hbm.3, ...), custom_call_target="tpu_custom_call" | custom-call | tf_op jit(solution)/shard_map/stage/pallas_call | solution.py:43
  9.3 1.4 %collective-permute-done.1.other_ref = f32[64,384]{1,0:T(8,128)S(1)} collective-permute-done((f32[64,384]{1,0:T(8,128)S(1)}, f32[64,384]{1,0:T(8,128)S(1)}, u32[]{:S(2)}, u32[]{:S(2)}) %collective-permute-start.1) | collective-permute-done | bytes 98336 | tf_op jit(solution)/shard_map/ppermute | solution.py:24
  10.7 0.2 kept_update.5
  10.9 0.1 collective-permute-start.2
  11.0 2.8 %collective-permute-start.9 = (f32[32,768]{1,0:T(8,128)S(1)}, f32[32,768]{1,0:T(8,128)S(1)}, u32[]{:S(2)}, u32[]{:S(2)}) collective-permute-start(f32[32,768]{1,0:T(8,128)S(1)} %get-tuple-element.39), channel_id=1, source_target_pairs={{0,2},{1,3},{2,0},{3,1},{4,6},{5,7},{6,4},{7,5},{8,10},{9,11},{10,... | collective-permute-start | bytes 294920 | tf_op jit(solution)/shard_map/ppermute | solution.py:24
  13.8 0.8 collective-permute-start.10
  14.6 3.2 %collective-permute-start.3 = (f32[32,768]{1,0:T(8,128)S(1)}, f32[32,768]{1,0:T(8,128)S(1)}, u32[]{:S(2)}, u32[]{:S(2)}) collective-permute-start(f32[32,768]{1,0:T(8,128)S(1)} %add.64.refs_0_), channel_id=1, source_target_pairs={{0,2},{1,3},{2,0},{3,1},{4,6},{5,7},{6,4},{7,5},{8,10},{9,11},{10,... | collective-permute-start | bytes 294920 | tf_op jit(solution)/shard_map/ppermute | solution.py:24
  17.7 0.8 collective-permute-start.4
  18.5 0.3 collective-permute-done.10
  18.8 0.2 collective-permute-done.8
  19.0 0.6 collective-permute-start.11
  19.6 1.2 %collective-permute-done.3.refs_1_ = f32[32,768]{1,0:T(8,128)S(1)} collective-permute-done((f32[32,768]{1,0:T(8,128)S(1)}, f32[32,768]{1,0:T(8,128)S(1)}, u32[]{:S(2)}, u32[]{:S(2)}) %collective-permute-start.3) | collective-permute-done | bytes 98336 | tf_op jit(solution)/shard_map/ppermute | solution.py:24
  20.8 3.2 %collective-permute-done.4.refs_2_ = f32[32,768]{1,0:T(8,128)S(1)} collective-permute-done((f32[32,768]{1,0:T(8,128)S(1)}, f32[32,768]{1,0:T(8,128)S(1)}, u32[]{:S(2)}, u32[]{:S(2)}) %collective-permute-start.4) | collective-permute-done | bytes 98336 | tf_op jit(solution)/shard_map/ppermute | solution.py:24
  24.0 0.2 next_solve.4
  24.2 2.2 %collective-permute-start.6 = (f32[32,384]{1,0:T(8,128)S(1)}, f32[32,384]{1,0:T(8,128)S(1)}, u32[]{:S(2)}, u32[]{:S(2)}) collective-permute-start(f32[32,384]{1,0:T(8,128)S(1)} %next_solve.4), channel_id=1, source_target_pairs={{0,32},{32,0},{1,33},{33,1},{2,34},{34,2},{3,35},{35,3},{4,36},{36... | collective-permute-start | bytes 147464 | tf_op jit(solution)/shard_map/ppermute | solution.py:24
  26.4 0.2 next_solve.5
  26.7 1.0 %collective-permute-start.12 = (f32[32,384]{1,0:T(8,128)S(1)}, f32[32,384]{1,0:T(8,128)S(1)}, u32[]{:S(2)}, u32[]{:S(2)}) collective-permute-start(f32[32,384]{1,0:T(8,128)S(1)} %next_solve.5), channel_id=1, source_target_pairs={{0,32},{32,0},{1,33},{33,1},{2,34},{34,2},{3,35},{35,3},{4,36},{36... | collective-permute-start | bytes 147464 | tf_op jit(solution)/shard_map/ppermute | solution.py:24
  27.7 1.3 %collective-permute-start.7 = (f32[32,384]{1,0:T(8,128)S(1)}, f32[32,384]{1,0:T(8,128)S(1)}, u32[]{:S(2)}, u32[]{:S(2)}) collective-permute-start(f32[32,384]{1,0:T(8,128)S(1)} %add.65.one_ref), channel_id=1, source_target_pairs={{0,64},{64,0},{1,65},{65,1},{2,66},{66,2},{3,67},{67,3},{4,68},{68... | collective-permute-start | bytes 147464 | tf_op jit(solution)/shard_map/ppermute | solution.py:24
  29.0 0.8 collective-permute-start.13
  29.8 0.2 early_update.4.refs_0_
  30.0 0.2 early_update.5.refs_0_
  30.3 0.9 collective-permute-done.7.other_ref
  31.2 0.2 kept_update.6
  31.4 0.1 collective-permute-start.14
  31.5 0.6 collective-permute-done.13.other_ref
  32.1 0.2 kept_update.7
  32.3 2.2 %collective-permute-start.21 = (f32[32,768]{1,0:T(8,128)S(1)}, f32[32,768]{1,0:T(8,128)S(1)}, u32[]{:S(2)}, u32[]{:S(2)}) collective-permute-start(f32[32,768]{1,0:T(8,128)S(1)} %get-tuple-element.50), channel_id=1, source_target_pairs={{0,2},{1,3},{2,0},{3,1},{4,6},{5,7},{6,4},{7,5},{8,10},{9,11},{10,... | collective-permute-start | bytes 294920 | tf_op jit(solution)/shard_map/ppermute | solution.py:24
  34.4 0.8 collective-permute-start.22
  35.2 3.2 %collective-permute-start.15 = (f32[32,768]{1,0:T(8,128)S(1)}, f32[32,768]{1,0:T(8,128)S(1)}, u32[]{:S(2)}, u32[]{:S(2)}) collective-permute-start(f32[32,768]{1,0:T(8,128)S(1)} %add.70.refs_0_), channel_id=1, source_target_pairs={{0,2},{1,3},{2,0},{3,1},{4,6},{5,7},{6,4},{7,5},{8,10},{9,11},{10,... | collective-permute-start | bytes 294920 | tf_op jit(solution)/shard_map/ppermute | solution.py:24
  38.4 0.8 collective-permute-start.16
  39.2 1.0 %collective-permute-done.22 = f32[32,768]{1,0:T(8,128)S(1)} collective-permute-done((f32[32,768]{1,0:T(8,128)S(1)}, f32[32,768]{1,0:T(8,128)S(1)}, u32[]{:S(2)}, u32[]{:S(2)}) %collective-permute-start.22) | collective-permute-done | bytes 98336 | tf_op jit(solution)/shard_map/ppermute | solution.py:24
  40.2 0.7 collective-permute-start.23
  41.0 0.9 masked.1.refs_2_.factor_ref
  41.9 0.3 early_update.6.refs_0_
  42.2 0.3 early_update.7.refs_0_
  42.6 2.1 %collective-permute-done.16.refs_2_ = f32[32,768]{1,0:T(8,128)S(1)} collective-permute-done((f32[32,768]{1,0:T(8,128)S(1)}, f32[32,768]{1,0:T(8,128)S(1)}, u32[]{:S(2)}, u32[]{:S(2)}) %collective-permute-start.16) | collective-permute-done | bytes 98336 | tf_op jit(solution)/shard_map/ppermute | solution.py:24
  44.7 0.2 next_solve.6
  44.9 2.2 %collective-permute-start.18 = (f32[32,384]{1,0:T(8,128)S(1)}, f32[32,384]{1,0:T(8,128)S(1)}, u32[]{:S(2)}, u32[]{:S(2)}) collective-permute-start(f32[32,384]{1,0:T(8,128)S(1)} %next_solve.6), channel_id=1, source_target_pairs={{0,32},{32,0},{1,33},{33,1},{2,34},{34,2},{3,35},{35,3},{4,36},{36... | collective-permute-start | bytes 147464 | tf_op jit(solution)/shard_map/ppermute | solution.py:24
  47.1 0.2 next_solve.7
  47.3 1.0 %collective-permute-start.24 = (f32[32,384]{1,0:T(8,128)S(1)}, f32[32,384]{1,0:T(8,128)S(1)}, u32[]{:S(2)}, u32[]{:S(2)}) collective-permute-start(f32[32,384]{1,0:T(8,128)S(1)} %next_solve.7), channel_id=1, source_target_pairs={{0,32},{32,0},{1,33},{33,1},{2,34},{34,2},{3,35},{35,3},{4,36},{36... | collective-permute-start | bytes 147464 | tf_op jit(solution)/shard_map/ppermute | solution.py:24
  48.4 0.9 collective-permute-start.19
  49.2 0.8 collective-permute-start.25
  50.1 1.7 %collective-permute-done.19.other_ref = f32[32,384]{1,0:T(8,128)S(1)} collective-permute-done((f32[32,384]{1,0:T(8,128)S(1)}, f32[32,384]{1,0:T(8,128)S(1)}, u32[]{:S(2)}, u32[]{:S(2)}) %collective-permute-start.19) | collective-permute-done | bytes 49184 | tf_op jit(solution)/shard_map/ppermute | solution.py:24
  51.8 0.2 kept_update.8
  52.0 0.4 collective-permute-done.25.other_ref
  52.4 0.2 kept_update.9
  52.7 8.4 %all_to_all.10 = f32[8,8,768]{2,1,0:T(8,128)S(1)} all-to-all(f32[8,8,768]{2,1,0:T(8,128)S(1)} %maximum_bitcast_fusion), channel_id=1, replica_groups={{7,6,5,4,3,2,1,0},{15,14,13,12,11,10,9,8},{23,22,21,20,19,18,17,16},{31..., dimensions={0} | all-to-all | bytes 393216 | tf_op jit(solution)/shard_map/all_to_all | solution.py:29
  61.1 2.5 %collective-permute-start.26 = (f32[8,768]{1,0:T(8,128)S(1)}, f32[8,768]{1,0:T(8,128)S(1)}, u32[]{:S(2)}, u32[]{:S(2)}) collective-permute-start(f32[8,768]{1,0:T(8,128)S(1)} %reduce_sum.9), channel_id=1, source_target_pairs={{0,128},{128,0},{1,129},{129,1},{2,130},{130,2},{3,131},{131,3},{4... | collective-permute-start | bytes 73736 | tf_op jit(solution)/shard_map/ppermute | solution.py:24
  63.6 0.8 stacked.1
  64.4 1.0 %collective-permute-done.26 = f32[8,768]{1,0:T(8,128)S(1)} collective-permute-done((f32[8,768]{1,0:T(8,128)S(1)}, f32[8,768]{1,0:T(8,128)S(1)}, u32[]{:S(2)}, u32[]{:S(2)}) %collective-permute-start.26) | collective-permute-done | bytes 24608 | tf_op jit(solution)/shard_map/ppermute | solution.py:24
  65.4 3.0 %collective-permute-start.27 = (f32[8,768]{1,0:T(8,128)S(1)}, f32[8,768]{1,0:T(8,128)S(1)}, u32[]{:S(2)}, u32[]{:S(2)}) collective-permute-start(f32[8,768]{1,0:T(8,128)S(1)} %add.77), channel_id=1, source_target_pairs={{0,8},{8,0},{16,24},{24,16},{1,9},{9,1},{17,25},{25,17},{2,10},{10... | collective-permute-start | bytes 73736 | tf_op jit(solution)/shard_map/ppermute | solution.py:24
  68.3 1.2 %collective-permute-done.27 = f32[8,768]{1,0:T(8,128)S(1)} collective-permute-done((f32[8,768]{1,0:T(8,128)S(1)}, f32[8,768]{1,0:T(8,128)S(1)}, u32[]{:S(2)}, u32[]{:S(2)}) %collective-permute-start.27) | collective-permute-done | bytes 24608 | tf_op jit(solution)/shard_map/ppermute | solution.py:24
  69.6 4.8 %collective-permute-start.28 = (f32[8,768]{1,0:T(8,128)S(1)}, f32[8,768]{1,0:T(8,128)S(1)}, u32[]{:S(2)}, u32[]{:S(2)}) collective-permute-start(f32[8,768]{1,0:T(8,128)S(1)} %add.78.one_ref), channel_id=1, source_target_pairs={{0,24},{8,16},{16,8},{24,0},{1,25},{9,17},{17,9},{25,1},{2,26},{10... | collective-permute-start | bytes 73736 | tf_op jit(solution)/shard_map/ppermute | solution.py:24
  74.4 1.2 %collective-permute-done.28.other_ref = f32[8,768]{1,0:T(8,128)S(1)} collective-permute-done((f32[8,768]{1,0:T(8,128)S(1)}, f32[8,768]{1,0:T(8,128)S(1)}, u32[]{:S(2)}, u32[]{:S(2)}) %collective-permute-start.28) | collective-permute-done | bytes 24608 | tf_op jit(solution)/shard_map/ppermute | solution.py:24
  75.6 0.4 root_part.1
  76.0 5.8 %collective-permute-start.29 = (f32[8,1536]{1,0:T(8,128)S(1)}, f32[8,1536]{1,0:T(8,128)S(1)}, u32[]{:S(2)}, u32[]{:S(2)}) collective-permute-start(f32[8,1536]{1,0:T(8,128)S(1)} %root_part.1), channel_id=1, source_target_pairs={{0,32},{32,0},{1,33},{33,1},{2,34},{34,2},{3,35},{35,3},{4,36},{36... | collective-permute-start | bytes 147464 | tf_op jit(solution)/shard_map/ppermute | solution.py:24
  81.8 0.9 collective-permute-done.29
  82.7 0.8 collective-permute-start.30
  83.5 2.1 %collective-permute-done.30 = f32[8,1536]{1,0:T(8,128)S(1)} collective-permute-done((f32[8,1536]{1,0:T(8,128)S(1)}, f32[8,1536]{1,0:T(8,128)S(1)}, u32[]{:S(2)}, u32[]{:S(2)}) %collective-permute-start.30) | collective-permute-done | bytes 49184 | tf_op jit(solution)/shard_map/ppermute | solution.py:24
  85.7 9.6 %all_to_all.11 = f32[8,8,1536]{2,1,0:T(8,128)S(1)} all-to-all(f32[8,8,1536]{2,1,0:T(8,128)S(1)} %broadcast_in_dim.2), channel_id=1, replica_groups={{7,6,5,4,3,2,1,0},{15,14,13,12,11,10,9,8},{23,22,21,20,19,18,17,16},{31..., dimensions={0} | all-to-all | bytes 786432 | tf_op jit(solution)/shard_map/all_to_all | solution.py:29
  95.3 0.7 copy.11
  (48 shorter events, 0.5 us)
Async XLA Ops:
  0.6 73.7 %copy-start = (f32[64,768]{1,0:T(8,128)S(1)}, f32[64,768]{1,0:T(8,128)}, u32[]{:S(2)}) copy-start(f32[64,768]{1,0:T(8,128)} %param.9) | copy-start | bytes 589828
  0.7 6.0 %copy-start.3 = (s32[3,3,24]{2,1,0:T(4,128)S(1)}, s32[3,3,24]{2,1,0:T(4,128)}, u32[]{:S(2)}) copy-start(s32[3,3,24]{2,1,0:T(4,128)} %param.13) | copy-start | bytes 2596
  2.3 4.3 %collective-permute-start = (f32[64,384]{1,0:T(8,128)S(1)}, f32[64,384]{1,0:T(8,128)S(1)}, u32[]{:S(2)}, u32[]{:S(2)}) collective-permute-start(f32[64,384]{1,0:T(8,128)S(1)} %first_solve.1), channel_id=1, source_target_pairs={{0,32},{32,0},{1,33},{33,1},{2,34},{34,2},{3,35},{35,3},{4,36},{36... | collective-permute-start | bytes 294920 | tf_op jit(solution)/shard_map/ppermute | solution.py:24
  6.5 4.1 %collective-permute-start.1 = (f32[64,384]{1,0:T(8,128)S(1)}, f32[64,384]{1,0:T(8,128)S(1)}, u32[]{:S(2)}, u32[]{:S(2)}) collective-permute-start(f32[64,384]{1,0:T(8,128)S(1)} %add.61.one_ref), channel_id=1, source_target_pairs={{0,64},{64,0},{1,65},{65,1},{2,66},{66,2},{3,67},{67,3},{4,68},{68... | collective-permute-start | bytes 294920 | tf_op jit(solution)/shard_map/ppermute | solution.py:24
  10.9 3.7 %collective-permute-start.2 = (f32[32,768]{1,0:T(8,128)S(1)}, f32[32,768]{1,0:T(8,128)S(1)}, u32[]{:S(2)}, u32[]{:S(2)}) collective-permute-start(f32[32,768]{1,0:T(8,128)S(1)} %get-tuple-element.35), channel_id=1, source_target_pairs={{0,4},{1,5},{2,6},{3,7},{4,0},{5,1},{6,2},{7,3},{8,12},{9,13},{10,... | collective-permute-start | bytes 294920 | tf_op jit(solution)/shard_map/ppermute | solution.py:24
  11.0 7.5 %collective-permute-start.9 = (f32[32,768]{1,0:T(8,128)S(1)}, f32[32,768]{1,0:T(8,128)S(1)}, u32[]{:S(2)}, u32[]{:S(2)}) collective-permute-start(f32[32,768]{1,0:T(8,128)S(1)} %get-tuple-element.39), channel_id=1, source_target_pairs={{0,2},{1,3},{2,0},{3,1},{4,6},{5,7},{6,4},{7,5},{8,10},{9,11},{10,... | collective-permute-start | bytes 294920 | tf_op jit(solution)/shard_map/ppermute | solution.py:24
  13.8 5.0 %collective-permute-start.10 = (f32[32,768]{1,0:T(8,128)S(1)}, f32[32,768]{1,0:T(8,128)S(1)}, u32[]{:S(2)}, u32[]{:S(2)}) collective-permute-start(f32[32,768]{1,0:T(8,128)S(1)} %get-tuple-element.39), channel_id=1, source_target_pairs={{0,3},{1,2},{2,1},{3,0},{4,7},{5,6},{6,5},{7,4},{8,11},{9,10},{10,... | collective-permute-start | bytes 294920 | tf_op jit(solution)/shard_map/ppermute | solution.py:24
  14.5 4.4 %collective-permute-start.8 = (f32[32,768]{1,0:T(8,128)S(1)}, f32[32,768]{1,0:T(8,128)S(1)}, u32[]{:S(2)}, u32[]{:S(2)}) collective-permute-start(f32[32,768]{1,0:T(8,128)S(1)} %get-tuple-element.39), channel_id=1, source_target_pairs={{0,1},{1,0},{2,3},{3,2},{4,5},{5,4},{6,7},{7,6},{8,9},{9,8},{10,11... | collective-permute-start | bytes 294920 | tf_op jit(solution)/shard_map/ppermute | solution.py:24
  14.6 6.2 %collective-permute-start.3 = (f32[32,768]{1,0:T(8,128)S(1)}, f32[32,768]{1,0:T(8,128)S(1)}, u32[]{:S(2)}, u32[]{:S(2)}) collective-permute-start(f32[32,768]{1,0:T(8,128)S(1)} %add.64.refs_0_), channel_id=1, source_target_pairs={{0,2},{1,3},{2,0},{3,1},{4,6},{5,7},{6,4},{7,5},{8,10},{9,11},{10,... | collective-permute-start | bytes 294920 | tf_op jit(solution)/shard_map/ppermute | solution.py:24
  17.7 6.3 %collective-permute-start.4 = (f32[32,768]{1,0:T(8,128)S(1)}, f32[32,768]{1,0:T(8,128)S(1)}, u32[]{:S(2)}, u32[]{:S(2)}) collective-permute-start(f32[32,768]{1,0:T(8,128)S(1)} %add.64.refs_0_), channel_id=1, source_target_pairs={{0,3},{1,2},{2,1},{3,0},{4,7},{5,6},{6,5},{7,4},{8,11},{9,10},{10,... | collective-permute-start | bytes 294920 | tf_op jit(solution)/shard_map/ppermute | solution.py:24
  18.5 5.5 %collective-permute-start.5 = (f32[32,768]{1,0:T(8,128)S(1)}, f32[32,768]{1,0:T(8,128)S(1)}, u32[]{:S(2)}, u32[]{:S(2)}) collective-permute-start(f32[32,768]{1,0:T(8,128)S(1)} %add.64.refs_0_), channel_id=1, source_target_pairs={{0,1},{1,0},{2,3},{3,2},{4,5},{5,4},{6,7},{7,6},{8,9},{9,8},{10,11... | collective-permute-start | bytes 294920 | tf_op jit(solution)/shard_map/ppermute | solution.py:24
  19.0 7.4 %collective-permute-start.11 = (f32[32,768]{1,0:T(8,128)S(1)}, f32[32,768]{1,0:T(8,128)S(1)}, u32[]{:S(2)}, u32[]{:S(2)}) collective-permute-start(f32[32,768]{1,0:T(8,128)S(1)} %add_add_fusion.1.refs_0_), channel_id=1, source_target_pairs={{0,4},{1,5},{2,6},{3,7},{4,0},{5,1},{6,2},{7,3},{8,12},{9,13},{10,... | collective-permute-start | bytes 294920 | tf_op jit(solution)/shard_map/ppermute | solution.py:24
  24.2 3.5 %collective-permute-start.6 = (f32[32,384]{1,0:T(8,128)S(1)}, f32[32,384]{1,0:T(8,128)S(1)}, u32[]{:S(2)}, u32[]{:S(2)}) collective-permute-start(f32[32,384]{1,0:T(8,128)S(1)} %next_solve.4), channel_id=1, source_target_pairs={{0,32},{32,0},{1,33},{33,1},{2,34},{34,2},{3,35},{35,3},{4,36},{36... | collective-permute-start | bytes 147464 | tf_op jit(solution)/shard_map/ppermute | solution.py:24
  26.7 2.4 %collective-permute-start.12 = (f32[32,384]{1,0:T(8,128)S(1)}, f32[32,384]{1,0:T(8,128)S(1)}, u32[]{:S(2)}, u32[]{:S(2)}) collective-permute-start(f32[32,384]{1,0:T(8,128)S(1)} %next_solve.5), channel_id=1, source_target_pairs={{0,32},{32,0},{1,33},{33,1},{2,34},{34,2},{3,35},{35,3},{4,36},{36... | collective-permute-start | bytes 147464 | tf_op jit(solution)/shard_map/ppermute | solution.py:24
  27.7 3.4 %collective-permute-start.7 = (f32[32,384]{1,0:T(8,128)S(1)}, f32[32,384]{1,0:T(8,128)S(1)}, u32[]{:S(2)}, u32[]{:S(2)}) collective-permute-start(f32[32,384]{1,0:T(8,128)S(1)} %add.65.one_ref), channel_id=1, source_target_pairs={{0,64},{64,0},{1,65},{65,1},{2,66},{66,2},{3,67},{67,3},{4,68},{68... | collective-permute-start | bytes 147464 | tf_op jit(solution)/shard_map/ppermute | solution.py:24
  29.0 3.0 %collective-permute-start.13 = (f32[32,384]{1,0:T(8,128)S(1)}, f32[32,384]{1,0:T(8,128)S(1)}, u32[]{:S(2)}, u32[]{:S(2)}) collective-permute-start(f32[32,384]{1,0:T(8,128)S(1)} %add.69.one_ref), channel_id=1, source_target_pairs={{0,64},{64,0},{1,65},{65,1},{2,66},{66,2},{3,67},{67,3},{4,68},{68... | collective-permute-start | bytes 147464 | tf_op jit(solution)/shard_map/ppermute | solution.py:24
  31.4 9.6 %copy-start.4 = (s32[3,3,24]{2,1,0:T(4,128)S(1)}, s32[3,3,24]{2,1,0:T(4,128)}, u32[]{:S(2)}) copy-start(s32[3,3,24]{2,1,0:T(4,128)} %param.15) | copy-start | bytes 2596
  31.4 9.6 %copy-start.2 = (bf16[3,384,768]{2,1,0:T(8,128)(2,1)S(1)}, bf16[3,384,768]{2,1,0:T(8,128)(2,1)}, u32[]{:S(2)}) copy-start(bf16[3,384,768]{2,1,0:T(8,128)(2,1)} %factor_ref.1) | copy-start | bytes 5308420
  31.4 3.8 %collective-permute-start.14 = (f32[32,768]{1,0:T(8,128)S(1)}, f32[32,768]{1,0:T(8,128)S(1)}, u32[]{:S(2)}, u32[]{:S(2)}) collective-permute-start(f32[32,768]{1,0:T(8,128)S(1)} %get-tuple-element.42), channel_id=1, source_target_pairs={{0,4},{1,5},{2,6},{3,7},{4,0},{5,1},{6,2},{7,3},{8,12},{9,13},{10,... | collective-permute-start | bytes 294920 | tf_op jit(solution)/shard_map/ppermute | solution.py:24
  32.3 6.9 %collective-permute-start.21 = (f32[32,768]{1,0:T(8,128)S(1)}, f32[32,768]{1,0:T(8,128)S(1)}, u32[]{:S(2)}, u32[]{:S(2)}) collective-permute-start(f32[32,768]{1,0:T(8,128)S(1)} %get-tuple-element.50), channel_id=1, source_target_pairs={{0,2},{1,3},{2,0},{3,1},{4,6},{5,7},{6,4},{7,5},{8,10},{9,11},{10,... | collective-permute-start | bytes 294920 | tf_op jit(solution)/shard_map/ppermute | solution.py:24
  34.4 5.7 %collective-permute-start.22 = (f32[32,768]{1,0:T(8,128)S(1)}, f32[32,768]{1,0:T(8,128)S(1)}, u32[]{:S(2)}, u32[]{:S(2)}) collective-permute-start(f32[32,768]{1,0:T(8,128)S(1)} %get-tuple-element.50), channel_id=1, source_target_pairs={{0,3},{1,2},{2,1},{3,0},{4,7},{5,6},{6,5},{7,4},{8,11},{9,10},{10,... | collective-permute-start | bytes 294920 | tf_op jit(solution)/shard_map/ppermute | solution.py:24
  35.2 5.0 %collective-permute-start.20 = (f32[32,768]{1,0:T(8,128)S(1)}, f32[32,768]{1,0:T(8,128)S(1)}, u32[]{:S(2)}, u32[]{:S(2)}) collective-permute-start(f32[32,768]{1,0:T(8,128)S(1)} %get-tuple-element.50), channel_id=1, source_target_pairs={{0,1},{1,0},{2,3},{3,2},{4,5},{5,4},{6,7},{7,6},{8,9},{9,8},{10,11... | collective-permute-start | bytes 294920 | tf_op jit(solution)/shard_map/ppermute | solution.py:24
  35.2 7.3 %collective-permute-start.15 = (f32[32,768]{1,0:T(8,128)S(1)}, f32[32,768]{1,0:T(8,128)S(1)}, u32[]{:S(2)}, u32[]{:S(2)}) collective-permute-start(f32[32,768]{1,0:T(8,128)S(1)} %add.70.refs_0_), channel_id=1, source_target_pairs={{0,2},{1,3},{2,0},{3,1},{4,6},{5,7},{6,4},{7,5},{8,10},{9,11},{10,... | collective-permute-start | bytes 294920 | tf_op jit(solution)/shard_map/ppermute | solution.py:24
  38.4 6.3 %collective-permute-start.16 = (f32[32,768]{1,0:T(8,128)S(1)}, f32[32,768]{1,0:T(8,128)S(1)}, u32[]{:S(2)}, u32[]{:S(2)}) collective-permute-start(f32[32,768]{1,0:T(8,128)S(1)} %add.70.refs_0_), channel_id=1, source_target_pairs={{0,3},{1,2},{2,1},{3,0},{4,7},{5,6},{6,5},{7,4},{8,11},{9,10},{10,... | collective-permute-start | bytes 294920 | tf_op jit(solution)/shard_map/ppermute | solution.py:24
  39.2 5.5 %collective-permute-start.17 = (f32[32,768]{1,0:T(8,128)S(1)}, f32[32,768]{1,0:T(8,128)S(1)}, u32[]{:S(2)}, u32[]{:S(2)}) collective-permute-start(f32[32,768]{1,0:T(8,128)S(1)} %add.70.refs_0_), channel_id=1, source_target_pairs={{0,1},{1,0},{2,3},{3,2},{4,5},{5,4},{6,7},{7,6},{8,9},{9,8},{10,11... | collective-permute-start | bytes 294920 | tf_op jit(solution)/shard_map/ppermute | solution.py:24
  40.2 6.9 %collective-permute-start.23 = (f32[32,768]{1,0:T(8,128)S(1)}, f32[32,768]{1,0:T(8,128)S(1)}, u32[]{:S(2)}, u32[]{:S(2)}) collective-permute-start(f32[32,768]{1,0:T(8,128)S(1)} %add_add_fusion.refs_0_), channel_id=1, source_target_pairs={{0,4},{1,5},{2,6},{3,7},{4,0},{5,1},{6,2},{7,3},{8,12},{9,13},{10,... | collective-permute-start | bytes 294920 | tf_op jit(solution)/shard_map/ppermute | solution.py:24
  44.9 3.5 %collective-permute-start.18 = (f32[32,384]{1,0:T(8,128)S(1)}, f32[32,384]{1,0:T(8,128)S(1)}, u32[]{:S(2)}, u32[]{:S(2)}) collective-permute-start(f32[32,384]{1,0:T(8,128)S(1)} %next_solve.6), channel_id=1, source_target_pairs={{0,32},{32,0},{1,33},{33,1},{2,34},{34,2},{3,35},{35,3},{4,36},{36... | collective-permute-start | bytes 147464 | tf_op jit(solution)/shard_map/ppermute | solution.py:24
  47.3 1.9 %collective-permute-start.24 = (f32[32,384]{1,0:T(8,128)S(1)}, f32[32,384]{1,0:T(8,128)S(1)}, u32[]{:S(2)}, u32[]{:S(2)}) collective-permute-start(f32[32,384]{1,0:T(8,128)S(1)} %next_solve.7), channel_id=1, source_target_pairs={{0,32},{32,0},{1,33},{33,1},{2,34},{34,2},{3,35},{35,3},{4,36},{36... | collective-permute-start | bytes 147464 | tf_op jit(solution)/shard_map/ppermute | solution.py:24
  48.4 3.4 %collective-permute-start.19 = (f32[32,384]{1,0:T(8,128)S(1)}, f32[32,384]{1,0:T(8,128)S(1)}, u32[]{:S(2)}, u32[]{:S(2)}) collective-permute-start(f32[32,384]{1,0:T(8,128)S(1)} %add.71.one_ref), channel_id=1, source_target_pairs={{0,64},{64,0},{1,65},{65,1},{2,66},{66,2},{3,67},{67,3},{4,68},{68... | collective-permute-start | bytes 147464 | tf_op jit(solution)/shard_map/ppermute | solution.py:24
  49.2 3.2 %collective-permute-start.25 = (f32[32,384]{1,0:T(8,128)S(1)}, f32[32,384]{1,0:T(8,128)S(1)}, u32[]{:S(2)}, u32[]{:S(2)}) collective-permute-start(f32[32,384]{1,0:T(8,128)S(1)} %add.75.one_ref), channel_id=1, source_target_pairs={{0,64},{64,0},{1,65},{65,1},{2,66},{66,2},{3,67},{67,3},{4,68},{68... | collective-permute-start | bytes 147464 | tf_op jit(solution)/shard_map/ppermute | solution.py:24
  52.0 23.6 %copy-start.1 = (bf16[768,1536]{1,0:T(8,128)(2,1)S(1)}, bf16[768,1536]{1,0:T(8,128)(2,1)}, u32[]{:S(2)}) copy-start(bf16[768,1536]{1,0:T(8,128)(2,1)} %inverse_ref.1) | copy-start | bytes 7077892
  61.1 4.3 %collective-permute-start.26 = (f32[8,768]{1,0:T(8,128)S(1)}, f32[8,768]{1,0:T(8,128)S(1)}, u32[]{:S(2)}, u32[]{:S(2)}) collective-permute-start(f32[8,768]{1,0:T(8,128)S(1)} %reduce_sum.9), channel_id=1, source_target_pairs={{0,128},{128,0},{1,129},{129,1},{2,130},{130,2},{3,131},{131,3},{4... | collective-permute-start | bytes 73736 | tf_op jit(solution)/shard_map/ppermute | solution.py:24
  65.4 4.2 %collective-permute-start.27 = (f32[8,768]{1,0:T(8,128)S(1)}, f32[8,768]{1,0:T(8,128)S(1)}, u32[]{:S(2)}, u32[]{:S(2)}) collective-permute-start(f32[8,768]{1,0:T(8,128)S(1)} %add.77), channel_id=1, source_target_pairs={{0,8},{8,0},{16,24},{24,16},{1,9},{9,1},{17,25},{25,17},{2,10},{10... | collective-permute-start | bytes 73736 | tf_op jit(solution)/shard_map/ppermute | solution.py:24
  69.6 6.0 %collective-permute-start.28 = (f32[8,768]{1,0:T(8,128)S(1)}, f32[8,768]{1,0:T(8,128)S(1)}, u32[]{:S(2)}, u32[]{:S(2)}) collective-permute-start(f32[8,768]{1,0:T(8,128)S(1)} %add.78.one_ref), channel_id=1, source_target_pairs={{0,24},{8,16},{16,8},{24,0},{1,25},{9,17},{17,9},{25,1},{2,26},{10... | collective-permute-start | bytes 73736 | tf_op jit(solution)/shard_map/ppermute | solution.py:24
  76.0 6.7 %collective-permute-start.29 = (f32[8,1536]{1,0:T(8,128)S(1)}, f32[8,1536]{1,0:T(8,128)S(1)}, u32[]{:S(2)}, u32[]{:S(2)}) collective-permute-start(f32[8,1536]{1,0:T(8,128)S(1)} %root_part.1), channel_id=1, source_target_pairs={{0,32},{32,0},{1,33},{33,1},{2,34},{34,2},{3,35},{35,3},{4,36},{36... | collective-permute-start | bytes 147464 | tf_op jit(solution)/shard_map/ppermute | solution.py:24
  82.7 2.9 %collective-permute-start.30 = (f32[8,1536]{1,0:T(8,128)S(1)}, f32[8,1536]{1,0:T(8,128)S(1)}, u32[]{:S(2)}, u32[]{:S(2)}) collective-permute-start(f32[8,1536]{1,0:T(8,128)S(1)} %add.79), channel_id=1, source_target_pairs={{0,64},{64,0},{1,65},{65,1},{2,66},{66,2},{3,67},{67,3},{4,68},{68... | collective-permute-start | bytes 147464 | tf_op jit(solution)/shard_map/ppermute | solution.py:24
